TPU v7x, 128 devices: a whole 4x4x4 slice. The times are simulated.
128 devices in a mesh: row: 8 (over z, y_hi), col: 4 (over y_lo, core), feat: 4 (over x).
Axes of the slice: x: 4, y: 4 (y_hi: 2, y_lo: 2; y = y_hi * 2 + y_lo), z: 4, core: 2. Of those that a mesh axis runs over, the one named last changes fastest.
Arguments:
- features: bfloat16 [262144, 128], P(('row', 'col'), 'feat'), may hold values from -6 to 6
- tiles: bfloat16 [8, 4, 1536, 128, 128], P('row', 'col', 'feat'), may hold values from 0 to 0.04321289
- tile_row: int32 [8, 4, 1536], P('row', 'col', 'feat'), may hold values from 0 to 255
- tile_col: int32 [8, 4, 1536], P('row', 'col', 'feat'), may hold values from 0 to 511
- tile_count: int32 [8, 4, 4], P('row', 'col', 'feat'), may hold values from 1 to 384, as said below
- weight: bfloat16 [128, 256], replicated, may hold values from -0.5 to 0.5
- bias: float32 [256], replicated, may hold values from -3 to 3
Outputs:
- output: bfloat16 [262144, 256], P(('row', 'col', 'feat'))
Inputs may be any that keep to these rules, and one draw needn't show every extreme that they name: `tile_count`: some device has all 384 slots live.
All inputs are finite; a program needn't handle non-finite values.
Results may differ from a plain program's by a relative error of at most 0.02.
Values may be sent and summed in bfloat16 or wider, within the bound.
No kernel may reach another device: no remote copies, remote signals or barrier semaphores. Data moves between devices by JAX's collectives and lax.ppermute only.
A program may use at most 128 MiB of HBM per device.

v0:
```python
import jax
import jax.numpy as jnp
from jax import lax
from jax.sharding import PartitionSpec as P


def body(features, tiles, tile_row, tile_col, tile_count, weight, bias):
    node_rows = lax.all_to_all(features, "feat", split_axis=0, concat_axis=1, tiled=True)
    sources = lax.all_gather(node_rows, ("row", "feat"), axis=0, tiled=True)
    tile_side = tiles.shape[-1]
    width = sources.shape[1]
    node_dev = features.shape[0] // lax.axis_size("feat")
    block_rows = lax.axis_size("col") * lax.axis_size("feat") * node_dev // tile_side
    src_blocks = sources.reshape(-1, tile_side, width)
    slot_total = tiles.shape[2]
    tile_stack = tiles.reshape(slot_total, tile_side, tile_side)
    row_index = tile_row.reshape(slot_total)
    col_index = tile_col.reshape(slot_total)
    live_count = tile_count.reshape(())
    block = min(32, slot_total)
    turns = (live_count + block - 1) // block

    def one_turn(turn, partial_value):
        start = turn * block
        tile_block = lax.dynamic_slice_in_dim(tile_stack, start, block, 0)
        rows_here = lax.dynamic_slice_in_dim(row_index, start, block, 0)
        cols_here = lax.dynamic_slice_in_dim(col_index, start, block, 0)
        picked = jnp.take(src_blocks, cols_here, axis=0)
        prods = jnp.einsum("tij,tjf->tif", tile_block, picked, preferred_element_type=jnp.float32)
        live = start + jnp.arange(block, dtype=jnp.int32) < live_count
        prods = jnp.where(live[:, None, None], prods, jnp.zeros_like(prods))
        return partial_value.at[rows_here].add(prods)

    empty = jnp.zeros((block_rows, tile_side, width), jnp.float32)
    partial_value = lax.fori_loop(0, turns, one_turn, empty)
    rounded = lax.optimization_barrier(
        partial_value.reshape(block_rows * tile_side, width).astype(jnp.bfloat16)
    )
    terms = rounded.astype(jnp.float32)
    agg = lax.psum_scatter(
        terms.astype(jnp.bfloat16), ("col", "feat"), scatter_dimension=0, tiled=True
    )
    hidden = jnp.dot(agg, weight, preferred_element_type=jnp.float32) + bias
    return jax.nn.relu(hidden).astype(jnp.bfloat16)


def solution(mesh):
    placed = (
        P(("row", "col"), "feat"),
        P("row", "col", "feat", None, None),
        P("row", "col", "feat"),
        P("row", "col", "feat"),
        P("row", "col", "feat"),
        P(),
        P(),
    )
    return jax.shard_map(
        body, mesh=mesh, in_specs=placed, out_specs=P(("row", "col", "feat"), None), check_vma=False
    )
```

profile of v0, /device:TPU:0, one launch (start us, length us, event | category | flops | bytes accessed | tf_op | source)
XLA Modules:
  0.0 500.7 jit_solution(782019901176667349)
XLA Ops:
  6.5 0.0 copy-start
  6.5 0.0 all-gather.2.cloned.1.call-start
  6.5 1.1 copy.17
  7.7 13.8 %all_to_all.19 = bf16[4,2048,32]{1,2,0:T(8,128)(2,1)} all-to-all(bf16[4,2048,32]{1,2,0:T(8,128)(2,1)S(1)} %bitcast.18), channel_id=1, replica_groups=mesh['row'=8,'col'=4,'feat'=4] {'feat'}, dimensions={0} | all-to-all | bytes 1048576 | tf_op jit(solution)/shard_map/all_to_all | solution.py:8
  21.4 0.0 all-gather.2.cloned.1.call-update
  21.4 0.0 reduce-scatter.2.cloned.1.call-start
  22.1 0.7 reduce
  22.8 0.7 reduce.1
  23.6 150.1 %all-gather.2.cloned.1.call-done = bf16[65536,128]{0,1:T(8,128)(2,1)} async-done(((bf16[2048,128]{0,1:T(8,128)(2,1)}), bf16[65536,128]{0,1:T(8,128)(2,1)}) %all-gather.2.cloned.1.call-update) | async-done | bytes 16777232 | tf_op jit(solution)/shard_map/all_gather | solution.py:9
  173.7 22.4 %copy.14 = bf16[65536,128]{1,0:T(8,128)(2,1)} copy(bf16[65536,128]{0,1:T(8,128)(2,1)} %all-gather.2.cloned.1.call-done) | data formatting | bytes 33554432 | tf_op jit(solution)/shard_map/while | solution.py:35
  196.1 7.8 %broadcast_in_dim.28 = f32[256,128,128]{2,1,0:T(8,128)} broadcast(f32[]{:T(128)} %constant.47.clone.1), dimensions={} | broadcast | bytes 16777220 | tf_op jit(solution)/shard_map/broadcast_in_dim | solution.py:34
  203.9 45.8 %while.10 = (s32[]{:T(128)}, f32[256,128,128]{2,1,0:T(8,128)}, s32[]{:T(128)}, s32[384]{0:T(512)S(1)}, s32[]{:T(128)}, /*index=5*/bf16[384,128,128]{2,1,0:T(8,12...) while((s32[]{:T(128)}, f32[256,128,128]{2,1,0:T(8,128)}, ...), condition=%wide.region_2.3_spmd, body=%wide.region_0.2_spmd.sunk | while | flops 135791968 | bytes 12588215 | solution.py:35
  203.9 0.1 compare_select_fusion.4
  204.0 0.7 compare_and_fusion.2
  204.8 6.5 %gather_fusion = bf16[32,128,128]{2,1,0:T(8,128)(2,1)S(1)} fusion(bf16[512,128,128]{2,1,0:T(8,128)(2,1)} %get-tuple-element.179, s32[1024]{0:T(1024)S(1)} %pad_clamp_fusion.2), kind=kCustom, calls=%fused_computation.clone.1 | custom fusion | bytes 2097280 | tf_op jit(solution)/shard_map/while/body/jit(_take)/gather | solution.py:28
  211.3 1.7 convolution_select_fusion.2
  213.0 6.1 %scatter_fusion = f32[256,128,128]{2,1,0:T(8,128)} fusion(f32[256,128,128]{2,1,0:T(8,128)} %get-tuple-element.161, s32[32]{0:T(128)S(1)} %compare_select_fusion.4, f32[32,128,128]{2,1,0:T(8,128)S(1)} %convolution_select_fusion.2), kind=kCustom, calls=%fused_computation.1.clone.1 | custom fusion | flops 524288 | bytes 6291584 | tf_op jit(solution)/shard_map/while/body/scatter-add | solution.py:32
  219.2 0.1 compare_select_fusion.4
  219.2 0.7 compare_and_fusion.2
  220.0 6.5 %gather_fusion = bf16[32,128,128]{2,1,0:T(8,128)(2,1)S(1)} fusion(bf16[512,128,128]{2,1,0:T(8,128)(2,1)} %get-tuple-element.179, s32[1024]{0:T(1024)S(1)} %pad_clamp_fusion.2), kind=kCustom, calls=%fused_computation.clone.1 | custom fusion | bytes 2097280 | tf_op jit(solution)/shard_map/while/body/jit(_take)/gather | solution.py:28
  226.5 1.7 convolution_select_fusion.2
  228.2 6.2 %scatter_fusion = f32[256,128,128]{2,1,0:T(8,128)} fusion(f32[256,128,128]{2,1,0:T(8,128)} %get-tuple-element.161, s32[32]{0:T(128)S(1)} %compare_select_fusion.4, f32[32,128,128]{2,1,0:T(8,128)S(1)} %convolution_select_fusion.2), kind=kCustom, calls=%fused_computation.1.clone.1 | custom fusion | flops 524288 | bytes 6291584 | tf_op jit(solution)/shard_map/while/body/scatter-add | solution.py:32
  234.5 0.1 compare_select_fusion.4
  234.5 0.7 compare_and_fusion.2
  235.3 6.5 %gather_fusion = bf16[32,128,128]{2,1,0:T(8,128)(2,1)S(1)} fusion(bf16[512,128,128]{2,1,0:T(8,128)(2,1)} %get-tuple-element.179, s32[1024]{0:T(1024)S(1)} %pad_clamp_fusion.2), kind=kCustom, calls=%fused_computation.clone.1 | custom fusion | bytes 2097280 | tf_op jit(solution)/shard_map/while/body/jit(_take)/gather | solution.py:28
  241.8 1.7 convolution_select_fusion.2
  243.5 6.2 %scatter_fusion = f32[256,128,128]{2,1,0:T(8,128)} fusion(f32[256,128,128]{2,1,0:T(8,128)} %get-tuple-element.161, s32[32]{0:T(128)S(1)} %compare_select_fusion.4, f32[32,128,128]{2,1,0:T(8,128)S(1)} %convolution_select_fusion.2), kind=kCustom, calls=%fused_computation.1.clone.1 | custom fusion | flops 524288 | bytes 6291584 | tf_op jit(solution)/shard_map/while/body/scatter-add | solution.py:32
  249.8 9.2 %convert_element_type.11 = bf16[256,128,128]{2,1,0:T(8,128)(2,1)} convert(f32[256,128,128]{2,1,0:T(8,128)} %get-tuple-element.48) | non-fusion elementwise | flops 4194304 | bytes 25165824 | tf_op jit(solution)/shard_map/convert_element_type | solution.py:37
  259.0 0.0 reduce-scatter.2.cloned.1.call-update
  259.0 232.4 %reduce-scatter.2.cloned.1.call-done = bf16[2048,128]{1,0:T(8,128)(2,1)} async-done(((bf16[32768,128]{1,0:T(8,128)(2,1)}), bf16[2048,128]{1,0:T(8,128)(2,1)}) %reduce-scatter.2.cloned.1.call-update) | async-done | bytes 524304 | tf_op jit(solution)/shard_map/reduce_scatter | solution.py:40
  491.5 0.0 copy-done
  491.5 2.4 fusion.7
  (5 shorter events, 0.0 us)
Async XLA Ops:
  6.5 484.9 %copy-start = (bf16[128,256]{1,0:T(8,128)(2,1)S(1)}, bf16[128,256]{1,0:T(8,128)(2,1)}, u32[]{:S(2)}) copy-start(bf16[128,256]{1,0:T(8,128)(2,1)} %param.14) | copy-start | bytes 196612
  6.5 167.2 %all-gather.2.cloned.1.call-start = ((), (), s32[]{:S(2)}) async-start(), calls=%async_computation.2 | async-start | bytes 17301504 | tf_op jit(solution)/shard_map/all_gather | solution.py:9
  21.4 470.0 %reduce-scatter.2.cloned.1.call-start = ((), (), s32[]{:S(2)}) async-start(), calls=%async_computation.3 | async-start | bytes 8912896 | tf_op jit(solution)/shard_map/reduce_scatter | solution.py:40
  249.8 241.7 %copy-start.1 = (f32[256]{0:T(256)S(1)}, f32[256]{0:T(256)}, u32[]{:S(2)}) copy-start(f32[256]{0:T(256)} %param.15) | copy-start | bytes 3076
Sparse Core Ops, SparseCore 0:
  21.6 152.0 all-gather.1
  259.1 232.2 reduce-scatter.1
where the time goes:
time: 504 us; the launch traced here: 501 us
  waiting for transfers between devices  383 us (76%)
  local copies, waits for them, and re-layouts  50.9 us (10%)
  other arithmetic  31.6 us (6%)
  between operations  14.1 us (3%)
  blocking collectives  13.8 us (3%)
  matrix products  7.64 us (2%)
    reduce_scatter x1, waiting for transfers between devices, body(): lax.psum_scatter(terms.astype(jnp.bfloat16), ('col', 'feat'), scatter_dim...  232 us
    all_gather x1, waiting for transfers between devices, body(): sources = lax.all_gather(node_rows, ('row', 'feat'), axis=0, tiled=True)  150 us
    while x1, local copies, waits for them, and re-layouts, body(): partial_value = lax.fori_loop(0, turns, one_turn, empty)  22.4 us
    gather x3, local copies, waits for them, and re-layouts, one_turn(): picked = jnp.take(src_blocks, cols_here, axis=0)  19.6 us
    scatter-add x3, other arithmetic, one_turn(): return partial_value.at[rows_here].add(prods)  18.6 us
    all_to_all x1, blocking collectives, body(): lax.all_to_all(features, 'feat', split_axis=0, concat_axis=1, tiled=True)  13.8 us
  transfers between devices with their start and end apart: 2, of which 2 were waited for; matrix products, arithmetic and copies ran while one was open for 0% of the time, Pallas kernels for 0%

commit v1 on v0

v1 whole, which is shorter than its diff:
```python
import jax
import jax.numpy as jnp
from jax import lax
from jax.experimental import pallas as pl
from jax.experimental.pallas import tpu as pltpu
from jax.sharding import PartitionSpec as P

LOAD = 32
STEP = 4
NT = (((1,), (1,)), ((), ()))


def aggregate_kernel(
    rows_ref, cols_ref, count_ref, tiles_hbm, src_hbm, out_hbm,
    tiles, src, acc, stage, tile_sem, src_sem, out_sem,
):
    side = tiles.shape[-1]
    per_row = src.shape[-1] // side
    count = count_ref[0]
    loads = (count + LOAD - 1) // LOAD

    def tile_copy(i):
        part = pl.ds(pl.multiple_of(i * LOAD, LOAD), LOAD)
        return pltpu.make_async_copy(tiles_hbm.at[part], tiles.at[part], tile_sem.at[i])

    def src_copy(r):
        return pltpu.make_async_copy(src_hbm.at[r], src.at[r], src_sem.at[r])

    groups = src.shape[0]
    for r in range(groups):
        src_copy(r).start()

    @pl.loop(0, loads)
    def _(i):
        tile_copy(i).start()

    zero_rows = 1024
    zeros = jnp.zeros((zero_rows, side), jnp.float32)

    @pl.loop(0, acc.shape[0] // zero_rows)
    def _(i):
        acc[pl.ds(pl.multiple_of(i * zero_rows, zero_rows), zero_rows), :] = zeros

    for r in range(groups):
        src_copy(r).wait()

    def product(k):
        col = cols_ref[k]
        group = col // per_row
        lane = pl.multiple_of((col % per_row) * side, side)
        block = src[group, :, pl.ds(lane, side)]
        return lax.dot_general(tiles[k], block, NT, preferred_element_type=jnp.float32)

    def add(k, value):
        at = pl.ds(pl.multiple_of(rows_ref[k] * side, side), side)
        acc[at, :] += value

    @pl.loop(0, loads)
    def _(i):
        tile_copy(i).wait()
        first = i * LOAD
        here = jnp.minimum(count - first, LOAD)
        whole = here // STEP

        @pl.loop(0, whole)
        def _(s):
            k = first + s * STEP
            values = [product(k + t) for t in range(STEP)]
            for t in range(STEP):
                add(k + t, values[t])

        @pl.loop(whole * STEP, here)
        def _(s):
            add(first + s, product(first + s))

    chunk = stage.shape[1]
    chunks = acc.shape[0] // chunk

    def out_copy(i):
        slot = i % 2
        part = pl.ds(pl.multiple_of(i * chunk, chunk), chunk)
        return pltpu.make_async_copy(stage.at[slot], out_hbm.at[part], out_sem.at[slot])

    for i in range(chunks):
        if i >= 2:
            out_copy(i - 2).wait()
        stage[i % 2] = acc[i * chunk : (i + 1) * chunk, :].astype(jnp.bfloat16)
        out_copy(i).start()
    for i in range(chunks - 2, chunks):
        out_copy(i).wait()


def aggregate(tiles, rows, cols, count, src, out_rows):
    slots, side, _ = tiles.shape
    any_space = pl.BlockSpec(memory_space=pl.ANY)
    return pl.pallas_call(
        aggregate_kernel,
        out_shape=jax.ShapeDtypeStruct((out_rows, side), jnp.bfloat16),
        grid_spec=pltpu.PrefetchScalarGridSpec(
            num_scalar_prefetch=3,
            grid=(1,),
            in_specs=[any_space, any_space],
            out_specs=any_space,
            scratch_shapes=[
                pltpu.VMEM(tiles.shape, jnp.bfloat16),
                pltpu.VMEM(src.shape, jnp.bfloat16),
                pltpu.VMEM((out_rows, side), jnp.float32),
                pltpu.VMEM((2, 2048, side), jnp.bfloat16),
                pltpu.SemaphoreType.DMA((slots // LOAD,)),
                pltpu.SemaphoreType.DMA((src.shape[0],)),
                pltpu.SemaphoreType.DMA((2,)),
            ],
        ),
        compiler_params=pltpu.CompilerParams(vmem_limit_bytes=56 * 2**20),
        name="aggregate",
    )(rows, cols, count, tiles, src)


def body(features, tiles, tile_row, tile_col, tile_count, weight, bias):
    n_row, n_feat = lax.axis_size("row"), lax.axis_size("feat")
    group = features.shape[0]
    node_dev = group // n_feat
    src = lax.all_gather(features.T, ("row", "feat")).reshape(n_row, -1, group)
    slots, side = tiles.shape[2], tiles.shape[3]
    partial = aggregate(
        tiles.reshape(slots, side, side),
        tile_row.reshape(slots),
        tile_col.reshape(slots),
        tile_count.reshape(1),
        src,
        lax.axis_size("col") * n_feat * node_dev,
    )
    agg = lax.psum_scatter(partial, ("col", "feat"), scatter_dimension=0, tiled=True)
    hidden = jnp.dot(agg, weight, preferred_element_type=jnp.float32) + bias
    return jax.nn.relu(hidden).astype(jnp.bfloat16)


def solution(mesh):
    placed = (
        P(("row", "col"), "feat"),
        P("row", "col", "feat", None, None),
        P("row", "col", "feat"),
        P("row", "col", "feat"),
        P("row", "col", "feat"),
        P(),
        P(),
    )
    return jax.shard_map(
        body, mesh=mesh, in_specs=placed, out_specs=P(("row", "col", "feat"), None), check_vma=False
    )
```

time: 504 us -> 310 us (0.62)
  waiting for transfers between devices: 383 us -> 254 us
  local copies, waits for them, and re-layouts: 50.9 us -> 0.01 us
  Pallas kernels: 0 us -> 36.2 us
  other arithmetic: 31.6 us -> 2.55 us
  blocking collectives: 13.8 us -> 0 us
  matrix products: 7.64 us -> 2.43 us
    reduce_scatter x1, waiting for transfers between devices: 232 us -> 95.6 us  [body(): lax.psum_scatter(partial, ('col', 'feat'), scatter_dimension=0, tiled=True)]
    pallas_call x0 -> x1, Pallas kernels: none -> 36.2 us  [aggregate(): pl.pallas_call(aggregate_kernel, out_shape=jax.ShapeDtypeStruct((out_rows...]
    while x1 -> x0, local copies, waits for them, and re-layouts: 22.4 us -> none  [body(): partial_value = lax.fori_loop(0, turns, one_turn, empty)]
    gather x3 -> x0, local copies, waits for them, and re-layouts: 19.6 us -> none  [one_turn(): picked = jnp.take(src_blocks, cols_here, axis=0)]
    scatter-add x3 -> x0, other arithmetic: 18.6 us -> none  [one_turn(): return partial_value.at[rows_here].add(prods)]
    all_to_all x1 -> x0, blocking collectives: 13.8 us -> none  [body(): lax.all_to_all(features, 'feat', split_axis=0, concat_axis=1, tiled=True)]
    convert_element_type x1 -> x0, other arithmetic: 9.21 us -> none  [body(): partial_value.reshape(block_rows * tile_side, width).astype(jnp.bfloat16)]
    broadcast_in_dim x1 -> x0, local copies, waits for them, and re-layouts: 7.84 us -> none  [body(): empty = jnp.zeros((block_rows, tile_side, width), jnp.float32)]
  transfers between devices with their start and end apart: 2 -> 2, of which waited for: 2 -> 2; matrix products, arithmetic and copies ran while one was open for 0% -> 1% of each run, Pallas kernels for 0% -> 0%
where the time goes in v1:
time: 310 us; the launch traced here: 309 us
  waiting for transfers between devices  254 us (82%)
  Pallas kernels  36.2 us (12%)
  between operations  14.1 us (5%)
    all_gather x1, waiting for transfers between devices, body(): src = lax.all_gather(features.T, ('row', 'feat')).reshape(n_row, -1, group)  158 us
    reduce_scatter x1, waiting for transfers between devices, body(): lax.psum_scatter(partial, ('col', 'feat'), scatter_dimension=0, tiled=True)  95.6 us
    pallas_call x1, Pallas kernels, aggregate(): pl.pallas_call(aggregate_kernel, out_shape=jax.ShapeDtypeStruct((out_rows...  36.2 us
  transfers between devices with their start and end apart: 2, of which 2 were waited for; matrix products, arithmetic and copies ran while one was open for 1% of the time, Pallas kernels for 0%

profile of v1, /device:TPU:0, one launch (start us, length us, event | category | flops | bytes accessed | tf_op | source)
XLA Modules:
  0.0 309.4 jit_solution(1298590261998130204)
XLA Ops:
  6.5 0.0 copy-start
  6.5 0.0 all-gather.3.cloned.1.call-start
  6.5 0.7 all-gather.3.cloned.1.call-update
  7.3 0.0 reduce-scatter.2.cloned.1.call-start
  8.0 1.3 reduce.rows_ref
  9.2 1.3 reduce.1.cols_ref
  10.5 157.7 %all-gather.3.cloned.1.call-done = bf16[1024,8192]{1,0:T(8,128)(2,1)} async-done(((bf16[32,8192]{1,0:T(8,128)(2,1)}), bf16[1024,8192]{1,0:T(8,128)(2,1)}) %all-gather.3.cloned.1.call-update) | async-done | bytes 16777232 | tf_op jit(solution)/shard_map/all_gather | solution.py:123
  168.2 36.2 %aggregate.1 = bf16[32768,128]{1,0:T(8,128)(2,1)} custom-call(s32[384]{0:T(512)} %reduce.rows_ref, s32[384]{0:T(512)} %reduce.1.cols_ref, s32[1]{0:T(128)} %bitcast.6.count_ref, bf16[384,128,128]{2,1,0:T(8,128)(2,1)} %bitcast.8, bf16[8,128,8192]{2,1,0:T(8,128)(2,1)} %bitcast.7), custom_call_target="tpu_custom_call" | custom-call | tf_op jit(solution)/shard_map/aggregate/pallas_call | solution.py:96
  204.4 0.0 copy-start.1
  204.4 0.0 reduce-scatter.2.cloned.1.call-update
  204.5 95.6 %reduce-scatter.2.cloned.1.call-done = bf16[2048,128]{1,0:T(8,128)(2,1)} async-done(((bf16[32768,128]{1,0:T(8,128)(2,1)}), bf16[2048,128]{1,0:T(8,128)(2,1)}) %reduce-scatter.2.cloned.1.call-update) | async-done | bytes 524304 | tf_op jit(solution)/shard_map/reduce_scatter | solution.py:133
  300.1 0.0 copy-done
  300.1 0.0 copy-done.1
  300.1 2.4 fusion.1
Async XLA Ops:
  6.5 293.6 %copy-start = (bf16[128,256]{1,0:T(8,128)(2,1)S(1)}, bf16[128,256]{1,0:T(8,128)(2,1)}, u32[]{:S(2)}) copy-start(bf16[128,256]{1,0:T(8,128)(2,1)} %param.12) | copy-start | bytes 196612
  6.5 161.7 %all-gather.3.cloned.1.call-start = ((), (), s32[]{:S(2)}) async-start(), calls=%async_computation.2 | async-start | bytes 17301504 | tf_op jit(solution)/shard_map/all_gather | solution.py:123
  7.3 292.8 %reduce-scatter.2.cloned.1.call-start = ((), (), s32[]{:S(2)}) async-start(), calls=%async_computation.1 | async-start | bytes 8912896 | tf_op jit(solution)/shard_map/reduce_scatter | solution.py:133
  204.4 95.7 %copy-start.1 = (f32[256]{0:T(256)S(1)}, f32[256]{0:T(256)}, u32[]{:S(2)}) copy-start(f32[256]{0:T(256)} %param.13) | copy-start | bytes 3076
Sparse Core Ops, SparseCore 0:
  10.6 157.6 all-gather.2
  204.6 95.4 reduce-scatter.1

commit v2 on v1

v2 whole, which is shorter than its diff:
```python
import jax
import jax.numpy as jnp
from jax import lax
from jax.experimental import pallas as pl
from jax.experimental.pallas import tpu as pltpu
from jax.sharding import Mesh
from jax.sharding import PartitionSpec as P

LOAD = 32
STEP = 4
EARLY = 20
FIRST_X = 1024
NT = (((1,), (1,)), ((), ()))
NAMES = ("rz", "ry", "cy", "cc", "fx")


def aggregate_kernel(
    rows_ref, cols_ref, info_ref, tiles_hbm, p0, p1, q0, q1, keep_a, keep_b, send_a, send_b,
    tiles, src, acc, stage, tile_sem, src_sem, out_sem,
):
    side = tiles.shape[-1]
    per_row = src.shape[-1] // side
    count, ry, cy, cc, fx = (info_ref[i] for i in range(5))
    loads = (count + LOAD - 1) // LOAD

    def tile_copy(i):
        part = pl.ds(pl.multiple_of(i * LOAD, LOAD), LOAD)
        return pltpu.make_async_copy(tiles_hbm.at[part], tiles.at[part], tile_sem.at[i])

    early = p0.shape[-1]
    src_copies = []
    for n, (ref, plane, lanes) in enumerate(
        (
            (p0, ry, pl.ds(0, early)),
            (p1, 1 - ry, pl.ds(0, early)),
            (q0, ry, pl.ds(early, q0.shape[-1])),
            (q1, 1 - ry, pl.ds(early, q1.shape[-1])),
        )
    ):
        for z in range(ref.shape[0]):
            src_copies.append(
                pltpu.make_async_copy(
                    ref.at[z], src.at[2 * z + plane, :, lanes], src_sem.at[4 * n + z]
                )
            )
    for copy in src_copies:
        copy.start()

    @pl.loop(0, loads)
    def _(i):
        tile_copy(i).start()

    zero_rows = 1024
    zeros = jnp.zeros((zero_rows, side), jnp.float32)

    @pl.loop(0, acc.shape[0] // zero_rows)
    def _(i):
        acc[pl.ds(pl.multiple_of(i * zero_rows, zero_rows), zero_rows), :] = zeros

    for copy in src_copies:
        copy.wait()

    def product(k):
        col = cols_ref[k]
        group = col // per_row
        lane = pl.multiple_of((col % per_row) * side, side)
        block = src[group, :, pl.ds(lane, side)]
        return lax.dot_general(tiles[k], block, NT, preferred_element_type=jnp.float32)

    def add(k, value):
        at = pl.ds(pl.multiple_of(rows_ref[k] * side, side), side)
        acc[at, :] += value

    @pl.loop(0, loads)
    def _(i):
        tile_copy(i).wait()
        first = i * LOAD
        here = jnp.minimum(count - first, LOAD)
        whole = here // STEP

        @pl.loop(0, whole)
        def _(s):
            k = first + s * STEP
            values = [product(k + t) for t in range(STEP)]
            for t in range(STEP):
                add(k + t, values[t])

        @pl.loop(whole * STEP, here)
        def _(s):
            add(first + s, product(first + s))

    chunk = stage.shape[1]
    copies = []
    for n in range(16):
        other, y, d = n < 8, 1 - (n // 4) % 2, n % 4
        slot = n % 2
        if n >= 2:
            for copy in copies[n - 2]:
                copy.wait()
        core = 1 - cc if other else cc
        shard = (jnp.bitwise_xor(cy, y) * 2 + core) * 4 + (fx + d) % 4
        stage[slot] = acc[pl.ds(pl.multiple_of(shard * chunk, chunk), chunk), :].astype(jnp.bfloat16)
        out_a, out_b = (send_a, send_b) if other else (keep_a, keep_b)
        copies.append(
            [
                pltpu.make_async_copy(
                    stage.at[slot, pl.ds(0, FIRST_X)], out_a.at[d, y], out_sem.at[slot, 0]
                ),
                pltpu.make_async_copy(
                    stage.at[slot, pl.ds(FIRST_X, chunk - FIRST_X)], out_b.at[y, d], out_sem.at[slot, 1]
                ),
            ]
        )
        for copy in copies[n]:
            copy.start()
    for n in (14, 15):
        for copy in copies[n]:
            copy.wait()


def aggregate(tiles, rows, cols, info, parts, node_dev):
    slots, side, _ = tiles.shape
    any_space = pl.BlockSpec(memory_space=pl.ANY)
    early, group = parts[0].shape[-1], parts[0].shape[-1] + parts[2].shape[-1]
    part_a = jax.ShapeDtypeStruct((4, 2, FIRST_X, side), jnp.bfloat16)
    part_b = jax.ShapeDtypeStruct((2, 4, node_dev - FIRST_X, side), jnp.bfloat16)
    return pl.pallas_call(
        aggregate_kernel,
        out_shape=(part_a, part_b, part_a, part_b),
        grid_spec=pltpu.PrefetchScalarGridSpec(
            num_scalar_prefetch=3,
            grid=(1,),
            in_specs=[any_space] * 5,
            out_specs=(any_space,) * 4,
            scratch_shapes=[
                pltpu.VMEM(tiles.shape, jnp.bfloat16),
                pltpu.VMEM((8, side, group), jnp.bfloat16),
                pltpu.VMEM((16 * node_dev, side), jnp.float32),
                pltpu.VMEM((2, node_dev, side), jnp.bfloat16),
                pltpu.SemaphoreType.DMA((slots // LOAD,)),
                pltpu.SemaphoreType.DMA((16,)),
                pltpu.SemaphoreType.DMA((2, 2)),
            ],
        ),
        compiler_params=pltpu.CompilerParams(vmem_limit_bytes=56 * 2**20),
        name="aggregate",
    )(rows, cols, info, tiles, *parts)


def swap(value, axis):
    return lax.ppermute(value, axis, [(0, 1), (1, 0)])


def shift(value, axis, by):
    n = lax.axis_size(axis)
    return lax.ppermute(value, axis, [(i, (i + by) % n) for i in range(n)])


def total(*values):
    wide = values[0].astype(jnp.float32)
    for value in values[1:]:
        wide = wide + value.astype(jnp.float32)
    return wide


def low(value):
    return value.astype(jnp.bfloat16)


def gather_sources(x):
    early = EARLY * 128
    p, q = x[:, :early], x[:, early:]
    q_other = swap(q, "ry")

    def plane(value):
        return lax.all_gather(value, ("rz", "fx")).reshape(4, -1, value.shape[-1])

    p0 = plane(p)
    p1 = swap(p0, "ry")
    return p0, p1, plane(q), plane(q_other)


def reduce_rows(keep_a, keep_b, send_a, send_b):
    got_b = swap(send_b, "cc")
    got_a = swap(send_a, "cc")
    b = swap(low(total(keep_b[1], got_b[1])), "cy")
    a = [shift(low(total(keep_a[d], got_a[d])), "fx", d) for d in (1, 2, 3)]
    b_here = [low(total(keep_b[0, d], got_b[0, d], b[d])) for d in (1, 2, 3)]
    b_got = [shift(v, "fx", d) for v, d in zip(b_here, (1, 2, 3))]
    a_here = total(keep_a[0], got_a[0], *a)
    a_got = swap(low(a_here[1]), "cy")
    a_sum = a_here[0] + a_got.astype(jnp.float32)
    b_sum = total(keep_b[0, 0], got_b[0, 0], b[0], *b_got)
    return jnp.concatenate([low(a_sum), low(b_sum)], axis=0)


def body(features, tiles, tile_row, tile_col, tile_count, weight, bias):
    node_dev = features.shape[0] // lax.axis_size("fx")
    slots, side = tiles.shape[2], tiles.shape[3]
    place = [lax.axis_index(n) for n in NAMES[1:]]
    info = jnp.stack([tile_count.reshape(())] + [i.astype(jnp.int32) for i in place])
    parts = aggregate(
        tiles.reshape(slots, side, side),
        tile_row.reshape(slots),
        tile_col.reshape(slots),
        info,
        gather_sources(features.T),
        node_dev,
    )
    agg = reduce_rows(*parts)
    hidden = jnp.dot(agg, weight, preferred_element_type=jnp.float32) + bias
    return jax.nn.relu(hidden).astype(jnp.bfloat16)


def solution(mesh):
    fine = Mesh(mesh.devices.reshape(4, 2, 2, 2, 4), NAMES)
    row, col = ("rz", "ry"), ("cy", "cc")
    placed = (
        P(row + col, "fx"),
        P(row, col, "fx", None, None),
        P(row, col, "fx"),
        P(row, col, "fx"),
        P(row, col, "fx"),
        P(),
        P(),
    )
    return jax.shard_map(
        body, mesh=fine, in_specs=placed, out_specs=P(NAMES, None), check_vma=False
    )
```

time: 310 us -> 275 us (0.89)
  waiting for transfers between devices: 254 us -> 194 us
  starting transfers between devices: 0.04 us -> 27.8 us
  Pallas kernels: 36.2 us -> 26.6 us
  local copies, waits for them, and re-layouts: 0.01 us -> 4.83 us
  other arithmetic: 2.55 us -> 6.73 us
    ppermute x0 -> x12, waiting for transfers between devices: none -> 97.3 us  [the longest x6 67.7 us: swap(): return lax.ppermute(value, axis, [(0, 1), (1, 0)])]
    reduce_scatter x1 -> x0, waiting for transfers between devices: 95.6 us -> none  [body(): lax.psum_scatter(partial, ('col', 'feat'), scatter_dimension=0, tiled=True)]
    all_gather x1 -> x3, waiting for transfers between devices: 158 us -> 96.7 us  [plane(): return lax.all_gather(value, ('rz', 'fx')).reshape(4, -1, value.shape[-1])]
    ppermute x0 -> x12, starting transfers between devices: none -> 27.8 us  [the longest x6 20 us: swap(): return lax.ppermute(value, axis, [(0, 1), (1, 0)])]
    pallas_call x1, Pallas kernels: 36.2 us -> 26.6 us  [aggregate(): pl.pallas_call(aggregate_kernel, out_shape=(part_a, part_b, part_a, part_...]
    slice x0 -> x2, local copies, waits for them, and re-layouts: none -> 3.36 us  [gather_sources(): p, q = (x[:, :early], x[:, early:])]
  transfers between devices with their start and end apart: 2 -> 15, of which waited for: 2 -> 13; matrix products, arithmetic and copies ran while one was open for 1% -> 3% of each run, Pallas kernels for 0% -> 0%
where the time goes in v2:
time: 275 us
  waiting for transfers between devices  194 us (71%)
  starting transfers between devices  27.8 us (10%)
  Pallas kernels  26.6 us (10%)
  between operations  13.8 us (5%)
  other arithmetic  6.73 us (2%)
  local copies, waits for them, and re-layouts  4.83 us (2%)
    all_gather x3, waiting for transfers between devices, plane(): return lax.all_gather(value, ('rz', 'fx')).reshape(4, -1, value.shape[-1])  96.7 us
    ppermute x6, waiting for transfers between devices, swap(): return lax.ppermute(value, axis, [(0, 1), (1, 0)])  67.7 us
    ppermute x6, waiting for transfers between devices, shift(): return lax.ppermute(value, axis, [(i, (i + by) % n) for i in range(n)])  29.5 us
    pallas_call x1, Pallas kernels, aggregate(): pl.pallas_call(aggregate_kernel, out_shape=(part_a, part_b, part_a, part_...  26.6 us
    ppermute x6, starting transfers between devices, swap(): return lax.ppermute(value, axis, [(0, 1), (1, 0)])  20 us
    ppermute x6, starting transfers between devices, shift(): return lax.ppermute(value, axis, [(i, (i + by) % n) for i in range(n)])  7.74 us
  transfers between devices with their start and end apart: 15, of which 13 were waited for; matrix products, arithmetic and copies ran while one was open for 3% of the time, Pallas kernels for 0%

profile of v2, /device:TPU:0, one launch (start us, length us, event | category | flops | bytes accessed | tf_op | source)
XLA Modules:
  0.0 275.2 jit_solution(3695086504002275643)
XLA Ops:
  6.5 1.6 slice.105
  8.2 1.7 slice.106
  10.0 3.4 %collective-permute-start.1 = (bf16[32,5632]{1,0:T(8,128)(2,1)}, bf16[32,5632]{1,0:T(8,128)(2,1)S(1)}, u32[]{:S(2)}, u32[]{:S(2)}) collective-permute-start(bf16[32,5632]{1,0:T(8,128)(2,1)} %slice.106), channel_id=1, source_target_pairs={{0,16},{16,0},{1,17},{17,1},{2,18},{18,2},{3,19},{19,3},{4,20},{20... | collective-permute-start | bytes 1081352 | tf_op jit(solution)/shard_map/ppermute | solution.py:151
  13.4 8.6 %collective-permute-done.1 = bf16[32,5632]{1,0:T(8,128)(2,1)S(1)} collective-permute-done((bf16[32,5632]{1,0:T(8,128)(2,1)}, bf16[32,5632]{1,0:T(8,128)(2,1)S(1)}, u32[]{:S(2)}, u32[]{:S(2)}) %collective-permute-start.1) | collective-permute-done | bytes 360480 | tf_op jit(solution)/shard_map/ppermute | solution.py:151
  22.0 0.7 copy-done.3
  22.8 35.6 %all-gather.7.cloned.1.call-done = bf16[512,2560]{1,0:T(8,128)(2,1)} async-done(((bf16[32,2560]{1,0:T(8,128)(2,1)}), bf16[512,2560]{1,0:T(8,128)(2,1)}) %all-gather.7.cloned.1.call-update) | async-done | bytes 2621456 | tf_op jit(solution)/shard_map/all_gather | solution.py:176
  58.4 3.0 %collective-permute-start = (bf16[4,128,2560]{2,1,0:T(8,128)(2,1)}, bf16[4,128,2560]{2,1,0:T(8,128)(2,1)S(1)}, u32[]{:S(2)}, u32[]{:S(2)}) collective-permute-start(bf16[4,128,2560]{2,1,0:T(8,128)(2,1)} %bitcast.65), channel_id=1, source_target_pairs={{0,16},{16,0},{1,17},{17,1},{2,18},{18,2},{3,19},{19,3},{4,20},{20... | collective-permute-start | bytes 7864328 | tf_op jit(solution)/shard_map/ppermute | solution.py:151
  62.0 1.3 reduce.rows_ref
  63.3 1.3 reduce.1.cols_ref
  64.6 0.7 stack.19.info_ref
  65.3 53.1 %collective-permute-done.p1 = bf16[4,128,2560]{2,1,0:T(8,128)(2,1)S(1)} collective-permute-done((bf16[4,128,2560]{2,1,0:T(8,128)(2,1)}, bf16[4,128,2560]{2,1,0:T(8,128)(2,1)S(1)}, u32[]{:S(2)}, u32[]{:S(2)}) %collective-permute-start) | collective-permute-done | bytes 2621472 | tf_op jit(solution)/shard_map/ppermute | solution.py:151
  118.4 0.4 all-gather.9.cloned.1.call-done
  118.8 60.8 %all-gather.11.cloned.1.call-done = bf16[512,5632]{1,0:T(8,128)(2,1)} async-done(((bf16[32,5632]{1,0:T(8,128)(2,1)}), bf16[512,5632]{1,0:T(8,128)(2,1)}) %all-gather.11.cloned.1.call-update) | async-done | bytes 5767184 | tf_op jit(solution)/shard_map/all_gather | solution.py:176
  179.6 26.6 %aggregate.1 = (bf16[4,2,1024,128]{3,2,1,0:T(8,128)(2,1)}, bf16[2,4,1024,128]{3,2,1,0:T(8,128)(2,1)}, bf16[4,2,1024,128]{3,2,1,0:T(8,128)(2,1)}, bf16[2,4,1024,128]{3,2,1,0:T(8,128)(2,1)}) custom-call(s32[384]{0:T(512)} %reduce.rows_ref, s32[384]{0:T(512)} %reduce.1.cols_ref, s32[5]{0:T(128)} %stack.19.info_ref, bf16[384,128,128]{2,1,0:T(8,128)(2,1)} %bitcast.62, ...), custom_call_target="tpu_custom_call" | custom-call | tf_op jit(solution)/shard_map/aggregate/pallas_call | solution.py:127
  206.1 9.6 %collective-permute-start.2 = (bf16[4,2,1024,128]{3,2,1,0:T(8,128)(2,1)}, bf16[4,2,1024,128]{3,2,1,0:T(8,128)(2,1)S(1)}, u32[]{:S(2)}, u32[]{:S(2)}) collective-permute-start(bf16[4,2,1024,128]{3,2,1,0:T(8,128)(2,1)} %get-tuple-element.10), channel_id=1, source_target_pairs={{0,4},{4,0},{1,5},{5,1},{2,6},{6,2},{3,7},{7,3},{8,12},{12,8},{9,1... | collective-permute-start | bytes 6291464 | tf_op jit(solution)/shard_map/ppermute | solution.py:151
  215.8 3.9 %collective-permute-done.2 = bf16[4,2,1024,128]{3,2,1,0:T(8,128)(2,1)S(1)} collective-permute-done((bf16[4,2,1024,128]{3,2,1,0:T(8,128)(2,1)}, bf16[4,2,1024,128]{3,2,1,0:T(8,128)(2,1)S(1)}, u32[]{:S(2)}, u32[]{:S(2)}) %collective-permute-start.2) | collective-permute-done | bytes 2097184 | tf_op jit(solution)/shard_map/ppermute | solution.py:151
  219.7 1.9 fusion.5
  221.7 3.2 %collective-permute-start.5 = (bf16[2,1024,128]{2,1,0:T(8,128)(2,1)S(1)}, bf16[2,1024,128]{2,1,0:T(8,128)(2,1)S(1)}, u32[]{:S(2)}, u32[]{:S(2)}) collective-permute-start(bf16[2,1024,128]{2,1,0:T(8,128)(2,1)S(1)} %get-tuple-element.17), channel_id=1, source_target_pairs={{0,3},{1,0},{2,1},{3,2},{4,7},{5,4},{6,5},{7,6},{8,11},{9,8},{10,9... | collective-permute-start | bytes 1572872 | tf_op jit(solution)/shard_map/ppermute | solution.py:156
  225.0 0.9 collective-permute-start.4
  226.1 2.1 collective-permute-start.8
  228.2 8.9 %collective-permute-done.3 = bf16[2,1024,128]{2,1,0:T(8,128)(2,1)S(1)} collective-permute-done((bf16[2,1024,128]{2,1,0:T(8,128)(2,1)S(1)}, bf16[2,1024,128]{2,1,0:T(8,128)(2,1)S(1)}, u32[]{:S(2)}, u32[]{:S(2)}) %collective-permute-start.3) | collective-permute-done | bytes 524320 | tf_op jit(solution)/shard_map/ppermute | solution.py:156
  237.1 10.5 %collective-permute-done.5 = bf16[2,1024,128]{2,1,0:T(8,128)(2,1)S(1)} collective-permute-done((bf16[2,1024,128]{2,1,0:T(8,128)(2,1)S(1)}, bf16[2,1024,128]{2,1,0:T(8,128)(2,1)S(1)}, u32[]{:S(2)}, u32[]{:S(2)}) %collective-permute-start.5) | collective-permute-done | bytes 524320 | tf_op jit(solution)/shard_map/ppermute | solution.py:156
  247.6 1.6 collective-permute-done.4
  249.2 1.4 fusion.4
  250.7 1.9 collective-permute-start.6
  252.9 1.2 collective-permute-start.9
  254.1 2.1 collective-permute-start.11
  256.4 2.1 collective-permute-done.6
  258.6 4.7 %collective-permute-done.9 = bf16[1024,128]{1,0:T(8,128)(2,1)S(1)} collective-permute-done((bf16[1024,128]{1,0:T(8,128)(2,1)S(1)}, bf16[1024,128]{1,0:T(8,128)(2,1)S(1)}, u32[]{:S(2)}, u32[]{:S(2)}) %collective-permute-start.9) | collective-permute-done | bytes 262176 | tf_op jit(solution)/shard_map/ppermute | solution.py:156
  263.3 3.0 %collective-permute-done.11 = bf16[1024,128]{1,0:T(8,128)(2,1)S(1)} collective-permute-done((bf16[1024,128]{1,0:T(8,128)(2,1)S(1)}, bf16[1024,128]{1,0:T(8,128)(2,1)S(1)}, u32[]{:S(2)}, u32[]{:S(2)}) %collective-permute-start.11) | collective-permute-done | bytes 262176 | tf_op jit(solution)/shard_map/ppermute | solution.py:156
  266.3 0.8 collective-permute-done.10
  267.3 1.4 fusion.1
  (25 shorter events, 1.4 us)
Async XLA Ops:
  6.5 260.8 %copy-start = (bf16[128,256]{1,0:T(8,128)(2,1)S(1)}, bf16[128,256]{1,0:T(8,128)(2,1)}, u32[]{:S(2)}) copy-start(bf16[128,256]{1,0:T(8,128)(2,1)} %param.12) | copy-start | bytes 196612
  6.5 51.8 %all-gather.7.cloned.1.call-start = ((), (), s32[]{:S(2)}) async-start(), calls=%async_computation | async-start | bytes 2785280 | tf_op jit(solution)/shard_map/all_gather | solution.py:176
  8.2 110.6 %all-gather.9.cloned.1.call-start = ((), (), s32[]{:S(2)}) async-start(), calls=%async_computation.1 | async-start | bytes 6127616 | tf_op jit(solution)/shard_map/all_gather | solution.py:176
  10.0 169.5 %all-gather.11.cloned.1.call-start = ((), (), s32[]{:S(2)}) async-start(), calls=%async_computation.2 | async-start | bytes 6127616 | tf_op jit(solution)/shard_map/all_gather | solution.py:176
  10.0 12.0 %collective-permute-start.1 = (bf16[32,5632]{1,0:T(8,128)(2,1)}, bf16[32,5632]{1,0:T(8,128)(2,1)S(1)}, u32[]{:S(2)}, u32[]{:S(2)}) collective-permute-start(bf16[32,5632]{1,0:T(8,128)(2,1)} %slice.106), channel_id=1, source_target_pairs={{0,16},{16,0},{1,17},{17,1},{2,18},{18,2},{3,19},{19,3},{4,20},{20... | collective-permute-start | bytes 1081352 | tf_op jit(solution)/shard_map/ppermute | solution.py:151
  22.0 0.7 copy-start.3
  58.4 60.0 %collective-permute-start = (bf16[4,128,2560]{2,1,0:T(8,128)(2,1)}, bf16[4,128,2560]{2,1,0:T(8,128)(2,1)S(1)}, u32[]{:S(2)}, u32[]{:S(2)}) collective-permute-start(bf16[4,128,2560]{2,1,0:T(8,128)(2,1)} %bitcast.65), channel_id=1, source_target_pairs={{0,16},{16,0},{1,17},{17,1},{2,18},{18,2},{3,19},{19,3},{4,20},{20... | collective-permute-start | bytes 7864328 | tf_op jit(solution)/shard_map/ppermute | solution.py:151
  118.4 61.2 %copy-start.1 = (bf16[4,128,2560]{2,1,0:T(8,128)(2,1)}, bf16[4,128,2560]{2,1,0:T(8,128)(2,1)S(1)}, u32[]{:S(2)}) copy-start(bf16[4,128,2560]{2,1,0:T(8,128)(2,1)S(1)} %collective-permute-done.p1) | copy-start | bytes 7864324
  206.1 13.6 %collective-permute-start.2 = (bf16[4,2,1024,128]{3,2,1,0:T(8,128)(2,1)}, bf16[4,2,1024,128]{3,2,1,0:T(8,128)(2,1)S(1)}, u32[]{:S(2)}, u32[]{:S(2)}) collective-permute-start(bf16[4,2,1024,128]{3,2,1,0:T(8,128)(2,1)} %get-tuple-element.10), channel_id=1, source_target_pairs={{0,4},{4,0},{1,5},{5,1},{2,6},{6,2},{3,7},{7,3},{8,12},{12,8},{9,1... | collective-permute-start | bytes 6291464 | tf_op jit(solution)/shard_map/ppermute | solution.py:151
  215.7 10.1 %collective-permute-start.7 = (bf16[2,4,1024,128]{3,2,1,0:T(8,128)(2,1)}, bf16[2,4,1024,128]{3,2,1,0:T(8,128)(2,1)S(1)}, u32[]{:S(2)}, u32[]{:S(2)}) collective-permute-start(bf16[2,4,1024,128]{3,2,1,0:T(8,128)(2,1)} %get-tuple-element.12), channel_id=1, source_target_pairs={{0,4},{4,0},{1,5},{5,1},{2,6},{6,2},{3,7},{7,3},{8,12},{12,8},{9,1... | collective-permute-start | bytes 6291464 | tf_op jit(solution)/shard_map/ppermute | solution.py:151
  219.7 6.1 %copy-start.2 = (bf16[2,4,1024,128]{3,2,1,0:T(8,128)(2,1)S(1)}, bf16[2,4,1024,128]{3,2,1,0:T(8,128)(2,1)}, u32[]{:S(2)}) copy-start(bf16[2,4,1024,128]{3,2,1,0:T(8,128)(2,1)} %get-tuple-element.11) | copy-start | bytes 6291460
  221.6 15.5 %collective-permute-start.3 = (bf16[2,1024,128]{2,1,0:T(8,128)(2,1)S(1)}, bf16[2,1024,128]{2,1,0:T(8,128)(2,1)S(1)}, u32[]{:S(2)}, u32[]{:S(2)}) collective-permute-start(bf16[2,1024,128]{2,1,0:T(8,128)(2,1)S(1)} %get-tuple-element.16), channel_id=1, source_target_pairs={{0,1},{1,2},{2,3},{3,0},{4,5},{5,6},{6,7},{7,4},{8,9},{9,10},{10,1... | collective-permute-start | bytes 1572872 | tf_op jit(solution)/shard_map/ppermute | solution.py:156
  221.7 25.9 %collective-permute-start.5 = (bf16[2,1024,128]{2,1,0:T(8,128)(2,1)S(1)}, bf16[2,1024,128]{2,1,0:T(8,128)(2,1)S(1)}, u32[]{:S(2)}, u32[]{:S(2)}) collective-permute-start(bf16[2,1024,128]{2,1,0:T(8,128)(2,1)S(1)} %get-tuple-element.17), channel_id=1, source_target_pairs={{0,3},{1,0},{2,1},{3,2},{4,7},{5,4},{6,5},{7,6},{8,11},{9,8},{10,9... | collective-permute-start | bytes 1572872 | tf_op jit(solution)/shard_map/ppermute | solution.py:156
  225.0 24.3 %collective-permute-start.4 = (bf16[2,1024,128]{2,1,0:T(8,128)(2,1)S(1)}, bf16[2,1024,128]{2,1,0:T(8,128)(2,1)S(1)}, u32[]{:S(2)}, u32[]{:S(2)}) collective-permute-start(bf16[2,1024,128]{2,1,0:T(8,128)(2,1)S(1)} %get-tuple-element.18), channel_id=1, source_target_pairs={{0,2},{1,3},{2,0},{3,1},{4,6},{5,7},{6,4},{7,5},{8,10},{9,11},{10,... | collective-permute-start | bytes 1572872 | tf_op jit(solution)/shard_map/ppermute | solution.py:156
  226.1 26.4 %collective-permute-start.8 = (bf16[4,1024,128]{2,1,0:T(8,128)(2,1)S(1)}, bf16[4,1024,128]{2,1,0:T(8,128)(2,1)S(1)}, u32[]{:S(2)}, u32[]{:S(2)}) collective-permute-start(bf16[4,1024,128]{2,1,0:T(8,128)(2,1)S(1)} %fusion.2), channel_id=1, source_target_pairs={{0,8},{8,0},{1,9},{9,1},{2,10},{10,2},{3,11},{11,3},{4,12},{12,4},... | collective-permute-start | bytes 3145736 | tf_op jit(solution)/shard_map/ppermute | solution.py:151
  250.7 7.8 %collective-permute-start.6 = (bf16[1024,128]{1,0:T(8,128)(2,1)S(1)}, bf16[1024,128]{1,0:T(8,128)(2,1)S(1)}, u32[]{:S(2)}, u32[]{:S(2)}) collective-permute-start(bf16[1024,128]{1,0:T(8,128)(2,1)S(1)} %fusion.20), channel_id=1, source_target_pairs={{0,8},{8,0},{1,9},{9,1},{2,10},{10,2},{3,11},{11,3},{4,12},{12,4},... | collective-permute-start | bytes 786440 | tf_op jit(solution)/shard_map/ppermute | solution.py:151
  252.8 14.5 %copy-start.4 = (f32[256]{0:T(256)S(1)}, f32[256]{0:T(256)}, u32[]{:S(2)}) copy-start(f32[256]{0:T(256)} %param.13) | copy-start | bytes 3076
  252.9 10.4 %collective-permute-start.9 = (bf16[1024,128]{1,0:T(8,128)(2,1)S(1)}, bf16[1024,128]{1,0:T(8,128)(2,1)S(1)}, u32[]{:S(2)}, u32[]{:S(2)}) collective-permute-start(bf16[1024,128]{1,0:T(8,128)(2,1)S(1)} %get-tuple-element.13), channel_id=1, source_target_pairs={{0,1},{1,2},{2,3},{3,0},{4,5},{5,6},{6,7},{7,4},{8,9},{9,10},{10,1... | collective-permute-start | bytes 786440 | tf_op jit(solution)/shard_map/ppermute | solution.py:156
  254.1 12.2 %collective-permute-start.11 = (bf16[1024,128]{1,0:T(8,128)(2,1)S(1)}, bf16[1024,128]{1,0:T(8,128)(2,1)S(1)}, u32[]{:S(2)}, u32[]{:S(2)}) collective-permute-start(bf16[1024,128]{1,0:T(8,128)(2,1)S(1)} %get-tuple-element.14), channel_id=1, source_target_pairs={{0,3},{1,0},{2,1},{3,2},{4,7},{5,4},{6,5},{7,6},{8,11},{9,8},{10,9... | collective-permute-start | bytes 786440 | tf_op jit(solution)/shard_map/ppermute | solution.py:156
  256.2 10.9 %collective-permute-start.10 = (bf16[1024,128]{1,0:T(8,128)(2,1)S(1)}, bf16[1024,128]{1,0:T(8,128)(2,1)S(1)}, u32[]{:S(2)}, u32[]{:S(2)}) collective-permute-start(bf16[1024,128]{1,0:T(8,128)(2,1)S(1)} %get-tuple-element.15), channel_id=1, source_target_pairs={{0,2},{1,3},{2,0},{3,1},{4,6},{5,7},{6,4},{7,5},{8,10},{9,11},{10,... | collective-permute-start | bytes 786440 | tf_op jit(solution)/shard_map/ppermute | solution.py:156
Sparse Core Ops, SparseCore 0:
  9.5 48.8 all-gather.6
  60.5 58.2 all-gather.8
  120.9 58.5 all-gather.10

commit v3 on v2

--- a/solution.py
+++ b/solution.py
@@ -1,3 +1,5 @@
+import functools
+
 import jax
 import jax.numpy as jnp
 from jax import lax
@@ -8,41 +10,32 @@
 
 LOAD = 32
 STEP = 4
-EARLY = 20
+EARLY = 25
+LATE_X = 29
 FIRST_X = 1024
 NT = (((1,), (1,)), ((), ()))
 NAMES = ("rz", "ry", "cy", "cc", "fx")
 
 
-def aggregate_kernel(
-    rows_ref, cols_ref, info_ref, tiles_hbm, p0, p1, q0, q1, keep_a, keep_b, send_a, send_b,
-    tiles, src, acc, stage, tile_sem, src_sem, out_sem,
-):
+def aggregate_kernel(where, n_parts, rows_ref, cols_ref, info_ref, tiles_hbm, *refs):
+    parts, (keep_a, keep_b, send_a, send_b) = refs[:n_parts], refs[n_parts : n_parts + 4]
+    tiles, src, acc, stage, tile_sem, src_sem, out_sem = refs[n_parts + 4 :]
     side = tiles.shape[-1]
     per_row = src.shape[-1] // side
-    count, ry, cy, cc, fx = (info_ref[i] for i in range(5))
+    count, rz, ry, cy, cc, fx = (info_ref[i] for i in range(6))
     loads = (count + LOAD - 1) // LOAD
 
     def tile_copy(i):
         part = pl.ds(pl.multiple_of(i * LOAD, LOAD), LOAD)
         return pltpu.make_async_copy(tiles_hbm.at[part], tiles.at[part], tile_sem.at[i])
 
-    early = p0.shape[-1]
     src_copies = []
-    for n, (ref, plane, lanes) in enumerate(
-        (
-            (p0, ry, pl.ds(0, early)),
-            (p1, 1 - ry, pl.ds(0, early)),
-            (q0, ry, pl.ds(early, q0.shape[-1])),
-            (q1, 1 - ry, pl.ds(early, q1.shape[-1])),
-        )
-    ):
-        for z in range(ref.shape[0]):
-            src_copies.append(
-                pltpu.make_async_copy(
-                    ref.at[z], src.at[2 * z + plane, :, lanes], src_sem.at[4 * n + z]
-                )
-            )
+    for ref, (first, offsets) in zip(parts, where):
+        for n, (z, y, x) in enumerate(offsets):
+            row = jnp.bitwise_and(rz + z, 3) * 2 + jnp.bitwise_xor(ry, y)
+            col = jnp.bitwise_and(fx + x, 3)
+            to = src.at[row, col, :, pl.ds(first, ref.shape[-1])]
+            src_copies.append(pltpu.make_async_copy(ref.at[n], to, src_sem.at[len(src_copies)]))
     for copy in src_copies:
         copy.start()
 
@@ -64,7 +57,7 @@
         col = cols_ref[k]
         group = col // per_row
         lane = pl.multiple_of((col % per_row) * side, side)
-        block = src[group, :, pl.ds(lane, side)]
+        block = src[group, :, :, pl.ds(lane, side)].reshape(side, side)
         return lax.dot_general(tiles[k], block, NT, preferred_element_type=jnp.float32)
 
     def add(k, value):
@@ -98,7 +91,7 @@
             for copy in copies[n - 2]:
                 copy.wait()
         core = 1 - cc if other else cc
-        shard = (jnp.bitwise_xor(cy, y) * 2 + core) * 4 + (fx + d) % 4
+        shard = (jnp.bitwise_xor(cy, y) * 2 + core) * 4 + jnp.bitwise_and(fx + d, 3)
         stage[slot] = acc[pl.ds(pl.multiple_of(shard * chunk, chunk), chunk), :].astype(jnp.bfloat16)
         out_a, out_b = (send_a, send_b) if other else (keep_a, keep_b)
         copies.append(
@@ -121,30 +114,30 @@
 def aggregate(tiles, rows, cols, info, parts, node_dev):
     slots, side, _ = tiles.shape
     any_space = pl.BlockSpec(memory_space=pl.ANY)
-    early, group = parts[0].shape[-1], parts[0].shape[-1] + parts[2].shape[-1]
+    arrays, where = [p[0] for p in parts], [p[1:] for p in parts]
     part_a = jax.ShapeDtypeStruct((4, 2, FIRST_X, side), jnp.bfloat16)
     part_b = jax.ShapeDtypeStruct((2, 4, node_dev - FIRST_X, side), jnp.bfloat16)
     return pl.pallas_call(
-        aggregate_kernel,
+        functools.partial(aggregate_kernel, where, len(arrays)),
         out_shape=(part_a, part_b, part_a, part_b),
         grid_spec=pltpu.PrefetchScalarGridSpec(
             num_scalar_prefetch=3,
             grid=(1,),
-            in_specs=[any_space] * 5,
+            in_specs=[any_space] * (1 + len(arrays)),
             out_specs=(any_space,) * 4,
             scratch_shapes=[
                 pltpu.VMEM(tiles.shape, jnp.bfloat16),
-                pltpu.VMEM((8, side, group), jnp.bfloat16),
+                pltpu.VMEM((8, 4, side // 4, 4 * node_dev), jnp.bfloat16),
                 pltpu.VMEM((16 * node_dev, side), jnp.float32),
                 pltpu.VMEM((2, node_dev, side), jnp.bfloat16),
                 pltpu.SemaphoreType.DMA((slots // LOAD,)),
-                pltpu.SemaphoreType.DMA((16,)),
+                pltpu.SemaphoreType.DMA((sum(len(w[1]) for w in where),)),
                 pltpu.SemaphoreType.DMA((2, 2)),
             ],
         ),
         compiler_params=pltpu.CompilerParams(vmem_limit_bytes=56 * 2**20),
         name="aggregate",
-    )(rows, cols, info, tiles, *parts)
+    )(rows, cols, info, tiles, *arrays)
 
 
 def swap(value, axis):
@@ -167,17 +160,37 @@
     return value.astype(jnp.bfloat16)
 
 
+STEPS = (0, -1, 1, 2)
+
+
+def ring(value, axis):
+    return [value] + [shift(value, axis, -d) for d in STEPS[1:]]
+
+
+def ring_forward(value, axis):
+    before, after = shift(value, axis, 1), shift(value, axis, -1)
+    half = value.shape[0] // 2
+    return [value, before, after, shift(before[:half], axis, 1), shift(after[half:], axis, -1)]
+
+
 def gather_sources(x):
-    early = EARLY * 128
-    p, q = x[:, :early], x[:, early:]
-    q_other = swap(q, "ry")
-
-    def plane(value):
-        return lax.all_gather(value, ("rz", "fx")).reshape(4, -1, value.shape[-1])
-
-    p0 = plane(p)
-    p1 = swap(p0, "ry")
-    return p0, p1, plane(q), plane(q_other)
+    late, last = EARLY * 128, (EARLY + LATE_X) * 128
+    p, q = x[:, :late], x[:, late:]
+    q = jnp.stack([q, swap(q, "ry")])
+    parts = []
+    for z, value in zip(STEPS, ring(jnp.stack(ring(p, "fx")), "rz")):
+        for y in (0, 1):
+            parts.append((swap(value, "ry") if y else value, 0, [(z, y, d) for d in STEPS]))
+    a, b = q[:, :, : last - late], q[:, :, last - late :]
+    for value, first, x_last in ((a, late, True), (b, last, False)):
+        one, two = ("rz", "fx") if x_last else ("fx", "rz")
+        done = ring_forward(jnp.stack(ring(value, one)), two)
+        for far, near, part in zip((0, -1, 1, 2, 2), (STEPS, STEPS, STEPS, STEPS[:2], STEPS[2:]), done):
+            offsets = [
+                (d, y, far) if x_last else (far, y, d) for d in near for y in (0, 1)
+            ]
+            parts.append((part.reshape(-1, *part.shape[2:]), first, offsets))
+    return parts
 
 
 def reduce_rows(keep_a, keep_b, send_a, send_b):
@@ -197,7 +210,7 @@
 def body(features, tiles, tile_row, tile_col, tile_count, weight, bias):
     node_dev = features.shape[0] // lax.axis_size("fx")
     slots, side = tiles.shape[2], tiles.shape[3]
-    place = [lax.axis_index(n) for n in NAMES[1:]]
+    place = [lax.axis_index(n) for n in NAMES]
     info = jnp.stack([tile_count.reshape(())] + [i.astype(jnp.int32) for i in place])
     parts = aggregate(
         tiles.reshape(slots, side, side),

time: 275 us -> 285 us (1.036)
  starting transfers between devices: 27.8 us -> 81 us
  waiting for transfers between devices: 194 us -> 169 us
  between operations: 13.8 us -> 0.95 us
  Pallas kernels: 26.6 us -> 20.7 us
    all_gather x3 -> x0, waiting for transfers between devices: 96.7 us -> none  [plane(): return lax.all_gather(value, ('rz', 'fx')).reshape(4, -1, value.shape[-1])]
    ppermute x6 -> x26, waiting for transfers between devices: 29.5 us -> 121 us  [shift(): return lax.ppermute(value, axis, [(i, (i + by) % n) for i in range(n)])]
    ppermute x6 -> x26, starting transfers between devices: 7.74 us -> 44.4 us  [shift(): return lax.ppermute(value, axis, [(i, (i + by) % n) for i in range(n)])]
    ppermute x6 -> x9, waiting for transfers between devices: 67.7 us -> 48.6 us  [swap(): return lax.ppermute(value, axis, [(0, 1), (1, 0)])]
    ppermute x6 -> x9, starting transfers between devices: 20 us -> 36.6 us  [swap(): return lax.ppermute(value, axis, [(0, 1), (1, 0)])]
    pallas_call x1, Pallas kernels: 26.6 us -> 20.7 us  [aggregate(): pl.pallas_call(functools.partial(aggregate_kernel, where, len(arrays)), o...]
  transfers between devices with their start and end apart: 15 -> 35, of which waited for: 13 -> 17; matrix products, arithmetic and copies ran while one was open for 3% -> 3% of each run, Pallas kernels for 0% -> 0%
where the time goes in v3:
time: 285 us; the launch traced here: 284 us
  waiting for transfers between devices  169 us (59%)
  starting transfers between devices  81 us (28%)
  Pallas kernels  20.7 us (7%)
  other arithmetic  5.98 us (2%)
  local copies, waits for them, and re-layouts  4.88 us (2%)
    ppermute x26, waiting for transfers between devices, shift(): return lax.ppermute(value, axis, [(i, (i + by) % n) for i in range(n)])  121 us
    ppermute x9, waiting for transfers between devices, swap(): return lax.ppermute(value, axis, [(0, 1), (1, 0)])  48.6 us
    ppermute x26, starting transfers between devices, shift(): return lax.ppermute(value, axis, [(i, (i + by) % n) for i in range(n)])  44.4 us
    ppermute x9, starting transfers between devices, swap(): return lax.ppermute(value, axis, [(0, 1), (1, 0)])  36.6 us
    pallas_call x1, Pallas kernels, aggregate(): pl.pallas_call(functools.partial(aggregate_kernel, where, len(arrays)), o...  20.7 us
  transfers between devices with their start and end apart: 35, of which 17 were waited for; matrix products, arithmetic and copies ran while one was open for 3% of the time, Pallas kernels for 0%

profile of v3, /device:TPU:0, one launch (start us, length us, event | category | flops | bytes accessed | tf_op | source)
XLA Modules:
  0.0 284.2 jit_solution(6715723776407161761)
XLA Ops:
  1.1 3.4 %collective-permute-start.10 = (bf16[32,4992]{1,0:T(8,128)(2,1)S(1)}, bf16[32,4992]{1,0:T(8,128)(2,1)S(1)}, u32[]{:S(2)}, u32[]{:S(2)}) collective-permute-start(bf16[32,4992]{1,0:T(8,128)(2,1)S(1)} %get-tuple-element.19), channel_id=1, source_target_pairs={{0,16},{16,0},{1,17},{17,1},{2,18},{18,2},{3,19},{19,3},{4,20},{20... | collective-permute-start | bytes 958472 | tf_op jit(solution)/shard_map/ppermute | solution.py:144
  5.4 2.8 collective-permute-start.1
  8.2 2.3 collective-permute-start.2
  12.0 4.2 %collective-permute-start.12 = (bf16[2,32,3712]{2,1,0:T(8,128)(2,1)S(1)}, bf16[2,32,3712]{2,1,0:T(8,128)(2,1)S(1)}, u32[]{:S(2)}, u32[]{:S(2)}) collective-permute-start(bf16[2,32,3712]{2,1,0:T(8,128)(2,1)S(1)} %fusion.20), channel_id=1, source_target_pairs={{0,96},{32,0},{64,32},{96,64},{1,97},{33,1},{65,33},{97,65},{2,98}... | collective-permute-start | bytes 1425416 | tf_op jit(solution)/shard_map/ppermute | solution.py:149
  16.7 3.9 %collective-permute-start.13 = (bf16[2,32,3712]{2,1,0:T(8,128)(2,1)S(1)}, bf16[2,32,3712]{2,1,0:T(8,128)(2,1)S(1)}, u32[]{:S(2)}, u32[]{:S(2)}) collective-permute-start(bf16[2,32,3712]{2,1,0:T(8,128)(2,1)S(1)} %fusion.20), channel_id=1, source_target_pairs={{0,64},{32,96},{64,0},{96,32},{1,65},{33,97},{65,1},{97,33},{2,66}... | collective-permute-start | bytes 1425416 | tf_op jit(solution)/shard_map/ppermute | solution.py:149
  20.8 14.8 %collective-permute-done.12 = bf16[2,32,3712]{2,1,0:T(8,128)(2,1)S(1)} collective-permute-done((bf16[2,32,3712]{2,1,0:T(8,128)(2,1)S(1)}, bf16[2,32,3712]{2,1,0:T(8,128)(2,1)S(1)}, u32[]{:S(2)}, u32[]{:S(2)}) %collective-permute-start.12) | collective-permute-done | bytes 475168 | tf_op jit(solution)/shard_map/ppermute | solution.py:149
  35.6 3.4 %collective-permute-done.11 = bf16[2,32,3712]{2,1,0:T(8,128)(2,1)S(1)} collective-permute-done((bf16[2,32,3712]{2,1,0:T(8,128)(2,1)S(1)}, bf16[2,32,3712]{2,1,0:T(8,128)(2,1)S(1)}, u32[]{:S(2)}, u32[]{:S(2)}) %collective-permute-start.11) | collective-permute-done | bytes 475168 | tf_op jit(solution)/shard_map/ppermute | solution.py:149
  39.3 2.8 collective-permute-start.15
  43.0 2.6 collective-permute-start.19
  46.9 42.9 %collective-permute-done.18 = bf16[2,32,1280]{2,1,0:T(8,128)(2,1)S(1)} collective-permute-done((bf16[2,32,1280]{2,1,0:T(8,128)(2,1)S(1)}, bf16[2,32,1280]{2,1,0:T(8,128)(2,1)S(1)}, u32[]{:S(2)}, u32[]{:S(2)}) %collective-permute-start.18) | collective-permute-done | bytes 163872 | tf_op jit(solution)/shard_map/ppermute | solution.py:149
  89.8 2.2 collective-permute-start.8
  94.2 17.7 %collective-permute-done.8.refs_6_ = bf16[4,32,3200]{2,1,0:T(8,128)(2,1)} collective-permute-done((bf16[4,32,3200]{2,1,0:T(8,128)(2,1)S(1)}, bf16[4,32,3200]{2,1,0:T(8,128)(2,1)}, u32[]{:S(2)}, u32[]{:S(2)}) %collective-permute-start.8) | collective-permute-done | bytes 819232 | tf_op jit(solution)/shard_map/ppermute | solution.py:149
  111.9 2.6 collective-permute-start.6
  114.5 11.3 %collective-permute-done.22 = bf16[4,2,32,1280]{3,2,1,0:T(8,128)(2,1)S(1)} collective-permute-done((bf16[4,2,32,1280]{3,2,1,0:T(8,128)(2,1)S(1)}, bf16[4,2,32,1280]{3,2,1,0:T(8,128)(2,1)S(1)}, u32[]{:S(2)}, u32[]{:S(2)}) %collective-permute-start.22) | collective-permute-done | bytes 655392 | tf_op jit(solution)/shard_map/ppermute | solution.py:149
  125.8 3.3 %collective-permute-start.3 = (bf16[4,32,3200]{2,1,0:T(8,128)(2,1)S(1)}, bf16[4,32,3200]{2,1,0:T(8,128)(2,1)S(1)}, u32[]{:S(2)}, u32[]{:S(2)}) collective-permute-start(bf16[4,32,3200]{2,1,0:T(8,128)(2,1)S(1)} %pad_maximum_fusion.1.refs_0_), channel_id=1, source_target_pairs={{0,16},{16,0},{1,17},{17,1},{2,18},{18,2},{3,19},{19,3},{4,20},{20... | collective-permute-start | bytes 2457608 | tf_op jit(solution)/shard_map/ppermute | solution.py:144
  129.2 3.3 %collective-permute-start.24 = (bf16[2,2,32,1280]{3,2,1,0:T(8,128)(2,1)S(1)}, bf16[2,2,32,1280]{3,2,1,0:T(8,128)(2,1)}, u32[]{:S(2)}, u32[]{:S(2)}) collective-permute-start(bf16[2,2,32,1280]{3,2,1,0:T(8,128)(2,1)S(1)} %slice.136), channel_id=1, source_target_pairs={{0,96},{32,0},{64,32},{96,64},{1,97},{33,1},{65,33},{97,65},{2,98}... | collective-permute-start | bytes 983048 | tf_op jit(solution)/shard_map/ppermute | solution.py:149
  133.9 6.4 %collective-permute-done.6.refs_4_ = bf16[4,32,3200]{2,1,0:T(8,128)(2,1)} collective-permute-done((bf16[4,32,3200]{2,1,0:T(8,128)(2,1)S(1)}, bf16[4,32,3200]{2,1,0:T(8,128)(2,1)}, u32[]{:S(2)}, u32[]{:S(2)}) %collective-permute-start.6) | collective-permute-done | bytes 819232 | tf_op jit(solution)/shard_map/ppermute | solution.py:149
  140.2 3.5 %collective-permute-done.4.refs_2_ = bf16[4,32,3200]{2,1,0:T(8,128)(2,1)} collective-permute-done((bf16[4,32,3200]{2,1,0:T(8,128)(2,1)S(1)}, bf16[4,32,3200]{2,1,0:T(8,128)(2,1)}, u32[]{:S(2)}, u32[]{:S(2)}) %collective-permute-start.4) | collective-permute-done | bytes 819232 | tf_op jit(solution)/shard_map/ppermute | solution.py:149
  144.7 3.2 %collective-permute-start.9 = (bf16[4,32,3200]{2,1,0:T(8,128)(2,1)}, bf16[4,32,3200]{2,1,0:T(8,128)(2,1)S(1)}, u32[]{:S(2)}, u32[]{:S(2)}) collective-permute-start(bf16[4,32,3200]{2,1,0:T(8,128)(2,1)} %collective-permute-done.8.refs_6_), channel_id=1, source_target_pairs={{0,16},{16,0},{1,17},{17,1},{2,18},{18,2},{3,19},{19,3},{4,20},{20... | collective-permute-start | bytes 2457608 | tf_op jit(solution)/shard_map/ppermute | solution.py:144
  148.2 3.2 %collective-permute-start.5 = (bf16[4,32,3200]{2,1,0:T(8,128)(2,1)}, bf16[4,32,3200]{2,1,0:T(8,128)(2,1)}, u32[]{:S(2)}, u32[]{:S(2)}) collective-permute-start(bf16[4,32,3200]{2,1,0:T(8,128)(2,1)} %collective-permute-done.4.refs_2_), channel_id=1, source_target_pairs={{0,16},{16,0},{1,17},{17,1},{2,18},{18,2},{3,19},{19,3},{4,20},{20... | collective-permute-start | bytes 2457608 | tf_op jit(solution)/shard_map/ppermute | solution.py:144
  153.9 13.7 %collective-permute-done.9.refs_7_ = bf16[4,32,3200]{2,1,0:T(8,128)(2,1)S(1)} collective-permute-done((bf16[4,32,3200]{2,1,0:T(8,128)(2,1)}, bf16[4,32,3200]{2,1,0:T(8,128)(2,1)S(1)}, u32[]{:S(2)}, u32[]{:S(2)}) %collective-permute-start.9) | collective-permute-done | bytes 819232 | tf_op jit(solution)/shard_map/ppermute | solution.py:144
  167.6 17.7 %collective-permute-done.7.refs_5_ = bf16[4,32,3200]{2,1,0:T(8,128)(2,1)} collective-permute-done((bf16[4,32,3200]{2,1,0:T(8,128)(2,1)}, bf16[4,32,3200]{2,1,0:T(8,128)(2,1)}, u32[]{:S(2)}, u32[]{:S(2)}) %collective-permute-start.7) | collective-permute-done | bytes 819232 | tf_op jit(solution)/shard_map/ppermute | solution.py:144
  185.2 9.8 %collective-permute-done.5.refs_3_ = bf16[4,32,3200]{2,1,0:T(8,128)(2,1)} collective-permute-done((bf16[4,32,3200]{2,1,0:T(8,128)(2,1)}, bf16[4,32,3200]{2,1,0:T(8,128)(2,1)}, u32[]{:S(2)}, u32[]{:S(2)}) %collective-permute-start.5) | collective-permute-done | bytes 819232 | tf_op jit(solution)/shard_map/ppermute | solution.py:144
  195.1 20.7 %aggregate.1 = (bf16[4,2,1024,128]{3,2,1,0:T(8,128)(2,1)}, bf16[2,4,1024,128]{3,2,1,0:T(8,128)(2,1)}, bf16[4,2,1024,128]{3,2,1,0:T(8,128)(2,1)}, bf16[2,4,1024,128]{3,2,1,0:T(8,128)(2,1)}) custom-call(s32[384]{0:T(512)} %reduce.rows_ref, s32[384]{0:T(512)} %reduce.1.cols_ref, s32[6]{0:T(128)} %stack.77.info_ref, bf16[384,128,128]{2,1,0:T(8,128)(2,1)} %bitcast.88, ...), custom_call_target="tpu_custom_call" | custom-call | tf_op jit(solution)/shard_map/aggregate/pallas_call | solution.py:120
  216.4 3.9 %collective-permute-done.25 = bf16[4,2,1024,128]{3,2,1,0:T(8,128)(2,1)S(1)} collective-permute-done((bf16[4,2,1024,128]{3,2,1,0:T(8,128)(2,1)}, bf16[4,2,1024,128]{3,2,1,0:T(8,128)(2,1)S(1)}, u32[]{:S(2)}, u32[]{:S(2)}) %collective-permute-start.25) | collective-permute-done | bytes 2097184 | tf_op jit(solution)/shard_map/ppermute | solution.py:144
  222.1 7.3 %collective-permute-start.26 = (bf16[2,1024,128]{2,1,0:T(8,128)(2,1)S(1)}, bf16[2,1024,128]{2,1,0:T(8,128)(2,1)S(1)}, u32[]{:S(2)}, u32[]{:S(2)}) collective-permute-start(bf16[2,1024,128]{2,1,0:T(8,128)(2,1)S(1)} %get-tuple-element.16), channel_id=1, source_target_pairs={{0,1},{1,2},{2,3},{3,0},{4,5},{5,6},{6,7},{7,4},{8,9},{9,10},{10,1... | collective-permute-start | bytes 1572872 | tf_op jit(solution)/shard_map/ppermute | solution.py:149
  232.4 11.3 %collective-permute-start.31 = (bf16[4,1024,128]{2,1,0:T(8,128)(2,1)S(1)}, bf16[4,1024,128]{2,1,0:T(8,128)(2,1)S(1)}, u32[]{:S(2)}, u32[]{:S(2)}) collective-permute-start(bf16[4,1024,128]{2,1,0:T(8,128)(2,1)S(1)} %fusion.2), channel_id=1, source_target_pairs={{0,8},{8,0},{1,9},{9,1},{2,10},{10,2},{3,11},{11,3},{4,12},{12,4},... | collective-permute-start | bytes 3145736 | tf_op jit(solution)/shard_map/ppermute | solution.py:144
  244.3 11.0 %collective-permute-done.27 = bf16[2,1024,128]{2,1,0:T(8,128)(2,1)S(1)} collective-permute-done((bf16[2,1024,128]{2,1,0:T(8,128)(2,1)S(1)}, bf16[2,1024,128]{2,1,0:T(8,128)(2,1)S(1)}, u32[]{:S(2)}, u32[]{:S(2)}) %collective-permute-start.27) | collective-permute-done | bytes 524320 | tf_op jit(solution)/shard_map/ppermute | solution.py:149
  256.7 11.3 %collective-permute-start.29 = (bf16[1024,128]{1,0:T(8,128)(2,1)S(1)}, bf16[1024,128]{1,0:T(8,128)(2,1)S(1)}, u32[]{:S(2)}, u32[]{:S(2)}) collective-permute-start(bf16[1024,128]{1,0:T(8,128)(2,1)S(1)} %fusion.21), channel_id=1, source_target_pairs={{0,8},{8,0},{1,9},{9,1},{2,10},{10,2},{3,11},{11,3},{4,12},{12,4},... | collective-permute-start | bytes 786440 | tf_op jit(solution)/shard_map/ppermute | solution.py:144
  269.6 2.1 collective-permute-start.34
  271.8 2.1 collective-permute-done.29
  273.9 8.6 %collective-permute-done.32 = bf16[1024,128]{1,0:T(8,128)(2,1)S(1)} collective-permute-done((bf16[1024,128]{1,0:T(8,128)(2,1)S(1)}, bf16[1024,128]{1,0:T(8,128)(2,1)S(1)}, u32[]{:S(2)}, u32[]{:S(2)}) %collective-permute-start.32) | collective-permute-done | bytes 262176 | tf_op jit(solution)/shard_map/ppermute | solution.py:149
  (91 shorter events, 24.1 us)
Async XLA Ops:
  5.4 11.3 %collective-permute-start.1 = (bf16[32,3200]{1,0:T(8,128)(2,1)S(1)}, bf16[32,3200]{1,0:T(8,128)(2,1)S(1)}, u32[]{:S(2)}, u32[]{:S(2)}) collective-permute-start(bf16[32,3200]{1,0:T(8,128)(2,1)S(1)} %get-tuple-element.22), channel_id=1, source_target_pairs={{0,3},{1,0},{2,1},{3,2},{4,7},{5,4},{6,5},{7,6},{8,11},{9,8},{10,9... | collective-permute-start | bytes 614408 | tf_op jit(solution)/shard_map/ppermute | solution.py:149
  8.2 12.4 %collective-permute-start = (bf16[32,3200]{1,0:T(8,128)(2,1)S(1)}, bf16[32,3200]{1,0:T(8,128)(2,1)S(1)}, u32[]{:S(2)}, u32[]{:S(2)}) collective-permute-start(bf16[32,3200]{1,0:T(8,128)(2,1)S(1)} %get-tuple-element.22), channel_id=1, source_target_pairs={{0,1},{1,2},{2,3},{3,0},{4,5},{5,6},{6,7},{7,4},{8,9},{9,10},{10,1... | collective-permute-start | bytes 614408 | tf_op jit(solution)/shard_map/ppermute | solution.py:149
  8.2 12.4 %collective-permute-start.2 = (bf16[32,3200]{1,0:T(8,128)(2,1)S(1)}, bf16[32,3200]{1,0:T(8,128)(2,1)S(1)}, u32[]{:S(2)}, u32[]{:S(2)}) collective-permute-start(bf16[32,3200]{1,0:T(8,128)(2,1)S(1)} %get-tuple-element.22), channel_id=1, source_target_pairs={{0,2},{1,3},{2,0},{3,1},{4,6},{5,7},{6,4},{7,5},{8,10},{9,11},{10,... | collective-permute-start | bytes 614408 | tf_op jit(solution)/shard_map/ppermute | solution.py:149
  12.0 23.6 %collective-permute-start.12 = (bf16[2,32,3712]{2,1,0:T(8,128)(2,1)S(1)}, bf16[2,32,3712]{2,1,0:T(8,128)(2,1)S(1)}, u32[]{:S(2)}, u32[]{:S(2)}) collective-permute-start(bf16[2,32,3712]{2,1,0:T(8,128)(2,1)S(1)} %fusion.20), channel_id=1, source_target_pairs={{0,96},{32,0},{64,32},{96,64},{1,97},{33,1},{65,33},{97,65},{2,98}... | collective-permute-start | bytes 1425416 | tf_op jit(solution)/shard_map/ppermute | solution.py:149
  16.2 22.9 %collective-permute-start.11 = (bf16[2,32,3712]{2,1,0:T(8,128)(2,1)S(1)}, bf16[2,32,3712]{2,1,0:T(8,128)(2,1)S(1)}, u32[]{:S(2)}, u32[]{:S(2)}) collective-permute-start(bf16[2,32,3712]{2,1,0:T(8,128)(2,1)S(1)} %fusion.20), channel_id=1, source_target_pairs={{0,32},{32,64},{64,96},{96,0},{1,33},{33,65},{65,97},{97,1},{2,34}... | collective-permute-start | bytes 1425416 | tf_op jit(solution)/shard_map/ppermute | solution.py:149
  16.7 22.3 %collective-permute-start.13 = (bf16[2,32,3712]{2,1,0:T(8,128)(2,1)S(1)}, bf16[2,32,3712]{2,1,0:T(8,128)(2,1)S(1)}, u32[]{:S(2)}, u32[]{:S(2)}) collective-permute-start(bf16[2,32,3712]{2,1,0:T(8,128)(2,1)S(1)} %fusion.20), channel_id=1, source_target_pairs={{0,64},{32,96},{64,0},{96,32},{1,65},{33,97},{65,1},{97,33},{2,66}... | collective-permute-start | bytes 1425416 | tf_op jit(solution)/shard_map/ppermute | solution.py:149
  39.3 89.9 %collective-permute-start.15 = (bf16[4,2,32,3712]{3,2,1,0:T(8,128)(2,1)S(1)}, bf16[4,2,32,3712]{3,2,1,0:T(8,128)(2,1)S(1)}, u32[]{:S(2)}, u32[]{:S(2)}) collective-permute-start(bf16[4,2,32,3712]{3,2,1,0:T(8,128)(2,1)S(1)} %pad_maximum_fusion), channel_id=1, source_target_pairs={{0,3},{1,0},{2,1},{3,2},{4,7},{5,4},{6,5},{7,6},{8,11},{9,8},{10,9... | collective-permute-start | bytes 5701640 | tf_op jit(solution)/shard_map/ppermute | solution.py:149
  42.1 90.4 %collective-permute-start.14 = (bf16[4,2,32,3712]{3,2,1,0:T(8,128)(2,1)S(1)}, bf16[4,2,32,3712]{3,2,1,0:T(8,128)(2,1)S(1)}, u32[]{:S(2)}, u32[]{:S(2)}) collective-permute-start(bf16[4,2,32,3712]{3,2,1,0:T(8,128)(2,1)S(1)} %pad_maximum_fusion), channel_id=1, source_target_pairs={{0,1},{1,2},{2,3},{3,0},{4,5},{5,6},{6,7},{7,4},{8,9},{9,10},{10,1... | collective-permute-start | bytes 5701640 | tf_op jit(solution)/shard_map/ppermute | solution.py:149
  42.2 47.7 %collective-permute-start.18 = (bf16[2,32,1280]{2,1,0:T(8,128)(2,1)S(1)}, bf16[2,32,1280]{2,1,0:T(8,128)(2,1)S(1)}, u32[]{:S(2)}, u32[]{:S(2)}) collective-permute-start(bf16[2,32,1280]{2,1,0:T(8,128)(2,1)S(1)} %pad_maximum_fusion.3), channel_id=1, source_target_pairs={{0,1},{1,2},{2,3},{3,0},{4,5},{5,6},{6,7},{7,4},{8,9},{9,10},{10,1... | collective-permute-start | bytes 491528 | tf_op jit(solution)/shard_map/ppermute | solution.py:149
  43.0 49.0 %collective-permute-start.19 = (bf16[2,32,1280]{2,1,0:T(8,128)(2,1)S(1)}, bf16[2,32,1280]{2,1,0:T(8,128)(2,1)S(1)}, u32[]{:S(2)}, u32[]{:S(2)}) collective-permute-start(bf16[2,32,1280]{2,1,0:T(8,128)(2,1)S(1)} %pad_maximum_fusion.3), channel_id=1, source_target_pairs={{0,3},{1,0},{2,1},{3,2},{4,7},{5,4},{6,5},{7,6},{8,11},{9,8},{10,9... | collective-permute-start | bytes 491528 | tf_op jit(solution)/shard_map/ppermute | solution.py:149
  45.5 46.5 %collective-permute-start.20 = (bf16[2,32,1280]{2,1,0:T(8,128)(2,1)S(1)}, bf16[2,32,1280]{2,1,0:T(8,128)(2,1)S(1)}, u32[]{:S(2)}, u32[]{:S(2)}) collective-permute-start(bf16[2,32,1280]{2,1,0:T(8,128)(2,1)S(1)} %pad_maximum_fusion.3), channel_id=1, source_target_pairs={{0,2},{1,3},{2,0},{3,1},{4,6},{5,7},{6,4},{7,5},{8,10},{9,11},{10,... | collective-permute-start | bytes 491528 | tf_op jit(solution)/shard_map/ppermute | solution.py:149
  89.8 22.1 %collective-permute-start.8 = (bf16[4,32,3200]{2,1,0:T(8,128)(2,1)S(1)}, bf16[4,32,3200]{2,1,0:T(8,128)(2,1)}, u32[]{:S(2)}, u32[]{:S(2)}) collective-permute-start(bf16[4,32,3200]{2,1,0:T(8,128)(2,1)S(1)} %pad_maximum_fusion.1.refs_0_), channel_id=1, source_target_pairs={{0,64},{32,96},{64,0},{96,32},{1,65},{33,97},{65,1},{97,33},{2,66}... | collective-permute-start | bytes 2457608 | tf_op jit(solution)/shard_map/ppermute | solution.py:149
  92.1 33.7 %collective-permute-start.22 = (bf16[4,2,32,1280]{3,2,1,0:T(8,128)(2,1)S(1)}, bf16[4,2,32,1280]{3,2,1,0:T(8,128)(2,1)S(1)}, u32[]{:S(2)}, u32[]{:S(2)}) collective-permute-start(bf16[4,2,32,1280]{3,2,1,0:T(8,128)(2,1)S(1)} %pad_maximum_fusion.2), channel_id=1, source_target_pairs={{0,96},{32,0},{64,32},{96,64},{1,97},{33,1},{65,33},{97,65},{2,98}... | collective-permute-start | bytes 1966088 | tf_op jit(solution)/shard_map/ppermute | solution.py:149
  92.6 33.2 %collective-permute-start.21 = (bf16[4,2,32,1280]{3,2,1,0:T(8,128)(2,1)S(1)}, bf16[4,2,32,1280]{3,2,1,0:T(8,128)(2,1)S(1)}, u32[]{:S(2)}, u32[]{:S(2)}) collective-permute-start(bf16[4,2,32,1280]{3,2,1,0:T(8,128)(2,1)S(1)} %pad_maximum_fusion.2), channel_id=1, source_target_pairs={{0,32},{32,64},{64,96},{96,0},{1,33},{33,65},{65,97},{97,1},{2,34}... | collective-permute-start | bytes 1966088 | tf_op jit(solution)/shard_map/ppermute | solution.py:149
  111.9 28.3 %collective-permute-start.6 = (bf16[4,32,3200]{2,1,0:T(8,128)(2,1)S(1)}, bf16[4,32,3200]{2,1,0:T(8,128)(2,1)}, u32[]{:S(2)}, u32[]{:S(2)}) collective-permute-start(bf16[4,32,3200]{2,1,0:T(8,128)(2,1)S(1)} %pad_maximum_fusion.1.refs_0_), channel_id=1, source_target_pairs={{0,96},{32,0},{64,32},{96,64},{1,97},{33,1},{65,33},{97,65},{2,98}... | collective-permute-start | bytes 2457608 | tf_op jit(solution)/shard_map/ppermute | solution.py:149
  125.8 17.9 %collective-permute-start.4 = (bf16[4,32,3200]{2,1,0:T(8,128)(2,1)S(1)}, bf16[4,32,3200]{2,1,0:T(8,128)(2,1)}, u32[]{:S(2)}, u32[]{:S(2)}) collective-permute-start(bf16[4,32,3200]{2,1,0:T(8,128)(2,1)S(1)} %pad_maximum_fusion.1.refs_0_), channel_id=1, source_target_pairs={{0,32},{32,64},{64,96},{96,0},{1,33},{33,65},{65,97},{97,1},{2,34}... | collective-permute-start | bytes 2457608 | tf_op jit(solution)/shard_map/ppermute | solution.py:149
  125.8 17.9 %collective-permute-start.3 = (bf16[4,32,3200]{2,1,0:T(8,128)(2,1)S(1)}, bf16[4,32,3200]{2,1,0:T(8,128)(2,1)S(1)}, u32[]{:S(2)}, u32[]{:S(2)}) collective-permute-start(bf16[4,32,3200]{2,1,0:T(8,128)(2,1)S(1)} %pad_maximum_fusion.1.refs_0_), channel_id=1, source_target_pairs={{0,16},{16,0},{1,17},{17,1},{2,18},{18,2},{3,19},{19,3},{4,20},{20... | collective-permute-start | bytes 2457608 | tf_op jit(solution)/shard_map/ppermute | solution.py:144
  129.2 18.7 %collective-permute-start.24 = (bf16[2,2,32,1280]{3,2,1,0:T(8,128)(2,1)S(1)}, bf16[2,2,32,1280]{3,2,1,0:T(8,128)(2,1)}, u32[]{:S(2)}, u32[]{:S(2)}) collective-permute-start(bf16[2,2,32,1280]{3,2,1,0:T(8,128)(2,1)S(1)} %slice.136), channel_id=1, source_target_pairs={{0,96},{32,0},{64,32},{96,64},{1,97},{33,1},{65,33},{97,65},{2,98}... | collective-permute-start | bytes 983048 | tf_op jit(solution)/shard_map/ppermute | solution.py:149
  132.5 15.7 %collective-permute-start.23 = (bf16[2,2,32,1280]{3,2,1,0:T(8,128)(2,1)S(1)}, bf16[2,2,32,1280]{3,2,1,0:T(8,128)(2,1)}, u32[]{:S(2)}, u32[]{:S(2)}) collective-permute-start(bf16[2,2,32,1280]{3,2,1,0:T(8,128)(2,1)S(1)} %slice.135), channel_id=1, source_target_pairs={{0,32},{32,64},{64,96},{96,0},{1,33},{33,65},{65,97},{97,1},{2,34}... | collective-permute-start | bytes 983048 | tf_op jit(solution)/shard_map/ppermute | solution.py:149
  140.2 54.8 %collective-permute-start.17 = (bf16[2,2,32,3712]{3,2,1,0:T(8,128)(2,1)S(1)}, bf16[2,2,32,3712]{3,2,1,0:T(8,128)(2,1)}, u32[]{:S(2)}, u32[]{:S(2)}) collective-permute-start(bf16[2,2,32,3712]{3,2,1,0:T(8,128)(2,1)S(1)} %slice.134), channel_id=1, source_target_pairs={{0,3},{1,0},{2,1},{3,2},{4,7},{5,4},{6,5},{7,6},{8,11},{9,8},{10,9... | collective-permute-start | bytes 2850824 | tf_op jit(solution)/shard_map/ppermute | solution.py:149
  143.7 51.3 %collective-permute-start.16 = (bf16[2,2,32,3712]{3,2,1,0:T(8,128)(2,1)S(1)}, bf16[2,2,32,3712]{3,2,1,0:T(8,128)(2,1)}, u32[]{:S(2)}, u32[]{:S(2)}) collective-permute-start(bf16[2,2,32,3712]{3,2,1,0:T(8,128)(2,1)S(1)} %slice.133), channel_id=1, source_target_pairs={{0,1},{1,2},{2,3},{3,0},{4,5},{5,6},{6,7},{7,4},{8,9},{9,10},{10,1... | collective-permute-start | bytes 2850824 | tf_op jit(solution)/shard_map/ppermute | solution.py:149
  144.7 22.9 %collective-permute-start.9 = (bf16[4,32,3200]{2,1,0:T(8,128)(2,1)}, bf16[4,32,3200]{2,1,0:T(8,128)(2,1)S(1)}, u32[]{:S(2)}, u32[]{:S(2)}) collective-permute-start(bf16[4,32,3200]{2,1,0:T(8,128)(2,1)} %collective-permute-done.8.refs_6_), channel_id=1, source_target_pairs={{0,16},{16,0},{1,17},{17,1},{2,18},{18,2},{3,19},{19,3},{4,20},{20... | collective-permute-start | bytes 2457608 | tf_op jit(solution)/shard_map/ppermute | solution.py:144
  147.9 37.4 %collective-permute-start.7 = (bf16[4,32,3200]{2,1,0:T(8,128)(2,1)}, bf16[4,32,3200]{2,1,0:T(8,128)(2,1)}, u32[]{:S(2)}, u32[]{:S(2)}) collective-permute-start(bf16[4,32,3200]{2,1,0:T(8,128)(2,1)} %collective-permute-done.6.refs_4_), channel_id=1, source_target_pairs={{0,16},{16,0},{1,17},{17,1},{2,18},{18,2},{3,19},{19,3},{4,20},{20... | collective-permute-start | bytes 2457608 | tf_op jit(solution)/shard_map/ppermute | solution.py:144
  148.2 46.8 %collective-permute-start.5 = (bf16[4,32,3200]{2,1,0:T(8,128)(2,1)}, bf16[4,32,3200]{2,1,0:T(8,128)(2,1)}, u32[]{:S(2)}, u32[]{:S(2)}) collective-permute-start(bf16[4,32,3200]{2,1,0:T(8,128)(2,1)} %collective-permute-done.4.refs_2_), channel_id=1, source_target_pairs={{0,16},{16,0},{1,17},{17,1},{2,18},{18,2},{3,19},{19,3},{4,20},{20... | collective-permute-start | bytes 2457608 | tf_op jit(solution)/shard_map/ppermute | solution.py:144
  215.9 16.3 %collective-permute-start.30 = (bf16[2,4,1024,128]{3,2,1,0:T(8,128)(2,1)}, bf16[2,4,1024,128]{3,2,1,0:T(8,128)(2,1)S(1)}, u32[]{:S(2)}, u32[]{:S(2)}) collective-permute-start(bf16[2,4,1024,128]{3,2,1,0:T(8,128)(2,1)} %get-tuple-element.12), channel_id=1, source_target_pairs={{0,4},{4,0},{1,5},{5,1},{2,6},{6,2},{3,7},{7,3},{8,12},{12,8},{9,1... | collective-permute-start | bytes 6291464 | tf_op jit(solution)/shard_map/ppermute | solution.py:144
  222.1 21.6 %collective-permute-start.26 = (bf16[2,1024,128]{2,1,0:T(8,128)(2,1)S(1)}, bf16[2,1024,128]{2,1,0:T(8,128)(2,1)S(1)}, u32[]{:S(2)}, u32[]{:S(2)}) collective-permute-start(bf16[2,1024,128]{2,1,0:T(8,128)(2,1)S(1)} %get-tuple-element.16), channel_id=1, source_target_pairs={{0,1},{1,2},{2,3},{3,0},{4,5},{5,6},{6,7},{7,4},{8,9},{9,10},{10,1... | collective-permute-start | bytes 1572872 | tf_op jit(solution)/shard_map/ppermute | solution.py:149
  229.4 14.8 %collective-permute-start.28 = (bf16[2,1024,128]{2,1,0:T(8,128)(2,1)S(1)}, bf16[2,1024,128]{2,1,0:T(8,128)(2,1)S(1)}, u32[]{:S(2)}, u32[]{:S(2)}) collective-permute-start(bf16[2,1024,128]{2,1,0:T(8,128)(2,1)S(1)} %get-tuple-element.17), channel_id=1, source_target_pairs={{0,3},{1,0},{2,1},{3,2},{4,7},{5,4},{6,5},{7,6},{8,11},{9,8},{10,9... | collective-permute-start | bytes 1572872 | tf_op jit(solution)/shard_map/ppermute | solution.py:149
  230.7 24.6 %collective-permute-start.27 = (bf16[2,1024,128]{2,1,0:T(8,128)(2,1)S(1)}, bf16[2,1024,128]{2,1,0:T(8,128)(2,1)S(1)}, u32[]{:S(2)}, u32[]{:S(2)}) collective-permute-start(bf16[2,1024,128]{2,1,0:T(8,128)(2,1)S(1)} %get-tuple-element.18), channel_id=1, source_target_pairs={{0,2},{1,3},{2,0},{3,1},{4,6},{5,7},{6,4},{7,5},{8,10},{9,11},{10,... | collective-permute-start | bytes 1572872 | tf_op jit(solution)/shard_map/ppermute | solution.py:149
  232.4 35.7 %collective-permute-start.31 = (bf16[4,1024,128]{2,1,0:T(8,128)(2,1)S(1)}, bf16[4,1024,128]{2,1,0:T(8,128)(2,1)S(1)}, u32[]{:S(2)}, u32[]{:S(2)}) collective-permute-start(bf16[4,1024,128]{2,1,0:T(8,128)(2,1)S(1)} %fusion.2), channel_id=1, source_target_pairs={{0,8},{8,0},{1,9},{9,1},{2,10},{10,2},{3,11},{11,3},{4,12},{12,4},... | collective-permute-start | bytes 3145736 | tf_op jit(solution)/shard_map/ppermute | solution.py:144
  256.7 17.1 %collective-permute-start.29 = (bf16[1024,128]{1,0:T(8,128)(2,1)S(1)}, bf16[1024,128]{1,0:T(8,128)(2,1)S(1)}, u32[]{:S(2)}, u32[]{:S(2)}) collective-permute-start(bf16[1024,128]{1,0:T(8,128)(2,1)S(1)} %fusion.21), channel_id=1, source_target_pairs={{0,8},{8,0},{1,9},{9,1},{2,10},{10,2},{3,11},{11,3},{4,12},{12,4},... | collective-permute-start | bytes 786440 | tf_op jit(solution)/shard_map/ppermute | solution.py:144
  268.4 14.1 %collective-permute-start.32 = (bf16[1024,128]{1,0:T(8,128)(2,1)S(1)}, bf16[1024,128]{1,0:T(8,128)(2,1)S(1)}, u32[]{:S(2)}, u32[]{:S(2)}) collective-permute-start(bf16[1024,128]{1,0:T(8,128)(2,1)S(1)} %get-tuple-element.13), channel_id=1, source_target_pairs={{0,1},{1,2},{2,3},{3,0},{4,5},{5,6},{6,7},{7,4},{8,9},{9,10},{10,1... | collective-permute-start | bytes 786440 | tf_op jit(solution)/shard_map/ppermute | solution.py:149
  269.6 12.9 %collective-permute-start.34 = (bf16[1024,128]{1,0:T(8,128)(2,1)S(1)}, bf16[1024,128]{1,0:T(8,128)(2,1)S(1)}, u32[]{:S(2)}, u32[]{:S(2)}) collective-permute-start(bf16[1024,128]{1,0:T(8,128)(2,1)S(1)} %get-tuple-element.14), channel_id=1, source_target_pairs={{0,3},{1,0},{2,1},{3,2},{4,7},{5,4},{6,5},{7,6},{8,11},{9,8},{10,9... | collective-permute-start | bytes 786440 | tf_op jit(solution)/shard_map/ppermute | solution.py:149
  (17 other events, 664.9 us)

commit v4 on v3

--- a/solution.py
+++ b/solution.py
@@ -10,8 +10,8 @@
 
 LOAD = 32
 STEP = 4
-EARLY = 25
-LATE_X = 29
+EARLY = 18
+LATE_X = 23
 FIRST_X = 1024
 NT = (((1,), (1,)), ((), ()))
 NAMES = ("rz", "ry", "cy", "cc", "fx")
@@ -31,9 +31,9 @@
 
     src_copies = []
     for ref, (first, offsets) in zip(parts, where):
-        for n, (z, y, x) in enumerate(offsets):
-            row = jnp.bitwise_and(rz + z, 3) * 2 + jnp.bitwise_xor(ry, y)
-            col = jnp.bitwise_and(fx + x, 3)
+        for n, (relative, z, y, x) in enumerate(offsets):
+            row = (jnp.bitwise_and(rz + z, 3) if relative else z) * 2 + jnp.bitwise_xor(ry, y)
+            col = jnp.bitwise_and(fx + x, 3) if relative else x
             to = src.at[row, col, :, pl.ds(first, ref.shape[-1])]
             src_copies.append(pltpu.make_async_copy(ref.at[n], to, src_sem.at[len(src_copies)]))
     for copy in src_copies:
@@ -167,30 +167,30 @@
     return [value] + [shift(value, axis, -d) for d in STEPS[1:]]
 
 
-def ring_forward(value, axis):
-    before, after = shift(value, axis, 1), shift(value, axis, -1)
-    half = value.shape[0] // 2
-    return [value, before, after, shift(before[:half], axis, 1), shift(after[half:], axis, -1)]
-
-
 def gather_sources(x):
     late, last = EARLY * 128, (EARLY + LATE_X) * 128
-    p, q = x[:, :late], x[:, late:]
+    tie = lax.optimization_barrier
+    p = lax.all_gather(x[:, :late], ("rz", "fx")).reshape(4, 4, -1, late)
+    q = x[:, late:]
     q = jnp.stack([q, swap(q, "ry")])
+    a = jnp.stack(ring(q[:, :, : last - late], "rz"))
+    b = jnp.stack(ring(q[:, :, last - late :], "fx"))
+    p, a, b = tie((p, a, b))
+    p_low = swap(p[:2], "ry")
+    sides = [shift(v, axis, by) for v, axis in ((a, "fx"), (b, "rz")) for by in (1, -1)]
+    p_low, *sides = tie((p_low, *sides))
+    p_high = swap(tie((p[2:], p_low))[0], "ry")
     parts = []
-    for z, value in zip(STEPS, ring(jnp.stack(ring(p, "fx")), "rz")):
-        for y in (0, 1):
-            parts.append((swap(value, "ry") if y else value, 0, [(z, y, d) for d in STEPS]))
-    a, b = q[:, :, : last - late], q[:, :, last - late :]
-    for value, first, x_last in ((a, late, True), (b, last, False)):
-        one, two = ("rz", "fx") if x_last else ("fx", "rz")
-        done = ring_forward(jnp.stack(ring(value, one)), two)
+    for value, y, zs in ((p, 0, (0, 1, 2, 3)), (p_low, 1, (0, 1)), (p_high, 1, (2, 3))):
+        parts.append((value, 0, [(False, z, y, f) for z in zs for f in range(4)]))
+    for value, first, axis, (before, after) in ((a, late, "fx", sides[:2]), (b, last, "rz", sides[2:])):
+        done = (value, before, after, shift(before[:2], axis, 1), shift(after[2:], axis, -1))
         for far, near, part in zip((0, -1, 1, 2, 2), (STEPS, STEPS, STEPS, STEPS[:2], STEPS[2:]), done):
             offsets = [
-                (d, y, far) if x_last else (far, y, d) for d in near for y in (0, 1)
+                (True, d, y, far) if axis == "fx" else (True, far, y, d) for d in near for y in (0, 1)
             ]
-            parts.append((part.reshape(-1, *part.shape[2:]), first, offsets))
-    return parts
+            parts.append((part, first, offsets))
+    return [(v.reshape(-1, *v.shape[2:]), first, offsets) for v, first, offsets in parts]
 
 
 def reduce_rows(keep_a, keep_b, send_a, send_b):

time: 285 us -> 231 us (0.81)
  waiting for transfers between devices: 169 us -> 124 us
  starting transfers between devices: 81 us -> 47.1 us
  between operations: 0.95 us -> 14.3 us
  Pallas kernels: 20.7 us -> 27.5 us
  local copies, waits for them, and re-layouts: 4.88 us -> 8.31 us
    ppermute x26 -> x20, waiting for transfers between devices: 121 us -> 63.6 us  [shift(): return lax.ppermute(value, axis, [(i, (i + by) % n) for i in range(n)])]
    ppermute x9 -> x7, starting transfers between devices: 36.6 us -> 15.7 us  [swap(): return lax.ppermute(value, axis, [(0, 1), (1, 0)])]
    all_gather x0 -> x1, waiting for transfers between devices: none -> 16.9 us  [gather_sources(): p = lax.all_gather(x[:, :late], ('rz', 'fx')).reshape(4, 4, -1, late)]
    ppermute x26 -> x20, starting transfers between devices: 44.4 us -> 31.4 us  [shift(): return lax.ppermute(value, axis, [(i, (i + by) % n) for i in range(n)])]
    pallas_call x1, Pallas kernels: 20.7 us -> 27.5 us  [aggregate(): pl.pallas_call(functools.partial(aggregate_kernel, where, len(arrays)), o...]
    slice x5 -> x7, local copies, waits for them, and re-layouts: 1.22 us -> 6.54 us  [the longest x1 2.81 us: gather_sources(): p_high = swap(tie((p[2:], p_low))[0], 'ry')]
    ppermute x9 -> x7, waiting for transfers between devices: 48.6 us -> 43.4 us  [swap(): return lax.ppermute(value, axis, [(0, 1), (1, 0)])]
  transfers between devices with their start and end apart: 35 -> 28, of which waited for: 17 -> 20; matrix products, arithmetic and copies ran while one was open for 3% -> 5% of each run, Pallas kernels for 0% -> 0%
where the time goes in v4:
time: 231 us; the launch traced here: 228 us
  waiting for transfers between devices  124 us (54%)
  starting transfers between devices  47.1 us (20%)
  Pallas kernels  27.5 us (12%)
  between operations  14.3 us (6%)
  local copies, waits for them, and re-layouts  8.31 us (4%)
  other arithmetic  5.88 us (3%)
    ppermute x20, waiting for transfers between devices, shift(): return lax.ppermute(value, axis, [(i, (i + by) % n) for i in range(n)])  63.6 us
    ppermute x7, waiting for transfers between devices, swap(): return lax.ppermute(value, axis, [(0, 1), (1, 0)])  43.4 us
    ppermute x20, starting transfers between devices, shift(): return lax.ppermute(value, axis, [(i, (i + by) % n) for i in range(n)])  31.4 us
    pallas_call x1, Pallas kernels, aggregate(): pl.pallas_call(functools.partial(aggregate_kernel, where, len(arrays)), o...  27.5 us
    all_gather x1, waiting for transfers between devices, gather_sources(): p = lax.all_gather(x[:, :late], ('rz', 'fx')).reshape(4, 4, -1, late)  16.9 us
    ppermute x7, starting transfers between devices, swap(): return lax.ppermute(value, axis, [(0, 1), (1, 0)])  15.7 us
  transfers between devices with their start and end apart: 28, of which 20 were waited for; matrix products, arithmetic and copies ran while one was open for 5% of the time, Pallas kernels for 0%

profile of v4, /device:TPU:0, one launch (start us, length us, event | category | flops | bytes accessed | tf_op | source)
XLA Modules:
  0.0 228.3 jit_solution(15295366480858475549)
XLA Ops:
  9.2 3.4 %collective-permute-start = (bf16[32,5888]{1,0:T(8,128)(2,1)S(1)}, bf16[32,5888]{1,0:T(8,128)(2,1)S(1)}, u32[]{:S(2)}, u32[]{:S(2)}) collective-permute-start(bf16[32,5888]{1,0:T(8,128)(2,1)S(1)} %get-tuple-element.41), channel_id=1, source_target_pairs={{0,16},{16,0},{1,17},{17,1},{2,18},{18,2},{3,19},{19,3},{4,20},{20... | collective-permute-start | bytes 1130504 | tf_op jit(solution)/shard_map/ppermute | solution.py:144
  12.6 8.8 %collective-permute-done = bf16[32,5888]{1,0:T(8,128)(2,1)S(1)} collective-permute-done((bf16[32,5888]{1,0:T(8,128)(2,1)S(1)}, bf16[32,5888]{1,0:T(8,128)(2,1)S(1)}, u32[]{:S(2)}, u32[]{:S(2)}) %collective-permute-start) | collective-permute-done | bytes 376864 | tf_op jit(solution)/shard_map/ppermute | solution.py:144
  21.4 2.9 %collective-permute-start.5 = (bf16[2,32,2944]{2,1,0:T(8,128)(2,1)S(1)}, bf16[2,32,2944]{2,1,0:T(8,128)(2,1)S(1)}, u32[]{:S(2)}, u32[]{:S(2)}) collective-permute-start(bf16[2,32,2944]{2,1,0:T(8,128)(2,1)S(1)} %get-tuple-element.39), channel_id=1, source_target_pairs={{0,3},{1,0},{2,1},{3,2},{4,7},{5,4},{6,5},{7,6},{8,11},{9,8},{10,9... | collective-permute-start | bytes 1130504 | tf_op jit(solution)/shard_map/ppermute | solution.py:149
  24.3 2.3 %collective-permute-start.6 = (bf16[2,32,2944]{2,1,0:T(8,128)(2,1)S(1)}, bf16[2,32,2944]{2,1,0:T(8,128)(2,1)S(1)}, u32[]{:S(2)}, u32[]{:S(2)}) collective-permute-start(bf16[2,32,2944]{2,1,0:T(8,128)(2,1)S(1)} %get-tuple-element.39), channel_id=1, source_target_pairs={{0,2},{1,3},{2,0},{3,1},{4,6},{5,7},{6,4},{7,5},{8,10},{9,11},{10,... | collective-permute-start | bytes 1130504 | tf_op jit(solution)/shard_map/ppermute | solution.py:149
  26.6 3.9 %collective-permute-start.3 = (bf16[2,32,2944]{2,1,0:T(8,128)(2,1)S(1)}, bf16[2,32,2944]{2,1,0:T(8,128)(2,1)S(1)}, u32[]{:S(2)}, u32[]{:S(2)}) collective-permute-start(bf16[2,32,2944]{2,1,0:T(8,128)(2,1)S(1)} %get-tuple-element.40), channel_id=1, source_target_pairs={{0,64},{32,96},{64,0},{96,32},{1,65},{33,97},{65,1},{97,33},{2,66}... | collective-permute-start | bytes 1130504 | tf_op jit(solution)/shard_map/ppermute | solution.py:149
  31.2 10.0 %collective-permute-done.5 = bf16[2,32,2944]{2,1,0:T(8,128)(2,1)S(1)} collective-permute-done((bf16[2,32,2944]{2,1,0:T(8,128)(2,1)S(1)}, bf16[2,32,2944]{2,1,0:T(8,128)(2,1)S(1)}, u32[]{:S(2)}, u32[]{:S(2)}) %collective-permute-start.5) | collective-permute-done | bytes 376864 | tf_op jit(solution)/shard_map/ppermute | solution.py:149
  44.7 2.4 %collective-permute-done.2 = bf16[2,32,2944]{2,1,0:T(8,128)(2,1)S(1)} collective-permute-done((bf16[2,32,2944]{2,1,0:T(8,128)(2,1)S(1)}, bf16[2,32,2944]{2,1,0:T(8,128)(2,1)S(1)}, u32[]{:S(2)}, u32[]{:S(2)}) %collective-permute-start.2) | collective-permute-done | bytes 376864 | tf_op jit(solution)/shard_map/ppermute | solution.py:149
  47.1 3.6 %collective-permute-done.1 = bf16[2,32,2944]{2,1,0:T(8,128)(2,1)S(1)} collective-permute-done((bf16[2,32,2944]{2,1,0:T(8,128)(2,1)S(1)}, bf16[2,32,2944]{2,1,0:T(8,128)(2,1)S(1)}, u32[]{:S(2)}, u32[]{:S(2)}) %collective-permute-start.1) | collective-permute-done | bytes 376864 | tf_op jit(solution)/shard_map/ppermute | solution.py:149
  51.0 16.9 %all-gather.3.cloned.1.call-done = bf16[512,2304]{1,0:T(8,128)(2,1)} async-done(((bf16[32,2304]{1,0:T(8,128)(2,1)}), bf16[512,2304]{1,0:T(8,128)(2,1)}) %all-gather.3.cloned.1.call-update) | async-done | bytes 2359312 | tf_op jit(solution)/shard_map/all_gather | solution.py:173
  67.9 2.4 %collective-permute-start.9 = (bf16[4,2,32,2944]{3,2,1,0:T(8,128)(2,1)S(1)}, bf16[4,2,32,2944]{3,2,1,0:T(8,128)(2,1)S(1)}, u32[]{:S(2)}, u32[]{:S(2)}) collective-permute-start(bf16[4,2,32,2944]{3,2,1,0:T(8,128)(2,1)S(1)} %pad_maximum_fusion), channel_id=1, source_target_pairs={{0,3},{1,0},{2,1},{3,2},{4,7},{5,4},{6,5},{7,6},{8,11},{9,8},{10,9... | collective-permute-start | bytes 4521992 | tf_op jit(solution)/shard_map/ppermute | solution.py:149
  70.2 2.0 collective-permute-start.11
  72.3 2.8 %fusion.23 = (bf16[2,4,32,2304]{3,2,1,0:T(8,128)(2,1)}, bf16[2,4,32,2304]{3,2,1,0:T(8,128)(2,1)S(1)}) fusion(bf16[4,4,32,2304]{3,2,1,0:T(8,128)(2,1)} %bitcast.86), kind=kLoop, calls=%fused_computation.45 | loop fusion | bytes 4718592 | tf_op jit(solution)/shard_map/slice | solution.py:182
  75.1 3.0 %collective-permute-start.7 = (bf16[2,4,32,2304]{3,2,1,0:T(8,128)(2,1)S(1)}, bf16[2,4,32,2304]{3,2,1,0:T(8,128)(2,1)S(1)}, u32[]{:S(2)}, u32[]{:S(2)}) collective-permute-start(bf16[2,4,32,2304]{3,2,1,0:T(8,128)(2,1)S(1)} %get-tuple-element.38), channel_id=1, source_target_pairs={{0,16},{16,0},{1,17},{17,1},{2,18},{18,2},{3,19},{19,3},{4,20},{20... | collective-permute-start | bytes 3538952 | tf_op jit(solution)/shard_map/ppermute | solution.py:144
  78.1 24.3 %collective-permute-done.7 = bf16[2,4,32,2304]{3,2,1,0:T(8,128)(2,1)S(1)} collective-permute-done((bf16[2,4,32,2304]{3,2,1,0:T(8,128)(2,1)S(1)}, bf16[2,4,32,2304]{3,2,1,0:T(8,128)(2,1)S(1)}, u32[]{:S(2)}, u32[]{:S(2)}) %collective-permute-start.7) | collective-permute-done | bytes 1179680 | tf_op jit(solution)/shard_map/ppermute | solution.py:144
  102.4 2.4 %collective-permute-done.8 = bf16[4,2,32,2944]{3,2,1,0:T(8,128)(2,1)S(1)} collective-permute-done((bf16[4,2,32,2944]{3,2,1,0:T(8,128)(2,1)S(1)}, bf16[4,2,32,2944]{3,2,1,0:T(8,128)(2,1)S(1)}, u32[]{:S(2)}, u32[]{:S(2)}) %collective-permute-start.8) | collective-permute-done | bytes 1507360 | tf_op jit(solution)/shard_map/ppermute | solution.py:149
  106.3 3.0 %collective-permute-start.12 = (bf16[2,4,32,2304]{3,2,1,0:T(8,128)(2,1)}, bf16[2,4,32,2304]{3,2,1,0:T(8,128)(2,1)S(1)}, u32[]{:S(2)}, u32[]{:S(2)}) collective-permute-start(bf16[2,4,32,2304]{3,2,1,0:T(8,128)(2,1)} %get-tuple-element.22), channel_id=1, source_target_pairs={{0,16},{16,0},{1,17},{17,1},{2,18},{18,2},{3,19},{19,3},{4,20},{20... | collective-permute-start | bytes 3538952 | tf_op jit(solution)/shard_map/ppermute | solution.py:144
  112.5 2.1 collective-permute-start.14
  117.2 9.1 %collective-permute-done.16 = bf16[2,2,32,2944]{3,2,1,0:T(8,128)(2,1)} collective-permute-done((bf16[2,2,32,2944]{3,2,1,0:T(8,128)(2,1)}, bf16[2,2,32,2944]{3,2,1,0:T(8,128)(2,1)}, u32[]{:S(2)}, u32[]{:S(2)}) %collective-permute-start.16) | collective-permute-done | bytes 753696 | tf_op jit(solution)/shard_map/ppermute | solution.py:149
  127.7 3.0 %collective-permute-done.13 = bf16[2,2,32,2944]{3,2,1,0:T(8,128)(2,1)} collective-permute-done((bf16[2,2,32,2944]{3,2,1,0:T(8,128)(2,1)S(1)}, bf16[2,2,32,2944]{3,2,1,0:T(8,128)(2,1)}, u32[]{:S(2)}, u32[]{:S(2)}) %collective-permute-start.13) | collective-permute-done | bytes 753696 | tf_op jit(solution)/shard_map/ppermute | solution.py:149
  130.7 2.2 collective-permute-done.12
  134.0 27.5 %aggregate.1 = (bf16[4,2,1024,128]{3,2,1,0:T(8,128)(2,1)}, bf16[2,4,1024,128]{3,2,1,0:T(8,128)(2,1)}, bf16[4,2,1024,128]{3,2,1,0:T(8,128)(2,1)}, bf16[2,4,1024,128]{3,2,1,0:T(8,128)(2,1)}) custom-call(s32[384]{0:T(512)} %reduce.rows_ref, s32[384]{0:T(512)} %reduce.1.cols_ref, s32[6]{0:T(128)} %stack.62.info_ref, bf16[384,128,128]{2,1,0:T(8,128)(2,1)} %bitcast.85, ...), custom_call_target="tpu_custom_call" | custom-call | tf_op jit(solution)/shard_map/aggregate/pallas_call | solution.py:120
  161.5 5.9 %collective-permute-start.17 = (bf16[4,2,1024,128]{3,2,1,0:T(8,128)(2,1)}, bf16[4,2,1024,128]{3,2,1,0:T(8,128)(2,1)S(1)}, u32[]{:S(2)}, u32[]{:S(2)}) collective-permute-start(bf16[4,2,1024,128]{3,2,1,0:T(8,128)(2,1)} %get-tuple-element.28), channel_id=1, source_target_pairs={{0,4},{4,0},{1,5},{5,1},{2,6},{6,2},{3,7},{7,3},{8,12},{12,8},{9,1... | collective-permute-start | bytes 6291464 | tf_op jit(solution)/shard_map/ppermute | solution.py:144
  167.5 3.9 %collective-permute-done.17 = bf16[4,2,1024,128]{3,2,1,0:T(8,128)(2,1)S(1)} collective-permute-done((bf16[4,2,1024,128]{3,2,1,0:T(8,128)(2,1)}, bf16[4,2,1024,128]{3,2,1,0:T(8,128)(2,1)S(1)}, u32[]{:S(2)}, u32[]{:S(2)}) %collective-permute-start.17) | collective-permute-done | bytes 2097184 | tf_op jit(solution)/shard_map/ppermute | solution.py:144
  173.4 3.2 %collective-permute-start.20 = (bf16[2,1024,128]{2,1,0:T(8,128)(2,1)S(1)}, bf16[2,1024,128]{2,1,0:T(8,128)(2,1)S(1)}, u32[]{:S(2)}, u32[]{:S(2)}) collective-permute-start(bf16[2,1024,128]{2,1,0:T(8,128)(2,1)S(1)} %get-tuple-element.35), channel_id=1, source_target_pairs={{0,3},{1,0},{2,1},{3,2},{4,7},{5,4},{6,5},{7,6},{8,11},{9,8},{10,9... | collective-permute-start | bytes 1572872 | tf_op jit(solution)/shard_map/ppermute | solution.py:149
  176.6 4.5 %collective-permute-start.19 = (bf16[2,1024,128]{2,1,0:T(8,128)(2,1)S(1)}, bf16[2,1024,128]{2,1,0:T(8,128)(2,1)S(1)}, u32[]{:S(2)}, u32[]{:S(2)}) collective-permute-start(bf16[2,1024,128]{2,1,0:T(8,128)(2,1)S(1)} %get-tuple-element.36), channel_id=1, source_target_pairs={{0,2},{1,3},{2,0},{3,1},{4,6},{5,7},{6,4},{7,5},{8,10},{9,11},{10,... | collective-permute-start | bytes 1572872 | tf_op jit(solution)/shard_map/ppermute | solution.py:149
  181.7 7.1 %collective-permute-done.18 = bf16[2,1024,128]{2,1,0:T(8,128)(2,1)S(1)} collective-permute-done((bf16[2,1024,128]{2,1,0:T(8,128)(2,1)S(1)}, bf16[2,1024,128]{2,1,0:T(8,128)(2,1)S(1)}, u32[]{:S(2)}, u32[]{:S(2)}) %collective-permute-start.18) | collective-permute-done | bytes 524320 | tf_op jit(solution)/shard_map/ppermute | solution.py:149
  188.8 3.0 %collective-permute-done.20 = bf16[2,1024,128]{2,1,0:T(8,128)(2,1)S(1)} collective-permute-done((bf16[2,1024,128]{2,1,0:T(8,128)(2,1)S(1)}, bf16[2,1024,128]{2,1,0:T(8,128)(2,1)S(1)}, u32[]{:S(2)}, u32[]{:S(2)}) %collective-permute-start.20) | collective-permute-done | bytes 524320 | tf_op jit(solution)/shard_map/ppermute | solution.py:149
  191.8 10.8 %collective-permute-done.19 = bf16[2,1024,128]{2,1,0:T(8,128)(2,1)S(1)} collective-permute-done((bf16[2,1024,128]{2,1,0:T(8,128)(2,1)S(1)}, bf16[2,1024,128]{2,1,0:T(8,128)(2,1)S(1)}, u32[]{:S(2)}, u32[]{:S(2)}) %collective-permute-start.19) | collective-permute-done | bytes 524320 | tf_op jit(solution)/shard_map/ppermute | solution.py:149
  204.1 2.0 collective-permute-done.23
  206.5 3.2 %collective-permute-start.26 = (bf16[1024,128]{1,0:T(8,128)(2,1)S(1)}, bf16[1024,128]{1,0:T(8,128)(2,1)S(1)}, u32[]{:S(2)}, u32[]{:S(2)}) collective-permute-start(bf16[1024,128]{1,0:T(8,128)(2,1)S(1)} %get-tuple-element.32), channel_id=1, source_target_pairs={{0,3},{1,0},{2,1},{3,2},{4,7},{5,4},{6,5},{7,6},{8,11},{9,8},{10,9... | collective-permute-start | bytes 786440 | tf_op jit(solution)/shard_map/ppermute | solution.py:149
  209.7 2.2 collective-permute-done.21
  212.0 7.9 %collective-permute-done.24 = bf16[1024,128]{1,0:T(8,128)(2,1)S(1)} collective-permute-done((bf16[1024,128]{1,0:T(8,128)(2,1)S(1)}, bf16[1024,128]{1,0:T(8,128)(2,1)S(1)}, u32[]{:S(2)}, u32[]{:S(2)}) %collective-permute-start.24) | collective-permute-done | bytes 262176 | tf_op jit(solution)/shard_map/ppermute | solution.py:149
  (73 shorter events, 22.4 us)
Async XLA Ops:
  6.5 213.5 %copy-start = (bf16[128,256]{1,0:T(8,128)(2,1)S(1)}, bf16[128,256]{1,0:T(8,128)(2,1)}, u32[]{:S(2)}) copy-start(bf16[128,256]{1,0:T(8,128)(2,1)} %param.12) | copy-start | bytes 196612
  6.5 61.3 %all-gather.3.cloned.1.call-start = ((), (), s32[]{:S(2)}) async-start(), calls=%async_computation | async-start | bytes 2506752 | tf_op jit(solution)/shard_map/all_gather | solution.py:173
  9.2 12.1 %collective-permute-start = (bf16[32,5888]{1,0:T(8,128)(2,1)S(1)}, bf16[32,5888]{1,0:T(8,128)(2,1)S(1)}, u32[]{:S(2)}, u32[]{:S(2)}) collective-permute-start(bf16[32,5888]{1,0:T(8,128)(2,1)S(1)} %get-tuple-element.41), channel_id=1, source_target_pairs={{0,16},{16,0},{1,17},{17,1},{2,18},{18,2},{3,19},{19,3},{4,20},{20... | collective-permute-start | bytes 1130504 | tf_op jit(solution)/shard_map/ppermute | solution.py:144
  21.4 19.7 %collective-permute-start.5 = (bf16[2,32,2944]{2,1,0:T(8,128)(2,1)S(1)}, bf16[2,32,2944]{2,1,0:T(8,128)(2,1)S(1)}, u32[]{:S(2)}, u32[]{:S(2)}) collective-permute-start(bf16[2,32,2944]{2,1,0:T(8,128)(2,1)S(1)} %get-tuple-element.39), channel_id=1, source_target_pairs={{0,3},{1,0},{2,1},{3,2},{4,7},{5,4},{6,5},{7,6},{8,11},{9,8},{10,9... | collective-permute-start | bytes 1130504 | tf_op jit(solution)/shard_map/ppermute | solution.py:149
  24.3 20.2 %collective-permute-start.4 = (bf16[2,32,2944]{2,1,0:T(8,128)(2,1)S(1)}, bf16[2,32,2944]{2,1,0:T(8,128)(2,1)S(1)}, u32[]{:S(2)}, u32[]{:S(2)}) collective-permute-start(bf16[2,32,2944]{2,1,0:T(8,128)(2,1)S(1)} %get-tuple-element.39), channel_id=1, source_target_pairs={{0,1},{1,2},{2,3},{3,0},{4,5},{5,6},{6,7},{7,4},{8,9},{9,10},{10,1... | collective-permute-start | bytes 1130504 | tf_op jit(solution)/shard_map/ppermute | solution.py:149
  24.3 20.2 %collective-permute-start.6 = (bf16[2,32,2944]{2,1,0:T(8,128)(2,1)S(1)}, bf16[2,32,2944]{2,1,0:T(8,128)(2,1)S(1)}, u32[]{:S(2)}, u32[]{:S(2)}) collective-permute-start(bf16[2,32,2944]{2,1,0:T(8,128)(2,1)S(1)} %get-tuple-element.39), channel_id=1, source_target_pairs={{0,2},{1,3},{2,0},{3,1},{4,6},{5,7},{6,4},{7,5},{8,10},{9,11},{10,... | collective-permute-start | bytes 1130504 | tf_op jit(solution)/shard_map/ppermute | solution.py:149
  26.6 18.2 %collective-permute-start.3 = (bf16[2,32,2944]{2,1,0:T(8,128)(2,1)S(1)}, bf16[2,32,2944]{2,1,0:T(8,128)(2,1)S(1)}, u32[]{:S(2)}, u32[]{:S(2)}) collective-permute-start(bf16[2,32,2944]{2,1,0:T(8,128)(2,1)S(1)} %get-tuple-element.40), channel_id=1, source_target_pairs={{0,64},{32,96},{64,0},{96,32},{1,65},{33,97},{65,1},{97,33},{2,66}... | collective-permute-start | bytes 1130504 | tf_op jit(solution)/shard_map/ppermute | solution.py:149
  30.4 16.7 %collective-permute-start.2 = (bf16[2,32,2944]{2,1,0:T(8,128)(2,1)S(1)}, bf16[2,32,2944]{2,1,0:T(8,128)(2,1)S(1)}, u32[]{:S(2)}, u32[]{:S(2)}) collective-permute-start(bf16[2,32,2944]{2,1,0:T(8,128)(2,1)S(1)} %get-tuple-element.40), channel_id=1, source_target_pairs={{0,96},{32,0},{64,32},{96,64},{1,97},{33,1},{65,33},{97,65},{2,98}... | collective-permute-start | bytes 1130504 | tf_op jit(solution)/shard_map/ppermute | solution.py:149
  41.1 9.6 %collective-permute-start.1 = (bf16[2,32,2944]{2,1,0:T(8,128)(2,1)S(1)}, bf16[2,32,2944]{2,1,0:T(8,128)(2,1)S(1)}, u32[]{:S(2)}, u32[]{:S(2)}) collective-permute-start(bf16[2,32,2944]{2,1,0:T(8,128)(2,1)S(1)} %get-tuple-element.40), channel_id=1, source_target_pairs={{0,32},{32,64},{64,96},{96,0},{1,33},{33,65},{65,97},{97,1},{2,34}... | collective-permute-start | bytes 1130504 | tf_op jit(solution)/shard_map/ppermute | solution.py:149
  44.7 30.4 %copy-start.1 = (bf16[4,2,32,2944]{3,2,1,0:T(8,128)(2,1)}, bf16[4,2,32,2944]{3,2,1,0:T(8,128)(2,1)S(1)}, u32[]{:S(2)}) copy-start(bf16[4,2,32,2944]{3,2,1,0:T(8,128)(2,1)S(1)} %pad_maximum_fusion.1) | copy-start | bytes 4521988
  51.0 24.1 %copy-start.2 = (bf16[4,2,32,2944]{3,2,1,0:T(8,128)(2,1)}, bf16[4,2,32,2944]{3,2,1,0:T(8,128)(2,1)S(1)}, u32[]{:S(2)}) copy-start(bf16[4,2,32,2944]{3,2,1,0:T(8,128)(2,1)S(1)} %pad_maximum_fusion) | copy-start | bytes 4521988
  67.9 34.5 %collective-permute-start.9 = (bf16[4,2,32,2944]{3,2,1,0:T(8,128)(2,1)S(1)}, bf16[4,2,32,2944]{3,2,1,0:T(8,128)(2,1)S(1)}, u32[]{:S(2)}, u32[]{:S(2)}) collective-permute-start(bf16[4,2,32,2944]{3,2,1,0:T(8,128)(2,1)S(1)} %pad_maximum_fusion), channel_id=1, source_target_pairs={{0,3},{1,0},{2,1},{3,2},{4,7},{5,4},{6,5},{7,6},{8,11},{9,8},{10,9... | collective-permute-start | bytes 4521992 | tf_op jit(solution)/shard_map/ppermute | solution.py:149
  70.2 34.6 %collective-permute-start.8 = (bf16[4,2,32,2944]{3,2,1,0:T(8,128)(2,1)S(1)}, bf16[4,2,32,2944]{3,2,1,0:T(8,128)(2,1)S(1)}, u32[]{:S(2)}, u32[]{:S(2)}) collective-permute-start(bf16[4,2,32,2944]{3,2,1,0:T(8,128)(2,1)S(1)} %pad_maximum_fusion), channel_id=1, source_target_pairs={{0,1},{1,2},{2,3},{3,0},{4,5},{5,6},{6,7},{7,4},{8,9},{9,10},{10,1... | collective-permute-start | bytes 4521992 | tf_op jit(solution)/shard_map/ppermute | solution.py:149
  70.2 34.6 %collective-permute-start.11 = (bf16[4,2,32,2944]{3,2,1,0:T(8,128)(2,1)S(1)}, bf16[4,2,32,2944]{3,2,1,0:T(8,128)(2,1)S(1)}, u32[]{:S(2)}, u32[]{:S(2)}) collective-permute-start(bf16[4,2,32,2944]{3,2,1,0:T(8,128)(2,1)S(1)} %pad_maximum_fusion.1), channel_id=1, source_target_pairs={{0,96},{32,0},{64,32},{96,64},{1,97},{33,1},{65,33},{97,65},{2,98}... | collective-permute-start | bytes 4521992 | tf_op jit(solution)/shard_map/ppermute | solution.py:149
  72.3 34.1 %collective-permute-start.10 = (bf16[4,2,32,2944]{3,2,1,0:T(8,128)(2,1)S(1)}, bf16[4,2,32,2944]{3,2,1,0:T(8,128)(2,1)S(1)}, u32[]{:S(2)}, u32[]{:S(2)}) collective-permute-start(bf16[4,2,32,2944]{3,2,1,0:T(8,128)(2,1)S(1)} %pad_maximum_fusion.1), channel_id=1, source_target_pairs={{0,32},{32,64},{64,96},{96,0},{1,33},{33,65},{65,97},{97,1},{2,34}... | collective-permute-start | bytes 4521992 | tf_op jit(solution)/shard_map/ppermute | solution.py:149
  75.1 27.3 %collective-permute-start.7 = (bf16[2,4,32,2304]{3,2,1,0:T(8,128)(2,1)S(1)}, bf16[2,4,32,2304]{3,2,1,0:T(8,128)(2,1)S(1)}, u32[]{:S(2)}, u32[]{:S(2)}) collective-permute-start(bf16[2,4,32,2304]{3,2,1,0:T(8,128)(2,1)S(1)} %get-tuple-element.38), channel_id=1, source_target_pairs={{0,16},{16,0},{1,17},{17,1},{2,18},{18,2},{3,19},{19,3},{4,20},{20... | collective-permute-start | bytes 3538952 | tf_op jit(solution)/shard_map/ppermute | solution.py:144
  106.3 26.6 %collective-permute-start.12 = (bf16[2,4,32,2304]{3,2,1,0:T(8,128)(2,1)}, bf16[2,4,32,2304]{3,2,1,0:T(8,128)(2,1)S(1)}, u32[]{:S(2)}, u32[]{:S(2)}) collective-permute-start(bf16[2,4,32,2304]{3,2,1,0:T(8,128)(2,1)} %get-tuple-element.22), channel_id=1, source_target_pairs={{0,16},{16,0},{1,17},{17,1},{2,18},{18,2},{3,19},{19,3},{4,20},{20... | collective-permute-start | bytes 3538952 | tf_op jit(solution)/shard_map/ppermute | solution.py:144
  110.5 15.8 %collective-permute-start.16 = (bf16[2,2,32,2944]{3,2,1,0:T(8,128)(2,1)}, bf16[2,2,32,2944]{3,2,1,0:T(8,128)(2,1)}, u32[]{:S(2)}, u32[]{:S(2)}) collective-permute-start(bf16[2,2,32,2944]{3,2,1,0:T(8,128)(2,1)} %slice.112), channel_id=1, source_target_pairs={{0,96},{32,0},{64,32},{96,64},{1,97},{33,1},{65,33},{97,65},{2,98}... | collective-permute-start | bytes 2261000 | tf_op jit(solution)/shard_map/ppermute | solution.py:149
  110.9 16.8 %collective-permute-start.15 = (bf16[2,2,32,2944]{3,2,1,0:T(8,128)(2,1)S(1)}, bf16[2,2,32,2944]{3,2,1,0:T(8,128)(2,1)}, u32[]{:S(2)}, u32[]{:S(2)}) collective-permute-start(bf16[2,2,32,2944]{3,2,1,0:T(8,128)(2,1)S(1)} %slice.111), channel_id=1, source_target_pairs={{0,32},{32,64},{64,96},{96,0},{1,33},{33,65},{65,97},{97,1},{2,34}... | collective-permute-start | bytes 2261000 | tf_op jit(solution)/shard_map/ppermute | solution.py:149
  112.5 15.2 %collective-permute-start.14 = (bf16[2,2,32,2944]{3,2,1,0:T(8,128)(2,1)S(1)}, bf16[2,2,32,2944]{3,2,1,0:T(8,128)(2,1)}, u32[]{:S(2)}, u32[]{:S(2)}) collective-permute-start(bf16[2,2,32,2944]{3,2,1,0:T(8,128)(2,1)S(1)} %slice.110), channel_id=1, source_target_pairs={{0,3},{1,0},{2,1},{3,2},{4,7},{5,4},{6,5},{7,6},{8,11},{9,8},{10,9... | collective-permute-start | bytes 2261000 | tf_op jit(solution)/shard_map/ppermute | solution.py:149
  114.7 16.0 %collective-permute-start.13 = (bf16[2,2,32,2944]{3,2,1,0:T(8,128)(2,1)S(1)}, bf16[2,2,32,2944]{3,2,1,0:T(8,128)(2,1)}, u32[]{:S(2)}, u32[]{:S(2)}) collective-permute-start(bf16[2,2,32,2944]{3,2,1,0:T(8,128)(2,1)S(1)} %slice.109), channel_id=1, source_target_pairs={{0,1},{1,2},{2,3},{3,0},{4,5},{5,6},{6,7},{7,4},{8,9},{9,10},{10,1... | collective-permute-start | bytes 2261000 | tf_op jit(solution)/shard_map/ppermute | solution.py:149
  161.5 9.9 %collective-permute-start.17 = (bf16[4,2,1024,128]{3,2,1,0:T(8,128)(2,1)}, bf16[4,2,1024,128]{3,2,1,0:T(8,128)(2,1)S(1)}, u32[]{:S(2)}, u32[]{:S(2)}) collective-permute-start(bf16[4,2,1024,128]{3,2,1,0:T(8,128)(2,1)} %get-tuple-element.28), channel_id=1, source_target_pairs={{0,4},{4,0},{1,5},{5,1},{2,6},{6,2},{3,7},{7,3},{8,12},{12,8},{9,1... | collective-permute-start | bytes 6291464 | tf_op jit(solution)/shard_map/ppermute | solution.py:144
  167.4 13.8 %collective-permute-start.22 = (bf16[2,4,1024,128]{3,2,1,0:T(8,128)(2,1)}, bf16[2,4,1024,128]{3,2,1,0:T(8,128)(2,1)S(1)}, u32[]{:S(2)}, u32[]{:S(2)}) collective-permute-start(bf16[2,4,1024,128]{3,2,1,0:T(8,128)(2,1)} %get-tuple-element.30), channel_id=1, source_target_pairs={{0,4},{4,0},{1,5},{5,1},{2,6},{6,2},{3,7},{7,3},{8,12},{12,8},{9,1... | collective-permute-start | bytes 6291464 | tf_op jit(solution)/shard_map/ppermute | solution.py:144
  173.3 15.5 %collective-permute-start.18 = (bf16[2,1024,128]{2,1,0:T(8,128)(2,1)S(1)}, bf16[2,1024,128]{2,1,0:T(8,128)(2,1)S(1)}, u32[]{:S(2)}, u32[]{:S(2)}) collective-permute-start(bf16[2,1024,128]{2,1,0:T(8,128)(2,1)S(1)} %get-tuple-element.34), channel_id=1, source_target_pairs={{0,1},{1,2},{2,3},{3,0},{4,5},{5,6},{6,7},{7,4},{8,9},{9,10},{10,1... | collective-permute-start | bytes 1572872 | tf_op jit(solution)/shard_map/ppermute | solution.py:149
  173.4 18.4 %collective-permute-start.20 = (bf16[2,1024,128]{2,1,0:T(8,128)(2,1)S(1)}, bf16[2,1024,128]{2,1,0:T(8,128)(2,1)S(1)}, u32[]{:S(2)}, u32[]{:S(2)}) collective-permute-start(bf16[2,1024,128]{2,1,0:T(8,128)(2,1)S(1)} %get-tuple-element.35), channel_id=1, source_target_pairs={{0,3},{1,0},{2,1},{3,2},{4,7},{5,4},{6,5},{7,6},{8,11},{9,8},{10,9... | collective-permute-start | bytes 1572872 | tf_op jit(solution)/shard_map/ppermute | solution.py:149
  176.6 26.0 %collective-permute-start.19 = (bf16[2,1024,128]{2,1,0:T(8,128)(2,1)S(1)}, bf16[2,1024,128]{2,1,0:T(8,128)(2,1)S(1)}, u32[]{:S(2)}, u32[]{:S(2)}) collective-permute-start(bf16[2,1024,128]{2,1,0:T(8,128)(2,1)S(1)} %get-tuple-element.36), channel_id=1, source_target_pairs={{0,2},{1,3},{2,0},{3,1},{4,6},{5,7},{6,4},{7,5},{8,10},{9,11},{10,... | collective-permute-start | bytes 1572872 | tf_op jit(solution)/shard_map/ppermute | solution.py:149
  181.4 24.6 %collective-permute-start.23 = (bf16[4,1024,128]{2,1,0:T(8,128)(2,1)S(1)}, bf16[4,1024,128]{2,1,0:T(8,128)(2,1)S(1)}, u32[]{:S(2)}, u32[]{:S(2)}) collective-permute-start(bf16[4,1024,128]{2,1,0:T(8,128)(2,1)S(1)} %fusion.2), channel_id=1, source_target_pairs={{0,8},{8,0},{1,9},{9,1},{2,10},{10,2},{3,11},{11,3},{4,12},{12,4},... | collective-permute-start | bytes 3145736 | tf_op jit(solution)/shard_map/ppermute | solution.py:144
  204.0 7.9 %collective-permute-start.21 = (bf16[1024,128]{1,0:T(8,128)(2,1)S(1)}, bf16[1024,128]{1,0:T(8,128)(2,1)S(1)}, u32[]{:S(2)}, u32[]{:S(2)}) collective-permute-start(bf16[1024,128]{1,0:T(8,128)(2,1)S(1)} %fusion.21), channel_id=1, source_target_pairs={{0,8},{8,0},{1,9},{9,1},{2,10},{10,2},{3,11},{11,3},{4,12},{12,4},... | collective-permute-start | bytes 786440 | tf_op jit(solution)/shard_map/ppermute | solution.py:144
  206.4 13.7 %copy-start.12 = (f32[256]{0:T(256)S(1)}, f32[256]{0:T(256)}, u32[]{:S(2)}) copy-start(f32[256]{0:T(256)} %param.13) | copy-start | bytes 3076
  206.4 13.5 %collective-permute-start.24 = (bf16[1024,128]{1,0:T(8,128)(2,1)S(1)}, bf16[1024,128]{1,0:T(8,128)(2,1)S(1)}, u32[]{:S(2)}, u32[]{:S(2)}) collective-permute-start(bf16[1024,128]{1,0:T(8,128)(2,1)S(1)} %get-tuple-element.31), channel_id=1, source_target_pairs={{0,1},{1,2},{2,3},{3,0},{4,5},{5,6},{6,7},{7,4},{8,9},{9,10},{10,1... | collective-permute-start | bytes 786440 | tf_op jit(solution)/shard_map/ppermute | solution.py:149
  206.5 13.4 %collective-permute-start.26 = (bf16[1024,128]{1,0:T(8,128)(2,1)S(1)}, bf16[1024,128]{1,0:T(8,128)(2,1)S(1)}, u32[]{:S(2)}, u32[]{:S(2)}) collective-permute-start(bf16[1024,128]{1,0:T(8,128)(2,1)S(1)} %get-tuple-element.32), channel_id=1, source_target_pairs={{0,3},{1,0},{2,1},{3,2},{4,7},{5,4},{6,5},{7,6},{8,11},{9,8},{10,9... | collective-permute-start | bytes 786440 | tf_op jit(solution)/shard_map/ppermute | solution.py:149
  209.7 10.2 %collective-permute-start.25 = (bf16[1024,128]{1,0:T(8,128)(2,1)S(1)}, bf16[1024,128]{1,0:T(8,128)(2,1)S(1)}, u32[]{:S(2)}, u32[]{:S(2)}) collective-permute-start(bf16[1024,128]{1,0:T(8,128)(2,1)S(1)} %get-tuple-element.33), channel_id=1, source_target_pairs={{0,2},{1,3},{2,0},{3,1},{4,6},{5,7},{6,4},{7,5},{8,10},{9,11},{10,... | collective-permute-start | bytes 786440 | tf_op jit(solution)/shard_map/ppermute | solution.py:149
  (9 other events, 47.9 us)
Sparse Core Ops, SparseCore 0:
  9.5 58.3 all-gather.2

commit v5 on v3

--- a/solution.py
+++ b/solution.py
@@ -10,8 +10,6 @@
 
 LOAD = 32
 STEP = 4
-EARLY = 25
-LATE_X = 29
 FIRST_X = 1024
 NT = (((1,), (1,)), ((), ()))
 NAMES = ("rz", "ry", "cy", "cc", "fx")
@@ -167,28 +165,17 @@
     return [value] + [shift(value, axis, -d) for d in STEPS[1:]]
 
 
-def ring_forward(value, axis):
-    before, after = shift(value, axis, 1), shift(value, axis, -1)
-    half = value.shape[0] // 2
-    return [value, before, after, shift(before[:half], axis, 1), shift(after[half:], axis, -1)]
-
-
 def gather_sources(x):
-    late, last = EARLY * 128, (EARLY + LATE_X) * 128
-    p, q = x[:, :late], x[:, late:]
-    q = jnp.stack([q, swap(q, "ry")])
+    other = swap(x, "ry")
+    half = x.shape[1] // 2
     parts = []
-    for z, value in zip(STEPS, ring(jnp.stack(ring(p, "fx")), "rz")):
-        for y in (0, 1):
-            parts.append((swap(value, "ry") if y else value, 0, [(z, y, d) for d in STEPS]))
-    a, b = q[:, :, : last - late], q[:, :, last - late :]
-    for value, first, x_last in ((a, late, True), (b, last, False)):
-        one, two = ("rz", "fx") if x_last else ("fx", "rz")
-        done = ring_forward(jnp.stack(ring(value, one)), two)
-        for far, near, part in zip((0, -1, 1, 2, 2), (STEPS, STEPS, STEPS, STEPS[:2], STEPS[2:]), done):
-            offsets = [
-                (d, y, far) if x_last else (far, y, d) for d in near for y in (0, 1)
-            ]
+    for first, one, two in ((0, "rz", "fx"), (half, "fx", "rz")):
+        lanes = slice(first, first + half)
+        value = jnp.stack([jnp.stack(ring(v[:, lanes], one)) for v in (x, other)])
+        before, after = shift(value, two, 1), shift(value, two, -1)
+        done = (value, before, after, shift(before[:1], two, 1), shift(after[1:], two, -1))
+        for far, ys, part in zip((0, -1, 1, 2, 2), ((0, 1), (0, 1), (0, 1), (0,), (1,)), done):
+            offsets = [(d, y, far) if two == "fx" else (far, y, d) for y in ys for d in STEPS]
             parts.append((part.reshape(-1, *part.shape[2:]), first, offsets))
     return parts
 

time: 285 us -> 216 us (0.76)
  waiting for transfers between devices: 169 us -> 104 us
  Pallas kernels: 20.7 us -> 16.1 us
  starting transfers between devices: 81 us -> 77.7 us
    ppermute x9 -> x5, waiting for transfers between devices: 48.6 us -> 5.84 us  [swap(): return lax.ppermute(value, axis, [(0, 1), (1, 0)])]
    ppermute x26, waiting for transfers between devices: 121 us -> 98.1 us  [shift(): return lax.ppermute(value, axis, [(i, (i + by) % n) for i in range(n)])]
    ppermute x9 -> x5, starting transfers between devices: 36.6 us -> 27.6 us  [swap(): return lax.ppermute(value, axis, [(0, 1), (1, 0)])]
    ppermute x26, starting transfers between devices: 44.4 us -> 50.1 us  [shift(): return lax.ppermute(value, axis, [(i, (i + by) % n) for i in range(n)])]
    pallas_call x1, Pallas kernels: 20.7 us -> 16.1 us  [aggregate(): pl.pallas_call(functools.partial(aggregate_kernel, where, len(arrays)), o...]
    slice x5 -> x4, local copies, waits for them, and re-layouts: 1.22 us -> 4.55 us  [the longest x2 2.32 us: gather_sources(): after[1:]]
  transfers between devices with their start and end apart: 35 -> 31, of which waited for: 17 -> 18; matrix products, arithmetic and copies ran while one was open for 3% -> 5% of each run, Pallas kernels for 0% -> 0%
where the time goes in v5:
time: 216 us; the launch traced here: 214 us
  waiting for transfers between devices  104 us (48%)
  starting transfers between devices  77.7 us (36%)
  Pallas kernels  16.1 us (7%)
  local copies, waits for them, and re-layouts  7.51 us (3%)
  other arithmetic  6.27 us (3%)
    ppermute x26, waiting for transfers between devices, shift(): return lax.ppermute(value, axis, [(i, (i + by) % n) for i in range(n)])  98.1 us
    ppermute x26, starting transfers between devices, shift(): return lax.ppermute(value, axis, [(i, (i + by) % n) for i in range(n)])  50.1 us
    ppermute x5, starting transfers between devices, swap(): return lax.ppermute(value, axis, [(0, 1), (1, 0)])  27.6 us
    pallas_call x1, Pallas kernels, aggregate(): pl.pallas_call(functools.partial(aggregate_kernel, where, len(arrays)), o...  16.1 us
    ppermute x5, waiting for transfers between devices, swap(): return lax.ppermute(value, axis, [(0, 1), (1, 0)])  5.84 us
  transfers between devices with their start and end apart: 31, of which 18 were waited for; matrix products, arithmetic and copies ran while one was open for 5% of the time, Pallas kernels for 0%

profile of v5, /device:TPU:0, one launch (start us, length us, event | category | flops | bytes accessed | tf_op | source)
XLA Modules:
  0.0 213.8 jit_solution(6650009677881969784)
XLA Ops:
  1.1 2.9 %collective-permute-start.12 = (bf16[32,4096]{1,0:T(8,128)(2,1)S(1)}, bf16[32,4096]{1,0:T(8,128)(2,1)S(1)}, u32[]{:S(2)}, u32[]{:S(2)}) collective-permute-start(bf16[32,4096]{1,0:T(8,128)(2,1)S(1)} %get-tuple-element.21), channel_id=1, source_target_pairs={{0,3},{1,0},{2,1},{3,2},{4,7},{5,4},{6,5},{7,6},{8,11},{9,8},{10,9... | collective-permute-start | bytes 786440 | tf_op jit(solution)/shard_map/ppermute | solution.py:147
  4.1 2.3 %collective-permute-start.13 = (bf16[32,4096]{1,0:T(8,128)(2,1)S(1)}, bf16[32,4096]{1,0:T(8,128)(2,1)S(1)}, u32[]{:S(2)}, u32[]{:S(2)}) collective-permute-start(bf16[32,4096]{1,0:T(8,128)(2,1)S(1)} %get-tuple-element.21), channel_id=1, source_target_pairs={{0,2},{1,3},{2,0},{3,1},{4,6},{5,7},{6,4},{7,5},{8,10},{9,11},{10,... | collective-permute-start | bytes 786440 | tf_op jit(solution)/shard_map/ppermute | solution.py:147
  6.3 3.2 %collective-permute-start.3 = (bf16[32,8192]{1,0:T(8,128)(2,1)}, bf16[32,8192]{1,0:T(8,128)(2,1)S(1)}, u32[]{:S(2)}, u32[]{:S(2)}) collective-permute-start(bf16[32,8192]{1,0:T(8,128)(2,1)} %bitcast.109), channel_id=1, source_target_pairs={{0,16},{16,0},{1,17},{17,1},{2,18},{18,2},{3,19},{19,3},{4,20},{20... | collective-permute-start | bytes 1572872 | tf_op jit(solution)/shard_map/ppermute | solution.py:142
  9.5 4.0 %collective-permute-start.1 = (bf16[32,4096]{1,0:T(8,128)(2,1)S(1)}, bf16[32,4096]{1,0:T(8,128)(2,1)S(1)}, u32[]{:S(2)}, u32[]{:S(2)}) collective-permute-start(bf16[32,4096]{1,0:T(8,128)(2,1)S(1)} %get-tuple-element.22), channel_id=1, source_target_pairs={{0,96},{32,0},{64,32},{96,64},{1,97},{33,1},{65,33},{97,65},{2,98}... | collective-permute-start | bytes 786440 | tf_op jit(solution)/shard_map/ppermute | solution.py:147
  13.6 1.7 collective-permute-done.12
  15.2 1.9 collective-permute-start
  18.6 3.9 %collective-permute-start.2 = (bf16[32,4096]{1,0:T(8,128)(2,1)S(1)}, bf16[32,4096]{1,0:T(8,128)(2,1)S(1)}, u32[]{:S(2)}, u32[]{:S(2)}) collective-permute-start(bf16[32,4096]{1,0:T(8,128)(2,1)S(1)} %get-tuple-element.22), channel_id=1, source_target_pairs={{0,64},{32,96},{64,0},{96,32},{1,65},{33,97},{65,1},{97,33},{2,66}... | collective-permute-start | bytes 786440 | tf_op jit(solution)/shard_map/ppermute | solution.py:147
  22.8 2.3 %collective-permute-start.5 = (bf16[32,4096]{1,0:T(8,128)(2,1)S(1)}, bf16[32,4096]{1,0:T(8,128)(2,1)S(1)}, u32[]{:S(2)}, u32[]{:S(2)}) collective-permute-start(bf16[32,4096]{1,0:T(8,128)(2,1)S(1)} %get-tuple-element.26), channel_id=1, source_target_pairs={{0,96},{32,0},{64,32},{96,64},{1,97},{33,1},{65,33},{97,65},{2,98}... | collective-permute-start | bytes 786440 | tf_op jit(solution)/shard_map/ppermute | solution.py:147
  25.1 1.9 collective-permute-start.6
  27.0 3.5 %collective-permute-done.2 = bf16[32,4096]{1,0:T(8,128)(2,1)S(1)} collective-permute-done((bf16[32,4096]{1,0:T(8,128)(2,1)S(1)}, bf16[32,4096]{1,0:T(8,128)(2,1)S(1)}, u32[]{:S(2)}, u32[]{:S(2)}) %collective-permute-start.2) | collective-permute-done | bytes 262176 | tf_op jit(solution)/shard_map/ppermute | solution.py:147
  30.6 6.9 %collective-permute-start.15 = (bf16[32,4096]{1,0:T(8,128)(2,1)S(1)}, bf16[32,4096]{1,0:T(8,128)(2,1)S(1)}, u32[]{:S(2)}, u32[]{:S(2)}) collective-permute-start(bf16[32,4096]{1,0:T(8,128)(2,1)S(1)} %get-tuple-element.25), channel_id=1, source_target_pairs={{0,3},{1,0},{2,1},{3,2},{4,7},{5,4},{6,5},{7,6},{8,11},{9,8},{10,9... | collective-permute-start | bytes 786440 | tf_op jit(solution)/shard_map/ppermute | solution.py:147
  40.2 6.7 %collective-permute-start.8 = (bf16[2,4,32,4096]{3,2,1,0:T(8,128)(2,1)S(1)}, bf16[2,4,32,4096]{3,2,1,0:T(8,128)(2,1)S(1)}, u32[]{:S(2)}, u32[]{:S(2)}) collective-permute-start(bf16[2,4,32,4096]{3,2,1,0:T(8,128)(2,1)S(1)} %pad_maximum_fusion), channel_id=1, source_target_pairs={{0,3},{1,0},{2,1},{3,2},{4,7},{5,4},{6,5},{7,6},{8,11},{9,8},{10,9... | collective-permute-start | bytes 6291464 | tf_op jit(solution)/shard_map/ppermute | solution.py:147
  46.9 1.9 collective-permute-done.14
  48.8 1.8 collective-permute-done.16
  53.1 38.3 %collective-permute-done.8 = bf16[2,4,32,4096]{3,2,1,0:T(8,128)(2,1)S(1)} collective-permute-done((bf16[2,4,32,4096]{3,2,1,0:T(8,128)(2,1)S(1)}, bf16[2,4,32,4096]{3,2,1,0:T(8,128)(2,1)S(1)}, u32[]{:S(2)}, u32[]{:S(2)}) %collective-permute-start.8) | collective-permute-done | bytes 2097184 | tf_op jit(solution)/shard_map/ppermute | solution.py:147
  92.5 3.7 %collective-permute-start.10 = (bf16[1,4,32,4096]{3,2,1,0:T(8,128)(2,1)}, bf16[1,4,32,4096]{3,2,1,0:T(8,128)(2,1)S(1)}, u32[]{:S(2)}, u32[]{:S(2)}) collective-permute-start(bf16[1,4,32,4096]{3,2,1,0:T(8,128)(2,1)} %slice.132), channel_id=1, source_target_pairs={{0,3},{1,0},{2,1},{3,2},{4,7},{5,4},{6,5},{7,6},{8,11},{9,8},{10,9... | collective-permute-start | bytes 3145736 | tf_op jit(solution)/shard_map/ppermute | solution.py:147
  104.8 12.7 %collective-permute-done.10 = bf16[1,4,32,4096]{3,2,1,0:T(8,128)(2,1)S(1)} collective-permute-done((bf16[1,4,32,4096]{3,2,1,0:T(8,128)(2,1)}, bf16[1,4,32,4096]{3,2,1,0:T(8,128)(2,1)S(1)}, u32[]{:S(2)}, u32[]{:S(2)}) %collective-permute-start.10) | collective-permute-done | bytes 1048608 | tf_op jit(solution)/shard_map/ppermute | solution.py:147
  117.6 4.5 %collective-permute-done.9 = bf16[1,4,32,4096]{3,2,1,0:T(8,128)(2,1)S(1)} collective-permute-done((bf16[1,4,32,4096]{3,2,1,0:T(8,128)(2,1)}, bf16[1,4,32,4096]{3,2,1,0:T(8,128)(2,1)S(1)}, u32[]{:S(2)}, u32[]{:S(2)}) %collective-permute-start.9) | collective-permute-done | bytes 1048608 | tf_op jit(solution)/shard_map/ppermute | solution.py:147
  122.1 3.5 %collective-permute-done.19 = bf16[1,4,32,4096]{3,2,1,0:T(8,128)(2,1)} collective-permute-done((bf16[1,4,32,4096]{3,2,1,0:T(8,128)(2,1)}, bf16[1,4,32,4096]{3,2,1,0:T(8,128)(2,1)}, u32[]{:S(2)}, u32[]{:S(2)}) %collective-permute-start.19) | collective-permute-done | bytes 1048608 | tf_op jit(solution)/shard_map/ppermute | solution.py:147
  125.6 16.1 %aggregate.1 = (bf16[4,2,1024,128]{3,2,1,0:T(8,128)(2,1)}, bf16[2,4,1024,128]{3,2,1,0:T(8,128)(2,1)}, bf16[4,2,1024,128]{3,2,1,0:T(8,128)(2,1)}, bf16[2,4,1024,128]{3,2,1,0:T(8,128)(2,1)}) custom-call(s32[384]{0:T(512)} %reduce.rows_ref, s32[384]{0:T(512)} %reduce.1.cols_ref, s32[6]{0:T(128)} %stack.101.info_ref, bf16[384,128,128]{2,1,0:T(8,128)(2,1)} %bitcast.98, ...), custom_call_target="tpu_custom_call" | custom-call | tf_op jit(solution)/shard_map/aggregate/pallas_call | solution.py:118
  141.7 18.2 %collective-permute-start.21 = (bf16[4,2,1024,128]{3,2,1,0:T(8,128)(2,1)}, bf16[4,2,1024,128]{3,2,1,0:T(8,128)(2,1)S(1)}, u32[]{:S(2)}, u32[]{:S(2)}) collective-permute-start(bf16[4,2,1024,128]{3,2,1,0:T(8,128)(2,1)} %get-tuple-element.10), channel_id=1, source_target_pairs={{0,4},{4,0},{1,5},{5,1},{2,6},{6,2},{3,7},{7,3},{8,12},{12,8},{9,1... | collective-permute-start | bytes 6291464 | tf_op jit(solution)/shard_map/ppermute | solution.py:142
  160.0 3.9 %collective-permute-done.21 = bf16[4,2,1024,128]{3,2,1,0:T(8,128)(2,1)S(1)} collective-permute-done((bf16[4,2,1024,128]{3,2,1,0:T(8,128)(2,1)}, bf16[4,2,1024,128]{3,2,1,0:T(8,128)(2,1)S(1)}, u32[]{:S(2)}, u32[]{:S(2)}) %collective-permute-start.21) | collective-permute-done | bytes 2097184 | tf_op jit(solution)/shard_map/ppermute | solution.py:142
  163.9 1.9 fusion.5
  166.4 2.9 %collective-permute-start.24 = (bf16[2,1024,128]{2,1,0:T(8,128)(2,1)S(1)}, bf16[2,1024,128]{2,1,0:T(8,128)(2,1)S(1)}, u32[]{:S(2)}, u32[]{:S(2)}) collective-permute-start(bf16[2,1024,128]{2,1,0:T(8,128)(2,1)S(1)} %get-tuple-element.17), channel_id=1, source_target_pairs={{0,3},{1,0},{2,1},{3,2},{4,7},{5,4},{6,5},{7,6},{8,11},{9,8},{10,9... | collective-permute-start | bytes 1572872 | tf_op jit(solution)/shard_map/ppermute | solution.py:147
  170.5 4.1 %collective-permute-start.27 = (bf16[4,1024,128]{2,1,0:T(8,128)(2,1)S(1)}, bf16[4,1024,128]{2,1,0:T(8,128)(2,1)S(1)}, u32[]{:S(2)}, u32[]{:S(2)}) collective-permute-start(bf16[4,1024,128]{2,1,0:T(8,128)(2,1)S(1)} %fusion.2), channel_id=1, source_target_pairs={{0,8},{8,0},{1,9},{9,1},{2,10},{10,2},{3,11},{11,3},{4,12},{12,4},... | collective-permute-start | bytes 3145736 | tf_op jit(solution)/shard_map/ppermute | solution.py:142
  174.5 6.9 %collective-permute-done.22 = bf16[2,1024,128]{2,1,0:T(8,128)(2,1)S(1)} collective-permute-done((bf16[2,1024,128]{2,1,0:T(8,128)(2,1)S(1)}, bf16[2,1024,128]{2,1,0:T(8,128)(2,1)S(1)}, u32[]{:S(2)}, u32[]{:S(2)}) %collective-permute-start.22) | collective-permute-done | bytes 524320 | tf_op jit(solution)/shard_map/ppermute | solution.py:147
  181.5 10.5 %collective-permute-done.24 = bf16[2,1024,128]{2,1,0:T(8,128)(2,1)S(1)} collective-permute-done((bf16[2,1024,128]{2,1,0:T(8,128)(2,1)S(1)}, bf16[2,1024,128]{2,1,0:T(8,128)(2,1)S(1)}, u32[]{:S(2)}, u32[]{:S(2)}) %collective-permute-start.24) | collective-permute-done | bytes 524320 | tf_op jit(solution)/shard_map/ppermute | solution.py:147
  195.0 2.1 collective-permute-start.25
  198.9 1.9 collective-permute-start.30
  201.3 1.9 collective-permute-done.25
  203.3 4.7 %collective-permute-done.28 = bf16[1024,128]{1,0:T(8,128)(2,1)S(1)} collective-permute-done((bf16[1024,128]{1,0:T(8,128)(2,1)S(1)}, bf16[1024,128]{1,0:T(8,128)(2,1)S(1)}, u32[]{:S(2)}, u32[]{:S(2)}) %collective-permute-start.28) | collective-permute-done | bytes 262176 | tf_op jit(solution)/shard_map/ppermute | solution.py:147
  208.0 3.2 %collective-permute-done.30 = bf16[1024,128]{1,0:T(8,128)(2,1)S(1)} collective-permute-done((bf16[1024,128]{1,0:T(8,128)(2,1)S(1)}, bf16[1024,128]{1,0:T(8,128)(2,1)S(1)}, u32[]{:S(2)}, u32[]{:S(2)}) %collective-permute-start.30) | collective-permute-done | bytes 262176 | tf_op jit(solution)/shard_map/ppermute | solution.py:147
  (82 shorter events, 27.0 us)
Async XLA Ops:
  0.0 212.4 %copy-start = (bf16[128,256]{1,0:T(8,128)(2,1)S(1)}, bf16[128,256]{1,0:T(8,128)(2,1)}, u32[]{:S(2)}) copy-start(bf16[128,256]{1,0:T(8,128)(2,1)} %param.12) | copy-start | bytes 196612
  1.1 14.1 %collective-permute-start.12 = (bf16[32,4096]{1,0:T(8,128)(2,1)S(1)}, bf16[32,4096]{1,0:T(8,128)(2,1)S(1)}, u32[]{:S(2)}, u32[]{:S(2)}) collective-permute-start(bf16[32,4096]{1,0:T(8,128)(2,1)S(1)} %get-tuple-element.21), channel_id=1, source_target_pairs={{0,3},{1,0},{2,1},{3,2},{4,7},{5,4},{6,5},{7,6},{8,11},{9,8},{10,9... | collective-permute-start | bytes 786440 | tf_op jit(solution)/shard_map/ppermute | solution.py:147
  4.0 14.6 %collective-permute-start.11 = (bf16[32,4096]{1,0:T(8,128)(2,1)S(1)}, bf16[32,4096]{1,0:T(8,128)(2,1)S(1)}, u32[]{:S(2)}, u32[]{:S(2)}) collective-permute-start(bf16[32,4096]{1,0:T(8,128)(2,1)S(1)} %get-tuple-element.21), channel_id=1, source_target_pairs={{0,1},{1,2},{2,3},{3,0},{4,5},{5,6},{6,7},{7,4},{8,9},{9,10},{10,1... | collective-permute-start | bytes 786440 | tf_op jit(solution)/shard_map/ppermute | solution.py:147
  4.1 18.5 %collective-permute-start.13 = (bf16[32,4096]{1,0:T(8,128)(2,1)S(1)}, bf16[32,4096]{1,0:T(8,128)(2,1)S(1)}, u32[]{:S(2)}, u32[]{:S(2)}) collective-permute-start(bf16[32,4096]{1,0:T(8,128)(2,1)S(1)} %get-tuple-element.21), channel_id=1, source_target_pairs={{0,2},{1,3},{2,0},{3,1},{4,6},{5,7},{6,4},{7,5},{8,10},{9,11},{10,... | collective-permute-start | bytes 786440 | tf_op jit(solution)/shard_map/ppermute | solution.py:147
  6.3 16.3 %collective-permute-start.3 = (bf16[32,8192]{1,0:T(8,128)(2,1)}, bf16[32,8192]{1,0:T(8,128)(2,1)S(1)}, u32[]{:S(2)}, u32[]{:S(2)}) collective-permute-start(bf16[32,8192]{1,0:T(8,128)(2,1)} %bitcast.109), channel_id=1, source_target_pairs={{0,16},{16,0},{1,17},{17,1},{2,18},{18,2},{3,19},{19,3},{4,20},{20... | collective-permute-start | bytes 1572872 | tf_op jit(solution)/shard_map/ppermute | solution.py:142
  9.5 15.6 %collective-permute-start.1 = (bf16[32,4096]{1,0:T(8,128)(2,1)S(1)}, bf16[32,4096]{1,0:T(8,128)(2,1)S(1)}, u32[]{:S(2)}, u32[]{:S(2)}) collective-permute-start(bf16[32,4096]{1,0:T(8,128)(2,1)S(1)} %get-tuple-element.22), channel_id=1, source_target_pairs={{0,96},{32,0},{64,32},{96,64},{1,97},{33,1},{65,33},{97,65},{2,98}... | collective-permute-start | bytes 786440 | tf_op jit(solution)/shard_map/ppermute | solution.py:147
  15.2 11.7 %collective-permute-start = (bf16[32,4096]{1,0:T(8,128)(2,1)S(1)}, bf16[32,4096]{1,0:T(8,128)(2,1)S(1)}, u32[]{:S(2)}, u32[]{:S(2)}) collective-permute-start(bf16[32,4096]{1,0:T(8,128)(2,1)S(1)} %get-tuple-element.22), channel_id=1, source_target_pairs={{0,32},{32,64},{64,96},{96,0},{1,33},{33,65},{65,97},{97,1},{2,34}... | collective-permute-start | bytes 786440 | tf_op jit(solution)/shard_map/ppermute | solution.py:147
  18.6 11.8 %collective-permute-start.2 = (bf16[32,4096]{1,0:T(8,128)(2,1)S(1)}, bf16[32,4096]{1,0:T(8,128)(2,1)S(1)}, u32[]{:S(2)}, u32[]{:S(2)}) collective-permute-start(bf16[32,4096]{1,0:T(8,128)(2,1)S(1)} %get-tuple-element.22), channel_id=1, source_target_pairs={{0,64},{32,96},{64,0},{96,32},{1,65},{33,97},{65,1},{97,33},{2,66}... | collective-permute-start | bytes 786440 | tf_op jit(solution)/shard_map/ppermute | solution.py:147
  22.8 14.7 %collective-permute-start.5 = (bf16[32,4096]{1,0:T(8,128)(2,1)S(1)}, bf16[32,4096]{1,0:T(8,128)(2,1)S(1)}, u32[]{:S(2)}, u32[]{:S(2)}) collective-permute-start(bf16[32,4096]{1,0:T(8,128)(2,1)S(1)} %get-tuple-element.26), channel_id=1, source_target_pairs={{0,96},{32,0},{64,32},{96,64},{1,97},{33,1},{65,33},{97,65},{2,98}... | collective-permute-start | bytes 786440 | tf_op jit(solution)/shard_map/ppermute | solution.py:147
  25.1 14.7 %collective-permute-start.4 = (bf16[32,4096]{1,0:T(8,128)(2,1)S(1)}, bf16[32,4096]{1,0:T(8,128)(2,1)S(1)}, u32[]{:S(2)}, u32[]{:S(2)}) collective-permute-start(bf16[32,4096]{1,0:T(8,128)(2,1)S(1)} %get-tuple-element.26), channel_id=1, source_target_pairs={{0,32},{32,64},{64,96},{96,0},{1,33},{33,65},{65,97},{97,1},{2,34}... | collective-permute-start | bytes 786440 | tf_op jit(solution)/shard_map/ppermute | solution.py:147
  25.1 14.7 %collective-permute-start.6 = (bf16[32,4096]{1,0:T(8,128)(2,1)S(1)}, bf16[32,4096]{1,0:T(8,128)(2,1)S(1)}, u32[]{:S(2)}, u32[]{:S(2)}) collective-permute-start(bf16[32,4096]{1,0:T(8,128)(2,1)S(1)} %get-tuple-element.26), channel_id=1, source_target_pairs={{0,64},{32,96},{64,0},{96,32},{1,65},{33,97},{65,1},{97,33},{2,66}... | collective-permute-start | bytes 786440 | tf_op jit(solution)/shard_map/ppermute | solution.py:147
  30.6 16.3 %collective-permute-start.15 = (bf16[32,4096]{1,0:T(8,128)(2,1)S(1)}, bf16[32,4096]{1,0:T(8,128)(2,1)S(1)}, u32[]{:S(2)}, u32[]{:S(2)}) collective-permute-start(bf16[32,4096]{1,0:T(8,128)(2,1)S(1)} %get-tuple-element.25), channel_id=1, source_target_pairs={{0,3},{1,0},{2,1},{3,2},{4,7},{5,4},{6,5},{7,6},{8,11},{9,8},{10,9... | collective-permute-start | bytes 786440 | tf_op jit(solution)/shard_map/ppermute | solution.py:147
  37.5 11.3 %collective-permute-start.14 = (bf16[32,4096]{1,0:T(8,128)(2,1)S(1)}, bf16[32,4096]{1,0:T(8,128)(2,1)S(1)}, u32[]{:S(2)}, u32[]{:S(2)}) collective-permute-start(bf16[32,4096]{1,0:T(8,128)(2,1)S(1)} %get-tuple-element.25), channel_id=1, source_target_pairs={{0,1},{1,2},{2,3},{3,0},{4,5},{5,6},{6,7},{7,4},{8,9},{9,10},{10,1... | collective-permute-start | bytes 786440 | tf_op jit(solution)/shard_map/ppermute | solution.py:147
  37.5 13.1 %collective-permute-start.16 = (bf16[32,4096]{1,0:T(8,128)(2,1)S(1)}, bf16[32,4096]{1,0:T(8,128)(2,1)S(1)}, u32[]{:S(2)}, u32[]{:S(2)}) collective-permute-start(bf16[32,4096]{1,0:T(8,128)(2,1)S(1)} %get-tuple-element.25), channel_id=1, source_target_pairs={{0,2},{1,3},{2,0},{3,1},{4,6},{5,7},{6,4},{7,5},{8,10},{9,11},{10,... | collective-permute-start | bytes 786440 | tf_op jit(solution)/shard_map/ppermute | solution.py:147
  40.2 51.2 %collective-permute-start.8 = (bf16[2,4,32,4096]{3,2,1,0:T(8,128)(2,1)S(1)}, bf16[2,4,32,4096]{3,2,1,0:T(8,128)(2,1)S(1)}, u32[]{:S(2)}, u32[]{:S(2)}) collective-permute-start(bf16[2,4,32,4096]{3,2,1,0:T(8,128)(2,1)S(1)} %pad_maximum_fusion), channel_id=1, source_target_pairs={{0,3},{1,0},{2,1},{3,2},{4,7},{5,4},{6,5},{7,6},{8,11},{9,8},{10,9... | collective-permute-start | bytes 6291464 | tf_op jit(solution)/shard_map/ppermute | solution.py:147
  46.9 49.3 %collective-permute-start.7 = (bf16[2,4,32,4096]{3,2,1,0:T(8,128)(2,1)S(1)}, bf16[2,4,32,4096]{3,2,1,0:T(8,128)(2,1)S(1)}, u32[]{:S(2)}, u32[]{:S(2)}) collective-permute-start(bf16[2,4,32,4096]{3,2,1,0:T(8,128)(2,1)S(1)} %pad_maximum_fusion), channel_id=1, source_target_pairs={{0,1},{1,2},{2,3},{3,0},{4,5},{5,6},{6,7},{7,4},{8,9},{9,10},{10,1... | collective-permute-start | bytes 6291464 | tf_op jit(solution)/shard_map/ppermute | solution.py:147
  51.0 46.4 %collective-permute-start.18 = (bf16[2,4,32,4096]{3,2,1,0:T(8,128)(2,1)S(1)}, bf16[2,4,32,4096]{3,2,1,0:T(8,128)(2,1)S(1)}, u32[]{:S(2)}, u32[]{:S(2)}) collective-permute-start(bf16[2,4,32,4096]{3,2,1,0:T(8,128)(2,1)S(1)} %pad_maximum_fusion.1), channel_id=1, source_target_pairs={{0,96},{32,0},{64,32},{96,64},{1,97},{33,1},{65,33},{97,65},{2,98}... | collective-permute-start | bytes 6291464 | tf_op jit(solution)/shard_map/ppermute | solution.py:147
  52.2 46.4 %collective-permute-start.17 = (bf16[2,4,32,4096]{3,2,1,0:T(8,128)(2,1)S(1)}, bf16[2,4,32,4096]{3,2,1,0:T(8,128)(2,1)S(1)}, u32[]{:S(2)}, u32[]{:S(2)}) collective-permute-start(bf16[2,4,32,4096]{3,2,1,0:T(8,128)(2,1)S(1)} %pad_maximum_fusion.1), channel_id=1, source_target_pairs={{0,32},{32,64},{64,96},{96,0},{1,33},{33,65},{65,97},{97,1},{2,34}... | collective-permute-start | bytes 6291464 | tf_op jit(solution)/shard_map/ppermute | solution.py:147
  92.5 25.1 %collective-permute-start.10 = (bf16[1,4,32,4096]{3,2,1,0:T(8,128)(2,1)}, bf16[1,4,32,4096]{3,2,1,0:T(8,128)(2,1)S(1)}, u32[]{:S(2)}, u32[]{:S(2)}) collective-permute-start(bf16[1,4,32,4096]{3,2,1,0:T(8,128)(2,1)} %slice.132), channel_id=1, source_target_pairs={{0,3},{1,0},{2,1},{3,2},{4,7},{5,4},{6,5},{7,6},{8,11},{9,8},{10,9... | collective-permute-start | bytes 3145736 | tf_op jit(solution)/shard_map/ppermute | solution.py:147
  97.3 24.8 %collective-permute-start.9 = (bf16[1,4,32,4096]{3,2,1,0:T(8,128)(2,1)}, bf16[1,4,32,4096]{3,2,1,0:T(8,128)(2,1)S(1)}, u32[]{:S(2)}, u32[]{:S(2)}) collective-permute-start(bf16[1,4,32,4096]{3,2,1,0:T(8,128)(2,1)} %slice.131), channel_id=1, source_target_pairs={{0,1},{1,2},{2,3},{3,0},{4,5},{5,6},{6,7},{7,4},{8,9},{9,10},{10,1... | collective-permute-start | bytes 3145736 | tf_op jit(solution)/shard_map/ppermute | solution.py:147
  98.6 23.5 %collective-permute-start.20 = (bf16[1,4,32,4096]{3,2,1,0:T(8,128)(2,1)}, bf16[1,4,32,4096]{3,2,1,0:T(8,128)(2,1)S(1)}, u32[]{:S(2)}, u32[]{:S(2)}) collective-permute-start(bf16[1,4,32,4096]{3,2,1,0:T(8,128)(2,1)} %slice.136), channel_id=1, source_target_pairs={{0,96},{32,0},{64,32},{96,64},{1,97},{33,1},{65,33},{97,65},{2,98}... | collective-permute-start | bytes 3145736 | tf_op jit(solution)/shard_map/ppermute | solution.py:147
  100.8 24.8 %collective-permute-start.19 = (bf16[1,4,32,4096]{3,2,1,0:T(8,128)(2,1)}, bf16[1,4,32,4096]{3,2,1,0:T(8,128)(2,1)}, u32[]{:S(2)}, u32[]{:S(2)}) collective-permute-start(bf16[1,4,32,4096]{3,2,1,0:T(8,128)(2,1)} %slice.135), channel_id=1, source_target_pairs={{0,32},{32,64},{64,96},{96,0},{1,33},{33,65},{65,97},{97,1},{2,34}... | collective-permute-start | bytes 3145736 | tf_op jit(solution)/shard_map/ppermute | solution.py:147
  141.7 22.2 %collective-permute-start.21 = (bf16[4,2,1024,128]{3,2,1,0:T(8,128)(2,1)}, bf16[4,2,1024,128]{3,2,1,0:T(8,128)(2,1)S(1)}, u32[]{:S(2)}, u32[]{:S(2)}) collective-permute-start(bf16[4,2,1024,128]{3,2,1,0:T(8,128)(2,1)} %get-tuple-element.10), channel_id=1, source_target_pairs={{0,4},{4,0},{1,5},{5,1},{2,6},{6,2},{3,7},{7,3},{8,12},{12,8},{9,1... | collective-permute-start | bytes 6291464 | tf_op jit(solution)/shard_map/ppermute | solution.py:142
  159.9 10.3 %collective-permute-start.26 = (bf16[2,4,1024,128]{3,2,1,0:T(8,128)(2,1)}, bf16[2,4,1024,128]{3,2,1,0:T(8,128)(2,1)S(1)}, u32[]{:S(2)}, u32[]{:S(2)}) collective-permute-start(bf16[2,4,1024,128]{3,2,1,0:T(8,128)(2,1)} %get-tuple-element.12), channel_id=1, source_target_pairs={{0,4},{4,0},{1,5},{5,1},{2,6},{6,2},{3,7},{7,3},{8,12},{12,8},{9,1... | collective-permute-start | bytes 6291464 | tf_op jit(solution)/shard_map/ppermute | solution.py:142
  165.8 15.7 %collective-permute-start.22 = (bf16[2,1024,128]{2,1,0:T(8,128)(2,1)S(1)}, bf16[2,1024,128]{2,1,0:T(8,128)(2,1)S(1)}, u32[]{:S(2)}, u32[]{:S(2)}) collective-permute-start(bf16[2,1024,128]{2,1,0:T(8,128)(2,1)S(1)} %get-tuple-element.16), channel_id=1, source_target_pairs={{0,1},{1,2},{2,3},{3,0},{4,5},{5,6},{6,7},{7,4},{8,9},{9,10},{10,1... | collective-permute-start | bytes 1572872 | tf_op jit(solution)/shard_map/ppermute | solution.py:147
  166.4 25.5 %collective-permute-start.24 = (bf16[2,1024,128]{2,1,0:T(8,128)(2,1)S(1)}, bf16[2,1024,128]{2,1,0:T(8,128)(2,1)S(1)}, u32[]{:S(2)}, u32[]{:S(2)}) collective-permute-start(bf16[2,1024,128]{2,1,0:T(8,128)(2,1)S(1)} %get-tuple-element.17), channel_id=1, source_target_pairs={{0,3},{1,0},{2,1},{3,2},{4,7},{5,4},{6,5},{7,6},{8,11},{9,8},{10,9... | collective-permute-start | bytes 1572872 | tf_op jit(solution)/shard_map/ppermute | solution.py:147
  169.3 24.3 %collective-permute-start.23 = (bf16[2,1024,128]{2,1,0:T(8,128)(2,1)S(1)}, bf16[2,1024,128]{2,1,0:T(8,128)(2,1)S(1)}, u32[]{:S(2)}, u32[]{:S(2)}) collective-permute-start(bf16[2,1024,128]{2,1,0:T(8,128)(2,1)S(1)} %get-tuple-element.18), channel_id=1, source_target_pairs={{0,2},{1,3},{2,0},{3,1},{4,6},{5,7},{6,4},{7,5},{8,10},{9,11},{10,... | collective-permute-start | bytes 1572872 | tf_op jit(solution)/shard_map/ppermute | solution.py:147
  170.5 26.7 %collective-permute-start.27 = (bf16[4,1024,128]{2,1,0:T(8,128)(2,1)S(1)}, bf16[4,1024,128]{2,1,0:T(8,128)(2,1)S(1)}, u32[]{:S(2)}, u32[]{:S(2)}) collective-permute-start(bf16[4,1024,128]{2,1,0:T(8,128)(2,1)S(1)} %fusion.2), channel_id=1, source_target_pairs={{0,8},{8,0},{1,9},{9,1},{2,10},{10,2},{3,11},{11,3},{4,12},{12,4},... | collective-permute-start | bytes 3145736 | tf_op jit(solution)/shard_map/ppermute | solution.py:142
  195.0 8.2 %collective-permute-start.25 = (bf16[1024,128]{1,0:T(8,128)(2,1)S(1)}, bf16[1024,128]{1,0:T(8,128)(2,1)S(1)}, u32[]{:S(2)}, u32[]{:S(2)}) collective-permute-start(bf16[1024,128]{1,0:T(8,128)(2,1)S(1)} %fusion.20), channel_id=1, source_target_pairs={{0,8},{8,0},{1,9},{9,1},{2,10},{10,2},{3,11},{11,3},{4,12},{12,4},... | collective-permute-start | bytes 786440 | tf_op jit(solution)/shard_map/ppermute | solution.py:142
  197.5 10.5 %collective-permute-start.28 = (bf16[1024,128]{1,0:T(8,128)(2,1)S(1)}, bf16[1024,128]{1,0:T(8,128)(2,1)S(1)}, u32[]{:S(2)}, u32[]{:S(2)}) collective-permute-start(bf16[1024,128]{1,0:T(8,128)(2,1)S(1)} %get-tuple-element.13), channel_id=1, source_target_pairs={{0,1},{1,2},{2,3},{3,0},{4,5},{5,6},{6,7},{7,4},{8,9},{9,10},{10,1... | collective-permute-start | bytes 786440 | tf_op jit(solution)/shard_map/ppermute | solution.py:147
  198.9 12.3 %collective-permute-start.30 = (bf16[1024,128]{1,0:T(8,128)(2,1)S(1)}, bf16[1024,128]{1,0:T(8,128)(2,1)S(1)}, u32[]{:S(2)}, u32[]{:S(2)}) collective-permute-start(bf16[1024,128]{1,0:T(8,128)(2,1)S(1)} %get-tuple-element.14), channel_id=1, source_target_pairs={{0,3},{1,0},{2,1},{3,2},{4,7},{5,4},{6,5},{7,6},{8,11},{9,8},{10,9... | collective-permute-start | bytes 786440 | tf_op jit(solution)/shard_map/ppermute | solution.py:147
  200.8 11.4 %collective-permute-start.29 = (bf16[1024,128]{1,0:T(8,128)(2,1)S(1)}, bf16[1024,128]{1,0:T(8,128)(2,1)S(1)}, u32[]{:S(2)}, u32[]{:S(2)}) collective-permute-start(bf16[1024,128]{1,0:T(8,128)(2,1)S(1)} %get-tuple-element.15), channel_id=1, source_target_pairs={{0,2},{1,3},{2,0},{3,1},{4,6},{5,7},{6,4},{7,5},{8,10},{9,11},{10,... | collective-permute-start | bytes 786440 | tf_op jit(solution)/shard_map/ppermute | solution.py:147
  (13 other events, 117.3 us)

commit v6 on v5

--- a/solution.py
+++ b/solution.py
@@ -9,7 +9,8 @@
 from jax.sharding import PartitionSpec as P
 
 LOAD = 32
-STEP = 4
+STEPS_AT_ONCE = (16, 4, 1)
+PACK = 256
 FIRST_X = 1024
 NT = (((1,), (1,)), ((), ()))
 NAMES = ("rz", "ry", "cy", "cc", "fx")
@@ -67,30 +68,36 @@
         tile_copy(i).wait()
         first = i * LOAD
         here = jnp.minimum(count - first, LOAD)
-        whole = here // STEP
-
-        @pl.loop(0, whole)
-        def _(s):
-            k = first + s * STEP
-            values = [product(k + t) for t in range(STEP)]
-            for t in range(STEP):
-                add(k + t, values[t])
-
-        @pl.loop(whole * STEP, here)
-        def _(s):
-            add(first + s, product(first + s))
-
-    chunk = stage.shape[1]
+        start = 0
+        for width in STEPS_AT_ONCE:
+            turns = (here - start) // width
+
+            @pl.loop(0, turns)
+            def _(s, start=start, width=width):
+                k = first + start + s * width
+                values = [product(k + t) for t in range(width)]
+                for t in range(width):
+                    add(k + t, values[t])
+
+            start = start + turns * width
+
+    slots, chunk = stage.shape[0], stage.shape[1]
     copies = []
     for n in range(16):
         other, y, d = n < 8, 1 - (n // 4) % 2, n % 4
-        slot = n % 2
-        if n >= 2:
-            for copy in copies[n - 2]:
+        slot = n % slots
+        if n >= slots:
+            for copy in copies[n - slots]:
                 copy.wait()
         core = 1 - cc if other else cc
         shard = (jnp.bitwise_xor(cy, y) * 2 + core) * 4 + jnp.bitwise_and(fx + d, 3)
-        stage[slot] = acc[pl.ds(pl.multiple_of(shard * chunk, chunk), chunk), :].astype(jnp.bfloat16)
+
+        @pl.loop(0, chunk // PACK)
+        def _(i, slot=slot, shard=shard):
+            at = pl.multiple_of(i * PACK, PACK)
+            rows = pl.ds(pl.multiple_of(shard * chunk + at, PACK), PACK)
+            stage[slot, pl.ds(at, PACK), :] = acc[rows, :].astype(jnp.bfloat16)
+
         out_a, out_b = (send_a, send_b) if other else (keep_a, keep_b)
         copies.append(
             [
@@ -104,7 +111,7 @@
         )
         for copy in copies[n]:
             copy.start()
-    for n in (14, 15):
+    for n in range(16 - slots, 16):
         for copy in copies[n]:
             copy.wait()
 
@@ -127,10 +134,10 @@
                 pltpu.VMEM(tiles.shape, jnp.bfloat16),
                 pltpu.VMEM((8, 4, side // 4, 4 * node_dev), jnp.bfloat16),
                 pltpu.VMEM((16 * node_dev, side), jnp.float32),
-                pltpu.VMEM((2, node_dev, side), jnp.bfloat16),
+                pltpu.VMEM((4, node_dev, side), jnp.bfloat16),
                 pltpu.SemaphoreType.DMA((slots // LOAD,)),
                 pltpu.SemaphoreType.DMA((sum(len(w[1]) for w in where),)),
-                pltpu.SemaphoreType.DMA((2, 2)),
+                pltpu.SemaphoreType.DMA((4, 2)),
             ],
         ),
         compiler_params=pltpu.CompilerParams(vmem_limit_bytes=56 * 2**20),

time: 216 us -> 203 us (0.940); the launches traced: 214 us -> 203 us
  starting transfers between devices: 77.7 us -> 62.9 us
  Pallas kernels: 16.1 us -> 18.9 us
    ppermute x5, starting transfers between devices: 27.6 us -> 7.08 us  [swap(): return lax.ppermute(value, axis, [(0, 1), (1, 0)])]
    ppermute x26, starting transfers between devices: 50.1 us -> 55.8 us  [shift(): return lax.ppermute(value, axis, [(i, (i + by) % n) for i in range(n)])]
    pallas_call x1, Pallas kernels: 16.1 us -> 18.9 us  [aggregate(): pl.pallas_call(functools.partial(aggregate_kernel, where, len(arrays)), o...]
  transfers between devices with their start and end apart: 31 -> 31, of which waited for: 18 -> 18; matrix products, arithmetic and copies ran while one was open for 5% -> 6% of each run, Pallas kernels for 0% -> 0%
where the time goes in v6:
time: 203 us
  waiting for transfers between devices  105 us (52%)
  starting transfers between devices  62.9 us (31%)
  Pallas kernels  18.9 us (9%)
  local copies, waits for them, and re-layouts  7.51 us (4%)
  other arithmetic  6.27 us (3%)
    ppermute x26, waiting for transfers between devices, shift(): return lax.ppermute(value, axis, [(i, (i + by) % n) for i in range(n)])  100 us
    ppermute x26, starting transfers between devices, shift(): return lax.ppermute(value, axis, [(i, (i + by) % n) for i in range(n)])  55.8 us
    pallas_call x1, Pallas kernels, aggregate(): pl.pallas_call(functools.partial(aggregate_kernel, where, len(arrays)), o...  18.9 us
    ppermute x5, starting transfers between devices, swap(): return lax.ppermute(value, axis, [(0, 1), (1, 0)])  7.08 us
    ppermute x5, waiting for transfers between devices, swap(): return lax.ppermute(value, axis, [(0, 1), (1, 0)])  5.17 us
  transfers between devices with their start and end apart: 31, of which 18 were waited for; matrix products, arithmetic and copies ran while one was open for 6% of the time, Pallas kernels for 0%

profile of v6, /device:TPU:0, one launch (start us, length us, event | category | flops | bytes accessed | tf_op | source)
XLA Modules:
  0.0 203.2 jit_solution(6540051406338838236)
XLA Ops:
  1.1 2.9 %collective-permute-start.12 = (bf16[32,4096]{1,0:T(8,128)(2,1)S(1)}, bf16[32,4096]{1,0:T(8,128)(2,1)S(1)}, u32[]{:S(2)}, u32[]{:S(2)}) collective-permute-start(bf16[32,4096]{1,0:T(8,128)(2,1)S(1)} %get-tuple-element.21), channel_id=1, source_target_pairs={{0,3},{1,0},{2,1},{3,2},{4,7},{5,4},{6,5},{7,6},{8,11},{9,8},{10,9... | collective-permute-start | bytes 786440 | tf_op jit(solution)/shard_map/ppermute | solution.py:154
  4.1 2.3 %collective-permute-start.13 = (bf16[32,4096]{1,0:T(8,128)(2,1)S(1)}, bf16[32,4096]{1,0:T(8,128)(2,1)S(1)}, u32[]{:S(2)}, u32[]{:S(2)}) collective-permute-start(bf16[32,4096]{1,0:T(8,128)(2,1)S(1)} %get-tuple-element.21), channel_id=1, source_target_pairs={{0,2},{1,3},{2,0},{3,1},{4,6},{5,7},{6,4},{7,5},{8,10},{9,11},{10,... | collective-permute-start | bytes 786440 | tf_op jit(solution)/shard_map/ppermute | solution.py:154
  6.3 3.2 %collective-permute-start.3 = (bf16[32,8192]{1,0:T(8,128)(2,1)}, bf16[32,8192]{1,0:T(8,128)(2,1)S(1)}, u32[]{:S(2)}, u32[]{:S(2)}) collective-permute-start(bf16[32,8192]{1,0:T(8,128)(2,1)} %bitcast.109), channel_id=1, source_target_pairs={{0,16},{16,0},{1,17},{17,1},{2,18},{18,2},{3,19},{19,3},{4,20},{20... | collective-permute-start | bytes 1572872 | tf_op jit(solution)/shard_map/ppermute | solution.py:149
  9.5 4.0 %collective-permute-start.1 = (bf16[32,4096]{1,0:T(8,128)(2,1)S(1)}, bf16[32,4096]{1,0:T(8,128)(2,1)S(1)}, u32[]{:S(2)}, u32[]{:S(2)}) collective-permute-start(bf16[32,4096]{1,0:T(8,128)(2,1)S(1)} %get-tuple-element.22), channel_id=1, source_target_pairs={{0,96},{32,0},{64,32},{96,64},{1,97},{33,1},{65,33},{97,65},{2,98}... | collective-permute-start | bytes 786440 | tf_op jit(solution)/shard_map/ppermute | solution.py:154
  13.6 1.7 collective-permute-done.12
  15.2 1.9 collective-permute-start
  18.6 3.9 %collective-permute-start.2 = (bf16[32,4096]{1,0:T(8,128)(2,1)S(1)}, bf16[32,4096]{1,0:T(8,128)(2,1)S(1)}, u32[]{:S(2)}, u32[]{:S(2)}) collective-permute-start(bf16[32,4096]{1,0:T(8,128)(2,1)S(1)} %get-tuple-element.22), channel_id=1, source_target_pairs={{0,64},{32,96},{64,0},{96,32},{1,65},{33,97},{65,1},{97,33},{2,66}... | collective-permute-start | bytes 786440 | tf_op jit(solution)/shard_map/ppermute | solution.py:154
  22.8 2.3 %collective-permute-start.5 = (bf16[32,4096]{1,0:T(8,128)(2,1)S(1)}, bf16[32,4096]{1,0:T(8,128)(2,1)S(1)}, u32[]{:S(2)}, u32[]{:S(2)}) collective-permute-start(bf16[32,4096]{1,0:T(8,128)(2,1)S(1)} %get-tuple-element.26), channel_id=1, source_target_pairs={{0,96},{32,0},{64,32},{96,64},{1,97},{33,1},{65,33},{97,65},{2,98}... | collective-permute-start | bytes 786440 | tf_op jit(solution)/shard_map/ppermute | solution.py:154
  25.1 1.9 collective-permute-start.6
  27.0 3.5 %collective-permute-done.2 = bf16[32,4096]{1,0:T(8,128)(2,1)S(1)} collective-permute-done((bf16[32,4096]{1,0:T(8,128)(2,1)S(1)}, bf16[32,4096]{1,0:T(8,128)(2,1)S(1)}, u32[]{:S(2)}, u32[]{:S(2)}) %collective-permute-start.2) | collective-permute-done | bytes 262176 | tf_op jit(solution)/shard_map/ppermute | solution.py:154
  30.6 6.9 %collective-permute-start.15 = (bf16[32,4096]{1,0:T(8,128)(2,1)S(1)}, bf16[32,4096]{1,0:T(8,128)(2,1)S(1)}, u32[]{:S(2)}, u32[]{:S(2)}) collective-permute-start(bf16[32,4096]{1,0:T(8,128)(2,1)S(1)} %get-tuple-element.25), channel_id=1, source_target_pairs={{0,3},{1,0},{2,1},{3,2},{4,7},{5,4},{6,5},{7,6},{8,11},{9,8},{10,9... | collective-permute-start | bytes 786440 | tf_op jit(solution)/shard_map/ppermute | solution.py:154
  40.2 6.7 %collective-permute-start.8 = (bf16[2,4,32,4096]{3,2,1,0:T(8,128)(2,1)S(1)}, bf16[2,4,32,4096]{3,2,1,0:T(8,128)(2,1)S(1)}, u32[]{:S(2)}, u32[]{:S(2)}) collective-permute-start(bf16[2,4,32,4096]{3,2,1,0:T(8,128)(2,1)S(1)} %pad_maximum_fusion), channel_id=1, source_target_pairs={{0,3},{1,0},{2,1},{3,2},{4,7},{5,4},{6,5},{7,6},{8,11},{9,8},{10,9... | collective-permute-start | bytes 6291464 | tf_op jit(solution)/shard_map/ppermute | solution.py:154
  46.9 1.9 collective-permute-done.14
  48.8 1.8 collective-permute-done.16
  53.1 38.3 %collective-permute-done.8 = bf16[2,4,32,4096]{3,2,1,0:T(8,128)(2,1)S(1)} collective-permute-done((bf16[2,4,32,4096]{3,2,1,0:T(8,128)(2,1)S(1)}, bf16[2,4,32,4096]{3,2,1,0:T(8,128)(2,1)S(1)}, u32[]{:S(2)}, u32[]{:S(2)}) %collective-permute-start.8) | collective-permute-done | bytes 2097184 | tf_op jit(solution)/shard_map/ppermute | solution.py:154
  92.5 3.7 %collective-permute-start.10 = (bf16[1,4,32,4096]{3,2,1,0:T(8,128)(2,1)}, bf16[1,4,32,4096]{3,2,1,0:T(8,128)(2,1)S(1)}, u32[]{:S(2)}, u32[]{:S(2)}) collective-permute-start(bf16[1,4,32,4096]{3,2,1,0:T(8,128)(2,1)} %slice.132), channel_id=1, source_target_pairs={{0,3},{1,0},{2,1},{3,2},{4,7},{5,4},{6,5},{7,6},{8,11},{9,8},{10,9... | collective-permute-start | bytes 3145736 | tf_op jit(solution)/shard_map/ppermute | solution.py:154
  100.8 1.6 collective-permute-start.19
  104.8 12.7 %collective-permute-done.10 = bf16[1,4,32,4096]{3,2,1,0:T(8,128)(2,1)S(1)} collective-permute-done((bf16[1,4,32,4096]{3,2,1,0:T(8,128)(2,1)}, bf16[1,4,32,4096]{3,2,1,0:T(8,128)(2,1)S(1)}, u32[]{:S(2)}, u32[]{:S(2)}) %collective-permute-start.10) | collective-permute-done | bytes 1048608 | tf_op jit(solution)/shard_map/ppermute | solution.py:154
  117.6 4.5 %collective-permute-done.9 = bf16[1,4,32,4096]{3,2,1,0:T(8,128)(2,1)S(1)} collective-permute-done((bf16[1,4,32,4096]{3,2,1,0:T(8,128)(2,1)}, bf16[1,4,32,4096]{3,2,1,0:T(8,128)(2,1)S(1)}, u32[]{:S(2)}, u32[]{:S(2)}) %collective-permute-start.9) | collective-permute-done | bytes 1048608 | tf_op jit(solution)/shard_map/ppermute | solution.py:154
  122.1 3.5 %collective-permute-done.19 = bf16[1,4,32,4096]{3,2,1,0:T(8,128)(2,1)} collective-permute-done((bf16[1,4,32,4096]{3,2,1,0:T(8,128)(2,1)}, bf16[1,4,32,4096]{3,2,1,0:T(8,128)(2,1)}, u32[]{:S(2)}, u32[]{:S(2)}) %collective-permute-start.19) | collective-permute-done | bytes 1048608 | tf_op jit(solution)/shard_map/ppermute | solution.py:154
  125.6 18.9 %aggregate.1 = (bf16[4,2,1024,128]{3,2,1,0:T(8,128)(2,1)}, bf16[2,4,1024,128]{3,2,1,0:T(8,128)(2,1)}, bf16[4,2,1024,128]{3,2,1,0:T(8,128)(2,1)}, bf16[2,4,1024,128]{3,2,1,0:T(8,128)(2,1)}) custom-call(s32[384]{0:T(512)} %reduce.rows_ref, s32[384]{0:T(512)} %reduce.1.cols_ref, s32[6]{0:T(128)} %stack.101.info_ref, bf16[384,128,128]{2,1,0:T(8,128)(2,1)} %bitcast.98, ...), custom_call_target="tpu_custom_call" | custom-call | tf_op jit(solution)/shard_map/aggregate/pallas_call | solution.py:125
  145.1 3.9 %collective-permute-done.21 = bf16[4,2,1024,128]{3,2,1,0:T(8,128)(2,1)S(1)} collective-permute-done((bf16[4,2,1024,128]{3,2,1,0:T(8,128)(2,1)}, bf16[4,2,1024,128]{3,2,1,0:T(8,128)(2,1)S(1)}, u32[]{:S(2)}, u32[]{:S(2)}) %collective-permute-start.21) | collective-permute-done | bytes 2097184 | tf_op jit(solution)/shard_map/ppermute | solution.py:149
  149.0 1.9 fusion.5
  151.0 8.4 %collective-permute-start.24 = (bf16[2,1024,128]{2,1,0:T(8,128)(2,1)S(1)}, bf16[2,1024,128]{2,1,0:T(8,128)(2,1)S(1)}, u32[]{:S(2)}, u32[]{:S(2)}) collective-permute-start(bf16[2,1024,128]{2,1,0:T(8,128)(2,1)S(1)} %get-tuple-element.17), channel_id=1, source_target_pairs={{0,3},{1,0},{2,1},{3,2},{4,7},{5,4},{6,5},{7,6},{8,11},{9,8},{10,9... | collective-permute-start | bytes 1572872 | tf_op jit(solution)/shard_map/ppermute | solution.py:154
  160.9 1.7 collective-permute-start.27
  162.5 8.8 %collective-permute-done.22 = bf16[2,1024,128]{2,1,0:T(8,128)(2,1)S(1)} collective-permute-done((bf16[2,1024,128]{2,1,0:T(8,128)(2,1)S(1)}, bf16[2,1024,128]{2,1,0:T(8,128)(2,1)S(1)}, u32[]{:S(2)}, u32[]{:S(2)}) %collective-permute-start.22) | collective-permute-done | bytes 524320 | tf_op jit(solution)/shard_map/ppermute | solution.py:154
  171.3 10.8 %collective-permute-done.24 = bf16[2,1024,128]{2,1,0:T(8,128)(2,1)S(1)} collective-permute-done((bf16[2,1024,128]{2,1,0:T(8,128)(2,1)S(1)}, bf16[2,1024,128]{2,1,0:T(8,128)(2,1)S(1)}, u32[]{:S(2)}, u32[]{:S(2)}) %collective-permute-start.24) | collective-permute-done | bytes 524320 | tf_op jit(solution)/shard_map/ppermute | solution.py:154
  182.1 1.7 collective-permute-done.23
  185.2 1.7 collective-permute-start.25
  188.4 2.1 %collective-permute-start.30 = (bf16[1024,128]{1,0:T(8,128)(2,1)S(1)}, bf16[1024,128]{1,0:T(8,128)(2,1)S(1)}, u32[]{:S(2)}, u32[]{:S(2)}) collective-permute-start(bf16[1024,128]{1,0:T(8,128)(2,1)S(1)} %get-tuple-element.14), channel_id=1, source_target_pairs={{0,3},{1,0},{2,1},{3,2},{4,7},{5,4},{6,5},{7,6},{8,11},{9,8},{10,9... | collective-permute-start | bytes 786440 | tf_op jit(solution)/shard_map/ppermute | solution.py:154
  192.8 4.6 %collective-permute-done.28 = bf16[1024,128]{1,0:T(8,128)(2,1)S(1)} collective-permute-done((bf16[1024,128]{1,0:T(8,128)(2,1)S(1)}, bf16[1024,128]{1,0:T(8,128)(2,1)S(1)}, u32[]{:S(2)}, u32[]{:S(2)}) %collective-permute-start.28) | collective-permute-done | bytes 262176 | tf_op jit(solution)/shard_map/ppermute | solution.py:154
  197.4 3.2 %collective-permute-done.30 = bf16[1024,128]{1,0:T(8,128)(2,1)S(1)} collective-permute-done((bf16[1024,128]{1,0:T(8,128)(2,1)S(1)}, bf16[1024,128]{1,0:T(8,128)(2,1)S(1)}, u32[]{:S(2)}, u32[]{:S(2)}) %collective-permute-start.30) | collective-permute-done | bytes 262176 | tf_op jit(solution)/shard_map/ppermute | solution.py:154
  (82 shorter events, 25.6 us)
Async XLA Ops:
  0.0 201.8 %copy-start = (bf16[128,256]{1,0:T(8,128)(2,1)S(1)}, bf16[128,256]{1,0:T(8,128)(2,1)}, u32[]{:S(2)}) copy-start(bf16[128,256]{1,0:T(8,128)(2,1)} %param.12) | copy-start | bytes 196612
  1.1 14.1 %collective-permute-start.12 = (bf16[32,4096]{1,0:T(8,128)(2,1)S(1)}, bf16[32,4096]{1,0:T(8,128)(2,1)S(1)}, u32[]{:S(2)}, u32[]{:S(2)}) collective-permute-start(bf16[32,4096]{1,0:T(8,128)(2,1)S(1)} %get-tuple-element.21), channel_id=1, source_target_pairs={{0,3},{1,0},{2,1},{3,2},{4,7},{5,4},{6,5},{7,6},{8,11},{9,8},{10,9... | collective-permute-start | bytes 786440 | tf_op jit(solution)/shard_map/ppermute | solution.py:154
  4.0 14.6 %collective-permute-start.11 = (bf16[32,4096]{1,0:T(8,128)(2,1)S(1)}, bf16[32,4096]{1,0:T(8,128)(2,1)S(1)}, u32[]{:S(2)}, u32[]{:S(2)}) collective-permute-start(bf16[32,4096]{1,0:T(8,128)(2,1)S(1)} %get-tuple-element.21), channel_id=1, source_target_pairs={{0,1},{1,2},{2,3},{3,0},{4,5},{5,6},{6,7},{7,4},{8,9},{9,10},{10,1... | collective-permute-start | bytes 786440 | tf_op jit(solution)/shard_map/ppermute | solution.py:154
  4.1 18.5 %collective-permute-start.13 = (bf16[32,4096]{1,0:T(8,128)(2,1)S(1)}, bf16[32,4096]{1,0:T(8,128)(2,1)S(1)}, u32[]{:S(2)}, u32[]{:S(2)}) collective-permute-start(bf16[32,4096]{1,0:T(8,128)(2,1)S(1)} %get-tuple-element.21), channel_id=1, source_target_pairs={{0,2},{1,3},{2,0},{3,1},{4,6},{5,7},{6,4},{7,5},{8,10},{9,11},{10,... | collective-permute-start | bytes 786440 | tf_op jit(solution)/shard_map/ppermute | solution.py:154
  6.3 16.3 %collective-permute-start.3 = (bf16[32,8192]{1,0:T(8,128)(2,1)}, bf16[32,8192]{1,0:T(8,128)(2,1)S(1)}, u32[]{:S(2)}, u32[]{:S(2)}) collective-permute-start(bf16[32,8192]{1,0:T(8,128)(2,1)} %bitcast.109), channel_id=1, source_target_pairs={{0,16},{16,0},{1,17},{17,1},{2,18},{18,2},{3,19},{19,3},{4,20},{20... | collective-permute-start | bytes 1572872 | tf_op jit(solution)/shard_map/ppermute | solution.py:149
  9.5 15.6 %collective-permute-start.1 = (bf16[32,4096]{1,0:T(8,128)(2,1)S(1)}, bf16[32,4096]{1,0:T(8,128)(2,1)S(1)}, u32[]{:S(2)}, u32[]{:S(2)}) collective-permute-start(bf16[32,4096]{1,0:T(8,128)(2,1)S(1)} %get-tuple-element.22), channel_id=1, source_target_pairs={{0,96},{32,0},{64,32},{96,64},{1,97},{33,1},{65,33},{97,65},{2,98}... | collective-permute-start | bytes 786440 | tf_op jit(solution)/shard_map/ppermute | solution.py:154
  15.2 11.7 %collective-permute-start = (bf16[32,4096]{1,0:T(8,128)(2,1)S(1)}, bf16[32,4096]{1,0:T(8,128)(2,1)S(1)}, u32[]{:S(2)}, u32[]{:S(2)}) collective-permute-start(bf16[32,4096]{1,0:T(8,128)(2,1)S(1)} %get-tuple-element.22), channel_id=1, source_target_pairs={{0,32},{32,64},{64,96},{96,0},{1,33},{33,65},{65,97},{97,1},{2,34}... | collective-permute-start | bytes 786440 | tf_op jit(solution)/shard_map/ppermute | solution.py:154
  18.6 11.8 %collective-permute-start.2 = (bf16[32,4096]{1,0:T(8,128)(2,1)S(1)}, bf16[32,4096]{1,0:T(8,128)(2,1)S(1)}, u32[]{:S(2)}, u32[]{:S(2)}) collective-permute-start(bf16[32,4096]{1,0:T(8,128)(2,1)S(1)} %get-tuple-element.22), channel_id=1, source_target_pairs={{0,64},{32,96},{64,0},{96,32},{1,65},{33,97},{65,1},{97,33},{2,66}... | collective-permute-start | bytes 786440 | tf_op jit(solution)/shard_map/ppermute | solution.py:154
  22.8 14.7 %collective-permute-start.5 = (bf16[32,4096]{1,0:T(8,128)(2,1)S(1)}, bf16[32,4096]{1,0:T(8,128)(2,1)S(1)}, u32[]{:S(2)}, u32[]{:S(2)}) collective-permute-start(bf16[32,4096]{1,0:T(8,128)(2,1)S(1)} %get-tuple-element.26), channel_id=1, source_target_pairs={{0,96},{32,0},{64,32},{96,64},{1,97},{33,1},{65,33},{97,65},{2,98}... | collective-permute-start | bytes 786440 | tf_op jit(solution)/shard_map/ppermute | solution.py:154
  25.1 14.7 %collective-permute-start.4 = (bf16[32,4096]{1,0:T(8,128)(2,1)S(1)}, bf16[32,4096]{1,0:T(8,128)(2,1)S(1)}, u32[]{:S(2)}, u32[]{:S(2)}) collective-permute-start(bf16[32,4096]{1,0:T(8,128)(2,1)S(1)} %get-tuple-element.26), channel_id=1, source_target_pairs={{0,32},{32,64},{64,96},{96,0},{1,33},{33,65},{65,97},{97,1},{2,34}... | collective-permute-start | bytes 786440 | tf_op jit(solution)/shard_map/ppermute | solution.py:154
  25.1 14.7 %collective-permute-start.6 = (bf16[32,4096]{1,0:T(8,128)(2,1)S(1)}, bf16[32,4096]{1,0:T(8,128)(2,1)S(1)}, u32[]{:S(2)}, u32[]{:S(2)}) collective-permute-start(bf16[32,4096]{1,0:T(8,128)(2,1)S(1)} %get-tuple-element.26), channel_id=1, source_target_pairs={{0,64},{32,96},{64,0},{96,32},{1,65},{33,97},{65,1},{97,33},{2,66}... | collective-permute-start | bytes 786440 | tf_op jit(solution)/shard_map/ppermute | solution.py:154
  30.6 16.3 %collective-permute-start.15 = (bf16[32,4096]{1,0:T(8,128)(2,1)S(1)}, bf16[32,4096]{1,0:T(8,128)(2,1)S(1)}, u32[]{:S(2)}, u32[]{:S(2)}) collective-permute-start(bf16[32,4096]{1,0:T(8,128)(2,1)S(1)} %get-tuple-element.25), channel_id=1, source_target_pairs={{0,3},{1,0},{2,1},{3,2},{4,7},{5,4},{6,5},{7,6},{8,11},{9,8},{10,9... | collective-permute-start | bytes 786440 | tf_op jit(solution)/shard_map/ppermute | solution.py:154
  37.5 11.3 %collective-permute-start.14 = (bf16[32,4096]{1,0:T(8,128)(2,1)S(1)}, bf16[32,4096]{1,0:T(8,128)(2,1)S(1)}, u32[]{:S(2)}, u32[]{:S(2)}) collective-permute-start(bf16[32,4096]{1,0:T(8,128)(2,1)S(1)} %get-tuple-element.25), channel_id=1, source_target_pairs={{0,1},{1,2},{2,3},{3,0},{4,5},{5,6},{6,7},{7,4},{8,9},{9,10},{10,1... | collective-permute-start | bytes 786440 | tf_op jit(solution)/shard_map/ppermute | solution.py:154
  37.5 13.1 %collective-permute-start.16 = (bf16[32,4096]{1,0:T(8,128)(2,1)S(1)}, bf16[32,4096]{1,0:T(8,128)(2,1)S(1)}, u32[]{:S(2)}, u32[]{:S(2)}) collective-permute-start(bf16[32,4096]{1,0:T(8,128)(2,1)S(1)} %get-tuple-element.25), channel_id=1, source_target_pairs={{0,2},{1,3},{2,0},{3,1},{4,6},{5,7},{6,4},{7,5},{8,10},{9,11},{10,... | collective-permute-start | bytes 786440 | tf_op jit(solution)/shard_map/ppermute | solution.py:154
  40.2 51.2 %collective-permute-start.8 = (bf16[2,4,32,4096]{3,2,1,0:T(8,128)(2,1)S(1)}, bf16[2,4,32,4096]{3,2,1,0:T(8,128)(2,1)S(1)}, u32[]{:S(2)}, u32[]{:S(2)}) collective-permute-start(bf16[2,4,32,4096]{3,2,1,0:T(8,128)(2,1)S(1)} %pad_maximum_fusion), channel_id=1, source_target_pairs={{0,3},{1,0},{2,1},{3,2},{4,7},{5,4},{6,5},{7,6},{8,11},{9,8},{10,9... | collective-permute-start | bytes 6291464 | tf_op jit(solution)/shard_map/ppermute | solution.py:154
  46.9 49.3 %collective-permute-start.7 = (bf16[2,4,32,4096]{3,2,1,0:T(8,128)(2,1)S(1)}, bf16[2,4,32,4096]{3,2,1,0:T(8,128)(2,1)S(1)}, u32[]{:S(2)}, u32[]{:S(2)}) collective-permute-start(bf16[2,4,32,4096]{3,2,1,0:T(8,128)(2,1)S(1)} %pad_maximum_fusion), channel_id=1, source_target_pairs={{0,1},{1,2},{2,3},{3,0},{4,5},{5,6},{6,7},{7,4},{8,9},{9,10},{10,1... | collective-permute-start | bytes 6291464 | tf_op jit(solution)/shard_map/ppermute | solution.py:154
  51.0 46.4 %collective-permute-start.18 = (bf16[2,4,32,4096]{3,2,1,0:T(8,128)(2,1)S(1)}, bf16[2,4,32,4096]{3,2,1,0:T(8,128)(2,1)S(1)}, u32[]{:S(2)}, u32[]{:S(2)}) collective-permute-start(bf16[2,4,32,4096]{3,2,1,0:T(8,128)(2,1)S(1)} %pad_maximum_fusion.1), channel_id=1, source_target_pairs={{0,96},{32,0},{64,32},{96,64},{1,97},{33,1},{65,33},{97,65},{2,98}... | collective-permute-start | bytes 6291464 | tf_op jit(solution)/shard_map/ppermute | solution.py:154
  52.2 46.4 %collective-permute-start.17 = (bf16[2,4,32,4096]{3,2,1,0:T(8,128)(2,1)S(1)}, bf16[2,4,32,4096]{3,2,1,0:T(8,128)(2,1)S(1)}, u32[]{:S(2)}, u32[]{:S(2)}) collective-permute-start(bf16[2,4,32,4096]{3,2,1,0:T(8,128)(2,1)S(1)} %pad_maximum_fusion.1), channel_id=1, source_target_pairs={{0,32},{32,64},{64,96},{96,0},{1,33},{33,65},{65,97},{97,1},{2,34}... | collective-permute-start | bytes 6291464 | tf_op jit(solution)/shard_map/ppermute | solution.py:154
  92.5 25.1 %collective-permute-start.10 = (bf16[1,4,32,4096]{3,2,1,0:T(8,128)(2,1)}, bf16[1,4,32,4096]{3,2,1,0:T(8,128)(2,1)S(1)}, u32[]{:S(2)}, u32[]{:S(2)}) collective-permute-start(bf16[1,4,32,4096]{3,2,1,0:T(8,128)(2,1)} %slice.132), channel_id=1, source_target_pairs={{0,3},{1,0},{2,1},{3,2},{4,7},{5,4},{6,5},{7,6},{8,11},{9,8},{10,9... | collective-permute-start | bytes 3145736 | tf_op jit(solution)/shard_map/ppermute | solution.py:154
  97.3 24.8 %collective-permute-start.9 = (bf16[1,4,32,4096]{3,2,1,0:T(8,128)(2,1)}, bf16[1,4,32,4096]{3,2,1,0:T(8,128)(2,1)S(1)}, u32[]{:S(2)}, u32[]{:S(2)}) collective-permute-start(bf16[1,4,32,4096]{3,2,1,0:T(8,128)(2,1)} %slice.131), channel_id=1, source_target_pairs={{0,1},{1,2},{2,3},{3,0},{4,5},{5,6},{6,7},{7,4},{8,9},{9,10},{10,1... | collective-permute-start | bytes 3145736 | tf_op jit(solution)/shard_map/ppermute | solution.py:154
  98.6 23.5 %collective-permute-start.20 = (bf16[1,4,32,4096]{3,2,1,0:T(8,128)(2,1)}, bf16[1,4,32,4096]{3,2,1,0:T(8,128)(2,1)S(1)}, u32[]{:S(2)}, u32[]{:S(2)}) collective-permute-start(bf16[1,4,32,4096]{3,2,1,0:T(8,128)(2,1)} %slice.136), channel_id=1, source_target_pairs={{0,96},{32,0},{64,32},{96,64},{1,97},{33,1},{65,33},{97,65},{2,98}... | collective-permute-start | bytes 3145736 | tf_op jit(solution)/shard_map/ppermute | solution.py:154
  100.8 24.8 %collective-permute-start.19 = (bf16[1,4,32,4096]{3,2,1,0:T(8,128)(2,1)}, bf16[1,4,32,4096]{3,2,1,0:T(8,128)(2,1)}, u32[]{:S(2)}, u32[]{:S(2)}) collective-permute-start(bf16[1,4,32,4096]{3,2,1,0:T(8,128)(2,1)} %slice.135), channel_id=1, source_target_pairs={{0,32},{32,64},{64,96},{96,0},{1,33},{33,65},{65,97},{97,1},{2,34}... | collective-permute-start | bytes 3145736 | tf_op jit(solution)/shard_map/ppermute | solution.py:154
  144.5 4.5 %collective-permute-start.21 = (bf16[4,2,1024,128]{3,2,1,0:T(8,128)(2,1)}, bf16[4,2,1024,128]{3,2,1,0:T(8,128)(2,1)S(1)}, u32[]{:S(2)}, u32[]{:S(2)}) collective-permute-start(bf16[4,2,1024,128]{3,2,1,0:T(8,128)(2,1)} %get-tuple-element.10), channel_id=1, source_target_pairs={{0,4},{4,0},{1,5},{5,1},{2,6},{6,2},{3,7},{7,3},{8,12},{12,8},{9,1... | collective-permute-start | bytes 6291464 | tf_op jit(solution)/shard_map/ppermute | solution.py:149
  144.6 16.0 %collective-permute-start.26 = (bf16[2,4,1024,128]{3,2,1,0:T(8,128)(2,1)}, bf16[2,4,1024,128]{3,2,1,0:T(8,128)(2,1)S(1)}, u32[]{:S(2)}, u32[]{:S(2)}) collective-permute-start(bf16[2,4,1024,128]{3,2,1,0:T(8,128)(2,1)} %get-tuple-element.12), channel_id=1, source_target_pairs={{0,4},{4,0},{1,5},{5,1},{2,6},{6,2},{3,7},{7,3},{8,12},{12,8},{9,1... | collective-permute-start | bytes 6291464 | tf_op jit(solution)/shard_map/ppermute | solution.py:149
  150.9 20.4 %collective-permute-start.22 = (bf16[2,1024,128]{2,1,0:T(8,128)(2,1)S(1)}, bf16[2,1024,128]{2,1,0:T(8,128)(2,1)S(1)}, u32[]{:S(2)}, u32[]{:S(2)}) collective-permute-start(bf16[2,1024,128]{2,1,0:T(8,128)(2,1)S(1)} %get-tuple-element.16), channel_id=1, source_target_pairs={{0,1},{1,2},{2,3},{3,0},{4,5},{5,6},{6,7},{7,4},{8,9},{9,10},{10,1... | collective-permute-start | bytes 1572872 | tf_op jit(solution)/shard_map/ppermute | solution.py:154
  151.0 31.1 %collective-permute-start.24 = (bf16[2,1024,128]{2,1,0:T(8,128)(2,1)S(1)}, bf16[2,1024,128]{2,1,0:T(8,128)(2,1)S(1)}, u32[]{:S(2)}, u32[]{:S(2)}) collective-permute-start(bf16[2,1024,128]{2,1,0:T(8,128)(2,1)S(1)} %get-tuple-element.17), channel_id=1, source_target_pairs={{0,3},{1,0},{2,1},{3,2},{4,7},{5,4},{6,5},{7,6},{8,11},{9,8},{10,9... | collective-permute-start | bytes 1572872 | tf_op jit(solution)/shard_map/ppermute | solution.py:154
  159.4 24.4 %collective-permute-start.23 = (bf16[2,1024,128]{2,1,0:T(8,128)(2,1)S(1)}, bf16[2,1024,128]{2,1,0:T(8,128)(2,1)S(1)}, u32[]{:S(2)}, u32[]{:S(2)}) collective-permute-start(bf16[2,1024,128]{2,1,0:T(8,128)(2,1)S(1)} %get-tuple-element.18), channel_id=1, source_target_pairs={{0,2},{1,3},{2,0},{3,1},{4,6},{5,7},{6,4},{7,5},{8,10},{9,11},{10,... | collective-permute-start | bytes 1572872 | tf_op jit(solution)/shard_map/ppermute | solution.py:154
  160.9 26.0 %collective-permute-start.27 = (bf16[4,1024,128]{2,1,0:T(8,128)(2,1)S(1)}, bf16[4,1024,128]{2,1,0:T(8,128)(2,1)S(1)}, u32[]{:S(2)}, u32[]{:S(2)}) collective-permute-start(bf16[4,1024,128]{2,1,0:T(8,128)(2,1)S(1)} %fusion.2), channel_id=1, source_target_pairs={{0,8},{8,0},{1,9},{9,1},{2,10},{10,2},{3,11},{11,3},{4,12},{12,4},... | collective-permute-start | bytes 3145736 | tf_op jit(solution)/shard_map/ppermute | solution.py:149
  185.2 7.6 %collective-permute-start.25 = (bf16[1024,128]{1,0:T(8,128)(2,1)S(1)}, bf16[1024,128]{1,0:T(8,128)(2,1)S(1)}, u32[]{:S(2)}, u32[]{:S(2)}) collective-permute-start(bf16[1024,128]{1,0:T(8,128)(2,1)S(1)} %fusion.20), channel_id=1, source_target_pairs={{0,8},{8,0},{1,9},{9,1},{2,10},{10,2},{3,11},{11,3},{4,12},{12,4},... | collective-permute-start | bytes 786440 | tf_op jit(solution)/shard_map/ppermute | solution.py:149
  187.2 10.3 %collective-permute-start.28 = (bf16[1024,128]{1,0:T(8,128)(2,1)S(1)}, bf16[1024,128]{1,0:T(8,128)(2,1)S(1)}, u32[]{:S(2)}, u32[]{:S(2)}) collective-permute-start(bf16[1024,128]{1,0:T(8,128)(2,1)S(1)} %get-tuple-element.13), channel_id=1, source_target_pairs={{0,1},{1,2},{2,3},{3,0},{4,5},{5,6},{6,7},{7,4},{8,9},{9,10},{10,1... | collective-permute-start | bytes 786440 | tf_op jit(solution)/shard_map/ppermute | solution.py:154
  188.4 12.2 %collective-permute-start.30 = (bf16[1024,128]{1,0:T(8,128)(2,1)S(1)}, bf16[1024,128]{1,0:T(8,128)(2,1)S(1)}, u32[]{:S(2)}, u32[]{:S(2)}) collective-permute-start(bf16[1024,128]{1,0:T(8,128)(2,1)S(1)} %get-tuple-element.14), channel_id=1, source_target_pairs={{0,3},{1,0},{2,1},{3,2},{4,7},{5,4},{6,5},{7,6},{8,11},{9,8},{10,9... | collective-permute-start | bytes 786440 | tf_op jit(solution)/shard_map/ppermute | solution.py:154
  190.5 11.1 %collective-permute-start.29 = (bf16[1024,128]{1,0:T(8,128)(2,1)S(1)}, bf16[1024,128]{1,0:T(8,128)(2,1)S(1)}, u32[]{:S(2)}, u32[]{:S(2)}) collective-permute-start(bf16[1024,128]{1,0:T(8,128)(2,1)S(1)} %get-tuple-element.15), channel_id=1, source_target_pairs={{0,2},{1,3},{2,0},{3,1},{4,6},{5,7},{6,4},{7,5},{8,10},{9,11},{10,... | collective-permute-start | bytes 786440 | tf_op jit(solution)/shard_map/ppermute | solution.py:154
  (13 other events, 122.3 us)

commit v7 on v6

--- a/solution.py
+++ b/solution.py
@@ -145,6 +145,9 @@
     )(rows, cols, info, tiles, *arrays)
 
 
+tie = lax.optimization_barrier
+
+
 def swap(value, axis):
     return lax.ppermute(value, axis, [(0, 1), (1, 0)])
 
@@ -188,7 +191,7 @@
 
 
 def reduce_rows(keep_a, keep_b, send_a, send_b):
-    got_b = swap(send_b, "cc")
+    send_a, got_b = tie((send_a, swap(send_b, "cc")))
     got_a = swap(send_a, "cc")
     b = swap(low(total(keep_b[1], got_b[1])), "cy")
     a = [shift(low(total(keep_a[d], got_a[d])), "fx", d) for d in (1, 2, 3)]

time: 203 us -> 200 us (0.985)
  waiting for transfers between devices: 105 us -> 99.8 us
  starting transfers between devices: 62.9 us -> 66.1 us
    ppermute x26, waiting for transfers between devices: 100 us -> 79.2 us  [shift(): return lax.ppermute(value, axis, [(i, (i + by) % n) for i in range(n)])]
    ppermute x5, waiting for transfers between devices: 5.17 us -> 20.6 us  [swap(): return lax.ppermute(value, axis, [(0, 1), (1, 0)])]
    ppermute x26, starting transfers between devices: 55.8 us -> 60.2 us  [shift(): return lax.ppermute(value, axis, [(i, (i + by) % n) for i in range(n)])]
  transfers between devices with their start and end apart: 31 -> 31, of which waited for: 18 -> 16; matrix products, arithmetic and copies ran while one was open for 6% -> 5% of each run, Pallas kernels for 0% -> 0%
where the time goes in v7:
time: 200 us; the launch traced here: 199 us
  waiting for transfers between devices  99.8 us (50%)
  starting transfers between devices  66.1 us (33%)
  Pallas kernels  18.8 us (9%)
  local copies, waits for them, and re-layouts  7.52 us (4%)
  other arithmetic  4.89 us (2%)
    ppermute x26, waiting for transfers between devices, shift(): return lax.ppermute(value, axis, [(i, (i + by) % n) for i in range(n)])  79.2 us
    ppermute x26, starting transfers between devices, shift(): return lax.ppermute(value, axis, [(i, (i + by) % n) for i in range(n)])  60.2 us
    ppermute x5, waiting for transfers between devices, swap(): return lax.ppermute(value, axis, [(0, 1), (1, 0)])  20.6 us
    pallas_call x1, Pallas kernels, aggregate(): pl.pallas_call(functools.partial(aggregate_kernel, where, len(arrays)), o...  18.8 us
    ppermute x5, starting transfers between devices, swap(): return lax.ppermute(value, axis, [(0, 1), (1, 0)])  5.92 us
  transfers between devices with their start and end apart: 31, of which 16 were waited for; matrix products, arithmetic and copies ran while one was open for 5% of the time, Pallas kernels for 0%

profile of v7, /device:TPU:0, one launch (start us, length us, event | category | flops | bytes accessed | tf_op | source)
XLA Modules:
  0.0 199.5 jit_solution(13799499886476180142)
XLA Ops:
  1.1 2.9 %collective-permute-start.12 = (bf16[32,4096]{1,0:T(8,128)(2,1)S(1)}, bf16[32,4096]{1,0:T(8,128)(2,1)S(1)}, u32[]{:S(2)}, u32[]{:S(2)}) collective-permute-start(bf16[32,4096]{1,0:T(8,128)(2,1)S(1)} %get-tuple-element.25), channel_id=1, source_target_pairs={{0,3},{1,0},{2,1},{3,2},{4,7},{5,4},{6,5},{7,6},{8,11},{9,8},{10,9... | collective-permute-start | bytes 786440 | tf_op jit(solution)/shard_map/ppermute | solution.py:157
  4.1 2.3 %collective-permute-start.13 = (bf16[32,4096]{1,0:T(8,128)(2,1)S(1)}, bf16[32,4096]{1,0:T(8,128)(2,1)S(1)}, u32[]{:S(2)}, u32[]{:S(2)}) collective-permute-start(bf16[32,4096]{1,0:T(8,128)(2,1)S(1)} %get-tuple-element.25), channel_id=1, source_target_pairs={{0,2},{1,3},{2,0},{3,1},{4,6},{5,7},{6,4},{7,5},{8,10},{9,11},{10,... | collective-permute-start | bytes 786440 | tf_op jit(solution)/shard_map/ppermute | solution.py:157
  6.3 3.2 %collective-permute-start.3 = (bf16[32,8192]{1,0:T(8,128)(2,1)}, bf16[32,8192]{1,0:T(8,128)(2,1)S(1)}, u32[]{:S(2)}, u32[]{:S(2)}) collective-permute-start(bf16[32,8192]{1,0:T(8,128)(2,1)} %bitcast.109), channel_id=1, source_target_pairs={{0,16},{16,0},{1,17},{17,1},{2,18},{18,2},{3,19},{19,3},{4,20},{20... | collective-permute-start | bytes 1572872 | tf_op jit(solution)/shard_map/ppermute | solution.py:152
  9.5 4.0 %collective-permute-start.1 = (bf16[32,4096]{1,0:T(8,128)(2,1)S(1)}, bf16[32,4096]{1,0:T(8,128)(2,1)S(1)}, u32[]{:S(2)}, u32[]{:S(2)}) collective-permute-start(bf16[32,4096]{1,0:T(8,128)(2,1)S(1)} %get-tuple-element.26), channel_id=1, source_target_pairs={{0,96},{32,0},{64,32},{96,64},{1,97},{33,1},{65,33},{97,65},{2,98}... | collective-permute-start | bytes 786440 | tf_op jit(solution)/shard_map/ppermute | solution.py:157
  13.6 1.7 collective-permute-done.12
  15.2 1.9 collective-permute-start
  18.6 3.9 %collective-permute-start.2 = (bf16[32,4096]{1,0:T(8,128)(2,1)S(1)}, bf16[32,4096]{1,0:T(8,128)(2,1)S(1)}, u32[]{:S(2)}, u32[]{:S(2)}) collective-permute-start(bf16[32,4096]{1,0:T(8,128)(2,1)S(1)} %get-tuple-element.26), channel_id=1, source_target_pairs={{0,64},{32,96},{64,0},{96,32},{1,65},{33,97},{65,1},{97,33},{2,66}... | collective-permute-start | bytes 786440 | tf_op jit(solution)/shard_map/ppermute | solution.py:157
  22.8 2.3 %collective-permute-start.5 = (bf16[32,4096]{1,0:T(8,128)(2,1)S(1)}, bf16[32,4096]{1,0:T(8,128)(2,1)S(1)}, u32[]{:S(2)}, u32[]{:S(2)}) collective-permute-start(bf16[32,4096]{1,0:T(8,128)(2,1)S(1)} %get-tuple-element.30), channel_id=1, source_target_pairs={{0,96},{32,0},{64,32},{96,64},{1,97},{33,1},{65,33},{97,65},{2,98}... | collective-permute-start | bytes 786440 | tf_op jit(solution)/shard_map/ppermute | solution.py:157
  25.1 1.9 collective-permute-start.6
  27.0 3.5 %collective-permute-done.2 = bf16[32,4096]{1,0:T(8,128)(2,1)S(1)} collective-permute-done((bf16[32,4096]{1,0:T(8,128)(2,1)S(1)}, bf16[32,4096]{1,0:T(8,128)(2,1)S(1)}, u32[]{:S(2)}, u32[]{:S(2)}) %collective-permute-start.2) | collective-permute-done | bytes 262176 | tf_op jit(solution)/shard_map/ppermute | solution.py:157
  30.6 6.9 %collective-permute-start.15 = (bf16[32,4096]{1,0:T(8,128)(2,1)S(1)}, bf16[32,4096]{1,0:T(8,128)(2,1)S(1)}, u32[]{:S(2)}, u32[]{:S(2)}) collective-permute-start(bf16[32,4096]{1,0:T(8,128)(2,1)S(1)} %get-tuple-element.29), channel_id=1, source_target_pairs={{0,3},{1,0},{2,1},{3,2},{4,7},{5,4},{6,5},{7,6},{8,11},{9,8},{10,9... | collective-permute-start | bytes 786440 | tf_op jit(solution)/shard_map/ppermute | solution.py:157
  40.2 6.7 %collective-permute-start.8 = (bf16[2,4,32,4096]{3,2,1,0:T(8,128)(2,1)S(1)}, bf16[2,4,32,4096]{3,2,1,0:T(8,128)(2,1)S(1)}, u32[]{:S(2)}, u32[]{:S(2)}) collective-permute-start(bf16[2,4,32,4096]{3,2,1,0:T(8,128)(2,1)S(1)} %pad_maximum_fusion), channel_id=1, source_target_pairs={{0,3},{1,0},{2,1},{3,2},{4,7},{5,4},{6,5},{7,6},{8,11},{9,8},{10,9... | collective-permute-start | bytes 6291464 | tf_op jit(solution)/shard_map/ppermute | solution.py:157
  46.9 1.9 collective-permute-done.14
  48.8 1.8 collective-permute-done.16
  53.1 38.3 %collective-permute-done.8 = bf16[2,4,32,4096]{3,2,1,0:T(8,128)(2,1)S(1)} collective-permute-done((bf16[2,4,32,4096]{3,2,1,0:T(8,128)(2,1)S(1)}, bf16[2,4,32,4096]{3,2,1,0:T(8,128)(2,1)S(1)}, u32[]{:S(2)}, u32[]{:S(2)}) %collective-permute-start.8) | collective-permute-done | bytes 2097184 | tf_op jit(solution)/shard_map/ppermute | solution.py:157
  92.5 3.7 %collective-permute-start.10 = (bf16[1,4,32,4096]{3,2,1,0:T(8,128)(2,1)}, bf16[1,4,32,4096]{3,2,1,0:T(8,128)(2,1)S(1)}, u32[]{:S(2)}, u32[]{:S(2)}) collective-permute-start(bf16[1,4,32,4096]{3,2,1,0:T(8,128)(2,1)} %slice.132), channel_id=1, source_target_pairs={{0,3},{1,0},{2,1},{3,2},{4,7},{5,4},{6,5},{7,6},{8,11},{9,8},{10,9... | collective-permute-start | bytes 3145736 | tf_op jit(solution)/shard_map/ppermute | solution.py:157
  100.8 1.6 collective-permute-start.19
  104.8 12.8 %collective-permute-done.10 = bf16[1,4,32,4096]{3,2,1,0:T(8,128)(2,1)S(1)} collective-permute-done((bf16[1,4,32,4096]{3,2,1,0:T(8,128)(2,1)}, bf16[1,4,32,4096]{3,2,1,0:T(8,128)(2,1)S(1)}, u32[]{:S(2)}, u32[]{:S(2)}) %collective-permute-start.10) | collective-permute-done | bytes 1048608 | tf_op jit(solution)/shard_map/ppermute | solution.py:157
  117.6 4.5 %collective-permute-done.9 = bf16[1,4,32,4096]{3,2,1,0:T(8,128)(2,1)S(1)} collective-permute-done((bf16[1,4,32,4096]{3,2,1,0:T(8,128)(2,1)}, bf16[1,4,32,4096]{3,2,1,0:T(8,128)(2,1)S(1)}, u32[]{:S(2)}, u32[]{:S(2)}) %collective-permute-start.9) | collective-permute-done | bytes 1048608 | tf_op jit(solution)/shard_map/ppermute | solution.py:157
  122.2 3.5 %collective-permute-done.19 = bf16[1,4,32,4096]{3,2,1,0:T(8,128)(2,1)} collective-permute-done((bf16[1,4,32,4096]{3,2,1,0:T(8,128)(2,1)}, bf16[1,4,32,4096]{3,2,1,0:T(8,128)(2,1)}, u32[]{:S(2)}, u32[]{:S(2)}) %collective-permute-start.19) | collective-permute-done | bytes 1048608 | tf_op jit(solution)/shard_map/ppermute | solution.py:157
  125.7 18.8 %aggregate.1 = (bf16[4,2,1024,128]{3,2,1,0:T(8,128)(2,1)}, bf16[2,4,1024,128]{3,2,1,0:T(8,128)(2,1)}, bf16[4,2,1024,128]{3,2,1,0:T(8,128)(2,1)}, bf16[2,4,1024,128]{3,2,1,0:T(8,128)(2,1)}) custom-call(s32[384]{0:T(512)} %reduce.rows_ref, s32[384]{0:T(512)} %reduce.1.cols_ref, s32[6]{0:T(128)} %stack.101.info_ref, bf16[384,128,128]{2,1,0:T(8,128)(2,1)} %bitcast.98, ...), custom_call_target="tpu_custom_call" | custom-call | tf_op jit(solution)/shard_map/aggregate/pallas_call | solution.py:125
  144.6 4.4 %collective-permute-done.21 = bf16[2,4,1024,128]{3,2,1,0:T(8,128)(2,1)S(1)} collective-permute-done((bf16[2,4,1024,128]{3,2,1,0:T(8,128)(2,1)}, bf16[2,4,1024,128]{3,2,1,0:T(8,128)(2,1)S(1)}, u32[]{:S(2)}, u32[]{:S(2)}) %collective-permute-start.21) | collective-permute-done | bytes 2097184 | tf_op jit(solution)/shard_map/ppermute | solution.py:152
  150.9 2.5 %collective-permute-done.22 = bf16[4,2,1024,128]{3,2,1,0:T(8,128)(2,1)S(1)} collective-permute-done((bf16[4,2,1024,128]{3,2,1,0:T(8,128)(2,1)}, bf16[4,2,1024,128]{3,2,1,0:T(8,128)(2,1)S(1)}, u32[]{:S(2)}, u32[]{:S(2)}) %collective-permute-start.22) | collective-permute-done | bytes 2097184 | tf_op jit(solution)/shard_map/ppermute | solution.py:152
  153.7 1.9 collective-permute-start.23
  155.6 5.5 %collective-permute-start.25 = (bf16[2,1024,128]{2,1,0:T(8,128)(2,1)S(1)}, bf16[2,1024,128]{2,1,0:T(8,128)(2,1)S(1)}, u32[]{:S(2)}, u32[]{:S(2)}) collective-permute-start(bf16[2,1024,128]{2,1,0:T(8,128)(2,1)S(1)} %get-tuple-element.21), channel_id=1, source_target_pairs={{0,3},{1,0},{2,1},{3,2},{4,7},{5,4},{6,5},{7,6},{8,11},{9,8},{10,9... | collective-permute-start | bytes 1572872 | tf_op jit(solution)/shard_map/ppermute | solution.py:157
  162.5 13.7 %collective-permute-done.27 = bf16[4,1024,128]{2,1,0:T(8,128)(2,1)S(1)} collective-permute-done((bf16[4,1024,128]{2,1,0:T(8,128)(2,1)S(1)}, bf16[4,1024,128]{2,1,0:T(8,128)(2,1)S(1)}, u32[]{:S(2)}, u32[]{:S(2)}) %collective-permute-start.27) | collective-permute-done | bytes 1048608 | tf_op jit(solution)/shard_map/ppermute | solution.py:152
  176.6 2.4 %collective-permute-start.28 = (bf16[1024,128]{1,0:T(8,128)(2,1)S(1)}, bf16[1024,128]{1,0:T(8,128)(2,1)S(1)}, u32[]{:S(2)}, u32[]{:S(2)}) collective-permute-start(bf16[1024,128]{1,0:T(8,128)(2,1)S(1)} %get-tuple-element.17), channel_id=1, source_target_pairs={{0,1},{1,2},{2,3},{3,0},{4,5},{5,6},{6,7},{7,4},{8,9},{9,10},{10,1... | collective-permute-start | bytes 786440 | tf_op jit(solution)/shard_map/ppermute | solution.py:157
  179.0 5.8 %collective-permute-start.30 = (bf16[1024,128]{1,0:T(8,128)(2,1)S(1)}, bf16[1024,128]{1,0:T(8,128)(2,1)S(1)}, u32[]{:S(2)}, u32[]{:S(2)}) collective-permute-start(bf16[1024,128]{1,0:T(8,128)(2,1)S(1)} %get-tuple-element.18), channel_id=1, source_target_pairs={{0,3},{1,0},{2,1},{3,2},{4,7},{5,4},{6,5},{7,6},{8,11},{9,8},{10,9... | collective-permute-start | bytes 786440 | tf_op jit(solution)/shard_map/ppermute | solution.py:157
  186.5 2.2 %collective-permute-start.26 = (bf16[1024,128]{1,0:T(8,128)(2,1)S(1)}, bf16[1024,128]{1,0:T(8,128)(2,1)S(1)}, u32[]{:S(2)}, u32[]{:S(2)}) collective-permute-start(bf16[1024,128]{1,0:T(8,128)(2,1)S(1)} %fusion.20), channel_id=1, source_target_pairs={{0,8},{8,0},{1,9},{9,1},{2,10},{10,2},{3,11},{11,3},{4,12},{12,4},... | collective-permute-start | bytes 786440 | tf_op jit(solution)/shard_map/ppermute | solution.py:152
  188.7 2.9 %collective-permute-done.28 = bf16[1024,128]{1,0:T(8,128)(2,1)S(1)} collective-permute-done((bf16[1024,128]{1,0:T(8,128)(2,1)S(1)}, bf16[1024,128]{1,0:T(8,128)(2,1)S(1)}, u32[]{:S(2)}, u32[]{:S(2)}) %collective-permute-start.28) | collective-permute-done | bytes 262176 | tf_op jit(solution)/shard_map/ppermute | solution.py:157
  191.6 4.2 %collective-permute-done.30 = bf16[1024,128]{1,0:T(8,128)(2,1)S(1)} collective-permute-done((bf16[1024,128]{1,0:T(8,128)(2,1)S(1)}, bf16[1024,128]{1,0:T(8,128)(2,1)S(1)}, u32[]{:S(2)}, u32[]{:S(2)}) %collective-permute-start.30) | collective-permute-done | bytes 262176 | tf_op jit(solution)/shard_map/ppermute | solution.py:157
  195.9 1.8 collective-permute-done.29
  (84 shorter events, 23.1 us)
Async XLA Ops:
  0.0 198.0 %copy-start = (bf16[128,256]{1,0:T(8,128)(2,1)S(1)}, bf16[128,256]{1,0:T(8,128)(2,1)}, u32[]{:S(2)}) copy-start(bf16[128,256]{1,0:T(8,128)(2,1)} %param.12) | copy-start | bytes 196612
  1.1 14.1 %collective-permute-start.12 = (bf16[32,4096]{1,0:T(8,128)(2,1)S(1)}, bf16[32,4096]{1,0:T(8,128)(2,1)S(1)}, u32[]{:S(2)}, u32[]{:S(2)}) collective-permute-start(bf16[32,4096]{1,0:T(8,128)(2,1)S(1)} %get-tuple-element.25), channel_id=1, source_target_pairs={{0,3},{1,0},{2,1},{3,2},{4,7},{5,4},{6,5},{7,6},{8,11},{9,8},{10,9... | collective-permute-start | bytes 786440 | tf_op jit(solution)/shard_map/ppermute | solution.py:157
  4.0 14.6 %collective-permute-start.11 = (bf16[32,4096]{1,0:T(8,128)(2,1)S(1)}, bf16[32,4096]{1,0:T(8,128)(2,1)S(1)}, u32[]{:S(2)}, u32[]{:S(2)}) collective-permute-start(bf16[32,4096]{1,0:T(8,128)(2,1)S(1)} %get-tuple-element.25), channel_id=1, source_target_pairs={{0,1},{1,2},{2,3},{3,0},{4,5},{5,6},{6,7},{7,4},{8,9},{9,10},{10,1... | collective-permute-start | bytes 786440 | tf_op jit(solution)/shard_map/ppermute | solution.py:157
  4.1 18.5 %collective-permute-start.13 = (bf16[32,4096]{1,0:T(8,128)(2,1)S(1)}, bf16[32,4096]{1,0:T(8,128)(2,1)S(1)}, u32[]{:S(2)}, u32[]{:S(2)}) collective-permute-start(bf16[32,4096]{1,0:T(8,128)(2,1)S(1)} %get-tuple-element.25), channel_id=1, source_target_pairs={{0,2},{1,3},{2,0},{3,1},{4,6},{5,7},{6,4},{7,5},{8,10},{9,11},{10,... | collective-permute-start | bytes 786440 | tf_op jit(solution)/shard_map/ppermute | solution.py:157
  6.3 16.3 %collective-permute-start.3 = (bf16[32,8192]{1,0:T(8,128)(2,1)}, bf16[32,8192]{1,0:T(8,128)(2,1)S(1)}, u32[]{:S(2)}, u32[]{:S(2)}) collective-permute-start(bf16[32,8192]{1,0:T(8,128)(2,1)} %bitcast.109), channel_id=1, source_target_pairs={{0,16},{16,0},{1,17},{17,1},{2,18},{18,2},{3,19},{19,3},{4,20},{20... | collective-permute-start | bytes 1572872 | tf_op jit(solution)/shard_map/ppermute | solution.py:152
  9.5 15.6 %collective-permute-start.1 = (bf16[32,4096]{1,0:T(8,128)(2,1)S(1)}, bf16[32,4096]{1,0:T(8,128)(2,1)S(1)}, u32[]{:S(2)}, u32[]{:S(2)}) collective-permute-start(bf16[32,4096]{1,0:T(8,128)(2,1)S(1)} %get-tuple-element.26), channel_id=1, source_target_pairs={{0,96},{32,0},{64,32},{96,64},{1,97},{33,1},{65,33},{97,65},{2,98}... | collective-permute-start | bytes 786440 | tf_op jit(solution)/shard_map/ppermute | solution.py:157
  15.2 11.7 %collective-permute-start = (bf16[32,4096]{1,0:T(8,128)(2,1)S(1)}, bf16[32,4096]{1,0:T(8,128)(2,1)S(1)}, u32[]{:S(2)}, u32[]{:S(2)}) collective-permute-start(bf16[32,4096]{1,0:T(8,128)(2,1)S(1)} %get-tuple-element.26), channel_id=1, source_target_pairs={{0,32},{32,64},{64,96},{96,0},{1,33},{33,65},{65,97},{97,1},{2,34}... | collective-permute-start | bytes 786440 | tf_op jit(solution)/shard_map/ppermute | solution.py:157
  18.6 11.8 %collective-permute-start.2 = (bf16[32,4096]{1,0:T(8,128)(2,1)S(1)}, bf16[32,4096]{1,0:T(8,128)(2,1)S(1)}, u32[]{:S(2)}, u32[]{:S(2)}) collective-permute-start(bf16[32,4096]{1,0:T(8,128)(2,1)S(1)} %get-tuple-element.26), channel_id=1, source_target_pairs={{0,64},{32,96},{64,0},{96,32},{1,65},{33,97},{65,1},{97,33},{2,66}... | collective-permute-start | bytes 786440 | tf_op jit(solution)/shard_map/ppermute | solution.py:157
  22.8 14.7 %collective-permute-start.5 = (bf16[32,4096]{1,0:T(8,128)(2,1)S(1)}, bf16[32,4096]{1,0:T(8,128)(2,1)S(1)}, u32[]{:S(2)}, u32[]{:S(2)}) collective-permute-start(bf16[32,4096]{1,0:T(8,128)(2,1)S(1)} %get-tuple-element.30), channel_id=1, source_target_pairs={{0,96},{32,0},{64,32},{96,64},{1,97},{33,1},{65,33},{97,65},{2,98}... | collective-permute-start | bytes 786440 | tf_op jit(solution)/shard_map/ppermute | solution.py:157
  25.1 14.7 %collective-permute-start.4 = (bf16[32,4096]{1,0:T(8,128)(2,1)S(1)}, bf16[32,4096]{1,0:T(8,128)(2,1)S(1)}, u32[]{:S(2)}, u32[]{:S(2)}) collective-permute-start(bf16[32,4096]{1,0:T(8,128)(2,1)S(1)} %get-tuple-element.30), channel_id=1, source_target_pairs={{0,32},{32,64},{64,96},{96,0},{1,33},{33,65},{65,97},{97,1},{2,34}... | collective-permute-start | bytes 786440 | tf_op jit(solution)/shard_map/ppermute | solution.py:157
  25.1 14.7 %collective-permute-start.6 = (bf16[32,4096]{1,0:T(8,128)(2,1)S(1)}, bf16[32,4096]{1,0:T(8,128)(2,1)S(1)}, u32[]{:S(2)}, u32[]{:S(2)}) collective-permute-start(bf16[32,4096]{1,0:T(8,128)(2,1)S(1)} %get-tuple-element.30), channel_id=1, source_target_pairs={{0,64},{32,96},{64,0},{96,32},{1,65},{33,97},{65,1},{97,33},{2,66}... | collective-permute-start | bytes 786440 | tf_op jit(solution)/shard_map/ppermute | solution.py:157
  30.6 16.3 %collective-permute-start.15 = (bf16[32,4096]{1,0:T(8,128)(2,1)S(1)}, bf16[32,4096]{1,0:T(8,128)(2,1)S(1)}, u32[]{:S(2)}, u32[]{:S(2)}) collective-permute-start(bf16[32,4096]{1,0:T(8,128)(2,1)S(1)} %get-tuple-element.29), channel_id=1, source_target_pairs={{0,3},{1,0},{2,1},{3,2},{4,7},{5,4},{6,5},{7,6},{8,11},{9,8},{10,9... | collective-permute-start | bytes 786440 | tf_op jit(solution)/shard_map/ppermute | solution.py:157
  37.5 11.3 %collective-permute-start.14 = (bf16[32,4096]{1,0:T(8,128)(2,1)S(1)}, bf16[32,4096]{1,0:T(8,128)(2,1)S(1)}, u32[]{:S(2)}, u32[]{:S(2)}) collective-permute-start(bf16[32,4096]{1,0:T(8,128)(2,1)S(1)} %get-tuple-element.29), channel_id=1, source_target_pairs={{0,1},{1,2},{2,3},{3,0},{4,5},{5,6},{6,7},{7,4},{8,9},{9,10},{10,1... | collective-permute-start | bytes 786440 | tf_op jit(solution)/shard_map/ppermute | solution.py:157
  37.5 13.1 %collective-permute-start.16 = (bf16[32,4096]{1,0:T(8,128)(2,1)S(1)}, bf16[32,4096]{1,0:T(8,128)(2,1)S(1)}, u32[]{:S(2)}, u32[]{:S(2)}) collective-permute-start(bf16[32,4096]{1,0:T(8,128)(2,1)S(1)} %get-tuple-element.29), channel_id=1, source_target_pairs={{0,2},{1,3},{2,0},{3,1},{4,6},{5,7},{6,4},{7,5},{8,10},{9,11},{10,... | collective-permute-start | bytes 786440 | tf_op jit(solution)/shard_map/ppermute | solution.py:157
  40.2 51.2 %collective-permute-start.8 = (bf16[2,4,32,4096]{3,2,1,0:T(8,128)(2,1)S(1)}, bf16[2,4,32,4096]{3,2,1,0:T(8,128)(2,1)S(1)}, u32[]{:S(2)}, u32[]{:S(2)}) collective-permute-start(bf16[2,4,32,4096]{3,2,1,0:T(8,128)(2,1)S(1)} %pad_maximum_fusion), channel_id=1, source_target_pairs={{0,3},{1,0},{2,1},{3,2},{4,7},{5,4},{6,5},{7,6},{8,11},{9,8},{10,9... | collective-permute-start | bytes 6291464 | tf_op jit(solution)/shard_map/ppermute | solution.py:157
  46.9 49.3 %collective-permute-start.7 = (bf16[2,4,32,4096]{3,2,1,0:T(8,128)(2,1)S(1)}, bf16[2,4,32,4096]{3,2,1,0:T(8,128)(2,1)S(1)}, u32[]{:S(2)}, u32[]{:S(2)}) collective-permute-start(bf16[2,4,32,4096]{3,2,1,0:T(8,128)(2,1)S(1)} %pad_maximum_fusion), channel_id=1, source_target_pairs={{0,1},{1,2},{2,3},{3,0},{4,5},{5,6},{6,7},{7,4},{8,9},{9,10},{10,1... | collective-permute-start | bytes 6291464 | tf_op jit(solution)/shard_map/ppermute | solution.py:157
  51.0 46.4 %collective-permute-start.18 = (bf16[2,4,32,4096]{3,2,1,0:T(8,128)(2,1)S(1)}, bf16[2,4,32,4096]{3,2,1,0:T(8,128)(2,1)S(1)}, u32[]{:S(2)}, u32[]{:S(2)}) collective-permute-start(bf16[2,4,32,4096]{3,2,1,0:T(8,128)(2,1)S(1)} %pad_maximum_fusion.1), channel_id=1, source_target_pairs={{0,96},{32,0},{64,32},{96,64},{1,97},{33,1},{65,33},{97,65},{2,98}... | collective-permute-start | bytes 6291464 | tf_op jit(solution)/shard_map/ppermute | solution.py:157
  52.2 46.4 %collective-permute-start.17 = (bf16[2,4,32,4096]{3,2,1,0:T(8,128)(2,1)S(1)}, bf16[2,4,32,4096]{3,2,1,0:T(8,128)(2,1)S(1)}, u32[]{:S(2)}, u32[]{:S(2)}) collective-permute-start(bf16[2,4,32,4096]{3,2,1,0:T(8,128)(2,1)S(1)} %pad_maximum_fusion.1), channel_id=1, source_target_pairs={{0,32},{32,64},{64,96},{96,0},{1,33},{33,65},{65,97},{97,1},{2,34}... | collective-permute-start | bytes 6291464 | tf_op jit(solution)/shard_map/ppermute | solution.py:157
  92.5 25.1 %collective-permute-start.10 = (bf16[1,4,32,4096]{3,2,1,0:T(8,128)(2,1)}, bf16[1,4,32,4096]{3,2,1,0:T(8,128)(2,1)S(1)}, u32[]{:S(2)}, u32[]{:S(2)}) collective-permute-start(bf16[1,4,32,4096]{3,2,1,0:T(8,128)(2,1)} %slice.132), channel_id=1, source_target_pairs={{0,3},{1,0},{2,1},{3,2},{4,7},{5,4},{6,5},{7,6},{8,11},{9,8},{10,9... | collective-permute-start | bytes 3145736 | tf_op jit(solution)/shard_map/ppermute | solution.py:157
  97.3 24.8 %collective-permute-start.9 = (bf16[1,4,32,4096]{3,2,1,0:T(8,128)(2,1)}, bf16[1,4,32,4096]{3,2,1,0:T(8,128)(2,1)S(1)}, u32[]{:S(2)}, u32[]{:S(2)}) collective-permute-start(bf16[1,4,32,4096]{3,2,1,0:T(8,128)(2,1)} %slice.131), channel_id=1, source_target_pairs={{0,1},{1,2},{2,3},{3,0},{4,5},{5,6},{6,7},{7,4},{8,9},{9,10},{10,1... | collective-permute-start | bytes 3145736 | tf_op jit(solution)/shard_map/ppermute | solution.py:157
  98.7 23.5 %collective-permute-start.20 = (bf16[1,4,32,4096]{3,2,1,0:T(8,128)(2,1)}, bf16[1,4,32,4096]{3,2,1,0:T(8,128)(2,1)S(1)}, u32[]{:S(2)}, u32[]{:S(2)}) collective-permute-start(bf16[1,4,32,4096]{3,2,1,0:T(8,128)(2,1)} %slice.136), channel_id=1, source_target_pairs={{0,96},{32,0},{64,32},{96,64},{1,97},{33,1},{65,33},{97,65},{2,98}... | collective-permute-start | bytes 3145736 | tf_op jit(solution)/shard_map/ppermute | solution.py:157
  100.8 24.8 %collective-permute-start.19 = (bf16[1,4,32,4096]{3,2,1,0:T(8,128)(2,1)}, bf16[1,4,32,4096]{3,2,1,0:T(8,128)(2,1)}, u32[]{:S(2)}, u32[]{:S(2)}) collective-permute-start(bf16[1,4,32,4096]{3,2,1,0:T(8,128)(2,1)} %slice.135), channel_id=1, source_target_pairs={{0,32},{32,64},{64,96},{96,0},{1,33},{33,65},{65,97},{97,1},{2,34}... | collective-permute-start | bytes 3145736 | tf_op jit(solution)/shard_map/ppermute | solution.py:157
  144.5 4.5 %collective-permute-start.21 = (bf16[2,4,1024,128]{3,2,1,0:T(8,128)(2,1)}, bf16[2,4,1024,128]{3,2,1,0:T(8,128)(2,1)S(1)}, u32[]{:S(2)}, u32[]{:S(2)}) collective-permute-start(bf16[2,4,1024,128]{3,2,1,0:T(8,128)(2,1)} %get-tuple-element.13), channel_id=1, source_target_pairs={{0,4},{4,0},{1,5},{5,1},{2,6},{6,2},{3,7},{7,3},{8,12},{12,8},{9,1... | collective-permute-start | bytes 6291464 | tf_op jit(solution)/shard_map/ppermute | solution.py:152
  149.0 4.4 %collective-permute-start.22 = (bf16[4,2,1024,128]{3,2,1,0:T(8,128)(2,1)}, bf16[4,2,1024,128]{3,2,1,0:T(8,128)(2,1)S(1)}, u32[]{:S(2)}, u32[]{:S(2)}) collective-permute-start(bf16[4,2,1024,128]{3,2,1,0:T(8,128)(2,1)} %get-tuple-element.14), channel_id=1, source_target_pairs={{0,4},{4,0},{1,5},{5,1},{2,6},{6,2},{3,7},{7,3},{8,12},{12,8},{9,1... | collective-permute-start | bytes 6291464 | tf_op jit(solution)/shard_map/ppermute | solution.py:152
  150.6 25.7 %collective-permute-start.27 = (bf16[4,1024,128]{2,1,0:T(8,128)(2,1)S(1)}, bf16[4,1024,128]{2,1,0:T(8,128)(2,1)S(1)}, u32[]{:S(2)}, u32[]{:S(2)}) collective-permute-start(bf16[4,1024,128]{2,1,0:T(8,128)(2,1)S(1)} %fusion.2), channel_id=1, source_target_pairs={{0,8},{8,0},{1,9},{9,1},{2,10},{10,2},{3,11},{11,3},{4,12},{12,4},... | collective-permute-start | bytes 3145736 | tf_op jit(solution)/shard_map/ppermute | solution.py:152
  153.7 31.0 %collective-permute-start.23 = (bf16[2,1024,128]{2,1,0:T(8,128)(2,1)S(1)}, bf16[2,1024,128]{2,1,0:T(8,128)(2,1)S(1)}, u32[]{:S(2)}, u32[]{:S(2)}) collective-permute-start(bf16[2,1024,128]{2,1,0:T(8,128)(2,1)S(1)} %get-tuple-element.20), channel_id=1, source_target_pairs={{0,1},{1,2},{2,3},{3,0},{4,5},{5,6},{6,7},{7,4},{8,9},{9,10},{10,1... | collective-permute-start | bytes 1572872 | tf_op jit(solution)/shard_map/ppermute | solution.py:157
  155.6 30.5 %collective-permute-start.25 = (bf16[2,1024,128]{2,1,0:T(8,128)(2,1)S(1)}, bf16[2,1024,128]{2,1,0:T(8,128)(2,1)S(1)}, u32[]{:S(2)}, u32[]{:S(2)}) collective-permute-start(bf16[2,1024,128]{2,1,0:T(8,128)(2,1)S(1)} %get-tuple-element.21), channel_id=1, source_target_pairs={{0,3},{1,0},{2,1},{3,2},{4,7},{5,4},{6,5},{7,6},{8,11},{9,8},{10,9... | collective-permute-start | bytes 1572872 | tf_op jit(solution)/shard_map/ppermute | solution.py:157
  161.2 25.0 %collective-permute-start.24 = (bf16[2,1024,128]{2,1,0:T(8,128)(2,1)S(1)}, bf16[2,1024,128]{2,1,0:T(8,128)(2,1)S(1)}, u32[]{:S(2)}, u32[]{:S(2)}) collective-permute-start(bf16[2,1024,128]{2,1,0:T(8,128)(2,1)S(1)} %get-tuple-element.22), channel_id=1, source_target_pairs={{0,2},{1,3},{2,0},{3,1},{4,6},{5,7},{6,4},{7,5},{8,10},{9,11},{10,... | collective-permute-start | bytes 1572872 | tf_op jit(solution)/shard_map/ppermute | solution.py:157
  176.6 15.0 %collective-permute-start.28 = (bf16[1024,128]{1,0:T(8,128)(2,1)S(1)}, bf16[1024,128]{1,0:T(8,128)(2,1)S(1)}, u32[]{:S(2)}, u32[]{:S(2)}) collective-permute-start(bf16[1024,128]{1,0:T(8,128)(2,1)S(1)} %get-tuple-element.17), channel_id=1, source_target_pairs={{0,1},{1,2},{2,3},{3,0},{4,5},{5,6},{6,7},{7,4},{8,9},{9,10},{10,1... | collective-permute-start | bytes 786440 | tf_op jit(solution)/shard_map/ppermute | solution.py:157
  179.0 16.9 %collective-permute-start.30 = (bf16[1024,128]{1,0:T(8,128)(2,1)S(1)}, bf16[1024,128]{1,0:T(8,128)(2,1)S(1)}, u32[]{:S(2)}, u32[]{:S(2)}) collective-permute-start(bf16[1024,128]{1,0:T(8,128)(2,1)S(1)} %get-tuple-element.18), channel_id=1, source_target_pairs={{0,3},{1,0},{2,1},{3,2},{4,7},{5,4},{6,5},{7,6},{8,11},{9,8},{10,9... | collective-permute-start | bytes 786440 | tf_op jit(solution)/shard_map/ppermute | solution.py:157
  184.7 13.0 %collective-permute-start.29 = (bf16[1024,128]{1,0:T(8,128)(2,1)S(1)}, bf16[1024,128]{1,0:T(8,128)(2,1)S(1)}, u32[]{:S(2)}, u32[]{:S(2)}) collective-permute-start(bf16[1024,128]{1,0:T(8,128)(2,1)S(1)} %get-tuple-element.19), channel_id=1, source_target_pairs={{0,2},{1,3},{2,0},{3,1},{4,6},{5,7},{6,4},{7,5},{8,10},{9,11},{10,... | collective-permute-start | bytes 786440 | tf_op jit(solution)/shard_map/ppermute | solution.py:157
  186.5 11.5 %collective-permute-start.26 = (bf16[1024,128]{1,0:T(8,128)(2,1)S(1)}, bf16[1024,128]{1,0:T(8,128)(2,1)S(1)}, u32[]{:S(2)}, u32[]{:S(2)}) collective-permute-start(bf16[1024,128]{1,0:T(8,128)(2,1)S(1)} %fusion.20), channel_id=1, source_target_pairs={{0,8},{8,0},{1,9},{9,1},{2,10},{10,2},{3,11},{11,3},{4,12},{12,4},... | collective-permute-start | bytes 786440 | tf_op jit(solution)/shard_map/ppermute | solution.py:152
  (14 other events, 139.5 us)

commit v8 on v7

--- a/solution.py
+++ b/solution.py
@@ -176,17 +176,31 @@
 
 
 def gather_sources(x):
+    half = x.shape[1] // 2
     other = swap(x, "ry")
-    half = x.shape[1] // 2
+    a_own, b_own = jnp.stack(ring(x[:, :half], "rz")), jnp.stack(ring(x[:, half:], "fx"))
+    a_own, b_own, other = tie((a_own, b_own, other))
+    a_near = shift(a_own, "fx", 1), shift(a_own, "fx", -1)
+    b_near = shift(b_own, "rz", 1), shift(b_own, "rz", -1)
+    a_other, b_other = jnp.stack(ring(other[:, :half], "rz")), jnp.stack(ring(other[:, half:], "fx"))
+    a_other, b_other, a_near, b_near = tie((a_other, b_other, a_near, b_near))
     parts = []
-    for first, one, two in ((0, "rz", "fx"), (half, "fx", "rz")):
-        lanes = slice(first, first + half)
-        value = jnp.stack([jnp.stack(ring(v[:, lanes], one)) for v in (x, other)])
-        before, after = shift(value, two, 1), shift(value, two, -1)
-        done = (value, before, after, shift(before[:1], two, 1), shift(after[1:], two, -1))
-        for far, ys, part in zip((0, -1, 1, 2, 2), ((0, 1), (0, 1), (0, 1), (0,), (1,)), done):
-            offsets = [(d, y, far) if two == "fx" else (far, y, d) for y in ys for d in STEPS]
-            parts.append((part.reshape(-1, *part.shape[2:]), first, offsets))
+    for own, other, near, axis, first in (
+        (a_own, a_other, a_near, "fx", 0),
+        (b_own, b_other, b_near, "rz", half),
+    ):
+        before, after = shift(other, axis, 1), shift(other, axis, -1)
+        for value, y, far in (
+            (own, 0, 0),
+            (other, 1, 0),
+            (near[0], 0, -1),
+            (near[1], 0, 1),
+            (before, 1, -1),
+            (after, 1, 1),
+            (shift(near[0], axis, 1), 0, 2),
+            (shift(after, axis, -1), 1, 2),
+        ):
+            parts.append((value, first, [(d, y, far) if axis == "fx" else (far, y, d) for d in STEPS]))
     return parts
 
 

time: 200 us -> 195 us (0.975)
  starting transfers between devices: 66.1 us -> 82 us
  waiting for transfers between devices: 99.8 us -> 88.1 us
  Pallas kernels: 18.8 us -> 12.7 us
  local copies, waits for them, and re-layouts: 7.52 us -> 2.02 us
    ppermute x26 -> x30, starting transfers between devices: 60.2 us -> 76.5 us  [shift(): return lax.ppermute(value, axis, [(i, (i + by) % n) for i in range(n)])]
    ppermute x5, waiting for transfers between devices: 20.6 us -> 12.4 us  [swap(): return lax.ppermute(value, axis, [(0, 1), (1, 0)])]
    pallas_call x1, Pallas kernels: 18.8 us -> 12.7 us  [aggregate(): pl.pallas_call(functools.partial(aggregate_kernel, where, len(arrays)), o...]
    slice x4 -> x0, local copies, waits for them, and re-layouts: 4.56 us -> none  [the longest x2 2.32 us: gather_sources(): after[1:]]
    ppermute x26 -> x30, waiting for transfers between devices: 79.2 us -> 75.7 us  [shift(): return lax.ppermute(value, axis, [(i, (i + by) % n) for i in range(n)])]
  transfers between devices with their start and end apart: 31 -> 35, of which waited for: 16 -> 15; matrix products, arithmetic and copies ran while one was open for 5% -> 3% of each run, Pallas kernels for 0% -> 0%
where the time goes in v8:
time: 195 us; the launch traced here: 193 us
  waiting for transfers between devices  88.1 us (45%)
  starting transfers between devices  82 us (42%)
  Pallas kernels  12.7 us (7%)
  other arithmetic  5.54 us (3%)
  local copies, waits for them, and re-layouts  2.02 us (1%)
    ppermute x30, starting transfers between devices, shift(): return lax.ppermute(value, axis, [(i, (i + by) % n) for i in range(n)])  76.5 us
    ppermute x30, waiting for transfers between devices, shift(): return lax.ppermute(value, axis, [(i, (i + by) % n) for i in range(n)])  75.7 us
    pallas_call x1, Pallas kernels, aggregate(): pl.pallas_call(functools.partial(aggregate_kernel, where, len(arrays)), o...  12.7 us
    ppermute x5, waiting for transfers between devices, swap(): return lax.ppermute(value, axis, [(0, 1), (1, 0)])  12.4 us
    ppermute x5, starting transfers between devices, swap(): return lax.ppermute(value, axis, [(0, 1), (1, 0)])  5.45 us
  transfers between devices with their start and end apart: 35, of which 15 were waited for; matrix products, arithmetic and copies ran while one was open for 3% of the time, Pallas kernels for 0%

profile of v8, /device:TPU:0, one launch (start us, length us, event | category | flops | bytes accessed | tf_op | source)
XLA Modules:
  0.0 192.7 jit_solution(7785141955106690701)
XLA Ops:
  1.2 2.9 %collective-permute-start.4 = (bf16[32,4096]{1,0:T(8,128)(2,1)S(1)}, bf16[32,4096]{1,0:T(8,128)(2,1)S(1)}, u32[]{:S(2)}, u32[]{:S(2)}) collective-permute-start(bf16[32,4096]{1,0:T(8,128)(2,1)S(1)} %get-tuple-element.47), channel_id=1, source_target_pairs={{0,3},{1,0},{2,1},{3,2},{4,7},{5,4},{6,5},{7,6},{8,11},{9,8},{10,9... | collective-permute-start | bytes 786440 | tf_op jit(solution)/shard_map/ppermute | solution.py:157
  4.1 2.3 %collective-permute-start.5 = (bf16[32,4096]{1,0:T(8,128)(2,1)S(1)}, bf16[32,4096]{1,0:T(8,128)(2,1)S(1)}, u32[]{:S(2)}, u32[]{:S(2)}) collective-permute-start(bf16[32,4096]{1,0:T(8,128)(2,1)S(1)} %get-tuple-element.47), channel_id=1, source_target_pairs={{0,2},{1,3},{2,0},{3,1},{4,6},{5,7},{6,4},{7,5},{8,10},{9,11},{10,... | collective-permute-start | bytes 786440 | tf_op jit(solution)/shard_map/ppermute | solution.py:157
  6.4 3.2 %collective-permute-start.6 = (bf16[32,8192]{1,0:T(8,128)(2,1)}, bf16[32,8192]{1,0:T(8,128)(2,1)S(1)}, u32[]{:S(2)}, u32[]{:S(2)}) collective-permute-start(bf16[32,8192]{1,0:T(8,128)(2,1)} %bitcast.82), channel_id=1, source_target_pairs={{0,16},{16,0},{1,17},{17,1},{2,18},{18,2},{3,19},{19,3},{4,20},{20... | collective-permute-start | bytes 1572872 | tf_op jit(solution)/shard_map/ppermute | solution.py:152
  9.6 4.0 %collective-permute-start.1 = (bf16[32,4096]{1,0:T(8,128)(2,1)S(1)}, bf16[32,4096]{1,0:T(8,128)(2,1)S(1)}, u32[]{:S(2)}, u32[]{:S(2)}) collective-permute-start(bf16[32,4096]{1,0:T(8,128)(2,1)S(1)} %get-tuple-element.48), channel_id=1, source_target_pairs={{0,96},{32,0},{64,32},{96,64},{1,97},{33,1},{65,33},{97,65},{2,98}... | collective-permute-start | bytes 786440 | tf_op jit(solution)/shard_map/ppermute | solution.py:157
  13.6 1.7 collective-permute-done.4
  15.3 1.9 %collective-permute-start = (bf16[32,4096]{1,0:T(8,128)(2,1)S(1)}, bf16[32,4096]{1,0:T(8,128)(2,1)S(1)}, u32[]{:S(2)}, u32[]{:S(2)}) collective-permute-start(bf16[32,4096]{1,0:T(8,128)(2,1)S(1)} %get-tuple-element.48), channel_id=1, source_target_pairs={{0,32},{32,64},{64,96},{96,0},{1,33},{33,65},{65,97},{97,1},{2,34}... | collective-permute-start | bytes 786440 | tf_op jit(solution)/shard_map/ppermute | solution.py:157
  18.7 3.9 %collective-permute-start.2 = (bf16[32,4096]{1,0:T(8,128)(2,1)S(1)}, bf16[32,4096]{1,0:T(8,128)(2,1)S(1)}, u32[]{:S(2)}, u32[]{:S(2)}) collective-permute-start(bf16[32,4096]{1,0:T(8,128)(2,1)S(1)} %get-tuple-element.48), channel_id=1, source_target_pairs={{0,64},{32,96},{64,0},{96,32},{1,65},{33,97},{65,1},{97,33},{2,66}... | collective-permute-start | bytes 786440 | tf_op jit(solution)/shard_map/ppermute | solution.py:157
  22.7 1.6 collective-permute-done
  24.3 3.7 %collective-permute-done.2 = bf16[32,4096]{1,0:T(8,128)(2,1)S(1)} collective-permute-done((bf16[32,4096]{1,0:T(8,128)(2,1)S(1)}, bf16[32,4096]{1,0:T(8,128)(2,1)S(1)}, u32[]{:S(2)}, u32[]{:S(2)}) %collective-permute-start.2) | collective-permute-done | bytes 262176 | tf_op jit(solution)/shard_map/ppermute | solution.py:157
  28.2 7.3 %collective-permute-start.11 = (bf16[32,4096]{1,0:T(8,128)(2,1)S(1)}, bf16[32,4096]{1,0:T(8,128)(2,1)S(1)}, u32[]{:S(2)}, u32[]{:S(2)}) collective-permute-start(bf16[32,4096]{1,0:T(8,128)(2,1)S(1)} %get-tuple-element.43), channel_id=1, source_target_pairs={{0,3},{1,0},{2,1},{3,2},{4,7},{5,4},{6,5},{7,6},{8,11},{9,8},{10,9... | collective-permute-start | bytes 786440 | tf_op jit(solution)/shard_map/ppermute | solution.py:157
  37.1 2.0 %collective-permute-start.7 = (bf16[32,4096]{1,0:T(8,128)(2,1)S(1)}, bf16[32,4096]{1,0:T(8,128)(2,1)S(1)}, u32[]{:S(2)}, u32[]{:S(2)}) collective-permute-start(bf16[32,4096]{1,0:T(8,128)(2,1)S(1)} %get-tuple-element.44), channel_id=1, source_target_pairs={{0,32},{32,64},{64,96},{96,0},{1,33},{33,65},{65,97},{97,1},{2,34}... | collective-permute-start | bytes 786440 | tf_op jit(solution)/shard_map/ppermute | solution.py:157
  39.1 7.8 %collective-permute-done.11 = bf16[32,4096]{1,0:T(8,128)(2,1)S(1)} collective-permute-done((bf16[32,4096]{1,0:T(8,128)(2,1)S(1)}, bf16[32,4096]{1,0:T(8,128)(2,1)S(1)}, u32[]{:S(2)}, u32[]{:S(2)}) %collective-permute-start.11) | collective-permute-done | bytes 262176 | tf_op jit(solution)/shard_map/ppermute | solution.py:157
  47.0 3.8 %collective-permute-start.14 = (bf16[4,32,4096]{2,1,0:T(8,128)(2,1)S(1)}, bf16[4,32,4096]{2,1,0:T(8,128)(2,1)S(1)}, u32[]{:S(2)}, u32[]{:S(2)}) collective-permute-start(bf16[4,32,4096]{2,1,0:T(8,128)(2,1)S(1)} %pad_maximum_fusion.refs_0_), channel_id=1, source_target_pairs={{0,3},{1,0},{2,1},{3,2},{4,7},{5,4},{6,5},{7,6},{8,11},{9,8},{10,9... | collective-permute-start | bytes 3145736 | tf_op jit(solution)/shard_map/ppermute | solution.py:157
  50.9 2.0 %collective-permute-start.15 = (bf16[4,32,4096]{2,1,0:T(8,128)(2,1)S(1)}, bf16[4,32,4096]{2,1,0:T(8,128)(2,1)}, u32[]{:S(2)}, u32[]{:S(2)}) collective-permute-start(bf16[4,32,4096]{2,1,0:T(8,128)(2,1)S(1)} %pad_maximum_fusion.1.refs_8_), channel_id=1, source_target_pairs={{0,32},{32,64},{64,96},{96,0},{1,33},{33,65},{65,97},{97,1},{2,34}... | collective-permute-start | bytes 3145736 | tf_op jit(solution)/shard_map/ppermute | solution.py:157
  53.2 20.9 %collective-permute-done.9 = bf16[32,4096]{1,0:T(8,128)(2,1)S(1)} collective-permute-done((bf16[32,4096]{1,0:T(8,128)(2,1)S(1)}, bf16[32,4096]{1,0:T(8,128)(2,1)S(1)}, u32[]{:S(2)}, u32[]{:S(2)}) %collective-permute-start.9) | collective-permute-done | bytes 262176 | tf_op jit(solution)/shard_map/ppermute | solution.py:157
  76.0 3.1 %collective-permute-start.18 = (bf16[4,32,4096]{2,1,0:T(8,128)(2,1)}, bf16[4,32,4096]{2,1,0:T(8,128)(2,1)S(1)}, u32[]{:S(2)}, u32[]{:S(2)}) collective-permute-start(bf16[4,32,4096]{2,1,0:T(8,128)(2,1)} %pad_maximum_fusion.2.refs_1_), channel_id=1, source_target_pairs={{0,3},{1,0},{2,1},{3,2},{4,7},{5,4},{6,5},{7,6},{8,11},{9,8},{10,9... | collective-permute-start | bytes 3145736 | tf_op jit(solution)/shard_map/ppermute | solution.py:157
  79.0 5.1 %collective-permute-start.22 = (bf16[4,32,4096]{2,1,0:T(8,128)(2,1)S(1)}, bf16[4,32,4096]{2,1,0:T(8,128)(2,1)}, u32[]{:S(2)}, u32[]{:S(2)}) collective-permute-start(bf16[4,32,4096]{2,1,0:T(8,128)(2,1)S(1)} %pad_maximum_fusion.3.refs_9_), channel_id=1, source_target_pairs={{0,96},{32,0},{64,32},{96,64},{1,97},{33,1},{65,33},{97,65},{2,98}... | collective-permute-start | bytes 3145736 | tf_op jit(solution)/shard_map/ppermute | solution.py:157
  84.1 19.0 %collective-permute-done.19.refs_6_ = bf16[4,32,4096]{2,1,0:T(8,128)(2,1)S(1)} collective-permute-done((bf16[4,32,4096]{2,1,0:T(8,128)(2,1)S(1)}, bf16[4,32,4096]{2,1,0:T(8,128)(2,1)S(1)}, u32[]{:S(2)}, u32[]{:S(2)}) %collective-permute-start.19) | collective-permute-done | bytes 1048608 | tf_op jit(solution)/shard_map/ppermute | solution.py:157
  103.1 1.6 collective-permute-start.23
  105.5 3.1 %collective-permute-start.24 = (bf16[4,32,4096]{2,1,0:T(8,128)(2,1)}, bf16[4,32,4096]{2,1,0:T(8,128)(2,1)}, u32[]{:S(2)}, u32[]{:S(2)}) collective-permute-start(bf16[4,32,4096]{2,1,0:T(8,128)(2,1)} %collective-permute-done.22.refs_13_), channel_id=1, source_target_pairs={{0,96},{32,0},{64,32},{96,64},{1,97},{33,1},{65,33},{97,65},{2,98}... | collective-permute-start | bytes 3145736 | tf_op jit(solution)/shard_map/ppermute | solution.py:157
  111.2 10.6 %collective-permute-done.23.refs_14_ = bf16[4,32,4096]{2,1,0:T(8,128)(2,1)} collective-permute-done((bf16[4,32,4096]{2,1,0:T(8,128)(2,1)}, bf16[4,32,4096]{2,1,0:T(8,128)(2,1)}, u32[]{:S(2)}, u32[]{:S(2)}) %collective-permute-start.23) | collective-permute-done | bytes 1048608 | tf_op jit(solution)/shard_map/ppermute | solution.py:157
  121.8 12.7 %aggregate.1 = (bf16[4,2,1024,128]{3,2,1,0:T(8,128)(2,1)}, bf16[2,4,1024,128]{3,2,1,0:T(8,128)(2,1)}, bf16[4,2,1024,128]{3,2,1,0:T(8,128)(2,1)}, bf16[2,4,1024,128]{3,2,1,0:T(8,128)(2,1)}) custom-call(s32[384]{0:T(512)} %reduce.rows_ref, s32[384]{0:T(512)} %reduce.1.cols_ref, s32[6]{0:T(128)} %stack.83.info_ref, bf16[384,128,128]{2,1,0:T(8,128)(2,1)} %bitcast.80, ...), custom_call_target="tpu_custom_call" | custom-call | tf_op jit(solution)/shard_map/aggregate/pallas_call | solution.py:125
  134.7 4.4 %collective-permute-done.25 = bf16[2,4,1024,128]{3,2,1,0:T(8,128)(2,1)S(1)} collective-permute-done((bf16[2,4,1024,128]{3,2,1,0:T(8,128)(2,1)}, bf16[2,4,1024,128]{3,2,1,0:T(8,128)(2,1)S(1)}, u32[]{:S(2)}, u32[]{:S(2)}) %collective-permute-start.25) | collective-permute-done | bytes 2097184 | tf_op jit(solution)/shard_map/ppermute | solution.py:152
  140.7 1.7 collective-permute-start.31
  143.8 13.2 %collective-permute-start.27 = (bf16[2,1024,128]{2,1,0:T(8,128)(2,1)S(1)}, bf16[2,1024,128]{2,1,0:T(8,128)(2,1)S(1)}, u32[]{:S(2)}, u32[]{:S(2)}) collective-permute-start(bf16[2,1024,128]{2,1,0:T(8,128)(2,1)S(1)} %get-tuple-element.38), channel_id=1, source_target_pairs={{0,1},{1,2},{2,3},{3,0},{4,5},{5,6},{6,7},{7,4},{8,9},{9,10},{10,1... | collective-permute-start | bytes 1572872 | tf_op jit(solution)/shard_map/ppermute | solution.py:157
  157.0 2.1 %collective-permute-start.28 = (bf16[2,1024,128]{2,1,0:T(8,128)(2,1)S(1)}, bf16[2,1024,128]{2,1,0:T(8,128)(2,1)S(1)}, u32[]{:S(2)}, u32[]{:S(2)}) collective-permute-start(bf16[2,1024,128]{2,1,0:T(8,128)(2,1)S(1)} %get-tuple-element.40), channel_id=1, source_target_pairs={{0,2},{1,3},{2,0},{3,1},{4,6},{5,7},{6,4},{7,5},{8,10},{9,11},{10,... | collective-permute-start | bytes 1572872 | tf_op jit(solution)/shard_map/ppermute | solution.py:157
  159.2 7.0 %collective-permute-done.31 = bf16[4,1024,128]{2,1,0:T(8,128)(2,1)S(1)} collective-permute-done((bf16[4,1024,128]{2,1,0:T(8,128)(2,1)S(1)}, bf16[4,1024,128]{2,1,0:T(8,128)(2,1)S(1)}, u32[]{:S(2)}, u32[]{:S(2)}) %collective-permute-start.31) | collective-permute-done | bytes 1048608 | tf_op jit(solution)/shard_map/ppermute | solution.py:152
  166.5 13.2 %collective-permute-start.32 = (bf16[1024,128]{1,0:T(8,128)(2,1)S(1)}, bf16[1024,128]{1,0:T(8,128)(2,1)S(1)}, u32[]{:S(2)}, u32[]{:S(2)}) collective-permute-start(bf16[1024,128]{1,0:T(8,128)(2,1)S(1)} %get-tuple-element.35), channel_id=1, source_target_pairs={{0,1},{1,2},{2,3},{3,0},{4,5},{5,6},{6,7},{7,4},{8,9},{9,10},{10,1... | collective-permute-start | bytes 786440 | tf_op jit(solution)/shard_map/ppermute | solution.py:157
  179.7 2.1 %collective-permute-start.33 = (bf16[1024,128]{1,0:T(8,128)(2,1)S(1)}, bf16[1024,128]{1,0:T(8,128)(2,1)S(1)}, u32[]{:S(2)}, u32[]{:S(2)}) collective-permute-start(bf16[1024,128]{1,0:T(8,128)(2,1)S(1)} %get-tuple-element.37), channel_id=1, source_target_pairs={{0,2},{1,3},{2,0},{3,1},{4,6},{5,7},{6,4},{7,5},{8,10},{9,11},{10,... | collective-permute-start | bytes 786440 | tf_op jit(solution)/shard_map/ppermute | solution.py:157
  182.6 3.9 %collective-permute-done.32 = bf16[1024,128]{1,0:T(8,128)(2,1)S(1)} collective-permute-done((bf16[1024,128]{1,0:T(8,128)(2,1)S(1)}, bf16[1024,128]{1,0:T(8,128)(2,1)S(1)}, u32[]{:S(2)}, u32[]{:S(2)}) %collective-permute-start.32) | collective-permute-done | bytes 262176 | tf_op jit(solution)/shard_map/ppermute | solution.py:157
  186.5 2.5 %collective-permute-done.34 = bf16[1024,128]{1,0:T(8,128)(2,1)S(1)} collective-permute-done((bf16[1024,128]{1,0:T(8,128)(2,1)S(1)}, bf16[1024,128]{1,0:T(8,128)(2,1)S(1)}, u32[]{:S(2)}, u32[]{:S(2)}) %collective-permute-start.34) | collective-permute-done | bytes 262176 | tf_op jit(solution)/shard_map/ppermute | solution.py:157
  188.9 2.0 %collective-permute-done.33 = bf16[1024,128]{1,0:T(8,128)(2,1)S(1)} collective-permute-done((bf16[1024,128]{1,0:T(8,128)(2,1)S(1)}, bf16[1024,128]{1,0:T(8,128)(2,1)S(1)}, u32[]{:S(2)}, u32[]{:S(2)}) %collective-permute-start.33) | collective-permute-done | bytes 262176 | tf_op jit(solution)/shard_map/ppermute | solution.py:157
  (84 shorter events, 15.3 us)
Async XLA Ops:
  1.2 14.1 %collective-permute-start.4 = (bf16[32,4096]{1,0:T(8,128)(2,1)S(1)}, bf16[32,4096]{1,0:T(8,128)(2,1)S(1)}, u32[]{:S(2)}, u32[]{:S(2)}) collective-permute-start(bf16[32,4096]{1,0:T(8,128)(2,1)S(1)} %get-tuple-element.47), channel_id=1, source_target_pairs={{0,3},{1,0},{2,1},{3,2},{4,7},{5,4},{6,5},{7,6},{8,11},{9,8},{10,9... | collective-permute-start | bytes 786440 | tf_op jit(solution)/shard_map/ppermute | solution.py:157
  4.1 14.6 %collective-permute-start.3 = (bf16[32,4096]{1,0:T(8,128)(2,1)S(1)}, bf16[32,4096]{1,0:T(8,128)(2,1)S(1)}, u32[]{:S(2)}, u32[]{:S(2)}) collective-permute-start(bf16[32,4096]{1,0:T(8,128)(2,1)S(1)} %get-tuple-element.47), channel_id=1, source_target_pairs={{0,1},{1,2},{2,3},{3,0},{4,5},{5,6},{6,7},{7,4},{8,9},{9,10},{10,1... | collective-permute-start | bytes 786440 | tf_op jit(solution)/shard_map/ppermute | solution.py:157
  4.1 18.5 %collective-permute-start.5 = (bf16[32,4096]{1,0:T(8,128)(2,1)S(1)}, bf16[32,4096]{1,0:T(8,128)(2,1)S(1)}, u32[]{:S(2)}, u32[]{:S(2)}) collective-permute-start(bf16[32,4096]{1,0:T(8,128)(2,1)S(1)} %get-tuple-element.47), channel_id=1, source_target_pairs={{0,2},{1,3},{2,0},{3,1},{4,6},{5,7},{6,4},{7,5},{8,10},{9,11},{10,... | collective-permute-start | bytes 786440 | tf_op jit(solution)/shard_map/ppermute | solution.py:157
  6.4 21.7 %collective-permute-start.6 = (bf16[32,8192]{1,0:T(8,128)(2,1)}, bf16[32,8192]{1,0:T(8,128)(2,1)S(1)}, u32[]{:S(2)}, u32[]{:S(2)}) collective-permute-start(bf16[32,8192]{1,0:T(8,128)(2,1)} %bitcast.82), channel_id=1, source_target_pairs={{0,16},{16,0},{1,17},{17,1},{2,18},{18,2},{3,19},{19,3},{4,20},{20... | collective-permute-start | bytes 1572872 | tf_op jit(solution)/shard_map/ppermute | solution.py:152
  9.6 13.1 %collective-permute-start.1 = (bf16[32,4096]{1,0:T(8,128)(2,1)S(1)}, bf16[32,4096]{1,0:T(8,128)(2,1)S(1)}, u32[]{:S(2)}, u32[]{:S(2)}) collective-permute-start(bf16[32,4096]{1,0:T(8,128)(2,1)S(1)} %get-tuple-element.48), channel_id=1, source_target_pairs={{0,96},{32,0},{64,32},{96,64},{1,97},{33,1},{65,33},{97,65},{2,98}... | collective-permute-start | bytes 786440 | tf_op jit(solution)/shard_map/ppermute | solution.py:157
  15.3 9.0 %collective-permute-start = (bf16[32,4096]{1,0:T(8,128)(2,1)S(1)}, bf16[32,4096]{1,0:T(8,128)(2,1)S(1)}, u32[]{:S(2)}, u32[]{:S(2)}) collective-permute-start(bf16[32,4096]{1,0:T(8,128)(2,1)S(1)} %get-tuple-element.48), channel_id=1, source_target_pairs={{0,32},{32,64},{64,96},{96,0},{1,33},{33,65},{65,97},{97,1},{2,34}... | collective-permute-start | bytes 786440 | tf_op jit(solution)/shard_map/ppermute | solution.py:157
  18.7 9.3 %collective-permute-start.2 = (bf16[32,4096]{1,0:T(8,128)(2,1)S(1)}, bf16[32,4096]{1,0:T(8,128)(2,1)S(1)}, u32[]{:S(2)}, u32[]{:S(2)}) collective-permute-start(bf16[32,4096]{1,0:T(8,128)(2,1)S(1)} %get-tuple-element.48), channel_id=1, source_target_pairs={{0,64},{32,96},{64,0},{96,32},{1,65},{33,97},{65,1},{97,33},{2,66}... | collective-permute-start | bytes 786440 | tf_op jit(solution)/shard_map/ppermute | solution.py:157
  28.2 18.8 %collective-permute-start.11 = (bf16[32,4096]{1,0:T(8,128)(2,1)S(1)}, bf16[32,4096]{1,0:T(8,128)(2,1)S(1)}, u32[]{:S(2)}, u32[]{:S(2)}) collective-permute-start(bf16[32,4096]{1,0:T(8,128)(2,1)S(1)} %get-tuple-element.43), channel_id=1, source_target_pairs={{0,3},{1,0},{2,1},{3,2},{4,7},{5,4},{6,5},{7,6},{8,11},{9,8},{10,9... | collective-permute-start | bytes 786440 | tf_op jit(solution)/shard_map/ppermute | solution.py:157
  35.6 15.2 %collective-permute-start.10 = (bf16[32,4096]{1,0:T(8,128)(2,1)S(1)}, bf16[32,4096]{1,0:T(8,128)(2,1)S(1)}, u32[]{:S(2)}, u32[]{:S(2)}) collective-permute-start(bf16[32,4096]{1,0:T(8,128)(2,1)S(1)} %get-tuple-element.43), channel_id=1, source_target_pairs={{0,1},{1,2},{2,3},{3,0},{4,5},{5,6},{6,7},{7,4},{8,9},{9,10},{10,1... | collective-permute-start | bytes 786440 | tf_op jit(solution)/shard_map/ppermute | solution.py:157
  35.6 15.3 %collective-permute-start.12 = (bf16[32,4096]{1,0:T(8,128)(2,1)S(1)}, bf16[32,4096]{1,0:T(8,128)(2,1)S(1)}, u32[]{:S(2)}, u32[]{:S(2)}) collective-permute-start(bf16[32,4096]{1,0:T(8,128)(2,1)S(1)} %get-tuple-element.43), channel_id=1, source_target_pairs={{0,2},{1,3},{2,0},{3,1},{4,6},{5,7},{6,4},{7,5},{8,10},{9,11},{10,... | collective-permute-start | bytes 786440 | tf_op jit(solution)/shard_map/ppermute | solution.py:157
  37.1 13.8 %collective-permute-start.8 = (bf16[32,4096]{1,0:T(8,128)(2,1)S(1)}, bf16[32,4096]{1,0:T(8,128)(2,1)S(1)}, u32[]{:S(2)}, u32[]{:S(2)}) collective-permute-start(bf16[32,4096]{1,0:T(8,128)(2,1)S(1)} %get-tuple-element.44), channel_id=1, source_target_pairs={{0,96},{32,0},{64,32},{96,64},{1,97},{33,1},{65,33},{97,65},{2,98}... | collective-permute-start | bytes 786440 | tf_op jit(solution)/shard_map/ppermute | solution.py:157
  37.1 15.8 %collective-permute-start.7 = (bf16[32,4096]{1,0:T(8,128)(2,1)S(1)}, bf16[32,4096]{1,0:T(8,128)(2,1)S(1)}, u32[]{:S(2)}, u32[]{:S(2)}) collective-permute-start(bf16[32,4096]{1,0:T(8,128)(2,1)S(1)} %get-tuple-element.44), channel_id=1, source_target_pairs={{0,32},{32,64},{64,96},{96,0},{1,33},{33,65},{65,97},{97,1},{2,34}... | collective-permute-start | bytes 786440 | tf_op jit(solution)/shard_map/ppermute | solution.py:157
  47.0 28.2 %collective-permute-start.14 = (bf16[4,32,4096]{2,1,0:T(8,128)(2,1)S(1)}, bf16[4,32,4096]{2,1,0:T(8,128)(2,1)S(1)}, u32[]{:S(2)}, u32[]{:S(2)}) collective-permute-start(bf16[4,32,4096]{2,1,0:T(8,128)(2,1)S(1)} %pad_maximum_fusion.refs_0_), channel_id=1, source_target_pairs={{0,3},{1,0},{2,1},{3,2},{4,7},{5,4},{6,5},{7,6},{8,11},{9,8},{10,9... | collective-permute-start | bytes 3145736 | tf_op jit(solution)/shard_map/ppermute | solution.py:157
  50.8 24.4 %collective-permute-start.13 = (bf16[4,32,4096]{2,1,0:T(8,128)(2,1)S(1)}, bf16[4,32,4096]{2,1,0:T(8,128)(2,1)S(1)}, u32[]{:S(2)}, u32[]{:S(2)}) collective-permute-start(bf16[4,32,4096]{2,1,0:T(8,128)(2,1)S(1)} %pad_maximum_fusion.refs_0_), channel_id=1, source_target_pairs={{0,1},{1,2},{2,3},{3,0},{4,5},{5,6},{6,7},{7,4},{8,9},{9,10},{10,1... | collective-permute-start | bytes 3145736 | tf_op jit(solution)/shard_map/ppermute | solution.py:157
  50.8 24.4 %collective-permute-start.16 = (bf16[4,32,4096]{2,1,0:T(8,128)(2,1)S(1)}, bf16[4,32,4096]{2,1,0:T(8,128)(2,1)S(1)}, u32[]{:S(2)}, u32[]{:S(2)}) collective-permute-start(bf16[4,32,4096]{2,1,0:T(8,128)(2,1)S(1)} %pad_maximum_fusion.1.refs_8_), channel_id=1, source_target_pairs={{0,96},{32,0},{64,32},{96,64},{1,97},{33,1},{65,33},{97,65},{2,98}... | collective-permute-start | bytes 3145736 | tf_op jit(solution)/shard_map/ppermute | solution.py:157
  50.9 24.9 %collective-permute-start.15 = (bf16[4,32,4096]{2,1,0:T(8,128)(2,1)S(1)}, bf16[4,32,4096]{2,1,0:T(8,128)(2,1)}, u32[]{:S(2)}, u32[]{:S(2)}) collective-permute-start(bf16[4,32,4096]{2,1,0:T(8,128)(2,1)S(1)} %pad_maximum_fusion.1.refs_8_), channel_id=1, source_target_pairs={{0,32},{32,64},{64,96},{96,0},{1,33},{33,65},{65,97},{97,1},{2,34}... | collective-permute-start | bytes 3145736 | tf_op jit(solution)/shard_map/ppermute | solution.py:157
  52.9 21.2 %collective-permute-start.9 = (bf16[32,4096]{1,0:T(8,128)(2,1)S(1)}, bf16[32,4096]{1,0:T(8,128)(2,1)S(1)}, u32[]{:S(2)}, u32[]{:S(2)}) collective-permute-start(bf16[32,4096]{1,0:T(8,128)(2,1)S(1)} %get-tuple-element.44), channel_id=1, source_target_pairs={{0,64},{32,96},{64,0},{96,32},{1,65},{33,97},{65,1},{97,33},{2,66}... | collective-permute-start | bytes 786440 | tf_op jit(solution)/shard_map/ppermute | solution.py:157
  75.8 27.3 %collective-permute-start.19 = (bf16[4,32,4096]{2,1,0:T(8,128)(2,1)S(1)}, bf16[4,32,4096]{2,1,0:T(8,128)(2,1)S(1)}, u32[]{:S(2)}, u32[]{:S(2)}) collective-permute-start(bf16[4,32,4096]{2,1,0:T(8,128)(2,1)S(1)} %collective-permute-done.13.refs_2_), channel_id=1, source_target_pairs={{0,1},{1,2},{2,3},{3,0},{4,5},{5,6},{6,7},{7,4},{8,9},{9,10},{10,1... | collective-permute-start | bytes 3145736 | tf_op jit(solution)/shard_map/ppermute | solution.py:157
  76.0 28.8 %collective-permute-start.18 = (bf16[4,32,4096]{2,1,0:T(8,128)(2,1)}, bf16[4,32,4096]{2,1,0:T(8,128)(2,1)S(1)}, u32[]{:S(2)}, u32[]{:S(2)}) collective-permute-start(bf16[4,32,4096]{2,1,0:T(8,128)(2,1)} %pad_maximum_fusion.2.refs_1_), channel_id=1, source_target_pairs={{0,3},{1,0},{2,1},{3,2},{4,7},{5,4},{6,5},{7,6},{8,11},{9,8},{10,9... | collective-permute-start | bytes 3145736 | tf_op jit(solution)/shard_map/ppermute | solution.py:157
  79.0 26.5 %collective-permute-start.22 = (bf16[4,32,4096]{2,1,0:T(8,128)(2,1)S(1)}, bf16[4,32,4096]{2,1,0:T(8,128)(2,1)}, u32[]{:S(2)}, u32[]{:S(2)}) collective-permute-start(bf16[4,32,4096]{2,1,0:T(8,128)(2,1)S(1)} %pad_maximum_fusion.3.refs_9_), channel_id=1, source_target_pairs={{0,96},{32,0},{64,32},{96,64},{1,97},{33,1},{65,33},{97,65},{2,98}... | collective-permute-start | bytes 3145736 | tf_op jit(solution)/shard_map/ppermute | solution.py:157
  84.1 37.7 %collective-permute-start.17 = (bf16[4,32,4096]{2,1,0:T(8,128)(2,1)}, bf16[4,32,4096]{2,1,0:T(8,128)(2,1)}, u32[]{:S(2)}, u32[]{:S(2)}) collective-permute-start(bf16[4,32,4096]{2,1,0:T(8,128)(2,1)} %pad_maximum_fusion.2.refs_1_), channel_id=1, source_target_pairs={{0,1},{1,2},{2,3},{3,0},{4,5},{5,6},{6,7},{7,4},{8,9},{9,10},{10,1... | collective-permute-start | bytes 3145736 | tf_op jit(solution)/shard_map/ppermute | solution.py:157
  84.1 37.7 %collective-permute-start.21 = (bf16[4,32,4096]{2,1,0:T(8,128)(2,1)S(1)}, bf16[4,32,4096]{2,1,0:T(8,128)(2,1)}, u32[]{:S(2)}, u32[]{:S(2)}) collective-permute-start(bf16[4,32,4096]{2,1,0:T(8,128)(2,1)S(1)} %pad_maximum_fusion.3.refs_9_), channel_id=1, source_target_pairs={{0,32},{32,64},{64,96},{96,0},{1,33},{33,65},{65,97},{97,1},{2,34}... | collective-permute-start | bytes 3145736 | tf_op jit(solution)/shard_map/ppermute | solution.py:157
  103.1 18.7 %collective-permute-start.23 = (bf16[4,32,4096]{2,1,0:T(8,128)(2,1)}, bf16[4,32,4096]{2,1,0:T(8,128)(2,1)}, u32[]{:S(2)}, u32[]{:S(2)}) collective-permute-start(bf16[4,32,4096]{2,1,0:T(8,128)(2,1)} %collective-permute-done.15.refs_10_), channel_id=1, source_target_pairs={{0,32},{32,64},{64,96},{96,0},{1,33},{33,65},{65,97},{97,1},{2,34}... | collective-permute-start | bytes 3145736 | tf_op jit(solution)/shard_map/ppermute | solution.py:157
  104.7 17.1 %collective-permute-start.20 = (bf16[4,32,4096]{2,1,0:T(8,128)(2,1)S(1)}, bf16[4,32,4096]{2,1,0:T(8,128)(2,1)}, u32[]{:S(2)}, u32[]{:S(2)}) collective-permute-start(bf16[4,32,4096]{2,1,0:T(8,128)(2,1)S(1)} %collective-permute-done.18.refs_5_), channel_id=1, source_target_pairs={{0,3},{1,0},{2,1},{3,2},{4,7},{5,4},{6,5},{7,6},{8,11},{9,8},{10,9... | collective-permute-start | bytes 3145736 | tf_op jit(solution)/shard_map/ppermute | solution.py:157
  105.5 16.3 %collective-permute-start.24 = (bf16[4,32,4096]{2,1,0:T(8,128)(2,1)}, bf16[4,32,4096]{2,1,0:T(8,128)(2,1)}, u32[]{:S(2)}, u32[]{:S(2)}) collective-permute-start(bf16[4,32,4096]{2,1,0:T(8,128)(2,1)} %collective-permute-done.22.refs_13_), channel_id=1, source_target_pairs={{0,96},{32,0},{64,32},{96,64},{1,97},{33,1},{65,33},{97,65},{2,98}... | collective-permute-start | bytes 3145736 | tf_op jit(solution)/shard_map/ppermute | solution.py:157
  140.7 25.5 %collective-permute-start.31 = (bf16[4,1024,128]{2,1,0:T(8,128)(2,1)S(1)}, bf16[4,1024,128]{2,1,0:T(8,128)(2,1)S(1)}, u32[]{:S(2)}, u32[]{:S(2)}) collective-permute-start(bf16[4,1024,128]{2,1,0:T(8,128)(2,1)S(1)} %fusion.2), channel_id=1, source_target_pairs={{0,8},{8,0},{1,9},{9,1},{2,10},{10,2},{3,11},{11,3},{4,12},{12,4},... | collective-permute-start | bytes 3145736 | tf_op jit(solution)/shard_map/ppermute | solution.py:152
  143.8 35.9 %collective-permute-start.27 = (bf16[2,1024,128]{2,1,0:T(8,128)(2,1)S(1)}, bf16[2,1024,128]{2,1,0:T(8,128)(2,1)S(1)}, u32[]{:S(2)}, u32[]{:S(2)}) collective-permute-start(bf16[2,1024,128]{2,1,0:T(8,128)(2,1)S(1)} %get-tuple-element.38), channel_id=1, source_target_pairs={{0,1},{1,2},{2,3},{3,0},{4,5},{5,6},{6,7},{7,4},{8,9},{9,10},{10,1... | collective-permute-start | bytes 1572872 | tf_op jit(solution)/shard_map/ppermute | solution.py:157
  157.0 24.8 %collective-permute-start.29 = (bf16[2,1024,128]{2,1,0:T(8,128)(2,1)S(1)}, bf16[2,1024,128]{2,1,0:T(8,128)(2,1)S(1)}, u32[]{:S(2)}, u32[]{:S(2)}) collective-permute-start(bf16[2,1024,128]{2,1,0:T(8,128)(2,1)S(1)} %get-tuple-element.39), channel_id=1, source_target_pairs={{0,3},{1,0},{2,1},{3,2},{4,7},{5,4},{6,5},{7,6},{8,11},{9,8},{10,9... | collective-permute-start | bytes 1572872 | tf_op jit(solution)/shard_map/ppermute | solution.py:157
  157.0 24.8 %collective-permute-start.28 = (bf16[2,1024,128]{2,1,0:T(8,128)(2,1)S(1)}, bf16[2,1024,128]{2,1,0:T(8,128)(2,1)S(1)}, u32[]{:S(2)}, u32[]{:S(2)}) collective-permute-start(bf16[2,1024,128]{2,1,0:T(8,128)(2,1)S(1)} %get-tuple-element.40), channel_id=1, source_target_pairs={{0,2},{1,3},{2,0},{3,1},{4,6},{5,7},{6,4},{7,5},{8,10},{9,11},{10,... | collective-permute-start | bytes 1572872 | tf_op jit(solution)/shard_map/ppermute | solution.py:157
  166.5 20.0 %collective-permute-start.32 = (bf16[1024,128]{1,0:T(8,128)(2,1)S(1)}, bf16[1024,128]{1,0:T(8,128)(2,1)S(1)}, u32[]{:S(2)}, u32[]{:S(2)}) collective-permute-start(bf16[1024,128]{1,0:T(8,128)(2,1)S(1)} %get-tuple-element.35), channel_id=1, source_target_pairs={{0,1},{1,2},{2,3},{3,0},{4,5},{5,6},{6,7},{7,4},{8,9},{9,10},{10,1... | collective-permute-start | bytes 786440 | tf_op jit(solution)/shard_map/ppermute | solution.py:157
  179.7 9.2 %collective-permute-start.34 = (bf16[1024,128]{1,0:T(8,128)(2,1)S(1)}, bf16[1024,128]{1,0:T(8,128)(2,1)S(1)}, u32[]{:S(2)}, u32[]{:S(2)}) collective-permute-start(bf16[1024,128]{1,0:T(8,128)(2,1)S(1)} %get-tuple-element.36), channel_id=1, source_target_pairs={{0,3},{1,0},{2,1},{3,2},{4,7},{5,4},{6,5},{7,6},{8,11},{9,8},{10,9... | collective-permute-start | bytes 786440 | tf_op jit(solution)/shard_map/ppermute | solution.py:157
  179.7 11.3 %collective-permute-start.33 = (bf16[1024,128]{1,0:T(8,128)(2,1)S(1)}, bf16[1024,128]{1,0:T(8,128)(2,1)S(1)}, u32[]{:S(2)}, u32[]{:S(2)}) collective-permute-start(bf16[1024,128]{1,0:T(8,128)(2,1)S(1)} %get-tuple-element.37), channel_id=1, source_target_pairs={{0,2},{1,3},{2,0},{3,1},{4,6},{5,7},{6,4},{7,5},{8,10},{9,11},{10,... | collective-permute-start | bytes 786440 | tf_op jit(solution)/shard_map/ppermute | solution.py:157
  (17 other events, 642.3 us)

commit v9 on v8

--- a/solution.py
+++ b/solution.py
@@ -172,14 +172,16 @@
 
 
 def ring(value, axis):
-    return [value] + [shift(value, axis, -d) for d in STEPS[1:]]
+    before, after = (shift(value, axis, -d) for d in STEPS[1:3])
+    again, before, after = tie((value, before, after))
+    return [value, before, after, shift(again, axis, 2)]
 
 
 def gather_sources(x):
     half = x.shape[1] // 2
     other = swap(x, "ry")
     a_own, b_own = jnp.stack(ring(x[:, :half], "rz")), jnp.stack(ring(x[:, half:], "fx"))
-    a_own, b_own, other = tie((a_own, b_own, other))
+    a_own, b_own = tie((a_own, b_own))
     a_near = shift(a_own, "fx", 1), shift(a_own, "fx", -1)
     b_near = shift(b_own, "rz", 1), shift(b_own, "rz", -1)
     a_other, b_other = jnp.stack(ring(other[:, :half], "rz")), jnp.stack(ring(other[:, half:], "fx"))

time: 195 us -> 190 us (0.974); the launches traced: 193 us -> 190 us
  starting transfers between devices: 82 us -> 48.8 us
  waiting for transfers between devices: 88.1 us -> 107 us
  Pallas kernels: 12.7 us -> 24.1 us
    ppermute x30, starting transfers between devices: 76.5 us -> 44.5 us  [shift(): return lax.ppermute(value, axis, [(i, (i + by) % n) for i in range(n)])]
    ppermute x5, waiting for transfers between devices: 12.4 us -> 24.4 us  [swap(): return lax.ppermute(value, axis, [(0, 1), (1, 0)])]
    pallas_call x1, Pallas kernels: 12.7 us -> 24.1 us  [aggregate(): pl.pallas_call(functools.partial(aggregate_kernel, where, len(arrays)), o...]
    ppermute x30, waiting for transfers between devices: 75.7 us -> 83 us  [shift(): return lax.ppermute(value, axis, [(i, (i + by) % n) for i in range(n)])]
  transfers between devices with their start and end apart: 35 -> 35, of which waited for: 15 -> 17; matrix products, arithmetic and copies ran while one was open for 3% -> 4% of each run, Pallas kernels for 0% -> 0%
where the time goes in v9:
time: 190 us
  waiting for transfers between devices  107 us (56%)
  starting transfers between devices  48.8 us (26%)
  Pallas kernels  24.1 us (13%)
  other arithmetic  5.54 us (3%)
  local copies, waits for them, and re-layouts  1.99 us (1%)
    ppermute x30, waiting for transfers between devices, shift(): return lax.ppermute(value, axis, [(i, (i + by) % n) for i in range(n)])  83 us
    ppermute x30, starting transfers between devices, shift(): return lax.ppermute(value, axis, [(i, (i + by) % n) for i in range(n)])  44.5 us
    ppermute x5, waiting for transfers between devices, swap(): return lax.ppermute(value, axis, [(0, 1), (1, 0)])  24.4 us
    pallas_call x1, Pallas kernels, aggregate(): pl.pallas_call(functools.partial(aggregate_kernel, where, len(arrays)), o...  24.1 us
    ppermute x5, starting transfers between devices, swap(): return lax.ppermute(value, axis, [(0, 1), (1, 0)])  4.37 us
  transfers between devices with their start and end apart: 35, of which 17 were waited for; matrix products, arithmetic and copies ran while one was open for 4% of the time, Pallas kernels for 0%

profile of v9, /device:TPU:0, one launch (start us, length us, event | category | flops | bytes accessed | tf_op | source)
XLA Modules:
  0.0 190.2 jit_solution(6835565250194427177)
XLA Ops:
  0.0 3.3 %collective-permute-start.6 = (bf16[32,8192]{1,0:T(8,128)(2,1)}, bf16[32,8192]{1,0:T(8,128)(2,1)S(1)}, u32[]{:S(2)}, u32[]{:S(2)}) collective-permute-start(bf16[32,8192]{1,0:T(8,128)(2,1)} %bitcast.81), channel_id=1, source_target_pairs={{0,16},{16,0},{1,17},{17,1},{2,18},{18,2},{3,19},{19,3},{4,20},{20... | collective-permute-start | bytes 1572872 | tf_op jit(solution)/shard_map/ppermute | solution.py:152
  4.4 2.8 %collective-permute-start.4 = (bf16[32,4096]{1,0:T(8,128)(2,1)S(1)}, bf16[32,4096]{1,0:T(8,128)(2,1)S(1)}, u32[]{:S(2)}, u32[]{:S(2)}) collective-permute-start(bf16[32,4096]{1,0:T(8,128)(2,1)S(1)} %get-tuple-element.36), channel_id=1, source_target_pairs={{0,3},{1,0},{2,1},{3,2},{4,7},{5,4},{6,5},{7,6},{8,11},{9,8},{10,9... | collective-permute-start | bytes 786440 | tf_op jit(solution)/shard_map/ppermute | solution.py:157
  7.2 4.0 %collective-permute-start.1 = (bf16[32,4096]{1,0:T(8,128)(2,1)S(1)}, bf16[32,4096]{1,0:T(8,128)(2,1)S(1)}, u32[]{:S(2)}, u32[]{:S(2)}) collective-permute-start(bf16[32,4096]{1,0:T(8,128)(2,1)S(1)} %get-tuple-element.33), channel_id=1, source_target_pairs={{0,96},{32,0},{64,32},{96,64},{1,97},{33,1},{65,33},{97,65},{2,98}... | collective-permute-start | bytes 786440 | tf_op jit(solution)/shard_map/ppermute | solution.py:157
  12.5 3.4 %collective-permute-done.3 = bf16[32,4096]{1,0:T(8,128)(2,1)S(1)} collective-permute-done((bf16[32,4096]{1,0:T(8,128)(2,1)S(1)}, bf16[32,4096]{1,0:T(8,128)(2,1)S(1)}, u32[]{:S(2)}, u32[]{:S(2)}) %collective-permute-start.3) | collective-permute-done | bytes 262176 | tf_op jit(solution)/shard_map/ppermute | solution.py:157
  16.3 3.4 %collective-permute-done = bf16[32,4096]{1,0:T(8,128)(2,1)S(1)} collective-permute-done((bf16[32,4096]{1,0:T(8,128)(2,1)S(1)}, bf16[32,4096]{1,0:T(8,128)(2,1)S(1)}, u32[]{:S(2)}, u32[]{:S(2)}) %collective-permute-start) | collective-permute-done | bytes 262176 | tf_op jit(solution)/shard_map/ppermute | solution.py:157
  20.0 2.8 %collective-permute-start.11 = (bf16[32,4096]{1,0:T(8,128)(2,1)S(1)}, bf16[32,4096]{1,0:T(8,128)(2,1)S(1)}, u32[]{:S(2)}, u32[]{:S(2)}) collective-permute-start(bf16[32,4096]{1,0:T(8,128)(2,1)S(1)} %get-tuple-element.43), channel_id=1, source_target_pairs={{0,3},{1,0},{2,1},{3,2},{4,7},{5,4},{6,5},{7,6},{8,11},{9,8},{10,9... | collective-permute-start | bytes 786440 | tf_op jit(solution)/shard_map/ppermute | solution.py:157
  22.8 1.7 collective-permute-start.8
  24.6 2.5 %collective-permute-start.7 = (bf16[32,4096]{1,0:T(8,128)(2,1)S(1)}, bf16[32,4096]{1,0:T(8,128)(2,1)S(1)}, u32[]{:S(2)}, u32[]{:S(2)}) collective-permute-start(bf16[32,4096]{1,0:T(8,128)(2,1)S(1)} %get-tuple-element.40), channel_id=1, source_target_pairs={{0,32},{32,64},{64,96},{96,0},{1,33},{33,65},{65,97},{97,1},{2,34}... | collective-permute-start | bytes 786440 | tf_op jit(solution)/shard_map/ppermute | solution.py:157
  27.5 2.9 %collective-permute-done.10 = bf16[32,4096]{1,0:T(8,128)(2,1)S(1)} collective-permute-done((bf16[32,4096]{1,0:T(8,128)(2,1)S(1)}, bf16[32,4096]{1,0:T(8,128)(2,1)S(1)}, u32[]{:S(2)}, u32[]{:S(2)}) %collective-permute-start.10) | collective-permute-done | bytes 262176 | tf_op jit(solution)/shard_map/ppermute | solution.py:157
  30.6 1.8 collective-permute-start.14
  32.7 3.5 %collective-permute-start.16 = (bf16[4,32,4096]{2,1,0:T(8,128)(2,1)S(1)}, bf16[4,32,4096]{2,1,0:T(8,128)(2,1)S(1)}, u32[]{:S(2)}, u32[]{:S(2)}) collective-permute-start(bf16[4,32,4096]{2,1,0:T(8,128)(2,1)S(1)} %pad_maximum_fusion.1.refs_8_), channel_id=1, source_target_pairs={{0,96},{32,0},{64,32},{96,64},{1,97},{33,1},{65,33},{97,65},{2,98}... | collective-permute-start | bytes 3145736 | tf_op jit(solution)/shard_map/ppermute | solution.py:157
  36.2 5.0 %collective-permute-done.12 = bf16[32,4096]{1,0:T(8,128)(2,1)S(1)} collective-permute-done((bf16[32,4096]{1,0:T(8,128)(2,1)S(1)}, bf16[32,4096]{1,0:T(8,128)(2,1)S(1)}, u32[]{:S(2)}, u32[]{:S(2)}) %collective-permute-start.12) | collective-permute-done | bytes 262176 | tf_op jit(solution)/shard_map/ppermute | solution.py:157
  41.2 3.8 %collective-permute-start.9 = (bf16[32,4096]{1,0:T(8,128)(2,1)S(1)}, bf16[32,4096]{1,0:T(8,128)(2,1)S(1)}, u32[]{:S(2)}, u32[]{:S(2)}) collective-permute-start(bf16[32,4096]{1,0:T(8,128)(2,1)S(1)} %get-tuple-element.40), channel_id=1, source_target_pairs={{0,64},{32,96},{64,0},{96,32},{1,65},{33,97},{65,1},{97,33},{2,66}... | collective-permute-start | bytes 786440 | tf_op jit(solution)/shard_map/ppermute | solution.py:157
  45.1 20.2 %collective-permute-done.9 = bf16[32,4096]{1,0:T(8,128)(2,1)S(1)} collective-permute-done((bf16[32,4096]{1,0:T(8,128)(2,1)S(1)}, bf16[32,4096]{1,0:T(8,128)(2,1)S(1)}, u32[]{:S(2)}, u32[]{:S(2)}) %collective-permute-start.9) | collective-permute-done | bytes 262176 | tf_op jit(solution)/shard_map/ppermute | solution.py:157
  67.2 2.8 %collective-permute-start.18 = (bf16[4,32,4096]{2,1,0:T(8,128)(2,1)}, bf16[4,32,4096]{2,1,0:T(8,128)(2,1)S(1)}, u32[]{:S(2)}, u32[]{:S(2)}) collective-permute-start(bf16[4,32,4096]{2,1,0:T(8,128)(2,1)} %pad_maximum_fusion.2.refs_1_), channel_id=1, source_target_pairs={{0,3},{1,0},{2,1},{3,2},{4,7},{5,4},{6,5},{7,6},{8,11},{9,8},{10,9... | collective-permute-start | bytes 3145736 | tf_op jit(solution)/shard_map/ppermute | solution.py:157
  70.2 1.8 collective-permute-start.21
  72.0 22.0 %collective-permute-done.19.refs_6_ = bf16[4,32,4096]{2,1,0:T(8,128)(2,1)S(1)} collective-permute-done((bf16[4,32,4096]{2,1,0:T(8,128)(2,1)S(1)}, bf16[4,32,4096]{2,1,0:T(8,128)(2,1)S(1)}, u32[]{:S(2)}, u32[]{:S(2)}) %collective-permute-start.19) | collective-permute-done | bytes 1048608 | tf_op jit(solution)/shard_map/ppermute | solution.py:157
  94.1 1.8 collective-permute-start.20
  95.9 3.2 %collective-permute-start.24 = (bf16[4,32,4096]{2,1,0:T(8,128)(2,1)}, bf16[4,32,4096]{2,1,0:T(8,128)(2,1)}, u32[]{:S(2)}, u32[]{:S(2)}) collective-permute-start(bf16[4,32,4096]{2,1,0:T(8,128)(2,1)} %collective-permute-done.22.refs_13_), channel_id=1, source_target_pairs={{0,96},{32,0},{64,32},{96,64},{1,97},{33,1},{65,33},{97,65},{2,98}... | collective-permute-start | bytes 3145736 | tf_op jit(solution)/shard_map/ppermute | solution.py:157
  101.6 14.5 %collective-permute-done.23.refs_14_ = bf16[4,32,4096]{2,1,0:T(8,128)(2,1)} collective-permute-done((bf16[4,32,4096]{2,1,0:T(8,128)(2,1)}, bf16[4,32,4096]{2,1,0:T(8,128)(2,1)}, u32[]{:S(2)}, u32[]{:S(2)}) %collective-permute-start.23) | collective-permute-done | bytes 1048608 | tf_op jit(solution)/shard_map/ppermute | solution.py:157
  116.2 24.1 %aggregate.1 = (bf16[4,2,1024,128]{3,2,1,0:T(8,128)(2,1)}, bf16[2,4,1024,128]{3,2,1,0:T(8,128)(2,1)}, bf16[4,2,1024,128]{3,2,1,0:T(8,128)(2,1)}, bf16[2,4,1024,128]{3,2,1,0:T(8,128)(2,1)}) custom-call(s32[384]{0:T(512)} %reduce.rows_ref, s32[384]{0:T(512)} %reduce.1.cols_ref, s32[6]{0:T(128)} %stack.83.info_ref, bf16[384,128,128]{2,1,0:T(8,128)(2,1)} %bitcast.80, ...), custom_call_target="tpu_custom_call" | custom-call | tf_op jit(solution)/shard_map/aggregate/pallas_call | solution.py:125
  140.4 4.4 %collective-permute-done.25 = bf16[2,4,1024,128]{3,2,1,0:T(8,128)(2,1)S(1)} collective-permute-done((bf16[2,4,1024,128]{3,2,1,0:T(8,128)(2,1)}, bf16[2,4,1024,128]{3,2,1,0:T(8,128)(2,1)S(1)}, u32[]{:S(2)}, u32[]{:S(2)}) %collective-permute-start.25) | collective-permute-done | bytes 2097184 | tf_op jit(solution)/shard_map/ppermute | solution.py:152
  144.9 1.5 fusion.2
  146.5 2.6 %collective-permute-done.26 = bf16[4,2,1024,128]{3,2,1,0:T(8,128)(2,1)S(1)} collective-permute-done((bf16[4,2,1024,128]{3,2,1,0:T(8,128)(2,1)}, bf16[4,2,1024,128]{3,2,1,0:T(8,128)(2,1)S(1)}, u32[]{:S(2)}, u32[]{:S(2)}) %collective-permute-start.26) | collective-permute-done | bytes 2097184 | tf_op jit(solution)/shard_map/ppermute | solution.py:152
  149.6 3.2 %collective-permute-start.29 = (bf16[2,1024,128]{2,1,0:T(8,128)(2,1)S(1)}, bf16[2,1024,128]{2,1,0:T(8,128)(2,1)S(1)}, u32[]{:S(2)}, u32[]{:S(2)}) collective-permute-start(bf16[2,1024,128]{2,1,0:T(8,128)(2,1)S(1)} %get-tuple-element.61), channel_id=1, source_target_pairs={{0,3},{1,0},{2,1},{3,2},{4,7},{5,4},{6,5},{7,6},{8,11},{9,8},{10,9... | collective-permute-start | bytes 1572872 | tf_op jit(solution)/shard_map/ppermute | solution.py:157
  152.9 1.6 collective-permute-start.28
  154.5 17.4 %collective-permute-done.31 = bf16[4,1024,128]{2,1,0:T(8,128)(2,1)S(1)} collective-permute-done((bf16[4,1024,128]{2,1,0:T(8,128)(2,1)S(1)}, bf16[4,1024,128]{2,1,0:T(8,128)(2,1)S(1)}, u32[]{:S(2)}, u32[]{:S(2)}) %collective-permute-start.31) | collective-permute-done | bytes 1048608 | tf_op jit(solution)/shard_map/ppermute | solution.py:152
  172.3 3.2 %collective-permute-start.34 = (bf16[1024,128]{1,0:T(8,128)(2,1)S(1)}, bf16[1024,128]{1,0:T(8,128)(2,1)S(1)}, u32[]{:S(2)}, u32[]{:S(2)}) collective-permute-start(bf16[1024,128]{1,0:T(8,128)(2,1)S(1)} %get-tuple-element.58), channel_id=1, source_target_pairs={{0,3},{1,0},{2,1},{3,2},{4,7},{5,4},{6,5},{7,6},{8,11},{9,8},{10,9... | collective-permute-start | bytes 786440 | tf_op jit(solution)/shard_map/ppermute | solution.py:157
  175.6 2.4 %collective-permute-start.33 = (bf16[1024,128]{1,0:T(8,128)(2,1)S(1)}, bf16[1024,128]{1,0:T(8,128)(2,1)S(1)}, u32[]{:S(2)}, u32[]{:S(2)}) collective-permute-start(bf16[1024,128]{1,0:T(8,128)(2,1)S(1)} %get-tuple-element.59), channel_id=1, source_target_pairs={{0,2},{1,3},{2,0},{3,1},{4,6},{5,7},{6,4},{7,5},{8,10},{9,11},{10,... | collective-permute-start | bytes 786440 | tf_op jit(solution)/shard_map/ppermute | solution.py:157
  179.1 4.8 %collective-permute-done.32 = bf16[1024,128]{1,0:T(8,128)(2,1)S(1)} collective-permute-done((bf16[1024,128]{1,0:T(8,128)(2,1)S(1)}, bf16[1024,128]{1,0:T(8,128)(2,1)S(1)}, u32[]{:S(2)}, u32[]{:S(2)}) %collective-permute-start.32) | collective-permute-done | bytes 262176 | tf_op jit(solution)/shard_map/ppermute | solution.py:157
  183.9 2.7 %collective-permute-done.34 = bf16[1024,128]{1,0:T(8,128)(2,1)S(1)} collective-permute-done((bf16[1024,128]{1,0:T(8,128)(2,1)S(1)}, bf16[1024,128]{1,0:T(8,128)(2,1)S(1)}, u32[]{:S(2)}, u32[]{:S(2)}) %collective-permute-start.34) | collective-permute-done | bytes 262176 | tf_op jit(solution)/shard_map/ppermute | solution.py:157
  186.7 1.8 collective-permute-done.33
  (84 shorter events, 12.0 us)
Async XLA Ops:
  0.0 19.9 %collective-permute-start.6 = (bf16[32,8192]{1,0:T(8,128)(2,1)}, bf16[32,8192]{1,0:T(8,128)(2,1)S(1)}, u32[]{:S(2)}, u32[]{:S(2)}) collective-permute-start(bf16[32,8192]{1,0:T(8,128)(2,1)} %bitcast.81), channel_id=1, source_target_pairs={{0,16},{16,0},{1,17},{17,1},{2,18},{18,2},{3,19},{19,3},{4,20},{20... | collective-permute-start | bytes 1572872 | tf_op jit(solution)/shard_map/ppermute | solution.py:152
  4.4 8.1 %collective-permute-start.4 = (bf16[32,4096]{1,0:T(8,128)(2,1)S(1)}, bf16[32,4096]{1,0:T(8,128)(2,1)S(1)}, u32[]{:S(2)}, u32[]{:S(2)}) collective-permute-start(bf16[32,4096]{1,0:T(8,128)(2,1)S(1)} %get-tuple-element.36), channel_id=1, source_target_pairs={{0,3},{1,0},{2,1},{3,2},{4,7},{5,4},{6,5},{7,6},{8,11},{9,8},{10,9... | collective-permute-start | bytes 786440 | tf_op jit(solution)/shard_map/ppermute | solution.py:157
  7.2 8.7 %collective-permute-start.3 = (bf16[32,4096]{1,0:T(8,128)(2,1)S(1)}, bf16[32,4096]{1,0:T(8,128)(2,1)S(1)}, u32[]{:S(2)}, u32[]{:S(2)}) collective-permute-start(bf16[32,4096]{1,0:T(8,128)(2,1)S(1)} %get-tuple-element.36), channel_id=1, source_target_pairs={{0,1},{1,2},{2,3},{3,0},{4,5},{5,6},{6,7},{7,4},{8,9},{9,10},{10,1... | collective-permute-start | bytes 786440 | tf_op jit(solution)/shard_map/ppermute | solution.py:157
  7.2 9.0 %collective-permute-start.1 = (bf16[32,4096]{1,0:T(8,128)(2,1)S(1)}, bf16[32,4096]{1,0:T(8,128)(2,1)S(1)}, u32[]{:S(2)}, u32[]{:S(2)}) collective-permute-start(bf16[32,4096]{1,0:T(8,128)(2,1)S(1)} %get-tuple-element.33), channel_id=1, source_target_pairs={{0,96},{32,0},{64,32},{96,64},{1,97},{33,1},{65,33},{97,65},{2,98}... | collective-permute-start | bytes 786440 | tf_op jit(solution)/shard_map/ppermute | solution.py:157
  11.3 8.4 %collective-permute-start = (bf16[32,4096]{1,0:T(8,128)(2,1)S(1)}, bf16[32,4096]{1,0:T(8,128)(2,1)S(1)}, u32[]{:S(2)}, u32[]{:S(2)}) collective-permute-start(bf16[32,4096]{1,0:T(8,128)(2,1)S(1)} %get-tuple-element.33), channel_id=1, source_target_pairs={{0,32},{32,64},{64,96},{96,0},{1,33},{33,65},{65,97},{97,1},{2,34}... | collective-permute-start | bytes 786440 | tf_op jit(solution)/shard_map/ppermute | solution.py:157
  15.9 8.6 %collective-permute-start.5 = (bf16[32,4096]{1,0:T(8,128)(2,1)S(1)}, bf16[32,4096]{1,0:T(8,128)(2,1)S(1)}, u32[]{:S(2)}, u32[]{:S(2)}) collective-permute-start(bf16[32,4096]{1,0:T(8,128)(2,1)S(1)} %get-tuple-element.36), channel_id=1, source_target_pairs={{0,2},{1,3},{2,0},{3,1},{4,6},{5,7},{6,4},{7,5},{8,10},{9,11},{10,... | collective-permute-start | bytes 786440 | tf_op jit(solution)/shard_map/ppermute | solution.py:157
  19.7 10.7 %collective-permute-start.2 = (bf16[32,4096]{1,0:T(8,128)(2,1)S(1)}, bf16[32,4096]{1,0:T(8,128)(2,1)S(1)}, u32[]{:S(2)}, u32[]{:S(2)}) collective-permute-start(bf16[32,4096]{1,0:T(8,128)(2,1)S(1)} %get-tuple-element.33), channel_id=1, source_target_pairs={{0,64},{32,96},{64,0},{96,32},{1,65},{33,97},{65,1},{97,33},{2,66}... | collective-permute-start | bytes 786440 | tf_op jit(solution)/shard_map/ppermute | solution.py:157
  22.8 7.6 %collective-permute-start.10 = (bf16[32,4096]{1,0:T(8,128)(2,1)S(1)}, bf16[32,4096]{1,0:T(8,128)(2,1)S(1)}, u32[]{:S(2)}, u32[]{:S(2)}) collective-permute-start(bf16[32,4096]{1,0:T(8,128)(2,1)S(1)} %get-tuple-element.43), channel_id=1, source_target_pairs={{0,1},{1,2},{2,3},{3,0},{4,5},{5,6},{6,7},{7,4},{8,9},{9,10},{10,1... | collective-permute-start | bytes 786440 | tf_op jit(solution)/shard_map/ppermute | solution.py:157
  22.8 9.8 %collective-permute-start.8 = (bf16[32,4096]{1,0:T(8,128)(2,1)S(1)}, bf16[32,4096]{1,0:T(8,128)(2,1)S(1)}, u32[]{:S(2)}, u32[]{:S(2)}) collective-permute-start(bf16[32,4096]{1,0:T(8,128)(2,1)S(1)} %get-tuple-element.40), channel_id=1, source_target_pairs={{0,96},{32,0},{64,32},{96,64},{1,97},{33,1},{65,33},{97,65},{2,98}... | collective-permute-start | bytes 786440 | tf_op jit(solution)/shard_map/ppermute | solution.py:157
  24.6 11.6 %collective-permute-start.7 = (bf16[32,4096]{1,0:T(8,128)(2,1)S(1)}, bf16[32,4096]{1,0:T(8,128)(2,1)S(1)}, u32[]{:S(2)}, u32[]{:S(2)}) collective-permute-start(bf16[32,4096]{1,0:T(8,128)(2,1)S(1)} %get-tuple-element.40), channel_id=1, source_target_pairs={{0,32},{32,64},{64,96},{96,0},{1,33},{33,65},{65,97},{97,1},{2,34}... | collective-permute-start | bytes 786440 | tf_op jit(solution)/shard_map/ppermute | solution.py:157
  30.4 10.7 %collective-permute-start.12 = (bf16[32,4096]{1,0:T(8,128)(2,1)S(1)}, bf16[32,4096]{1,0:T(8,128)(2,1)S(1)}, u32[]{:S(2)}, u32[]{:S(2)}) collective-permute-start(bf16[32,4096]{1,0:T(8,128)(2,1)S(1)} %get-tuple-element.43), channel_id=1, source_target_pairs={{0,2},{1,3},{2,0},{3,1},{4,6},{5,7},{6,4},{7,5},{8,10},{9,11},{10,... | collective-permute-start | bytes 786440 | tf_op jit(solution)/shard_map/ppermute | solution.py:157
  30.6 35.9 %collective-permute-start.14 = (bf16[4,32,4096]{2,1,0:T(8,128)(2,1)S(1)}, bf16[4,32,4096]{2,1,0:T(8,128)(2,1)S(1)}, u32[]{:S(2)}, u32[]{:S(2)}) collective-permute-start(bf16[4,32,4096]{2,1,0:T(8,128)(2,1)S(1)} %pad_maximum_fusion.refs_0_), channel_id=1, source_target_pairs={{0,3},{1,0},{2,1},{3,2},{4,7},{5,4},{6,5},{7,6},{8,11},{9,8},{10,9... | collective-permute-start | bytes 3145736 | tf_op jit(solution)/shard_map/ppermute | solution.py:157
  32.4 34.1 %collective-permute-start.13 = (bf16[4,32,4096]{2,1,0:T(8,128)(2,1)S(1)}, bf16[4,32,4096]{2,1,0:T(8,128)(2,1)S(1)}, u32[]{:S(2)}, u32[]{:S(2)}) collective-permute-start(bf16[4,32,4096]{2,1,0:T(8,128)(2,1)S(1)} %pad_maximum_fusion.refs_0_), channel_id=1, source_target_pairs={{0,1},{1,2},{2,3},{3,0},{4,5},{5,6},{6,7},{7,4},{8,9},{9,10},{10,1... | collective-permute-start | bytes 3145736 | tf_op jit(solution)/shard_map/ppermute | solution.py:157
  32.7 33.8 %collective-permute-start.16 = (bf16[4,32,4096]{2,1,0:T(8,128)(2,1)S(1)}, bf16[4,32,4096]{2,1,0:T(8,128)(2,1)S(1)}, u32[]{:S(2)}, u32[]{:S(2)}) collective-permute-start(bf16[4,32,4096]{2,1,0:T(8,128)(2,1)S(1)} %pad_maximum_fusion.1.refs_8_), channel_id=1, source_target_pairs={{0,96},{32,0},{64,32},{96,64},{1,97},{33,1},{65,33},{97,65},{2,98}... | collective-permute-start | bytes 3145736 | tf_op jit(solution)/shard_map/ppermute | solution.py:157
  36.2 30.6 %collective-permute-start.15 = (bf16[4,32,4096]{2,1,0:T(8,128)(2,1)S(1)}, bf16[4,32,4096]{2,1,0:T(8,128)(2,1)}, u32[]{:S(2)}, u32[]{:S(2)}) collective-permute-start(bf16[4,32,4096]{2,1,0:T(8,128)(2,1)S(1)} %pad_maximum_fusion.1.refs_8_), channel_id=1, source_target_pairs={{0,32},{32,64},{64,96},{96,0},{1,33},{33,65},{65,97},{97,1},{2,34}... | collective-permute-start | bytes 3145736 | tf_op jit(solution)/shard_map/ppermute | solution.py:157
  41.2 24.2 %collective-permute-start.9 = (bf16[32,4096]{1,0:T(8,128)(2,1)S(1)}, bf16[32,4096]{1,0:T(8,128)(2,1)S(1)}, u32[]{:S(2)}, u32[]{:S(2)}) collective-permute-start(bf16[32,4096]{1,0:T(8,128)(2,1)S(1)} %get-tuple-element.40), channel_id=1, source_target_pairs={{0,64},{32,96},{64,0},{96,32},{1,65},{33,97},{65,1},{97,33},{2,66}... | collective-permute-start | bytes 786440 | tf_op jit(solution)/shard_map/ppermute | solution.py:157
  66.8 27.3 %collective-permute-start.19 = (bf16[4,32,4096]{2,1,0:T(8,128)(2,1)S(1)}, bf16[4,32,4096]{2,1,0:T(8,128)(2,1)S(1)}, u32[]{:S(2)}, u32[]{:S(2)}) collective-permute-start(bf16[4,32,4096]{2,1,0:T(8,128)(2,1)S(1)} %collective-permute-done.13.refs_2_), channel_id=1, source_target_pairs={{0,1},{1,2},{2,3},{3,0},{4,5},{5,6},{6,7},{7,4},{8,9},{9,10},{10,1... | collective-permute-start | bytes 3145736 | tf_op jit(solution)/shard_map/ppermute | solution.py:157
  67.2 26.9 %collective-permute-start.18 = (bf16[4,32,4096]{2,1,0:T(8,128)(2,1)}, bf16[4,32,4096]{2,1,0:T(8,128)(2,1)S(1)}, u32[]{:S(2)}, u32[]{:S(2)}) collective-permute-start(bf16[4,32,4096]{2,1,0:T(8,128)(2,1)} %pad_maximum_fusion.2.refs_1_), channel_id=1, source_target_pairs={{0,3},{1,0},{2,1},{3,2},{4,7},{5,4},{6,5},{7,6},{8,11},{9,8},{10,9... | collective-permute-start | bytes 3145736 | tf_op jit(solution)/shard_map/ppermute | solution.py:157
  70.0 25.9 %collective-permute-start.22 = (bf16[4,32,4096]{2,1,0:T(8,128)(2,1)S(1)}, bf16[4,32,4096]{2,1,0:T(8,128)(2,1)}, u32[]{:S(2)}, u32[]{:S(2)}) collective-permute-start(bf16[4,32,4096]{2,1,0:T(8,128)(2,1)S(1)} %pad_maximum_fusion.3.refs_9_), channel_id=1, source_target_pairs={{0,96},{32,0},{64,32},{96,64},{1,97},{33,1},{65,33},{97,65},{2,98}... | collective-permute-start | bytes 3145736 | tf_op jit(solution)/shard_map/ppermute | solution.py:157
  70.2 46.0 %collective-permute-start.17 = (bf16[4,32,4096]{2,1,0:T(8,128)(2,1)}, bf16[4,32,4096]{2,1,0:T(8,128)(2,1)}, u32[]{:S(2)}, u32[]{:S(2)}) collective-permute-start(bf16[4,32,4096]{2,1,0:T(8,128)(2,1)} %pad_maximum_fusion.2.refs_1_), channel_id=1, source_target_pairs={{0,1},{1,2},{2,3},{3,0},{4,5},{5,6},{6,7},{7,4},{8,9},{9,10},{10,1... | collective-permute-start | bytes 3145736 | tf_op jit(solution)/shard_map/ppermute | solution.py:157
  70.2 46.0 %collective-permute-start.21 = (bf16[4,32,4096]{2,1,0:T(8,128)(2,1)S(1)}, bf16[4,32,4096]{2,1,0:T(8,128)(2,1)}, u32[]{:S(2)}, u32[]{:S(2)}) collective-permute-start(bf16[4,32,4096]{2,1,0:T(8,128)(2,1)S(1)} %pad_maximum_fusion.3.refs_9_), channel_id=1, source_target_pairs={{0,32},{32,64},{64,96},{96,0},{1,33},{33,65},{65,97},{97,1},{2,34}... | collective-permute-start | bytes 3145736 | tf_op jit(solution)/shard_map/ppermute | solution.py:157
  94.1 22.1 %collective-permute-start.23 = (bf16[4,32,4096]{2,1,0:T(8,128)(2,1)}, bf16[4,32,4096]{2,1,0:T(8,128)(2,1)}, u32[]{:S(2)}, u32[]{:S(2)}) collective-permute-start(bf16[4,32,4096]{2,1,0:T(8,128)(2,1)} %collective-permute-done.15.refs_10_), channel_id=1, source_target_pairs={{0,32},{32,64},{64,96},{96,0},{1,33},{33,65},{65,97},{97,1},{2,34}... | collective-permute-start | bytes 3145736 | tf_op jit(solution)/shard_map/ppermute | solution.py:157
  94.1 22.1 %collective-permute-start.20 = (bf16[4,32,4096]{2,1,0:T(8,128)(2,1)S(1)}, bf16[4,32,4096]{2,1,0:T(8,128)(2,1)}, u32[]{:S(2)}, u32[]{:S(2)}) collective-permute-start(bf16[4,32,4096]{2,1,0:T(8,128)(2,1)S(1)} %collective-permute-done.18.refs_5_), channel_id=1, source_target_pairs={{0,3},{1,0},{2,1},{3,2},{4,7},{5,4},{6,5},{7,6},{8,11},{9,8},{10,9... | collective-permute-start | bytes 3145736 | tf_op jit(solution)/shard_map/ppermute | solution.py:157
  95.9 20.3 %collective-permute-start.24 = (bf16[4,32,4096]{2,1,0:T(8,128)(2,1)}, bf16[4,32,4096]{2,1,0:T(8,128)(2,1)}, u32[]{:S(2)}, u32[]{:S(2)}) collective-permute-start(bf16[4,32,4096]{2,1,0:T(8,128)(2,1)} %collective-permute-done.22.refs_13_), channel_id=1, source_target_pairs={{0,96},{32,0},{64,32},{96,64},{1,97},{33,1},{65,33},{97,65},{2,98}... | collective-permute-start | bytes 3145736 | tf_op jit(solution)/shard_map/ppermute | solution.py:157
  146.4 25.5 %collective-permute-start.31 = (bf16[4,1024,128]{2,1,0:T(8,128)(2,1)S(1)}, bf16[4,1024,128]{2,1,0:T(8,128)(2,1)S(1)}, u32[]{:S(2)}, u32[]{:S(2)}) collective-permute-start(bf16[4,1024,128]{2,1,0:T(8,128)(2,1)S(1)} %fusion.2), channel_id=1, source_target_pairs={{0,8},{8,0},{1,9},{9,1},{2,10},{10,2},{3,11},{11,3},{4,12},{12,4},... | collective-permute-start | bytes 3145736 | tf_op jit(solution)/shard_map/ppermute | solution.py:152
  149.6 26.0 %collective-permute-start.27 = (bf16[2,1024,128]{2,1,0:T(8,128)(2,1)S(1)}, bf16[2,1024,128]{2,1,0:T(8,128)(2,1)S(1)}, u32[]{:S(2)}, u32[]{:S(2)}) collective-permute-start(bf16[2,1024,128]{2,1,0:T(8,128)(2,1)S(1)} %get-tuple-element.60), channel_id=1, source_target_pairs={{0,1},{1,2},{2,3},{3,0},{4,5},{5,6},{6,7},{7,4},{8,9},{9,10},{10,1... | collective-permute-start | bytes 1572872 | tf_op jit(solution)/shard_map/ppermute | solution.py:157
  149.6 28.3 %collective-permute-start.29 = (bf16[2,1024,128]{2,1,0:T(8,128)(2,1)S(1)}, bf16[2,1024,128]{2,1,0:T(8,128)(2,1)S(1)}, u32[]{:S(2)}, u32[]{:S(2)}) collective-permute-start(bf16[2,1024,128]{2,1,0:T(8,128)(2,1)S(1)} %get-tuple-element.61), channel_id=1, source_target_pairs={{0,3},{1,0},{2,1},{3,2},{4,7},{5,4},{6,5},{7,6},{8,11},{9,8},{10,9... | collective-permute-start | bytes 1572872 | tf_op jit(solution)/shard_map/ppermute | solution.py:157
  152.9 25.1 %collective-permute-start.28 = (bf16[2,1024,128]{2,1,0:T(8,128)(2,1)S(1)}, bf16[2,1024,128]{2,1,0:T(8,128)(2,1)S(1)}, u32[]{:S(2)}, u32[]{:S(2)}) collective-permute-start(bf16[2,1024,128]{2,1,0:T(8,128)(2,1)S(1)} %get-tuple-element.62), channel_id=1, source_target_pairs={{0,2},{1,3},{2,0},{3,1},{4,6},{5,7},{6,4},{7,5},{8,10},{9,11},{10,... | collective-permute-start | bytes 1572872 | tf_op jit(solution)/shard_map/ppermute | solution.py:157
  172.2 11.7 %collective-permute-start.32 = (bf16[1024,128]{1,0:T(8,128)(2,1)S(1)}, bf16[1024,128]{1,0:T(8,128)(2,1)S(1)}, u32[]{:S(2)}, u32[]{:S(2)}) collective-permute-start(bf16[1024,128]{1,0:T(8,128)(2,1)S(1)} %get-tuple-element.57), channel_id=1, source_target_pairs={{0,1},{1,2},{2,3},{3,0},{4,5},{5,6},{6,7},{7,4},{8,9},{9,10},{10,1... | collective-permute-start | bytes 786440 | tf_op jit(solution)/shard_map/ppermute | solution.py:157
  172.3 14.3 %collective-permute-start.34 = (bf16[1024,128]{1,0:T(8,128)(2,1)S(1)}, bf16[1024,128]{1,0:T(8,128)(2,1)S(1)}, u32[]{:S(2)}, u32[]{:S(2)}) collective-permute-start(bf16[1024,128]{1,0:T(8,128)(2,1)S(1)} %get-tuple-element.58), channel_id=1, source_target_pairs={{0,3},{1,0},{2,1},{3,2},{4,7},{5,4},{6,5},{7,6},{8,11},{9,8},{10,9... | collective-permute-start | bytes 786440 | tf_op jit(solution)/shard_map/ppermute | solution.py:157
  175.6 12.9 %collective-permute-start.33 = (bf16[1024,128]{1,0:T(8,128)(2,1)S(1)}, bf16[1024,128]{1,0:T(8,128)(2,1)S(1)}, u32[]{:S(2)}, u32[]{:S(2)}) collective-permute-start(bf16[1024,128]{1,0:T(8,128)(2,1)S(1)} %get-tuple-element.59), channel_id=1, source_target_pairs={{0,2},{1,3},{2,0},{3,1},{4,6},{5,7},{6,4},{7,5},{8,10},{9,11},{10,... | collective-permute-start | bytes 786440 | tf_op jit(solution)/shard_map/ppermute | solution.py:157
  178.4 10.3 %collective-permute-start.30 = (bf16[1024,128]{1,0:T(8,128)(2,1)S(1)}, bf16[1024,128]{1,0:T(8,128)(2,1)S(1)}, u32[]{:S(2)}, u32[]{:S(2)}) collective-permute-start(bf16[1024,128]{1,0:T(8,128)(2,1)S(1)} %fusion.20), channel_id=1, source_target_pairs={{0,8},{8,0},{1,9},{9,1},{2,10},{10,2},{3,11},{11,3},{4,12},{12,4},... | collective-permute-start | bytes 786440 | tf_op jit(solution)/shard_map/ppermute | solution.py:152
  (17 other events, 621.0 us)

commit v10 on v9

--- a/solution.py
+++ b/solution.py
@@ -168,23 +168,28 @@
     return value.astype(jnp.bfloat16)
 
 
-STEPS = (0, -1, 1, 2)
+STEPS = (0, 1, -1, 2)
 
 
 def ring(value, axis):
-    before, after = (shift(value, axis, -d) for d in STEPS[1:3])
-    again, before, after = tie((value, before, after))
-    return [value, before, after, shift(again, axis, 2)]
+    after, before = (shift(value, axis, -d) for d in STEPS[1:3])
+    again, after, before = tie((value, after, before))
+    return jnp.stack([value, after, before, shift(again, axis, 2)])
+
+
+def ring_of_other(value, axis, own):
+    return jnp.concatenate([jnp.stack([value, shift(value, axis, -1)]), swap(own[2:], "ry")])
 
 
 def gather_sources(x):
     half = x.shape[1] // 2
     other = swap(x, "ry")
-    a_own, b_own = jnp.stack(ring(x[:, :half], "rz")), jnp.stack(ring(x[:, half:], "fx"))
+    a_own, b_own = ring(x[:, :half], "rz"), ring(x[:, half:], "fx")
     a_own, b_own = tie((a_own, b_own))
     a_near = shift(a_own, "fx", 1), shift(a_own, "fx", -1)
     b_near = shift(b_own, "rz", 1), shift(b_own, "rz", -1)
-    a_other, b_other = jnp.stack(ring(other[:, :half], "rz")), jnp.stack(ring(other[:, half:], "fx"))
+    a_other = ring_of_other(other[:, :half], "rz", a_own)
+    b_other = ring_of_other(other[:, half:], "fx", b_own)
     a_other, b_other, a_near, b_near = tie((a_other, b_other, a_near, b_near))
     parts = []
     for own, other, near, axis, first in (

time: 190 us -> 182 us (0.958)
  waiting for transfers between devices: 107 us -> 89.9 us
  starting transfers between devices: 48.8 us -> 62.1 us
  Pallas kernels: 24.1 us -> 18.9 us
    ppermute x30 -> x26, waiting for transfers between devices: 83 us -> 55.9 us  [shift(): return lax.ppermute(value, axis, [(i, (i + by) % n) for i in range(n)])]
    ppermute x5 -> x7, starting transfers between devices: 4.37 us -> 17.3 us  [swap(): return lax.ppermute(value, axis, [(0, 1), (1, 0)])]
    ppermute x5 -> x7, waiting for transfers between devices: 24.4 us -> 34.1 us  [swap(): return lax.ppermute(value, axis, [(0, 1), (1, 0)])]
    pallas_call x1, Pallas kernels: 24.1 us -> 18.9 us  [aggregate(): pl.pallas_call(functools.partial(aggregate_kernel, where, len(arrays)), o...]
    ppermute x30 -> x26, starting transfers between devices: 44.5 us -> 44.7 us  [shift(): return lax.ppermute(value, axis, [(i, (i + by) % n) for i in range(n)])]
  transfers between devices with their start and end apart: 35 -> 33, of which waited for: 17 -> 14; matrix products, arithmetic and copies ran while one was open for 4% -> 3% of each run, Pallas kernels for 0% -> 0%
where the time goes in v10:
time: 182 us; the launch traced here: 181 us
  waiting for transfers between devices  89.9 us (49%)
  starting transfers between devices  62.1 us (34%)
  Pallas kernels  18.9 us (10%)
  other arithmetic  5.44 us (3%)
  local copies, waits for them, and re-layouts  2.08 us (1%)
    ppermute x26, waiting for transfers between devices, shift(): return lax.ppermute(value, axis, [(i, (i + by) % n) for i in range(n)])  55.9 us
    ppermute x26, starting transfers between devices, shift(): return lax.ppermute(value, axis, [(i, (i + by) % n) for i in range(n)])  44.7 us
    ppermute x7, waiting for transfers between devices, swap(): return lax.ppermute(value, axis, [(0, 1), (1, 0)])  34.1 us
    pallas_call x1, Pallas kernels, aggregate(): pl.pallas_call(functools.partial(aggregate_kernel, where, len(arrays)), o...  18.9 us
    ppermute x7, starting transfers between devices, swap(): return lax.ppermute(value, axis, [(0, 1), (1, 0)])  17.3 us
  transfers between devices with their start and end apart: 33, of which 14 were waited for; matrix products, arithmetic and copies ran while one was open for 3% of the time, Pallas kernels for 0%

profile of v10, /device:TPU:0, one launch (start us, length us, event | category | flops | bytes accessed | tf_op | source)
XLA Modules:
  0.0 180.7 jit_solution(8406573244942784034)
XLA Ops:
  1.2 1.6 collective-permute-start.4
  2.8 1.7 collective-permute-start.3
  4.5 2.0 %collective-permute-start.1 = (bf16[32,4096]{1,0:T(8,128)(2,1)S(1)}, bf16[32,4096]{1,0:T(8,128)(2,1)S(1)}, u32[]{:S(2)}, u32[]{:S(2)}) collective-permute-start(bf16[32,4096]{1,0:T(8,128)(2,1)S(1)} %get-tuple-element.27), channel_id=1, source_target_pairs={{0,32},{32,64},{64,96},{96,0},{1,33},{33,65},{65,97},{97,1},{2,34}... | collective-permute-start | bytes 786440 | tf_op jit(solution)/shard_map/ppermute | solution.py:157
  6.5 2.1 %collective-permute-start = (bf16[32,4096]{1,0:T(8,128)(2,1)S(1)}, bf16[32,4096]{1,0:T(8,128)(2,1)S(1)}, u32[]{:S(2)}, u32[]{:S(2)}) collective-permute-start(bf16[32,4096]{1,0:T(8,128)(2,1)S(1)} %get-tuple-element.27), channel_id=1, source_target_pairs={{0,96},{32,0},{64,32},{96,64},{1,97},{33,1},{65,33},{97,65},{2,98}... | collective-permute-start | bytes 786440 | tf_op jit(solution)/shard_map/ppermute | solution.py:157
  8.6 1.8 collective-permute-done.4
  10.6 2.7 %collective-permute-start.5 = (bf16[32,4096]{1,0:T(8,128)(2,1)S(1)}, bf16[32,4096]{1,0:T(8,128)(2,1)S(1)}, u32[]{:S(2)}, u32[]{:S(2)}) collective-permute-start(bf16[32,4096]{1,0:T(8,128)(2,1)S(1)} %get-tuple-element.30), channel_id=1, source_target_pairs={{0,2},{1,3},{2,0},{3,1},{4,6},{5,7},{6,4},{7,5},{8,10},{9,11},{10,... | collective-permute-start | bytes 786440 | tf_op jit(solution)/shard_map/ppermute | solution.py:157
  13.3 3.2 %collective-permute-start.6 = (bf16[32,8192]{1,0:T(8,128)(2,1)}, bf16[32,8192]{1,0:T(8,128)(2,1)S(1)}, u32[]{:S(2)}, u32[]{:S(2)}) collective-permute-start(bf16[32,8192]{1,0:T(8,128)(2,1)} %bitcast.78), channel_id=1, source_target_pairs={{0,16},{16,0},{1,17},{17,1},{2,18},{18,2},{3,19},{19,3},{4,20},{20... | collective-permute-start | bytes 1572872 | tf_op jit(solution)/shard_map/ppermute | solution.py:152
  16.5 3.9 %collective-permute-start.2 = (bf16[32,4096]{1,0:T(8,128)(2,1)S(1)}, bf16[32,4096]{1,0:T(8,128)(2,1)S(1)}, u32[]{:S(2)}, u32[]{:S(2)}) collective-permute-start(bf16[32,4096]{1,0:T(8,128)(2,1)S(1)} %get-tuple-element.27), channel_id=1, source_target_pairs={{0,64},{32,96},{64,0},{96,32},{1,65},{33,97},{65,1},{97,33},{2,66}... | collective-permute-start | bytes 786440 | tf_op jit(solution)/shard_map/ppermute | solution.py:157
  20.5 4.4 %collective-permute-done.2 = bf16[32,4096]{1,0:T(8,128)(2,1)S(1)} collective-permute-done((bf16[32,4096]{1,0:T(8,128)(2,1)S(1)}, bf16[32,4096]{1,0:T(8,128)(2,1)S(1)}, u32[]{:S(2)}, u32[]{:S(2)}) %collective-permute-start.2) | collective-permute-done | bytes 262176 | tf_op jit(solution)/shard_map/ppermute | solution.py:157
  26.2 2.7 %collective-permute-done.6 = bf16[32,8192]{1,0:T(8,128)(2,1)S(1)} collective-permute-done((bf16[32,8192]{1,0:T(8,128)(2,1)}, bf16[32,8192]{1,0:T(8,128)(2,1)S(1)}, u32[]{:S(2)}, u32[]{:S(2)}) %collective-permute-start.6) | collective-permute-done | bytes 524320 | tf_op jit(solution)/shard_map/ppermute | solution.py:152
  30.4 4.5 %collective-permute-start.7 = (bf16[32,4096]{1,0:T(8,128)(2,1)S(1)}, bf16[32,4096]{1,0:T(8,128)(2,1)S(1)}, u32[]{:S(2)}, u32[]{:S(2)}) collective-permute-start(bf16[32,4096]{1,0:T(8,128)(2,1)S(1)} %get-tuple-element.54), channel_id=1, source_target_pairs={{0,96},{32,0},{64,32},{96,64},{1,97},{33,1},{65,33},{97,65},{2,98}... | collective-permute-start | bytes 786440 | tf_op jit(solution)/shard_map/ppermute | solution.py:157
  34.9 1.9 %collective-permute-start.11 = (bf16[4,32,4096]{2,1,0:T(8,128)(2,1)S(1)}, bf16[4,32,4096]{2,1,0:T(8,128)(2,1)S(1)}, u32[]{:S(2)}, u32[]{:S(2)}) collective-permute-start(bf16[4,32,4096]{2,1,0:T(8,128)(2,1)S(1)} %pad_maximum_fusion.refs_0_), channel_id=1, source_target_pairs={{0,1},{1,2},{2,3},{3,0},{4,5},{5,6},{6,7},{7,4},{8,9},{9,10},{10,1... | collective-permute-start | bytes 3145736 | tf_op jit(solution)/shard_map/ppermute | solution.py:157
  38.2 4.4 %collective-permute-start.14 = (bf16[4,32,4096]{2,1,0:T(8,128)(2,1)S(1)}, bf16[4,32,4096]{2,1,0:T(8,128)(2,1)S(1)}, u32[]{:S(2)}, u32[]{:S(2)}) collective-permute-start(bf16[4,32,4096]{2,1,0:T(8,128)(2,1)S(1)} %pad_maximum_fusion.1.refs_8_), channel_id=1, source_target_pairs={{0,96},{32,0},{64,32},{96,64},{1,97},{33,1},{65,33},{97,65},{2,98}... | collective-permute-start | bytes 3145736 | tf_op jit(solution)/shard_map/ppermute | solution.py:157
  42.7 4.0 %collective-permute-start.8 = (bf16[2,32,4096]{2,1,0:T(8,128)(2,1)S(1)}, bf16[2,32,4096]{2,1,0:T(8,128)(2,1)S(1)}, u32[]{:S(2)}, u32[]{:S(2)}) collective-permute-start(bf16[2,32,4096]{2,1,0:T(8,128)(2,1)S(1)} %slice.94), channel_id=1, source_target_pairs={{0,16},{16,0},{1,17},{17,1},{2,18},{18,2},{3,19},{19,3},{4,20},{20... | collective-permute-start | bytes 1572872 | tf_op jit(solution)/shard_map/ppermute | solution.py:152
  46.8 7.0 %collective-permute-done.8 = bf16[2,32,4096]{2,1,0:T(8,128)(2,1)S(1)} collective-permute-done((bf16[2,32,4096]{2,1,0:T(8,128)(2,1)S(1)}, bf16[2,32,4096]{2,1,0:T(8,128)(2,1)S(1)}, u32[]{:S(2)}, u32[]{:S(2)}) %collective-permute-start.8) | collective-permute-done | bytes 524320 | tf_op jit(solution)/shard_map/ppermute | solution.py:152
  54.9 2.7 %collective-permute-done.12.refs_3_ = bf16[4,32,4096]{2,1,0:T(8,128)(2,1)S(1)} collective-permute-done((bf16[4,32,4096]{2,1,0:T(8,128)(2,1)S(1)}, bf16[4,32,4096]{2,1,0:T(8,128)(2,1)S(1)}, u32[]{:S(2)}, u32[]{:S(2)}) %collective-permute-start.12) | collective-permute-done | bytes 1048608 | tf_op jit(solution)/shard_map/ppermute | solution.py:157
  57.7 2.1 %collective-permute-done.14.refs_11_ = bf16[4,32,4096]{2,1,0:T(8,128)(2,1)S(1)} collective-permute-done((bf16[4,32,4096]{2,1,0:T(8,128)(2,1)S(1)}, bf16[4,32,4096]{2,1,0:T(8,128)(2,1)S(1)}, u32[]{:S(2)}, u32[]{:S(2)}) %collective-permute-start.14) | collective-permute-done | bytes 1048608 | tf_op jit(solution)/shard_map/ppermute | solution.py:157
  60.5 1.4 collective-permute-start.17
  61.9 1.8 %collective-permute-start.16 = (bf16[4,32,4096]{2,1,0:T(8,128)(2,1)}, bf16[4,32,4096]{2,1,0:T(8,128)(2,1)S(1)}, u32[]{:S(2)}, u32[]{:S(2)}) collective-permute-start(bf16[4,32,4096]{2,1,0:T(8,128)(2,1)} %pad_maximum_fusion.2.refs_1_), channel_id=1, source_target_pairs={{0,3},{1,0},{2,1},{3,2},{4,7},{5,4},{6,5},{7,6},{8,11},{9,8},{10,9... | collective-permute-start | bytes 3145736 | tf_op jit(solution)/shard_map/ppermute | solution.py:157
  63.7 3.0 %collective-permute-start.20 = (bf16[4,32,4096]{2,1,0:T(8,128)(2,1)S(1)}, bf16[4,32,4096]{2,1,0:T(8,128)(2,1)}, u32[]{:S(2)}, u32[]{:S(2)}) collective-permute-start(bf16[4,32,4096]{2,1,0:T(8,128)(2,1)S(1)} %pad_maximum_fusion.3.refs_9_), channel_id=1, source_target_pairs={{0,96},{32,0},{64,32},{96,64},{1,97},{33,1},{65,33},{97,65},{2,98}... | collective-permute-start | bytes 3145736 | tf_op jit(solution)/shard_map/ppermute | solution.py:157
  67.6 20.2 %collective-permute-done.17.refs_6_ = bf16[4,32,4096]{2,1,0:T(8,128)(2,1)S(1)} collective-permute-done((bf16[4,32,4096]{2,1,0:T(8,128)(2,1)S(1)}, bf16[4,32,4096]{2,1,0:T(8,128)(2,1)S(1)}, u32[]{:S(2)}, u32[]{:S(2)}) %collective-permute-start.17) | collective-permute-done | bytes 1048608 | tf_op jit(solution)/shard_map/ppermute | solution.py:157
  89.6 2.9 %collective-permute-start.22 = (bf16[4,32,4096]{2,1,0:T(8,128)(2,1)}, bf16[4,32,4096]{2,1,0:T(8,128)(2,1)}, u32[]{:S(2)}, u32[]{:S(2)}) collective-permute-start(bf16[4,32,4096]{2,1,0:T(8,128)(2,1)} %collective-permute-done.20.refs_13_), channel_id=1, source_target_pairs={{0,96},{32,0},{64,32},{96,64},{1,97},{33,1},{65,33},{97,65},{2,98}... | collective-permute-start | bytes 3145736 | tf_op jit(solution)/shard_map/ppermute | solution.py:157
  95.0 13.4 %collective-permute-done.21.refs_14_ = bf16[4,32,4096]{2,1,0:T(8,128)(2,1)} collective-permute-done((bf16[4,32,4096]{2,1,0:T(8,128)(2,1)}, bf16[4,32,4096]{2,1,0:T(8,128)(2,1)}, u32[]{:S(2)}, u32[]{:S(2)}) %collective-permute-start.21) | collective-permute-done | bytes 1048608 | tf_op jit(solution)/shard_map/ppermute | solution.py:157
  108.4 18.9 %aggregate.1 = (bf16[4,2,1024,128]{3,2,1,0:T(8,128)(2,1)}, bf16[2,4,1024,128]{3,2,1,0:T(8,128)(2,1)}, bf16[4,2,1024,128]{3,2,1,0:T(8,128)(2,1)}, bf16[2,4,1024,128]{3,2,1,0:T(8,128)(2,1)}) custom-call(s32[384]{0:T(512)} %reduce.rows_ref, s32[384]{0:T(512)} %reduce.1.cols_ref, s32[6]{0:T(128)} %stack.65.info_ref, bf16[384,128,128]{2,1,0:T(8,128)(2,1)} %bitcast.76, ...), custom_call_target="tpu_custom_call" | custom-call | tf_op jit(solution)/shard_map/aggregate/pallas_call | solution.py:125
  127.4 4.4 %collective-permute-done.23 = bf16[2,4,1024,128]{3,2,1,0:T(8,128)(2,1)S(1)} collective-permute-done((bf16[2,4,1024,128]{3,2,1,0:T(8,128)(2,1)}, bf16[2,4,1024,128]{3,2,1,0:T(8,128)(2,1)S(1)}, u32[]{:S(2)}, u32[]{:S(2)}) %collective-permute-start.23) | collective-permute-done | bytes 2097184 | tf_op jit(solution)/shard_map/ppermute | solution.py:152
  131.9 1.5 fusion.2
  133.4 6.7 %collective-permute-start.29 = (bf16[4,1024,128]{2,1,0:T(8,128)(2,1)S(1)}, bf16[4,1024,128]{2,1,0:T(8,128)(2,1)S(1)}, u32[]{:S(2)}, u32[]{:S(2)}) collective-permute-start(bf16[4,1024,128]{2,1,0:T(8,128)(2,1)S(1)} %fusion.2), channel_id=1, source_target_pairs={{0,8},{8,0},{1,9},{9,1},{2,10},{10,2},{3,11},{11,3},{4,12},{12,4},... | collective-permute-start | bytes 3145736 | tf_op jit(solution)/shard_map/ppermute | solution.py:152
  140.6 3.2 %collective-permute-start.27 = (bf16[2,1024,128]{2,1,0:T(8,128)(2,1)S(1)}, bf16[2,1024,128]{2,1,0:T(8,128)(2,1)S(1)}, u32[]{:S(2)}, u32[]{:S(2)}) collective-permute-start(bf16[2,1024,128]{2,1,0:T(8,128)(2,1)S(1)} %get-tuple-element.49), channel_id=1, source_target_pairs={{0,3},{1,0},{2,1},{3,2},{4,7},{5,4},{6,5},{7,6},{8,11},{9,8},{10,9... | collective-permute-start | bytes 1572872 | tf_op jit(solution)/shard_map/ppermute | solution.py:157
  143.8 20.0 %collective-permute-done.29 = bf16[4,1024,128]{2,1,0:T(8,128)(2,1)S(1)} collective-permute-done((bf16[4,1024,128]{2,1,0:T(8,128)(2,1)S(1)}, bf16[4,1024,128]{2,1,0:T(8,128)(2,1)S(1)}, u32[]{:S(2)}, u32[]{:S(2)}) %collective-permute-start.29) | collective-permute-done | bytes 1048608 | tf_op jit(solution)/shard_map/ppermute | solution.py:152
  164.1 3.2 %collective-permute-start.32 = (bf16[1024,128]{1,0:T(8,128)(2,1)S(1)}, bf16[1024,128]{1,0:T(8,128)(2,1)S(1)}, u32[]{:S(2)}, u32[]{:S(2)}) collective-permute-start(bf16[1024,128]{1,0:T(8,128)(2,1)S(1)} %get-tuple-element.46), channel_id=1, source_target_pairs={{0,3},{1,0},{2,1},{3,2},{4,7},{5,4},{6,5},{7,6},{8,11},{9,8},{10,9... | collective-permute-start | bytes 786440 | tf_op jit(solution)/shard_map/ppermute | solution.py:157
  167.8 2.2 %collective-permute-start.28 = (bf16[1024,128]{1,0:T(8,128)(2,1)S(1)}, bf16[1024,128]{1,0:T(8,128)(2,1)S(1)}, u32[]{:S(2)}, u32[]{:S(2)}) collective-permute-start(bf16[1024,128]{1,0:T(8,128)(2,1)S(1)} %fusion.20), channel_id=1, source_target_pairs={{0,8},{8,0},{1,9},{9,1},{2,10},{10,2},{3,11},{11,3},{4,12},{12,4},... | collective-permute-start | bytes 786440 | tf_op jit(solution)/shard_map/ppermute | solution.py:152
  170.0 9.0 %collective-permute-done.30 = bf16[1024,128]{1,0:T(8,128)(2,1)S(1)} collective-permute-done((bf16[1024,128]{1,0:T(8,128)(2,1)S(1)}, bf16[1024,128]{1,0:T(8,128)(2,1)S(1)}, u32[]{:S(2)}, u32[]{:S(2)}) %collective-permute-start.30) | collective-permute-done | bytes 262176 | tf_op jit(solution)/shard_map/ppermute | solution.py:157
  (82 shorter events, 15.3 us)
Async XLA Ops:
  1.2 9.2 %collective-permute-start.4 = (bf16[32,4096]{1,0:T(8,128)(2,1)S(1)}, bf16[32,4096]{1,0:T(8,128)(2,1)S(1)}, u32[]{:S(2)}, u32[]{:S(2)}) collective-permute-start(bf16[32,4096]{1,0:T(8,128)(2,1)S(1)} %get-tuple-element.30), channel_id=1, source_target_pairs={{0,1},{1,2},{2,3},{3,0},{4,5},{5,6},{6,7},{7,4},{8,9},{9,10},{10,1... | collective-permute-start | bytes 786440 | tf_op jit(solution)/shard_map/ppermute | solution.py:157
  2.8 7.8 %collective-permute-start.3 = (bf16[32,4096]{1,0:T(8,128)(2,1)S(1)}, bf16[32,4096]{1,0:T(8,128)(2,1)S(1)}, u32[]{:S(2)}, u32[]{:S(2)}) collective-permute-start(bf16[32,4096]{1,0:T(8,128)(2,1)S(1)} %get-tuple-element.30), channel_id=1, source_target_pairs={{0,3},{1,0},{2,1},{3,2},{4,7},{5,4},{6,5},{7,6},{8,11},{9,8},{10,9... | collective-permute-start | bytes 786440 | tf_op jit(solution)/shard_map/ppermute | solution.py:157
  4.5 12.0 %collective-permute-start.1 = (bf16[32,4096]{1,0:T(8,128)(2,1)S(1)}, bf16[32,4096]{1,0:T(8,128)(2,1)S(1)}, u32[]{:S(2)}, u32[]{:S(2)}) collective-permute-start(bf16[32,4096]{1,0:T(8,128)(2,1)S(1)} %get-tuple-element.27), channel_id=1, source_target_pairs={{0,32},{32,64},{64,96},{96,0},{1,33},{33,65},{65,97},{97,1},{2,34}... | collective-permute-start | bytes 786440 | tf_op jit(solution)/shard_map/ppermute | solution.py:157
  6.5 10.0 %collective-permute-start = (bf16[32,4096]{1,0:T(8,128)(2,1)S(1)}, bf16[32,4096]{1,0:T(8,128)(2,1)S(1)}, u32[]{:S(2)}, u32[]{:S(2)}) collective-permute-start(bf16[32,4096]{1,0:T(8,128)(2,1)S(1)} %get-tuple-element.27), channel_id=1, source_target_pairs={{0,96},{32,0},{64,32},{96,64},{1,97},{33,1},{65,33},{97,65},{2,98}... | collective-permute-start | bytes 786440 | tf_op jit(solution)/shard_map/ppermute | solution.py:157
  10.6 9.8 %collective-permute-start.5 = (bf16[32,4096]{1,0:T(8,128)(2,1)S(1)}, bf16[32,4096]{1,0:T(8,128)(2,1)S(1)}, u32[]{:S(2)}, u32[]{:S(2)}) collective-permute-start(bf16[32,4096]{1,0:T(8,128)(2,1)S(1)} %get-tuple-element.30), channel_id=1, source_target_pairs={{0,2},{1,3},{2,0},{3,1},{4,6},{5,7},{6,4},{7,5},{8,10},{9,11},{10,... | collective-permute-start | bytes 786440 | tf_op jit(solution)/shard_map/ppermute | solution.py:157
  13.3 15.6 %collective-permute-start.6 = (bf16[32,8192]{1,0:T(8,128)(2,1)}, bf16[32,8192]{1,0:T(8,128)(2,1)S(1)}, u32[]{:S(2)}, u32[]{:S(2)}) collective-permute-start(bf16[32,8192]{1,0:T(8,128)(2,1)} %bitcast.78), channel_id=1, source_target_pairs={{0,16},{16,0},{1,17},{17,1},{2,18},{18,2},{3,19},{19,3},{4,20},{20... | collective-permute-start | bytes 1572872 | tf_op jit(solution)/shard_map/ppermute | solution.py:152
  16.5 8.4 %collective-permute-start.2 = (bf16[32,4096]{1,0:T(8,128)(2,1)S(1)}, bf16[32,4096]{1,0:T(8,128)(2,1)S(1)}, u32[]{:S(2)}, u32[]{:S(2)}) collective-permute-start(bf16[32,4096]{1,0:T(8,128)(2,1)S(1)} %get-tuple-element.27), channel_id=1, source_target_pairs={{0,64},{32,96},{64,0},{96,32},{1,65},{33,97},{65,1},{97,33},{2,66}... | collective-permute-start | bytes 786440 | tf_op jit(solution)/shard_map/ppermute | solution.py:157
  25.1 17.6 %collective-permute-start.10 = (bf16[2,32,4096]{2,1,0:T(8,128)(2,1)S(1)}, bf16[2,32,4096]{2,1,0:T(8,128)(2,1)S(1)}, u32[]{:S(2)}, u32[]{:S(2)}) collective-permute-start(bf16[2,32,4096]{2,1,0:T(8,128)(2,1)S(1)} %slice.96), channel_id=1, source_target_pairs={{0,16},{16,0},{1,17},{17,1},{2,18},{18,2},{3,19},{19,3},{4,20},{20... | collective-permute-start | bytes 1572872 | tf_op jit(solution)/shard_map/ppermute | solution.py:152
  29.0 9.2 %collective-permute-start.9 = (bf16[32,4096]{1,0:T(8,128)(2,1)S(1)}, bf16[32,4096]{1,0:T(8,128)(2,1)S(1)}, u32[]{:S(2)}, u32[]{:S(2)}) collective-permute-start(bf16[32,4096]{1,0:T(8,128)(2,1)S(1)} %get-tuple-element.53), channel_id=1, source_target_pairs={{0,3},{1,0},{2,1},{3,2},{4,7},{5,4},{6,5},{7,6},{8,11},{9,8},{10,9... | collective-permute-start | bytes 786440 | tf_op jit(solution)/shard_map/ppermute | solution.py:157
  30.4 12.3 %collective-permute-start.7 = (bf16[32,4096]{1,0:T(8,128)(2,1)S(1)}, bf16[32,4096]{1,0:T(8,128)(2,1)S(1)}, u32[]{:S(2)}, u32[]{:S(2)}) collective-permute-start(bf16[32,4096]{1,0:T(8,128)(2,1)S(1)} %get-tuple-element.54), channel_id=1, source_target_pairs={{0,96},{32,0},{64,32},{96,64},{1,97},{33,1},{65,33},{97,65},{2,98}... | collective-permute-start | bytes 786440 | tf_op jit(solution)/shard_map/ppermute | solution.py:157
  34.8 22.8 %collective-permute-start.12 = (bf16[4,32,4096]{2,1,0:T(8,128)(2,1)S(1)}, bf16[4,32,4096]{2,1,0:T(8,128)(2,1)S(1)}, u32[]{:S(2)}, u32[]{:S(2)}) collective-permute-start(bf16[4,32,4096]{2,1,0:T(8,128)(2,1)S(1)} %pad_maximum_fusion.refs_0_), channel_id=1, source_target_pairs={{0,3},{1,0},{2,1},{3,2},{4,7},{5,4},{6,5},{7,6},{8,11},{9,8},{10,9... | collective-permute-start | bytes 3145736 | tf_op jit(solution)/shard_map/ppermute | solution.py:157
  34.9 22.7 %collective-permute-start.11 = (bf16[4,32,4096]{2,1,0:T(8,128)(2,1)S(1)}, bf16[4,32,4096]{2,1,0:T(8,128)(2,1)S(1)}, u32[]{:S(2)}, u32[]{:S(2)}) collective-permute-start(bf16[4,32,4096]{2,1,0:T(8,128)(2,1)S(1)} %pad_maximum_fusion.refs_0_), channel_id=1, source_target_pairs={{0,1},{1,2},{2,3},{3,0},{4,5},{5,6},{6,7},{7,4},{8,9},{9,10},{10,1... | collective-permute-start | bytes 3145736 | tf_op jit(solution)/shard_map/ppermute | solution.py:157
  38.2 21.5 %collective-permute-start.14 = (bf16[4,32,4096]{2,1,0:T(8,128)(2,1)S(1)}, bf16[4,32,4096]{2,1,0:T(8,128)(2,1)S(1)}, u32[]{:S(2)}, u32[]{:S(2)}) collective-permute-start(bf16[4,32,4096]{2,1,0:T(8,128)(2,1)S(1)} %pad_maximum_fusion.1.refs_8_), channel_id=1, source_target_pairs={{0,96},{32,0},{64,32},{96,64},{1,97},{33,1},{65,33},{97,65},{2,98}... | collective-permute-start | bytes 3145736 | tf_op jit(solution)/shard_map/ppermute | solution.py:157
  42.7 17.8 %collective-permute-start.13 = (bf16[4,32,4096]{2,1,0:T(8,128)(2,1)S(1)}, bf16[4,32,4096]{2,1,0:T(8,128)(2,1)}, u32[]{:S(2)}, u32[]{:S(2)}) collective-permute-start(bf16[4,32,4096]{2,1,0:T(8,128)(2,1)S(1)} %pad_maximum_fusion.1.refs_8_), channel_id=1, source_target_pairs={{0,32},{32,64},{64,96},{96,0},{1,33},{33,65},{65,97},{97,1},{2,34}... | collective-permute-start | bytes 3145736 | tf_op jit(solution)/shard_map/ppermute | solution.py:157
  42.7 11.1 %collective-permute-start.8 = (bf16[2,32,4096]{2,1,0:T(8,128)(2,1)S(1)}, bf16[2,32,4096]{2,1,0:T(8,128)(2,1)S(1)}, u32[]{:S(2)}, u32[]{:S(2)}) collective-permute-start(bf16[2,32,4096]{2,1,0:T(8,128)(2,1)S(1)} %slice.94), channel_id=1, source_target_pairs={{0,16},{16,0},{1,17},{17,1},{2,18},{18,2},{3,19},{19,3},{4,20},{20... | collective-permute-start | bytes 1572872 | tf_op jit(solution)/shard_map/ppermute | solution.py:152
  60.5 27.3 %collective-permute-start.17 = (bf16[4,32,4096]{2,1,0:T(8,128)(2,1)S(1)}, bf16[4,32,4096]{2,1,0:T(8,128)(2,1)S(1)}, u32[]{:S(2)}, u32[]{:S(2)}) collective-permute-start(bf16[4,32,4096]{2,1,0:T(8,128)(2,1)S(1)} %collective-permute-done.11.refs_2_), channel_id=1, source_target_pairs={{0,1},{1,2},{2,3},{3,0},{4,5},{5,6},{6,7},{7,4},{8,9},{9,10},{10,1... | collective-permute-start | bytes 3145736 | tf_op jit(solution)/shard_map/ppermute | solution.py:157
  61.9 26.5 %collective-permute-start.16 = (bf16[4,32,4096]{2,1,0:T(8,128)(2,1)}, bf16[4,32,4096]{2,1,0:T(8,128)(2,1)S(1)}, u32[]{:S(2)}, u32[]{:S(2)}) collective-permute-start(bf16[4,32,4096]{2,1,0:T(8,128)(2,1)} %pad_maximum_fusion.2.refs_1_), channel_id=1, source_target_pairs={{0,3},{1,0},{2,1},{3,2},{4,7},{5,4},{6,5},{7,6},{8,11},{9,8},{10,9... | collective-permute-start | bytes 3145736 | tf_op jit(solution)/shard_map/ppermute | solution.py:157
  63.7 25.8 %collective-permute-start.20 = (bf16[4,32,4096]{2,1,0:T(8,128)(2,1)S(1)}, bf16[4,32,4096]{2,1,0:T(8,128)(2,1)}, u32[]{:S(2)}, u32[]{:S(2)}) collective-permute-start(bf16[4,32,4096]{2,1,0:T(8,128)(2,1)S(1)} %pad_maximum_fusion.3.refs_9_), channel_id=1, source_target_pairs={{0,96},{32,0},{64,32},{96,64},{1,97},{33,1},{65,33},{97,65},{2,98}... | collective-permute-start | bytes 3145736 | tf_op jit(solution)/shard_map/ppermute | solution.py:157
  66.7 41.6 %collective-permute-start.15 = (bf16[4,32,4096]{2,1,0:T(8,128)(2,1)}, bf16[4,32,4096]{2,1,0:T(8,128)(2,1)}, u32[]{:S(2)}, u32[]{:S(2)}) collective-permute-start(bf16[4,32,4096]{2,1,0:T(8,128)(2,1)} %pad_maximum_fusion.2.refs_1_), channel_id=1, source_target_pairs={{0,1},{1,2},{2,3},{3,0},{4,5},{5,6},{6,7},{7,4},{8,9},{9,10},{10,1... | collective-permute-start | bytes 3145736 | tf_op jit(solution)/shard_map/ppermute | solution.py:157
  67.6 40.7 %collective-permute-start.19 = (bf16[4,32,4096]{2,1,0:T(8,128)(2,1)S(1)}, bf16[4,32,4096]{2,1,0:T(8,128)(2,1)}, u32[]{:S(2)}, u32[]{:S(2)}) collective-permute-start(bf16[4,32,4096]{2,1,0:T(8,128)(2,1)S(1)} %pad_maximum_fusion.3.refs_9_), channel_id=1, source_target_pairs={{0,32},{32,64},{64,96},{96,0},{1,33},{33,65},{65,97},{97,1},{2,34}... | collective-permute-start | bytes 3145736 | tf_op jit(solution)/shard_map/ppermute | solution.py:157
  87.8 20.5 %collective-permute-start.21 = (bf16[4,32,4096]{2,1,0:T(8,128)(2,1)}, bf16[4,32,4096]{2,1,0:T(8,128)(2,1)}, u32[]{:S(2)}, u32[]{:S(2)}) collective-permute-start(bf16[4,32,4096]{2,1,0:T(8,128)(2,1)} %collective-permute-done.13.refs_10_), channel_id=1, source_target_pairs={{0,32},{32,64},{64,96},{96,0},{1,33},{33,65},{65,97},{97,1},{2,34}... | collective-permute-start | bytes 3145736 | tf_op jit(solution)/shard_map/ppermute | solution.py:157
  88.4 20.0 %collective-permute-start.18 = (bf16[4,32,4096]{2,1,0:T(8,128)(2,1)S(1)}, bf16[4,32,4096]{2,1,0:T(8,128)(2,1)}, u32[]{:S(2)}, u32[]{:S(2)}) collective-permute-start(bf16[4,32,4096]{2,1,0:T(8,128)(2,1)S(1)} %collective-permute-done.16.refs_5_), channel_id=1, source_target_pairs={{0,3},{1,0},{2,1},{3,2},{4,7},{5,4},{6,5},{7,6},{8,11},{9,8},{10,9... | collective-permute-start | bytes 3145736 | tf_op jit(solution)/shard_map/ppermute | solution.py:157
  89.6 18.8 %collective-permute-start.22 = (bf16[4,32,4096]{2,1,0:T(8,128)(2,1)}, bf16[4,32,4096]{2,1,0:T(8,128)(2,1)}, u32[]{:S(2)}, u32[]{:S(2)}) collective-permute-start(bf16[4,32,4096]{2,1,0:T(8,128)(2,1)} %collective-permute-done.20.refs_13_), channel_id=1, source_target_pairs={{0,96},{32,0},{64,32},{96,64},{1,97},{33,1},{65,33},{97,65},{2,98}... | collective-permute-start | bytes 3145736 | tf_op jit(solution)/shard_map/ppermute | solution.py:157
  131.8 8.3 %collective-permute-start.24 = (bf16[4,2,1024,128]{3,2,1,0:T(8,128)(2,1)}, bf16[4,2,1024,128]{3,2,1,0:T(8,128)(2,1)S(1)}, u32[]{:S(2)}, u32[]{:S(2)}) collective-permute-start(bf16[4,2,1024,128]{3,2,1,0:T(8,128)(2,1)} %get-tuple-element.42), channel_id=1, source_target_pairs={{0,4},{4,0},{1,5},{5,1},{2,6},{6,2},{3,7},{7,3},{8,12},{12,8},{9,1... | collective-permute-start | bytes 6291464 | tf_op jit(solution)/shard_map/ppermute | solution.py:152
  133.4 30.4 %collective-permute-start.29 = (bf16[4,1024,128]{2,1,0:T(8,128)(2,1)S(1)}, bf16[4,1024,128]{2,1,0:T(8,128)(2,1)S(1)}, u32[]{:S(2)}, u32[]{:S(2)}) collective-permute-start(bf16[4,1024,128]{2,1,0:T(8,128)(2,1)S(1)} %fusion.2), channel_id=1, source_target_pairs={{0,8},{8,0},{1,9},{9,1},{2,10},{10,2},{3,11},{11,3},{4,12},{12,4},... | collective-permute-start | bytes 3145736 | tf_op jit(solution)/shard_map/ppermute | solution.py:152
  140.5 26.9 %collective-permute-start.25 = (bf16[2,1024,128]{2,1,0:T(8,128)(2,1)S(1)}, bf16[2,1024,128]{2,1,0:T(8,128)(2,1)S(1)}, u32[]{:S(2)}, u32[]{:S(2)}) collective-permute-start(bf16[2,1024,128]{2,1,0:T(8,128)(2,1)S(1)} %get-tuple-element.48), channel_id=1, source_target_pairs={{0,1},{1,2},{2,3},{3,0},{4,5},{5,6},{6,7},{7,4},{8,9},{9,10},{10,1... | collective-permute-start | bytes 1572872 | tf_op jit(solution)/shard_map/ppermute | solution.py:157
  140.6 26.8 %collective-permute-start.27 = (bf16[2,1024,128]{2,1,0:T(8,128)(2,1)S(1)}, bf16[2,1024,128]{2,1,0:T(8,128)(2,1)S(1)}, u32[]{:S(2)}, u32[]{:S(2)}) collective-permute-start(bf16[2,1024,128]{2,1,0:T(8,128)(2,1)S(1)} %get-tuple-element.49), channel_id=1, source_target_pairs={{0,3},{1,0},{2,1},{3,2},{4,7},{5,4},{6,5},{7,6},{8,11},{9,8},{10,9... | collective-permute-start | bytes 1572872 | tf_op jit(solution)/shard_map/ppermute | solution.py:157
  143.8 23.6 %collective-permute-start.26 = (bf16[2,1024,128]{2,1,0:T(8,128)(2,1)S(1)}, bf16[2,1024,128]{2,1,0:T(8,128)(2,1)S(1)}, u32[]{:S(2)}, u32[]{:S(2)}) collective-permute-start(bf16[2,1024,128]{2,1,0:T(8,128)(2,1)S(1)} %get-tuple-element.50), channel_id=1, source_target_pairs={{0,2},{1,3},{2,0},{3,1},{4,6},{5,7},{6,4},{7,5},{8,10},{9,11},{10,... | collective-permute-start | bytes 1572872 | tf_op jit(solution)/shard_map/ppermute | solution.py:157
  164.1 14.9 %collective-permute-start.30 = (bf16[1024,128]{1,0:T(8,128)(2,1)S(1)}, bf16[1024,128]{1,0:T(8,128)(2,1)S(1)}, u32[]{:S(2)}, u32[]{:S(2)}) collective-permute-start(bf16[1024,128]{1,0:T(8,128)(2,1)S(1)} %get-tuple-element.45), channel_id=1, source_target_pairs={{0,1},{1,2},{2,3},{3,0},{4,5},{5,6},{6,7},{7,4},{8,9},{9,10},{10,1... | collective-permute-start | bytes 786440 | tf_op jit(solution)/shard_map/ppermute | solution.py:157
  164.1 14.8 %collective-permute-start.32 = (bf16[1024,128]{1,0:T(8,128)(2,1)S(1)}, bf16[1024,128]{1,0:T(8,128)(2,1)S(1)}, u32[]{:S(2)}, u32[]{:S(2)}) collective-permute-start(bf16[1024,128]{1,0:T(8,128)(2,1)S(1)} %get-tuple-element.46), channel_id=1, source_target_pairs={{0,3},{1,0},{2,1},{3,2},{4,7},{5,4},{6,5},{7,6},{8,11},{9,8},{10,9... | collective-permute-start | bytes 786440 | tf_op jit(solution)/shard_map/ppermute | solution.py:157
  167.4 11.6 %collective-permute-start.31 = (bf16[1024,128]{1,0:T(8,128)(2,1)S(1)}, bf16[1024,128]{1,0:T(8,128)(2,1)S(1)}, u32[]{:S(2)}, u32[]{:S(2)}) collective-permute-start(bf16[1024,128]{1,0:T(8,128)(2,1)S(1)} %get-tuple-element.47), channel_id=1, source_target_pairs={{0,2},{1,3},{2,0},{3,1},{4,6},{5,7},{6,4},{7,5},{8,10},{9,11},{10,... | collective-permute-start | bytes 786440 | tf_op jit(solution)/shard_map/ppermute | solution.py:157
  167.8 11.5 %collective-permute-start.28 = (bf16[1024,128]{1,0:T(8,128)(2,1)S(1)}, bf16[1024,128]{1,0:T(8,128)(2,1)S(1)}, u32[]{:S(2)}, u32[]{:S(2)}) collective-permute-start(bf16[1024,128]{1,0:T(8,128)(2,1)S(1)} %fusion.20), channel_id=1, source_target_pairs={{0,8},{8,0},{1,9},{9,1},{2,10},{10,2},{3,11},{11,3},{4,12},{12,4},... | collective-permute-start | bytes 786440 | tf_op jit(solution)/shard_map/ppermute | solution.py:152
  (15 other events, 570.8 us)

commit v11 on v8

--- a/solution.py
+++ b/solution.py
@@ -168,21 +168,26 @@
     return value.astype(jnp.bfloat16)
 
 
-STEPS = (0, -1, 1, 2)
-
-
-def ring(value, axis):
-    return [value] + [shift(value, axis, -d) for d in STEPS[1:]]
+STEPS = (0, 1, -1, 2)
+
+
+def ring(value, axis, ahead):
+    after, before = (shift(value, axis, -d) for d in STEPS[1:3])
+    again, after, before, ahead = tie((value, after, before, ahead))
+    return jnp.stack([value, after, before, shift(again, axis, 2)]), ahead
 
 
 def gather_sources(x):
     half = x.shape[1] // 2
     other = swap(x, "ry")
-    a_own, b_own = jnp.stack(ring(x[:, :half], "rz")), jnp.stack(ring(x[:, half:], "fx"))
-    a_own, b_own, other = tie((a_own, b_own, other))
+    a_own, other = ring(x[:, :half], "rz", other)
+    b_own, other = ring(x[:, half:], "fx", other)
+    a_next, b_next = shift(other[:, :half], "rz", -1), shift(other[:, half:], "fx", -1)
+    a_own, b_own, a_next, b_next = tie((a_own, b_own, a_next, b_next))
     a_near = shift(a_own, "fx", 1), shift(a_own, "fx", -1)
     b_near = shift(b_own, "rz", 1), shift(b_own, "rz", -1)
-    a_other, b_other = jnp.stack(ring(other[:, :half], "rz")), jnp.stack(ring(other[:, half:], "fx"))
+    a_other = jnp.concatenate([jnp.stack([other[:, :half], a_next]), swap(a_own[2:], "ry")])
+    b_other = jnp.concatenate([jnp.stack([other[:, half:], b_next]), swap(b_own[2:], "ry")])
     a_other, b_other, a_near, b_near = tie((a_other, b_other, a_near, b_near))
     parts = []
     for own, other, near, axis, first in (

time: 195 us -> 191 us (0.979)
  starting transfers between devices: 82 us -> 68.9 us
  waiting for transfers between devices: 88.1 us -> 99.3 us
    ppermute x30 -> x26, starting transfers between devices: 76.5 us -> 48.3 us  [shift(): return lax.ppermute(value, axis, [(i, (i + by) % n) for i in range(n)])]
    ppermute x5 -> x7, waiting for transfers between devices: 12.4 us -> 34 us  [swap(): return lax.ppermute(value, axis, [(0, 1), (1, 0)])]
    ppermute x5 -> x7, starting transfers between devices: 5.45 us -> 20.6 us  [swap(): return lax.ppermute(value, axis, [(0, 1), (1, 0)])]
    ppermute x30 -> x26, waiting for transfers between devices: 75.7 us -> 65.3 us  [shift(): return lax.ppermute(value, axis, [(i, (i + by) % n) for i in range(n)])]
  transfers between devices with their start and end apart: 35 -> 33, of which waited for: 15 -> 20; matrix products, arithmetic and copies ran while one was open for 3% -> 4% of each run, Pallas kernels for 0% -> 0%
where the time goes in v11:
time: 191 us
  waiting for transfers between devices  99.3 us (52%)
  starting transfers between devices  68.9 us (36%)
  Pallas kernels  12.7 us (7%)
  other arithmetic  5.44 us (3%)
  local copies, waits for them, and re-layouts  2.02 us (1%)
    ppermute x26, waiting for transfers between devices, shift(): return lax.ppermute(value, axis, [(i, (i + by) % n) for i in range(n)])  65.3 us
    ppermute x26, starting transfers between devices, shift(): return lax.ppermute(value, axis, [(i, (i + by) % n) for i in range(n)])  48.3 us
    ppermute x7, waiting for transfers between devices, swap(): return lax.ppermute(value, axis, [(0, 1), (1, 0)])  34 us
    ppermute x7, starting transfers between devices, swap(): return lax.ppermute(value, axis, [(0, 1), (1, 0)])  20.6 us
    pallas_call x1, Pallas kernels, aggregate(): pl.pallas_call(functools.partial(aggregate_kernel, where, len(arrays)), o...  12.7 us
  transfers between devices with their start and end apart: 33, of which 20 were waited for; matrix products, arithmetic and copies ran while one was open for 4% of the time, Pallas kernels for 0%

profile of v11, /device:TPU:0, one launch (start us, length us, event | category | flops | bytes accessed | tf_op | source)
XLA Modules:
  0.0 190.6 jit_solution(18418149440039279495)
XLA Ops:
  0.0 3.3 %collective-permute-start.2 = (bf16[32,8192]{1,0:T(8,128)(2,1)}, bf16[32,8192]{1,0:T(8,128)(2,1)S(1)}, u32[]{:S(2)}, u32[]{:S(2)}) collective-permute-start(bf16[32,8192]{1,0:T(8,128)(2,1)} %bitcast.77), channel_id=1, source_target_pairs={{0,16},{16,0},{1,17},{17,1},{2,18},{18,2},{3,19},{19,3},{4,20},{20... | collective-permute-start | bytes 1572872 | tf_op jit(solution)/shard_map/ppermute | solution.py:152
  4.4 2.0 %collective-permute-start.1 = (bf16[32,4096]{1,0:T(8,128)(2,1)S(1)}, bf16[32,4096]{1,0:T(8,128)(2,1)S(1)}, u32[]{:S(2)}, u32[]{:S(2)}) collective-permute-start(bf16[32,4096]{1,0:T(8,128)(2,1)S(1)} %get-tuple-element.31), channel_id=1, source_target_pairs={{0,32},{32,64},{64,96},{96,0},{1,33},{33,65},{65,97},{97,1},{2,34}... | collective-permute-start | bytes 786440 | tf_op jit(solution)/shard_map/ppermute | solution.py:157
  6.4 2.2 %collective-permute-start = (bf16[32,4096]{1,0:T(8,128)(2,1)S(1)}, bf16[32,4096]{1,0:T(8,128)(2,1)S(1)}, u32[]{:S(2)}, u32[]{:S(2)}) collective-permute-start(bf16[32,4096]{1,0:T(8,128)(2,1)S(1)} %get-tuple-element.31), channel_id=1, source_target_pairs={{0,96},{32,0},{64,32},{96,64},{1,97},{33,1},{65,33},{97,65},{2,98}... | collective-permute-start | bytes 786440 | tf_op jit(solution)/shard_map/ppermute | solution.py:157
  10.1 1.7 collective-permute-start.4
  11.8 2.7 %collective-permute-done.1 = bf16[32,4096]{1,0:T(8,128)(2,1)S(1)} collective-permute-done((bf16[32,4096]{1,0:T(8,128)(2,1)S(1)}, bf16[32,4096]{1,0:T(8,128)(2,1)S(1)}, u32[]{:S(2)}, u32[]{:S(2)}) %collective-permute-start.1) | collective-permute-done | bytes 262176 | tf_op jit(solution)/shard_map/ppermute | solution.py:157
  15.4 1.9 collective-permute-done.5
  17.3 2.7 %collective-permute-start.6 = (bf16[32,4096]{1,0:T(8,128)(2,1)S(1)}, bf16[32,4096]{1,0:T(8,128)(2,1)S(1)}, u32[]{:S(2)}, u32[]{:S(2)}) collective-permute-start(bf16[32,4096]{1,0:T(8,128)(2,1)S(1)} %get-tuple-element.35), channel_id=1, source_target_pairs={{0,2},{1,3},{2,0},{3,1},{4,6},{5,7},{6,4},{7,5},{8,10},{9,11},{10,... | collective-permute-start | bytes 786440 | tf_op jit(solution)/shard_map/ppermute | solution.py:157
  20.0 2.3 %collective-permute-start.3 = (bf16[32,4096]{1,0:T(8,128)(2,1)S(1)}, bf16[32,4096]{1,0:T(8,128)(2,1)S(1)}, u32[]{:S(2)}, u32[]{:S(2)}) collective-permute-start(bf16[32,4096]{1,0:T(8,128)(2,1)S(1)} %get-tuple-element.31), channel_id=1, source_target_pairs={{0,64},{32,96},{64,0},{96,32},{1,65},{33,97},{65,1},{97,33},{2,66}... | collective-permute-start | bytes 786440 | tf_op jit(solution)/shard_map/ppermute | solution.py:157
  25.5 2.4 %collective-permute-done.3 = bf16[32,4096]{1,0:T(8,128)(2,1)S(1)} collective-permute-done((bf16[32,4096]{1,0:T(8,128)(2,1)S(1)}, bf16[32,4096]{1,0:T(8,128)(2,1)S(1)}, u32[]{:S(2)}, u32[]{:S(2)}) %collective-permute-start.3) | collective-permute-done | bytes 262176 | tf_op jit(solution)/shard_map/ppermute | solution.py:157
  28.1 3.0 %collective-permute-done.8 = bf16[32,4096]{1,0:T(8,128)(2,1)S(1)} collective-permute-done((bf16[32,4096]{1,0:T(8,128)(2,1)S(1)}, bf16[32,4096]{1,0:T(8,128)(2,1)S(1)}, u32[]{:S(2)}, u32[]{:S(2)}) %collective-permute-start.8) | collective-permute-done | bytes 262176 | tf_op jit(solution)/shard_map/ppermute | solution.py:157
  31.1 2.8 %collective-permute-done.7 = bf16[32,4096]{1,0:T(8,128)(2,1)S(1)} collective-permute-done((bf16[32,4096]{1,0:T(8,128)(2,1)S(1)}, bf16[32,4096]{1,0:T(8,128)(2,1)S(1)}, u32[]{:S(2)}, u32[]{:S(2)}) %collective-permute-start.7) | collective-permute-done | bytes 262176 | tf_op jit(solution)/shard_map/ppermute | solution.py:157
  34.0 3.3 %collective-permute-start.10 = (bf16[2,32,4096]{2,1,0:T(8,128)(2,1)S(1)}, bf16[2,32,4096]{2,1,0:T(8,128)(2,1)S(1)}, u32[]{:S(2)}, u32[]{:S(2)}) collective-permute-start(bf16[2,32,4096]{2,1,0:T(8,128)(2,1)S(1)} %slice.98), channel_id=1, source_target_pairs={{0,16},{16,0},{1,17},{17,1},{2,18},{18,2},{3,19},{19,3},{4,20},{20... | collective-permute-start | bytes 1572872 | tf_op jit(solution)/shard_map/ppermute | solution.py:152
  39.3 2.6 %collective-permute-start.14 = (bf16[4,32,4096]{2,1,0:T(8,128)(2,1)S(1)}, bf16[4,32,4096]{2,1,0:T(8,128)(2,1)S(1)}, u32[]{:S(2)}, u32[]{:S(2)}) collective-permute-start(bf16[4,32,4096]{2,1,0:T(8,128)(2,1)S(1)} %pad_maximum_fusion.1.refs_8_), channel_id=1, source_target_pairs={{0,96},{32,0},{64,32},{96,64},{1,97},{33,1},{65,33},{97,65},{2,98}... | collective-permute-start | bytes 3145736 | tf_op jit(solution)/shard_map/ppermute | solution.py:157
  41.9 6.2 %collective-permute-done.10 = bf16[2,32,4096]{2,1,0:T(8,128)(2,1)S(1)} collective-permute-done((bf16[2,32,4096]{2,1,0:T(8,128)(2,1)S(1)}, bf16[2,32,4096]{2,1,0:T(8,128)(2,1)S(1)}, u32[]{:S(2)}, u32[]{:S(2)}) %collective-permute-start.10) | collective-permute-done | bytes 524320 | tf_op jit(solution)/shard_map/ppermute | solution.py:152
  48.1 3.2 %collective-permute-start.9 = (bf16[2,32,4096]{2,1,0:T(8,128)(2,1)S(1)}, bf16[2,32,4096]{2,1,0:T(8,128)(2,1)S(1)}, u32[]{:S(2)}, u32[]{:S(2)}) collective-permute-start(bf16[2,32,4096]{2,1,0:T(8,128)(2,1)S(1)} %slice.97), channel_id=1, source_target_pairs={{0,16},{16,0},{1,17},{17,1},{2,18},{18,2},{3,19},{19,3},{4,20},{20... | collective-permute-start | bytes 1572872 | tf_op jit(solution)/shard_map/ppermute | solution.py:152
  51.4 9.9 %collective-permute-done.9 = bf16[2,32,4096]{2,1,0:T(8,128)(2,1)S(1)} collective-permute-done((bf16[2,32,4096]{2,1,0:T(8,128)(2,1)S(1)}, bf16[2,32,4096]{2,1,0:T(8,128)(2,1)S(1)}, u32[]{:S(2)}, u32[]{:S(2)}) %collective-permute-start.9) | collective-permute-done | bytes 524320 | tf_op jit(solution)/shard_map/ppermute | solution.py:152
  63.4 3.5 %collective-permute-done.13.refs_10_ = bf16[4,32,4096]{2,1,0:T(8,128)(2,1)} collective-permute-done((bf16[4,32,4096]{2,1,0:T(8,128)(2,1)S(1)}, bf16[4,32,4096]{2,1,0:T(8,128)(2,1)}, u32[]{:S(2)}, u32[]{:S(2)}) %collective-permute-start.13) | collective-permute-done | bytes 1048608 | tf_op jit(solution)/shard_map/ppermute | solution.py:157
  67.3 2.9 %collective-permute-start.16 = (bf16[4,32,4096]{2,1,0:T(8,128)(2,1)}, bf16[4,32,4096]{2,1,0:T(8,128)(2,1)S(1)}, u32[]{:S(2)}, u32[]{:S(2)}) collective-permute-start(bf16[4,32,4096]{2,1,0:T(8,128)(2,1)} %pad_maximum_fusion.2.refs_1_), channel_id=1, source_target_pairs={{0,3},{1,0},{2,1},{3,2},{4,7},{5,4},{6,5},{7,6},{8,11},{9,8},{10,9... | collective-permute-start | bytes 3145736 | tf_op jit(solution)/shard_map/ppermute | solution.py:157
  70.5 1.7 collective-permute-start.19
  72.2 22.0 %collective-permute-done.17.refs_6_ = bf16[4,32,4096]{2,1,0:T(8,128)(2,1)S(1)} collective-permute-done((bf16[4,32,4096]{2,1,0:T(8,128)(2,1)S(1)}, bf16[4,32,4096]{2,1,0:T(8,128)(2,1)S(1)}, u32[]{:S(2)}, u32[]{:S(2)}) %collective-permute-start.17) | collective-permute-done | bytes 1048608 | tf_op jit(solution)/shard_map/ppermute | solution.py:157
  95.7 3.2 %collective-permute-start.22 = (bf16[4,32,4096]{2,1,0:T(8,128)(2,1)}, bf16[4,32,4096]{2,1,0:T(8,128)(2,1)}, u32[]{:S(2)}, u32[]{:S(2)}) collective-permute-start(bf16[4,32,4096]{2,1,0:T(8,128)(2,1)} %collective-permute-done.20.refs_13_), channel_id=1, source_target_pairs={{0,96},{32,0},{64,32},{96,64},{1,97},{33,1},{65,33},{97,65},{2,98}... | collective-permute-start | bytes 3145736 | tf_op jit(solution)/shard_map/ppermute | solution.py:157
  101.4 15.2 %collective-permute-done.21.refs_14_ = bf16[4,32,4096]{2,1,0:T(8,128)(2,1)} collective-permute-done((bf16[4,32,4096]{2,1,0:T(8,128)(2,1)}, bf16[4,32,4096]{2,1,0:T(8,128)(2,1)}, u32[]{:S(2)}, u32[]{:S(2)}) %collective-permute-start.21) | collective-permute-done | bytes 1048608 | tf_op jit(solution)/shard_map/ppermute | solution.py:157
  116.7 12.7 %aggregate.1 = (bf16[4,2,1024,128]{3,2,1,0:T(8,128)(2,1)}, bf16[2,4,1024,128]{3,2,1,0:T(8,128)(2,1)}, bf16[4,2,1024,128]{3,2,1,0:T(8,128)(2,1)}, bf16[2,4,1024,128]{3,2,1,0:T(8,128)(2,1)}) custom-call(s32[384]{0:T(512)} %reduce.rows_ref, s32[384]{0:T(512)} %reduce.1.cols_ref, s32[6]{0:T(128)} %stack.65.info_ref, bf16[384,128,128]{2,1,0:T(8,128)(2,1)} %bitcast.76, ...), custom_call_target="tpu_custom_call" | custom-call | tf_op jit(solution)/shard_map/aggregate/pallas_call | solution.py:125
  129.4 6.3 %collective-permute-start.23 = (bf16[2,4,1024,128]{3,2,1,0:T(8,128)(2,1)}, bf16[2,4,1024,128]{3,2,1,0:T(8,128)(2,1)S(1)}, u32[]{:S(2)}, u32[]{:S(2)}) collective-permute-start(bf16[2,4,1024,128]{3,2,1,0:T(8,128)(2,1)} %get-tuple-element.49), channel_id=1, source_target_pairs={{0,4},{4,0},{1,5},{5,1},{2,6},{6,2},{3,7},{7,3},{8,12},{12,8},{9,1... | collective-permute-start | bytes 6291464 | tf_op jit(solution)/shard_map/ppermute | solution.py:152
  135.6 4.0 %collective-permute-done.23 = bf16[2,4,1024,128]{3,2,1,0:T(8,128)(2,1)S(1)} collective-permute-done((bf16[2,4,1024,128]{3,2,1,0:T(8,128)(2,1)}, bf16[2,4,1024,128]{3,2,1,0:T(8,128)(2,1)S(1)}, u32[]{:S(2)}, u32[]{:S(2)}) %collective-permute-start.23) | collective-permute-done | bytes 2097184 | tf_op jit(solution)/shard_map/ppermute | solution.py:152
  141.5 2.6 %collective-permute-start.29 = (bf16[4,1024,128]{2,1,0:T(8,128)(2,1)S(1)}, bf16[4,1024,128]{2,1,0:T(8,128)(2,1)S(1)}, u32[]{:S(2)}, u32[]{:S(2)}) collective-permute-start(bf16[4,1024,128]{2,1,0:T(8,128)(2,1)S(1)} %fusion.2), channel_id=1, source_target_pairs={{0,8},{8,0},{1,9},{9,1},{2,10},{10,2},{3,11},{11,3},{4,12},{12,4},... | collective-permute-start | bytes 3145736 | tf_op jit(solution)/shard_map/ppermute | solution.py:152
  145.6 7.5 %collective-permute-start.27 = (bf16[2,1024,128]{2,1,0:T(8,128)(2,1)S(1)}, bf16[2,1024,128]{2,1,0:T(8,128)(2,1)S(1)}, u32[]{:S(2)}, u32[]{:S(2)}) collective-permute-start(bf16[2,1024,128]{2,1,0:T(8,128)(2,1)S(1)} %get-tuple-element.57), channel_id=1, source_target_pairs={{0,3},{1,0},{2,1},{3,2},{4,7},{5,4},{6,5},{7,6},{8,11},{9,8},{10,9... | collective-permute-start | bytes 1572872 | tf_op jit(solution)/shard_map/ppermute | solution.py:157
  154.5 13.1 %collective-permute-done.29 = bf16[4,1024,128]{2,1,0:T(8,128)(2,1)S(1)} collective-permute-done((bf16[4,1024,128]{2,1,0:T(8,128)(2,1)S(1)}, bf16[4,1024,128]{2,1,0:T(8,128)(2,1)S(1)}, u32[]{:S(2)}, u32[]{:S(2)}) %collective-permute-start.29) | collective-permute-done | bytes 1048608 | tf_op jit(solution)/shard_map/ppermute | solution.py:152
  168.5 7.5 %collective-permute-start.32 = (bf16[1024,128]{1,0:T(8,128)(2,1)S(1)}, bf16[1024,128]{1,0:T(8,128)(2,1)S(1)}, u32[]{:S(2)}, u32[]{:S(2)}) collective-permute-start(bf16[1024,128]{1,0:T(8,128)(2,1)S(1)} %get-tuple-element.54), channel_id=1, source_target_pairs={{0,3},{1,0},{2,1},{3,2},{4,7},{5,4},{6,5},{7,6},{8,11},{9,8},{10,9... | collective-permute-start | bytes 786440 | tf_op jit(solution)/shard_map/ppermute | solution.py:157
  179.7 4.8 %collective-permute-done.30 = bf16[1024,128]{1,0:T(8,128)(2,1)S(1)} collective-permute-done((bf16[1024,128]{1,0:T(8,128)(2,1)S(1)}, bf16[1024,128]{1,0:T(8,128)(2,1)S(1)}, u32[]{:S(2)}, u32[]{:S(2)}) %collective-permute-start.30) | collective-permute-done | bytes 262176 | tf_op jit(solution)/shard_map/ppermute | solution.py:157
  184.6 2.5 %collective-permute-done.32 = bf16[1024,128]{1,0:T(8,128)(2,1)S(1)} collective-permute-done((bf16[1024,128]{1,0:T(8,128)(2,1)S(1)}, bf16[1024,128]{1,0:T(8,128)(2,1)S(1)}, u32[]{:S(2)}, u32[]{:S(2)}) %collective-permute-start.32) | collective-permute-done | bytes 262176 | tf_op jit(solution)/shard_map/ppermute | solution.py:157
  187.1 1.8 collective-permute-done.31
  (82 shorter events, 26.2 us)
Async XLA Ops:
  0.0 15.4 %collective-permute-start.2 = (bf16[32,8192]{1,0:T(8,128)(2,1)}, bf16[32,8192]{1,0:T(8,128)(2,1)S(1)}, u32[]{:S(2)}, u32[]{:S(2)}) collective-permute-start(bf16[32,8192]{1,0:T(8,128)(2,1)} %bitcast.77), channel_id=1, source_target_pairs={{0,16},{16,0},{1,17},{17,1},{2,18},{18,2},{3,19},{19,3},{4,20},{20... | collective-permute-start | bytes 1572872 | tf_op jit(solution)/shard_map/ppermute | solution.py:152
  4.4 10.1 %collective-permute-start.1 = (bf16[32,4096]{1,0:T(8,128)(2,1)S(1)}, bf16[32,4096]{1,0:T(8,128)(2,1)S(1)}, u32[]{:S(2)}, u32[]{:S(2)}) collective-permute-start(bf16[32,4096]{1,0:T(8,128)(2,1)S(1)} %get-tuple-element.31), channel_id=1, source_target_pairs={{0,32},{32,64},{64,96},{96,0},{1,33},{33,65},{65,97},{97,1},{2,34}... | collective-permute-start | bytes 786440 | tf_op jit(solution)/shard_map/ppermute | solution.py:157
  6.4 8.1 %collective-permute-start = (bf16[32,4096]{1,0:T(8,128)(2,1)S(1)}, bf16[32,4096]{1,0:T(8,128)(2,1)S(1)}, u32[]{:S(2)}, u32[]{:S(2)}) collective-permute-start(bf16[32,4096]{1,0:T(8,128)(2,1)S(1)} %get-tuple-element.31), channel_id=1, source_target_pairs={{0,96},{32,0},{64,32},{96,64},{1,97},{33,1},{65,33},{97,65},{2,98}... | collective-permute-start | bytes 786440 | tf_op jit(solution)/shard_map/ppermute | solution.py:157
  8.6 8.7 %collective-permute-start.5 = (bf16[32,4096]{1,0:T(8,128)(2,1)S(1)}, bf16[32,4096]{1,0:T(8,128)(2,1)S(1)}, u32[]{:S(2)}, u32[]{:S(2)}) collective-permute-start(bf16[32,4096]{1,0:T(8,128)(2,1)S(1)} %get-tuple-element.35), channel_id=1, source_target_pairs={{0,1},{1,2},{2,3},{3,0},{4,5},{5,6},{6,7},{7,4},{8,9},{9,10},{10,1... | collective-permute-start | bytes 786440 | tf_op jit(solution)/shard_map/ppermute | solution.py:157
  10.1 7.2 %collective-permute-start.4 = (bf16[32,4096]{1,0:T(8,128)(2,1)S(1)}, bf16[32,4096]{1,0:T(8,128)(2,1)S(1)}, u32[]{:S(2)}, u32[]{:S(2)}) collective-permute-start(bf16[32,4096]{1,0:T(8,128)(2,1)S(1)} %get-tuple-element.35), channel_id=1, source_target_pairs={{0,3},{1,0},{2,1},{3,2},{4,7},{5,4},{6,5},{7,6},{8,11},{9,8},{10,9... | collective-permute-start | bytes 786440 | tf_op jit(solution)/shard_map/ppermute | solution.py:157
  17.3 8.1 %collective-permute-start.6 = (bf16[32,4096]{1,0:T(8,128)(2,1)S(1)}, bf16[32,4096]{1,0:T(8,128)(2,1)S(1)}, u32[]{:S(2)}, u32[]{:S(2)}) collective-permute-start(bf16[32,4096]{1,0:T(8,128)(2,1)S(1)} %get-tuple-element.35), channel_id=1, source_target_pairs={{0,2},{1,3},{2,0},{3,1},{4,6},{5,7},{6,4},{7,5},{8,10},{9,11},{10,... | collective-permute-start | bytes 786440 | tf_op jit(solution)/shard_map/ppermute | solution.py:157
  20.0 7.9 %collective-permute-start.3 = (bf16[32,4096]{1,0:T(8,128)(2,1)S(1)}, bf16[32,4096]{1,0:T(8,128)(2,1)S(1)}, u32[]{:S(2)}, u32[]{:S(2)}) collective-permute-start(bf16[32,4096]{1,0:T(8,128)(2,1)S(1)} %get-tuple-element.31), channel_id=1, source_target_pairs={{0,64},{32,96},{64,0},{96,32},{1,65},{33,97},{65,1},{97,33},{2,66}... | collective-permute-start | bytes 786440 | tf_op jit(solution)/shard_map/ppermute | solution.py:157
  22.5 8.6 %collective-permute-start.8 = (bf16[32,4096]{1,0:T(8,128)(2,1)S(1)}, bf16[32,4096]{1,0:T(8,128)(2,1)S(1)}, u32[]{:S(2)}, u32[]{:S(2)}) collective-permute-start(bf16[32,4096]{1,0:T(8,128)(2,1)S(1)} %get-tuple-element.61), channel_id=1, source_target_pairs={{0,3},{1,0},{2,1},{3,2},{4,7},{5,4},{6,5},{7,6},{8,11},{9,8},{10,9... | collective-permute-start | bytes 786440 | tf_op jit(solution)/shard_map/ppermute | solution.py:157
  23.7 10.3 %collective-permute-start.7 = (bf16[32,4096]{1,0:T(8,128)(2,1)S(1)}, bf16[32,4096]{1,0:T(8,128)(2,1)S(1)}, u32[]{:S(2)}, u32[]{:S(2)}) collective-permute-start(bf16[32,4096]{1,0:T(8,128)(2,1)S(1)} %get-tuple-element.62), channel_id=1, source_target_pairs={{0,96},{32,0},{64,32},{96,64},{1,97},{33,1},{65,33},{97,65},{2,98}... | collective-permute-start | bytes 786440 | tf_op jit(solution)/shard_map/ppermute | solution.py:157
  34.0 14.2 %collective-permute-start.10 = (bf16[2,32,4096]{2,1,0:T(8,128)(2,1)S(1)}, bf16[2,32,4096]{2,1,0:T(8,128)(2,1)S(1)}, u32[]{:S(2)}, u32[]{:S(2)}) collective-permute-start(bf16[2,32,4096]{2,1,0:T(8,128)(2,1)S(1)} %slice.98), channel_id=1, source_target_pairs={{0,16},{16,0},{1,17},{17,1},{2,18},{18,2},{3,19},{19,3},{4,20},{20... | collective-permute-start | bytes 1572872 | tf_op jit(solution)/shard_map/ppermute | solution.py:152
  37.2 25.2 %collective-permute-start.12 = (bf16[4,32,4096]{2,1,0:T(8,128)(2,1)S(1)}, bf16[4,32,4096]{2,1,0:T(8,128)(2,1)S(1)}, u32[]{:S(2)}, u32[]{:S(2)}) collective-permute-start(bf16[4,32,4096]{2,1,0:T(8,128)(2,1)S(1)} %pad_maximum_fusion.refs_0_), channel_id=1, source_target_pairs={{0,3},{1,0},{2,1},{3,2},{4,7},{5,4},{6,5},{7,6},{8,11},{9,8},{10,9... | collective-permute-start | bytes 3145736 | tf_op jit(solution)/shard_map/ppermute | solution.py:157
  38.4 24.7 %collective-permute-start.11 = (bf16[4,32,4096]{2,1,0:T(8,128)(2,1)S(1)}, bf16[4,32,4096]{2,1,0:T(8,128)(2,1)S(1)}, u32[]{:S(2)}, u32[]{:S(2)}) collective-permute-start(bf16[4,32,4096]{2,1,0:T(8,128)(2,1)S(1)} %pad_maximum_fusion.refs_0_), channel_id=1, source_target_pairs={{0,1},{1,2},{2,3},{3,0},{4,5},{5,6},{6,7},{7,4},{8,9},{9,10},{10,1... | collective-permute-start | bytes 3145736 | tf_op jit(solution)/shard_map/ppermute | solution.py:157
  39.3 24.2 %collective-permute-start.14 = (bf16[4,32,4096]{2,1,0:T(8,128)(2,1)S(1)}, bf16[4,32,4096]{2,1,0:T(8,128)(2,1)S(1)}, u32[]{:S(2)}, u32[]{:S(2)}) collective-permute-start(bf16[4,32,4096]{2,1,0:T(8,128)(2,1)S(1)} %pad_maximum_fusion.1.refs_8_), channel_id=1, source_target_pairs={{0,96},{32,0},{64,32},{96,64},{1,97},{33,1},{65,33},{97,65},{2,98}... | collective-permute-start | bytes 3145736 | tf_op jit(solution)/shard_map/ppermute | solution.py:157
  41.9 25.1 %collective-permute-start.13 = (bf16[4,32,4096]{2,1,0:T(8,128)(2,1)S(1)}, bf16[4,32,4096]{2,1,0:T(8,128)(2,1)}, u32[]{:S(2)}, u32[]{:S(2)}) collective-permute-start(bf16[4,32,4096]{2,1,0:T(8,128)(2,1)S(1)} %pad_maximum_fusion.1.refs_8_), channel_id=1, source_target_pairs={{0,32},{32,64},{64,96},{96,0},{1,33},{33,65},{65,97},{97,1},{2,34}... | collective-permute-start | bytes 3145736 | tf_op jit(solution)/shard_map/ppermute | solution.py:157
  48.1 13.2 %collective-permute-start.9 = (bf16[2,32,4096]{2,1,0:T(8,128)(2,1)S(1)}, bf16[2,32,4096]{2,1,0:T(8,128)(2,1)S(1)}, u32[]{:S(2)}, u32[]{:S(2)}) collective-permute-start(bf16[2,32,4096]{2,1,0:T(8,128)(2,1)S(1)} %slice.97), channel_id=1, source_target_pairs={{0,16},{16,0},{1,17},{17,1},{2,18},{18,2},{3,19},{19,3},{4,20},{20... | collective-permute-start | bytes 1572872 | tf_op jit(solution)/shard_map/ppermute | solution.py:152
  67.0 27.3 %collective-permute-start.17 = (bf16[4,32,4096]{2,1,0:T(8,128)(2,1)S(1)}, bf16[4,32,4096]{2,1,0:T(8,128)(2,1)S(1)}, u32[]{:S(2)}, u32[]{:S(2)}) collective-permute-start(bf16[4,32,4096]{2,1,0:T(8,128)(2,1)S(1)} %collective-permute-done.11.refs_2_), channel_id=1, source_target_pairs={{0,1},{1,2},{2,3},{3,0},{4,5},{5,6},{6,7},{7,4},{8,9},{9,10},{10,1... | collective-permute-start | bytes 3145736 | tf_op jit(solution)/shard_map/ppermute | solution.py:157
  67.3 26.9 %collective-permute-start.16 = (bf16[4,32,4096]{2,1,0:T(8,128)(2,1)}, bf16[4,32,4096]{2,1,0:T(8,128)(2,1)S(1)}, u32[]{:S(2)}, u32[]{:S(2)}) collective-permute-start(bf16[4,32,4096]{2,1,0:T(8,128)(2,1)} %pad_maximum_fusion.2.refs_1_), channel_id=1, source_target_pairs={{0,3},{1,0},{2,1},{3,2},{4,7},{5,4},{6,5},{7,6},{8,11},{9,8},{10,9... | collective-permute-start | bytes 3145736 | tf_op jit(solution)/shard_map/ppermute | solution.py:157
  70.2 25.5 %collective-permute-start.20 = (bf16[4,32,4096]{2,1,0:T(8,128)(2,1)S(1)}, bf16[4,32,4096]{2,1,0:T(8,128)(2,1)}, u32[]{:S(2)}, u32[]{:S(2)}) collective-permute-start(bf16[4,32,4096]{2,1,0:T(8,128)(2,1)S(1)} %pad_maximum_fusion.3.refs_9_), channel_id=1, source_target_pairs={{0,96},{32,0},{64,32},{96,64},{1,97},{33,1},{65,33},{97,65},{2,98}... | collective-permute-start | bytes 3145736 | tf_op jit(solution)/shard_map/ppermute | solution.py:157
  70.5 46.1 %collective-permute-start.15 = (bf16[4,32,4096]{2,1,0:T(8,128)(2,1)}, bf16[4,32,4096]{2,1,0:T(8,128)(2,1)}, u32[]{:S(2)}, u32[]{:S(2)}) collective-permute-start(bf16[4,32,4096]{2,1,0:T(8,128)(2,1)} %pad_maximum_fusion.2.refs_1_), channel_id=1, source_target_pairs={{0,1},{1,2},{2,3},{3,0},{4,5},{5,6},{6,7},{7,4},{8,9},{9,10},{10,1... | collective-permute-start | bytes 3145736 | tf_op jit(solution)/shard_map/ppermute | solution.py:157
  70.5 46.1 %collective-permute-start.19 = (bf16[4,32,4096]{2,1,0:T(8,128)(2,1)S(1)}, bf16[4,32,4096]{2,1,0:T(8,128)(2,1)}, u32[]{:S(2)}, u32[]{:S(2)}) collective-permute-start(bf16[4,32,4096]{2,1,0:T(8,128)(2,1)S(1)} %pad_maximum_fusion.3.refs_9_), channel_id=1, source_target_pairs={{0,32},{32,64},{64,96},{96,0},{1,33},{33,65},{65,97},{97,1},{2,34}... | collective-permute-start | bytes 3145736 | tf_op jit(solution)/shard_map/ppermute | solution.py:157
  94.3 22.3 %collective-permute-start.21 = (bf16[4,32,4096]{2,1,0:T(8,128)(2,1)}, bf16[4,32,4096]{2,1,0:T(8,128)(2,1)}, u32[]{:S(2)}, u32[]{:S(2)}) collective-permute-start(bf16[4,32,4096]{2,1,0:T(8,128)(2,1)} %collective-permute-done.13.refs_10_), channel_id=1, source_target_pairs={{0,32},{32,64},{64,96},{96,0},{1,33},{33,65},{65,97},{97,1},{2,34}... | collective-permute-start | bytes 3145736 | tf_op jit(solution)/shard_map/ppermute | solution.py:157
  94.3 22.3 %collective-permute-start.18 = (bf16[4,32,4096]{2,1,0:T(8,128)(2,1)S(1)}, bf16[4,32,4096]{2,1,0:T(8,128)(2,1)}, u32[]{:S(2)}, u32[]{:S(2)}) collective-permute-start(bf16[4,32,4096]{2,1,0:T(8,128)(2,1)S(1)} %collective-permute-done.16.refs_5_), channel_id=1, source_target_pairs={{0,3},{1,0},{2,1},{3,2},{4,7},{5,4},{6,5},{7,6},{8,11},{9,8},{10,9... | collective-permute-start | bytes 3145736 | tf_op jit(solution)/shard_map/ppermute | solution.py:157
  95.7 20.9 %collective-permute-start.22 = (bf16[4,32,4096]{2,1,0:T(8,128)(2,1)}, bf16[4,32,4096]{2,1,0:T(8,128)(2,1)}, u32[]{:S(2)}, u32[]{:S(2)}) collective-permute-start(bf16[4,32,4096]{2,1,0:T(8,128)(2,1)} %collective-permute-done.20.refs_13_), channel_id=1, source_target_pairs={{0,96},{32,0},{64,32},{96,64},{1,97},{33,1},{65,33},{97,65},{2,98}... | collective-permute-start | bytes 3145736 | tf_op jit(solution)/shard_map/ppermute | solution.py:157
  129.4 10.3 %collective-permute-start.23 = (bf16[2,4,1024,128]{3,2,1,0:T(8,128)(2,1)}, bf16[2,4,1024,128]{3,2,1,0:T(8,128)(2,1)S(1)}, u32[]{:S(2)}, u32[]{:S(2)}) collective-permute-start(bf16[2,4,1024,128]{3,2,1,0:T(8,128)(2,1)} %get-tuple-element.49), channel_id=1, source_target_pairs={{0,4},{4,0},{1,5},{5,1},{2,6},{6,2},{3,7},{7,3},{8,12},{12,8},{9,1... | collective-permute-start | bytes 6291464 | tf_op jit(solution)/shard_map/ppermute | solution.py:152
  141.5 26.0 %collective-permute-start.29 = (bf16[4,1024,128]{2,1,0:T(8,128)(2,1)S(1)}, bf16[4,1024,128]{2,1,0:T(8,128)(2,1)S(1)}, u32[]{:S(2)}, u32[]{:S(2)}) collective-permute-start(bf16[4,1024,128]{2,1,0:T(8,128)(2,1)S(1)} %fusion.2), channel_id=1, source_target_pairs={{0,8},{8,0},{1,9},{9,1},{2,10},{10,2},{3,11},{11,3},{4,12},{12,4},... | collective-permute-start | bytes 3145736 | tf_op jit(solution)/shard_map/ppermute | solution.py:152
  144.5 31.4 %collective-permute-start.25 = (bf16[2,1024,128]{2,1,0:T(8,128)(2,1)S(1)}, bf16[2,1024,128]{2,1,0:T(8,128)(2,1)S(1)}, u32[]{:S(2)}, u32[]{:S(2)}) collective-permute-start(bf16[2,1024,128]{2,1,0:T(8,128)(2,1)S(1)} %get-tuple-element.56), channel_id=1, source_target_pairs={{0,1},{1,2},{2,3},{3,0},{4,5},{5,6},{6,7},{7,4},{8,9},{9,10},{10,1... | collective-permute-start | bytes 1572872 | tf_op jit(solution)/shard_map/ppermute | solution.py:157
  145.6 31.7 %collective-permute-start.27 = (bf16[2,1024,128]{2,1,0:T(8,128)(2,1)S(1)}, bf16[2,1024,128]{2,1,0:T(8,128)(2,1)S(1)}, u32[]{:S(2)}, u32[]{:S(2)}) collective-permute-start(bf16[2,1024,128]{2,1,0:T(8,128)(2,1)S(1)} %get-tuple-element.57), channel_id=1, source_target_pairs={{0,3},{1,0},{2,1},{3,2},{4,7},{5,4},{6,5},{7,6},{8,11},{9,8},{10,9... | collective-permute-start | bytes 1572872 | tf_op jit(solution)/shard_map/ppermute | solution.py:157
  153.1 24.7 %collective-permute-start.26 = (bf16[2,1024,128]{2,1,0:T(8,128)(2,1)S(1)}, bf16[2,1024,128]{2,1,0:T(8,128)(2,1)S(1)}, u32[]{:S(2)}, u32[]{:S(2)}) collective-permute-start(bf16[2,1024,128]{2,1,0:T(8,128)(2,1)S(1)} %get-tuple-element.58), channel_id=1, source_target_pairs={{0,2},{1,3},{2,0},{3,1},{4,6},{5,7},{6,4},{7,5},{8,10},{9,11},{10,... | collective-permute-start | bytes 1572872 | tf_op jit(solution)/shard_map/ppermute | solution.py:157
  167.9 16.7 %collective-permute-start.30 = (bf16[1024,128]{1,0:T(8,128)(2,1)S(1)}, bf16[1024,128]{1,0:T(8,128)(2,1)S(1)}, u32[]{:S(2)}, u32[]{:S(2)}) collective-permute-start(bf16[1024,128]{1,0:T(8,128)(2,1)S(1)} %get-tuple-element.53), channel_id=1, source_target_pairs={{0,1},{1,2},{2,3},{3,0},{4,5},{5,6},{6,7},{7,4},{8,9},{9,10},{10,1... | collective-permute-start | bytes 786440 | tf_op jit(solution)/shard_map/ppermute | solution.py:157
  168.5 18.5 %collective-permute-start.32 = (bf16[1024,128]{1,0:T(8,128)(2,1)S(1)}, bf16[1024,128]{1,0:T(8,128)(2,1)S(1)}, u32[]{:S(2)}, u32[]{:S(2)}) collective-permute-start(bf16[1024,128]{1,0:T(8,128)(2,1)S(1)} %get-tuple-element.54), channel_id=1, source_target_pairs={{0,3},{1,0},{2,1},{3,2},{4,7},{5,4},{6,5},{7,6},{8,11},{9,8},{10,9... | collective-permute-start | bytes 786440 | tf_op jit(solution)/shard_map/ppermute | solution.py:157
  176.0 12.9 %collective-permute-start.31 = (bf16[1024,128]{1,0:T(8,128)(2,1)S(1)}, bf16[1024,128]{1,0:T(8,128)(2,1)S(1)}, u32[]{:S(2)}, u32[]{:S(2)}) collective-permute-start(bf16[1024,128]{1,0:T(8,128)(2,1)S(1)} %get-tuple-element.55), channel_id=1, source_target_pairs={{0,2},{1,3},{2,0},{3,1},{4,6},{5,7},{6,4},{7,5},{8,10},{9,11},{10,... | collective-permute-start | bytes 786440 | tf_op jit(solution)/shard_map/ppermute | solution.py:157
  178.1 11.0 %collective-permute-start.28 = (bf16[1024,128]{1,0:T(8,128)(2,1)S(1)}, bf16[1024,128]{1,0:T(8,128)(2,1)S(1)}, u32[]{:S(2)}, u32[]{:S(2)}) collective-permute-start(bf16[1024,128]{1,0:T(8,128)(2,1)S(1)} %fusion.20), channel_id=1, source_target_pairs={{0,8},{8,0},{1,9},{9,1},{2,10},{10,2},{3,11},{11,3},{4,12},{12,4},... | collective-permute-start | bytes 786440 | tf_op jit(solution)/shard_map/ppermute | solution.py:152
  (15 other events, 594.3 us)

commit v12 on v10

--- a/solution.py
+++ b/solution.py
@@ -11,6 +11,7 @@
 LOAD = 32
 STEPS_AT_ONCE = (16, 4, 1)
 PACK = 256
+SPLIT = 28
 FIRST_X = 1024
 NT = (((1,), (1,)), ((), ()))
 NAMES = ("rz", "ry", "cy", "cc", "fx")
@@ -177,37 +178,44 @@
     return jnp.stack([value, after, before, shift(again, axis, 2)])
 
 
-def ring_of_other(value, axis, own):
-    return jnp.concatenate([jnp.stack([value, shift(value, axis, -1)]), swap(own[2:], "ry")])
-
-
 def gather_sources(x):
-    half = x.shape[1] // 2
+    half = SPLIT * 128
     other = swap(x, "ry")
     a_own, b_own = ring(x[:, :half], "rz"), ring(x[:, half:], "fx")
     a_own, b_own = tie((a_own, b_own))
     a_near = shift(a_own, "fx", 1), shift(a_own, "fx", -1)
     b_near = shift(b_own, "rz", 1), shift(b_own, "rz", -1)
-    a_other = ring_of_other(other[:, :half], "rz", a_own)
-    b_other = ring_of_other(other[:, half:], "fx", b_own)
+    a_cross, b_half = tie((swap(a_own[2:], "ry"), b_own[2:]))
+    b_cross = swap(b_half, "ry")
+    a_other = jnp.concatenate([jnp.stack([other[:, :half], shift(other[:, :half], "rz", -1)]), a_cross])
+    b_other = jnp.concatenate([jnp.stack([other[:, half:], shift(other[:, half:], "fx", -1)]), b_cross])
     a_other, b_other, a_near, b_near = tie((a_other, b_other, a_near, b_near))
+    a_before, a_after = shift(a_other, "fx", 1), shift(a_other, "fx", -1)
+    b_before, b_after = swap(b_near[0], "ry"), shift(b_other, "rz", -1)
     parts = []
-    for own, other, near, axis, first in (
-        (a_own, a_other, a_near, "fx", 0),
-        (b_own, b_other, b_near, "rz", half),
+    for value, y, far in (
+        (a_own, 0, 0),
+        (a_other, 1, 0),
+        (a_near[0], 0, -1),
+        (a_near[1], 0, 1),
+        (a_before, 1, -1),
+        (a_after, 1, 1),
+        (shift(a_near[0], "fx", 1), 0, 2),
+        (shift(a_after, "fx", -1), 1, 2),
     ):
-        before, after = shift(other, axis, 1), shift(other, axis, -1)
-        for value, y, far in (
-            (own, 0, 0),
-            (other, 1, 0),
-            (near[0], 0, -1),
-            (near[1], 0, 1),
-            (before, 1, -1),
-            (after, 1, 1),
-            (shift(near[0], axis, 1), 0, 2),
-            (shift(after, axis, -1), 1, 2),
-        ):
-            parts.append((value, first, [(d, y, far) if axis == "fx" else (far, y, d) for d in STEPS]))
+        parts.append((value, 0, [(d, y, far) for d in STEPS]))
+    for value, y, far, near in (
+        (b_own, 0, 0, STEPS),
+        (b_other, 1, 0, STEPS),
+        (b_near[0], 0, -1, STEPS),
+        (b_near[1], 0, 1, STEPS),
+        (b_before, 1, -1, STEPS),
+        (b_after, 1, 1, STEPS),
+        (shift(b_near[0], "rz", 1), 0, 2, STEPS),
+        (shift(b_before[:2], "rz", 1), 1, 2, STEPS[:2]),
+        (shift(b_after[2:], "rz", -1), 1, 2, STEPS[2:]),
+    ):
+        parts.append((value, half, [(far, y, d) for d in near]))
     return parts
 
 

time: 182 us -> 184 us (1.011); the launches traced: 181 us -> 185 us
  Pallas kernels: 18.9 us -> 15 us
  waiting for transfers between devices: 89.9 us -> 93.1 us
  local copies, waits for them, and re-layouts: 2.08 us -> 4.61 us
  starting transfers between devices: 62.1 us -> 64.2 us
    pallas_call x1, Pallas kernels: 18.9 us -> 15 us  [aggregate(): pl.pallas_call(functools.partial(aggregate_kernel, where, len(arrays)), o...]
    ppermute x7 -> x8, waiting for transfers between devices: 34.1 us -> 37.4 us  [swap(): return lax.ppermute(value, axis, [(0, 1), (1, 0)])]
    ppermute x26, starting transfers between devices: 44.7 us -> 47.6 us  [shift(): return lax.ppermute(value, axis, [(i, (i + by) % n) for i in range(n)])]
    ppermute x7 -> x8, starting transfers between devices: 17.3 us -> 16.6 us  [swap(): return lax.ppermute(value, axis, [(0, 1), (1, 0)])]
  transfers between devices with their start and end apart: 33 -> 34, of which waited for: 14 -> 19; matrix products, arithmetic and copies ran while one was open for 3% -> 5% of each run, Pallas kernels for 0% -> 0%
where the time goes in v12:
time: 184 us; the launch traced here: 185 us
  waiting for transfers between devices  93.1 us (51%)
  starting transfers between devices  64.2 us (35%)
  Pallas kernels  15 us (8%)
  other arithmetic  5.41 us (3%)
  local copies, waits for them, and re-layouts  4.61 us (3%)
    ppermute x26, waiting for transfers between devices, shift(): return lax.ppermute(value, axis, [(i, (i + by) % n) for i in range(n)])  55.8 us
    ppermute x26, starting transfers between devices, shift(): return lax.ppermute(value, axis, [(i, (i + by) % n) for i in range(n)])  47.6 us
    ppermute x8, waiting for transfers between devices, swap(): return lax.ppermute(value, axis, [(0, 1), (1, 0)])  37.4 us
    ppermute x8, starting transfers between devices, swap(): return lax.ppermute(value, axis, [(0, 1), (1, 0)])  16.6 us
    pallas_call x1, Pallas kernels, aggregate(): pl.pallas_call(functools.partial(aggregate_kernel, where, len(arrays)), o...  15 us
  transfers between devices with their start and end apart: 34, of which 19 were waited for; matrix products, arithmetic and copies ran while one was open for 5% of the time, Pallas kernels for 0%

profile of v12, /device:TPU:0, one launch (start us, length us, event | category | flops | bytes accessed | tf_op | source)
XLA Modules:
  0.0 184.7 jit_solution(2226381756929050418)
XLA Ops:
  1.0 2.1 %collective-permute-start.1 = (bf16[32,3584]{1,0:T(8,128)(2,1)S(1)}, bf16[32,3584]{1,0:T(8,128)(2,1)S(1)}, u32[]{:S(2)}, u32[]{:S(2)}) collective-permute-start(bf16[32,3584]{1,0:T(8,128)(2,1)S(1)} %get-tuple-element.29), channel_id=1, source_target_pairs={{0,32},{32,64},{64,96},{96,0},{1,33},{33,65},{65,97},{97,1},{2,34}... | collective-permute-start | bytes 688136 | tf_op jit(solution)/shard_map/ppermute | solution.py:158
  3.1 2.2 %collective-permute-start = (bf16[32,3584]{1,0:T(8,128)(2,1)S(1)}, bf16[32,3584]{1,0:T(8,128)(2,1)S(1)}, u32[]{:S(2)}, u32[]{:S(2)}) collective-permute-start(bf16[32,3584]{1,0:T(8,128)(2,1)S(1)} %get-tuple-element.29), channel_id=1, source_target_pairs={{0,96},{32,0},{64,32},{96,64},{1,97},{33,1},{65,33},{97,65},{2,98}... | collective-permute-start | bytes 688136 | tf_op jit(solution)/shard_map/ppermute | solution.py:158
  6.3 1.6 collective-permute-start.4
  7.8 1.7 collective-permute-start.3
  10.8 2.9 %collective-permute-start.2 = (bf16[32,3584]{1,0:T(8,128)(2,1)S(1)}, bf16[32,3584]{1,0:T(8,128)(2,1)S(1)}, u32[]{:S(2)}, u32[]{:S(2)}) collective-permute-start(bf16[32,3584]{1,0:T(8,128)(2,1)S(1)} %get-tuple-element.29), channel_id=1, source_target_pairs={{0,64},{32,96},{64,0},{96,32},{1,65},{33,97},{65,1},{97,33},{2,66}... | collective-permute-start | bytes 688136 | tf_op jit(solution)/shard_map/ppermute | solution.py:158
  13.7 3.2 %collective-permute-start.6 = (bf16[32,8192]{1,0:T(8,128)(2,1)}, bf16[32,8192]{1,0:T(8,128)(2,1)S(1)}, u32[]{:S(2)}, u32[]{:S(2)}) collective-permute-start(bf16[32,8192]{1,0:T(8,128)(2,1)} %bitcast.79), channel_id=1, source_target_pairs={{0,16},{16,0},{1,17},{17,1},{2,18},{18,2},{3,19},{19,3},{4,20},{20... | collective-permute-start | bytes 1572872 | tf_op jit(solution)/shard_map/ppermute | solution.py:153
  16.9 3.0 %collective-permute-start.5 = (bf16[32,4608]{1,0:T(8,128)(2,1)S(1)}, bf16[32,4608]{1,0:T(8,128)(2,1)S(1)}, u32[]{:S(2)}, u32[]{:S(2)}) collective-permute-start(bf16[32,4608]{1,0:T(8,128)(2,1)S(1)} %get-tuple-element.32), channel_id=1, source_target_pairs={{0,2},{1,3},{2,0},{3,1},{4,6},{5,7},{6,4},{7,5},{8,10},{9,11},{10,... | collective-permute-start | bytes 884744 | tf_op jit(solution)/shard_map/ppermute | solution.py:158
  20.1 7.5 %collective-permute-done.6 = bf16[32,8192]{1,0:T(8,128)(2,1)S(1)} collective-permute-done((bf16[32,8192]{1,0:T(8,128)(2,1)}, bf16[32,8192]{1,0:T(8,128)(2,1)S(1)}, u32[]{:S(2)}, u32[]{:S(2)}) %collective-permute-start.6) | collective-permute-done | bytes 524320 | tf_op jit(solution)/shard_map/ppermute | solution.py:153
  27.7 2.8 %collective-permute-start.9 = (bf16[32,4608]{1,0:T(8,128)(2,1)S(1)}, bf16[32,4608]{1,0:T(8,128)(2,1)S(1)}, u32[]{:S(2)}, u32[]{:S(2)}) collective-permute-start(bf16[32,4608]{1,0:T(8,128)(2,1)S(1)} %get-tuple-element.56), channel_id=1, source_target_pairs={{0,3},{1,0},{2,1},{3,2},{4,7},{5,4},{6,5},{7,6},{8,11},{9,8},{10,9... | collective-permute-start | bytes 884744 | tf_op jit(solution)/shard_map/ppermute | solution.py:158
  30.7 3.3 %collective-permute-start.8 = (bf16[2,32,3584]{2,1,0:T(8,128)(2,1)S(1)}, bf16[2,32,3584]{2,1,0:T(8,128)(2,1)S(1)}, u32[]{:S(2)}, u32[]{:S(2)}) collective-permute-start(bf16[2,32,3584]{2,1,0:T(8,128)(2,1)S(1)} %slice.102), channel_id=1, source_target_pairs={{0,16},{16,0},{1,17},{17,1},{2,18},{18,2},{3,19},{19,3},{4,20},{20... | collective-permute-start | bytes 1376264 | tf_op jit(solution)/shard_map/ppermute | solution.py:153
  35.1 6.7 %collective-permute-done.8 = bf16[2,32,3584]{2,1,0:T(8,128)(2,1)S(1)} collective-permute-done((bf16[2,32,3584]{2,1,0:T(8,128)(2,1)S(1)}, bf16[2,32,3584]{2,1,0:T(8,128)(2,1)S(1)}, u32[]{:S(2)}, u32[]{:S(2)}) %collective-permute-start.8) | collective-permute-done | bytes 458784 | tf_op jit(solution)/shard_map/ppermute | solution.py:153
  41.9 3.2 %collective-permute-start.10 = (bf16[2,32,4608]{2,1,0:T(8,128)(2,1)S(1)}, bf16[2,32,4608]{2,1,0:T(8,128)(2,1)S(1)}, u32[]{:S(2)}, u32[]{:S(2)}) collective-permute-start(bf16[2,32,4608]{2,1,0:T(8,128)(2,1)S(1)} %slice.103), channel_id=1, source_target_pairs={{0,16},{16,0},{1,17},{17,1},{2,18},{18,2},{3,19},{19,3},{4,20},{20... | collective-permute-start | bytes 1769480 | tf_op jit(solution)/shard_map/ppermute | solution.py:153
  50.2 4.7 %collective-permute-done.10 = bf16[2,32,4608]{2,1,0:T(8,128)(2,1)S(1)} collective-permute-done((bf16[2,32,4608]{2,1,0:T(8,128)(2,1)S(1)}, bf16[2,32,4608]{2,1,0:T(8,128)(2,1)S(1)}, u32[]{:S(2)}, u32[]{:S(2)}) %collective-permute-start.10) | collective-permute-done | bytes 589856 | tf_op jit(solution)/shard_map/ppermute | solution.py:153
  55.0 9.9 %collective-permute-done.12.refs_3_ = bf16[4,32,3584]{2,1,0:T(8,128)(2,1)S(1)} collective-permute-done((bf16[4,32,3584]{2,1,0:T(8,128)(2,1)S(1)}, bf16[4,32,3584]{2,1,0:T(8,128)(2,1)S(1)}, u32[]{:S(2)}, u32[]{:S(2)}) %collective-permute-start.12) | collective-permute-done | bytes 917536 | tf_op jit(solution)/shard_map/ppermute | solution.py:158
  64.9 1.8 collective-permute-done.11.refs_2_
  66.7 3.1 %collective-permute-done.14.refs_11_ = bf16[4,32,4608]{2,1,0:T(8,128)(2,1)S(1)} collective-permute-done((bf16[4,32,4608]{2,1,0:T(8,128)(2,1)S(1)}, bf16[4,32,4608]{2,1,0:T(8,128)(2,1)S(1)}, u32[]{:S(2)}, u32[]{:S(2)}) %collective-permute-start.14) | collective-permute-done | bytes 1179680 | tf_op jit(solution)/shard_map/ppermute | solution.py:158
  75.3 14.1 %collective-permute-done.16.refs_5_ = bf16[4,32,3584]{2,1,0:T(8,128)(2,1)S(1)} collective-permute-done((bf16[4,32,3584]{2,1,0:T(8,128)(2,1)}, bf16[4,32,3584]{2,1,0:T(8,128)(2,1)S(1)}, u32[]{:S(2)}, u32[]{:S(2)}) %collective-permute-start.16) | collective-permute-done | bytes 917536 | tf_op jit(solution)/shard_map/ppermute | solution.py:158
  89.4 5.5 %collective-permute-done.20.refs_13_ = bf16[4,32,4608]{2,1,0:T(8,128)(2,1)S(1)} collective-permute-done((bf16[4,32,4608]{2,1,0:T(8,128)(2,1)S(1)}, bf16[4,32,4608]{2,1,0:T(8,128)(2,1)S(1)}, u32[]{:S(2)}, u32[]{:S(2)}) %collective-permute-start.20) | collective-permute-done | bytes 1179680 | tf_op jit(solution)/shard_map/ppermute | solution.py:158
  99.1 1.8 collective-permute-start.22
  103.5 7.3 %collective-permute-done.15.refs_4_ = bf16[4,32,3584]{2,1,0:T(8,128)(2,1)} collective-permute-done((bf16[4,32,3584]{2,1,0:T(8,128)(2,1)}, bf16[4,32,3584]{2,1,0:T(8,128)(2,1)}, u32[]{:S(2)}, u32[]{:S(2)}) %collective-permute-start.15) | collective-permute-done | bytes 917536 | tf_op jit(solution)/shard_map/ppermute | solution.py:158
  111.5 15.0 %aggregate.1 = (bf16[4,2,1024,128]{3,2,1,0:T(8,128)(2,1)}, bf16[2,4,1024,128]{3,2,1,0:T(8,128)(2,1)}, bf16[4,2,1024,128]{3,2,1,0:T(8,128)(2,1)}, bf16[2,4,1024,128]{3,2,1,0:T(8,128)(2,1)}) custom-call(s32[384]{0:T(512)} %reduce.rows_ref, s32[384]{0:T(512)} %reduce.1.cols_ref, s32[6]{0:T(128)} %stack.65.info_ref, bf16[384,128,128]{2,1,0:T(8,128)(2,1)} %bitcast.76, ...), custom_call_target="tpu_custom_call" | custom-call | tf_op jit(solution)/shard_map/aggregate/pallas_call | solution.py:126
  126.6 4.4 %collective-permute-done.24 = bf16[2,4,1024,128]{3,2,1,0:T(8,128)(2,1)S(1)} collective-permute-done((bf16[2,4,1024,128]{3,2,1,0:T(8,128)(2,1)}, bf16[2,4,1024,128]{3,2,1,0:T(8,128)(2,1)S(1)}, u32[]{:S(2)}, u32[]{:S(2)}) %collective-permute-start.24) | collective-permute-done | bytes 2097184 | tf_op jit(solution)/shard_map/ppermute | solution.py:153
  131.1 1.5 fusion.2
  132.6 6.3 %collective-permute-start.30 = (bf16[4,1024,128]{2,1,0:T(8,128)(2,1)S(1)}, bf16[4,1024,128]{2,1,0:T(8,128)(2,1)S(1)}, u32[]{:S(2)}, u32[]{:S(2)}) collective-permute-start(bf16[4,1024,128]{2,1,0:T(8,128)(2,1)S(1)} %fusion.2), channel_id=1, source_target_pairs={{0,8},{8,0},{1,9},{9,1},{2,10},{10,2},{3,11},{11,3},{4,12},{12,4},... | collective-permute-start | bytes 3145736 | tf_op jit(solution)/shard_map/ppermute | solution.py:153
  139.4 7.8 %collective-permute-start.28 = (bf16[2,1024,128]{2,1,0:T(8,128)(2,1)S(1)}, bf16[2,1024,128]{2,1,0:T(8,128)(2,1)S(1)}, u32[]{:S(2)}, u32[]{:S(2)}) collective-permute-start(bf16[2,1024,128]{2,1,0:T(8,128)(2,1)S(1)} %get-tuple-element.53), channel_id=1, source_target_pairs={{0,3},{1,0},{2,1},{3,2},{4,7},{5,4},{6,5},{7,6},{8,11},{9,8},{10,9... | collective-permute-start | bytes 1572872 | tf_op jit(solution)/shard_map/ppermute | solution.py:158
  148.5 13.8 %collective-permute-done.30 = bf16[4,1024,128]{2,1,0:T(8,128)(2,1)S(1)} collective-permute-done((bf16[4,1024,128]{2,1,0:T(8,128)(2,1)S(1)}, bf16[4,1024,128]{2,1,0:T(8,128)(2,1)S(1)}, u32[]{:S(2)}, u32[]{:S(2)}) %collective-permute-start.30) | collective-permute-done | bytes 1048608 | tf_op jit(solution)/shard_map/ppermute | solution.py:153
  162.7 7.3 %collective-permute-start.33 = (bf16[1024,128]{1,0:T(8,128)(2,1)S(1)}, bf16[1024,128]{1,0:T(8,128)(2,1)S(1)}, u32[]{:S(2)}, u32[]{:S(2)}) collective-permute-start(bf16[1024,128]{1,0:T(8,128)(2,1)S(1)} %get-tuple-element.50), channel_id=1, source_target_pairs={{0,3},{1,0},{2,1},{3,2},{4,7},{5,4},{6,5},{7,6},{8,11},{9,8},{10,9... | collective-permute-start | bytes 786440 | tf_op jit(solution)/shard_map/ppermute | solution.py:158
  170.0 1.4 collective-permute-start.32
  172.3 6.3 %collective-permute-done.31 = bf16[1024,128]{1,0:T(8,128)(2,1)S(1)} collective-permute-done((bf16[1024,128]{1,0:T(8,128)(2,1)S(1)}, bf16[1024,128]{1,0:T(8,128)(2,1)S(1)}, u32[]{:S(2)}, u32[]{:S(2)}) %collective-permute-start.31) | collective-permute-done | bytes 262176 | tf_op jit(solution)/shard_map/ppermute | solution.py:158
  178.6 2.5 %collective-permute-done.33 = bf16[1024,128]{1,0:T(8,128)(2,1)S(1)} collective-permute-done((bf16[1024,128]{1,0:T(8,128)(2,1)S(1)}, bf16[1024,128]{1,0:T(8,128)(2,1)S(1)}, u32[]{:S(2)}, u32[]{:S(2)}) %collective-permute-start.33) | collective-permute-done | bytes 262176 | tf_op jit(solution)/shard_map/ppermute | solution.py:158
  181.1 1.8 collective-permute-done.32
  183.3 1.4 fusion.1
  (92 shorter events, 25.9 us)
Async XLA Ops:
  1.0 9.8 %collective-permute-start.1 = (bf16[32,3584]{1,0:T(8,128)(2,1)S(1)}, bf16[32,3584]{1,0:T(8,128)(2,1)S(1)}, u32[]{:S(2)}, u32[]{:S(2)}) collective-permute-start(bf16[32,3584]{1,0:T(8,128)(2,1)S(1)} %get-tuple-element.29), channel_id=1, source_target_pairs={{0,32},{32,64},{64,96},{96,0},{1,33},{33,65},{65,97},{97,1},{2,34}... | collective-permute-start | bytes 688136 | tf_op jit(solution)/shard_map/ppermute | solution.py:158
  6.3 10.6 %collective-permute-start.4 = (bf16[32,4608]{1,0:T(8,128)(2,1)S(1)}, bf16[32,4608]{1,0:T(8,128)(2,1)S(1)}, u32[]{:S(2)}, u32[]{:S(2)}) collective-permute-start(bf16[32,4608]{1,0:T(8,128)(2,1)S(1)} %get-tuple-element.32), channel_id=1, source_target_pairs={{0,1},{1,2},{2,3},{3,0},{4,5},{5,6},{6,7},{7,4},{8,9},{9,10},{10,1... | collective-permute-start | bytes 884744 | tf_op jit(solution)/shard_map/ppermute | solution.py:158
  7.8 9.1 %collective-permute-start.3 = (bf16[32,4608]{1,0:T(8,128)(2,1)S(1)}, bf16[32,4608]{1,0:T(8,128)(2,1)S(1)}, u32[]{:S(2)}, u32[]{:S(2)}) collective-permute-start(bf16[32,4608]{1,0:T(8,128)(2,1)S(1)} %get-tuple-element.32), channel_id=1, source_target_pairs={{0,3},{1,0},{2,1},{3,2},{4,7},{5,4},{6,5},{7,6},{8,11},{9,8},{10,9... | collective-permute-start | bytes 884744 | tf_op jit(solution)/shard_map/ppermute | solution.py:158
  10.8 9.2 %collective-permute-start.2 = (bf16[32,3584]{1,0:T(8,128)(2,1)S(1)}, bf16[32,3584]{1,0:T(8,128)(2,1)S(1)}, u32[]{:S(2)}, u32[]{:S(2)}) collective-permute-start(bf16[32,3584]{1,0:T(8,128)(2,1)S(1)} %get-tuple-element.29), channel_id=1, source_target_pairs={{0,64},{32,96},{64,0},{96,32},{1,65},{33,97},{65,1},{97,33},{2,66}... | collective-permute-start | bytes 688136 | tf_op jit(solution)/shard_map/ppermute | solution.py:158
  13.7 13.9 %collective-permute-start.6 = (bf16[32,8192]{1,0:T(8,128)(2,1)}, bf16[32,8192]{1,0:T(8,128)(2,1)S(1)}, u32[]{:S(2)}, u32[]{:S(2)}) collective-permute-start(bf16[32,8192]{1,0:T(8,128)(2,1)} %bitcast.79), channel_id=1, source_target_pairs={{0,16},{16,0},{1,17},{17,1},{2,18},{18,2},{3,19},{19,3},{4,20},{20... | collective-permute-start | bytes 1572872 | tf_op jit(solution)/shard_map/ppermute | solution.py:153
  16.9 13.6 %collective-permute-start.5 = (bf16[32,4608]{1,0:T(8,128)(2,1)S(1)}, bf16[32,4608]{1,0:T(8,128)(2,1)S(1)}, u32[]{:S(2)}, u32[]{:S(2)}) collective-permute-start(bf16[32,4608]{1,0:T(8,128)(2,1)S(1)} %get-tuple-element.32), channel_id=1, source_target_pairs={{0,2},{1,3},{2,0},{3,1},{4,6},{5,7},{6,4},{7,5},{8,10},{9,11},{10,... | collective-permute-start | bytes 884744 | tf_op jit(solution)/shard_map/ppermute | solution.py:158
  27.7 20.3 %collective-permute-start.9 = (bf16[32,4608]{1,0:T(8,128)(2,1)S(1)}, bf16[32,4608]{1,0:T(8,128)(2,1)S(1)}, u32[]{:S(2)}, u32[]{:S(2)}) collective-permute-start(bf16[32,4608]{1,0:T(8,128)(2,1)S(1)} %get-tuple-element.56), channel_id=1, source_target_pairs={{0,3},{1,0},{2,1},{3,2},{4,7},{5,4},{6,5},{7,6},{8,11},{9,8},{10,9... | collective-permute-start | bytes 884744 | tf_op jit(solution)/shard_map/ppermute | solution.py:158
  30.7 11.2 %collective-permute-start.8 = (bf16[2,32,3584]{2,1,0:T(8,128)(2,1)S(1)}, bf16[2,32,3584]{2,1,0:T(8,128)(2,1)S(1)}, u32[]{:S(2)}, u32[]{:S(2)}) collective-permute-start(bf16[2,32,3584]{2,1,0:T(8,128)(2,1)S(1)} %slice.102), channel_id=1, source_target_pairs={{0,16},{16,0},{1,17},{17,1},{2,18},{18,2},{3,19},{19,3},{4,20},{20... | collective-permute-start | bytes 1376264 | tf_op jit(solution)/shard_map/ppermute | solution.py:153
  34.0 13.1 %collective-permute-start.7 = (bf16[32,3584]{1,0:T(8,128)(2,1)S(1)}, bf16[32,3584]{1,0:T(8,128)(2,1)S(1)}, u32[]{:S(2)}, u32[]{:S(2)}) collective-permute-start(bf16[32,3584]{1,0:T(8,128)(2,1)S(1)} %get-tuple-element.58), channel_id=1, source_target_pairs={{0,96},{32,0},{64,32},{96,64},{1,97},{33,1},{65,33},{97,65},{2,98}... | collective-permute-start | bytes 688136 | tf_op jit(solution)/shard_map/ppermute | solution.py:158
  41.9 13.0 %collective-permute-start.10 = (bf16[2,32,4608]{2,1,0:T(8,128)(2,1)S(1)}, bf16[2,32,4608]{2,1,0:T(8,128)(2,1)S(1)}, u32[]{:S(2)}, u32[]{:S(2)}) collective-permute-start(bf16[2,32,4608]{2,1,0:T(8,128)(2,1)S(1)} %slice.103), channel_id=1, source_target_pairs={{0,16},{16,0},{1,17},{17,1},{2,18},{18,2},{3,19},{19,3},{4,20},{20... | collective-permute-start | bytes 1769480 | tf_op jit(solution)/shard_map/ppermute | solution.py:153
  45.1 24.7 %collective-permute-start.14 = (bf16[4,32,4608]{2,1,0:T(8,128)(2,1)S(1)}, bf16[4,32,4608]{2,1,0:T(8,128)(2,1)S(1)}, u32[]{:S(2)}, u32[]{:S(2)}) collective-permute-start(bf16[4,32,4608]{2,1,0:T(8,128)(2,1)S(1)} %pad_maximum_fusion.refs_8_), channel_id=1, source_target_pairs={{0,96},{32,0},{64,32},{96,64},{1,97},{33,1},{65,33},{97,65},{2,98}... | collective-permute-start | bytes 3538952 | tf_op jit(solution)/shard_map/ppermute | solution.py:158
  46.1 24.9 %collective-permute-start.13 = (bf16[4,32,4608]{2,1,0:T(8,128)(2,1)S(1)}, bf16[4,32,4608]{2,1,0:T(8,128)(2,1)}, u32[]{:S(2)}, u32[]{:S(2)}) collective-permute-start(bf16[4,32,4608]{2,1,0:T(8,128)(2,1)S(1)} %pad_maximum_fusion.refs_8_), channel_id=1, source_target_pairs={{0,32},{32,64},{64,96},{96,0},{1,33},{33,65},{65,97},{97,1},{2,34}... | collective-permute-start | bytes 3538952 | tf_op jit(solution)/shard_map/ppermute | solution.py:158
  47.1 17.8 %collective-permute-start.12 = (bf16[4,32,3584]{2,1,0:T(8,128)(2,1)S(1)}, bf16[4,32,3584]{2,1,0:T(8,128)(2,1)S(1)}, u32[]{:S(2)}, u32[]{:S(2)}) collective-permute-start(bf16[4,32,3584]{2,1,0:T(8,128)(2,1)S(1)} %pad_maximum_fusion.2.refs_0_), channel_id=1, source_target_pairs={{0,3},{1,0},{2,1},{3,2},{4,7},{5,4},{6,5},{7,6},{8,11},{9,8},{10,9... | collective-permute-start | bytes 2752520 | tf_op jit(solution)/shard_map/ppermute | solution.py:158
  47.9 18.8 %collective-permute-start.11 = (bf16[4,32,3584]{2,1,0:T(8,128)(2,1)S(1)}, bf16[4,32,3584]{2,1,0:T(8,128)(2,1)S(1)}, u32[]{:S(2)}, u32[]{:S(2)}) collective-permute-start(bf16[4,32,3584]{2,1,0:T(8,128)(2,1)S(1)} %pad_maximum_fusion.2.refs_0_), channel_id=1, source_target_pairs={{0,1},{1,2},{2,3},{3,0},{4,5},{5,6},{6,7},{7,4},{8,9},{9,10},{10,1... | collective-permute-start | bytes 2752520 | tf_op jit(solution)/shard_map/ppermute | solution.py:158
  71.0 23.9 %collective-permute-start.20 = (bf16[4,32,4608]{2,1,0:T(8,128)(2,1)S(1)}, bf16[4,32,4608]{2,1,0:T(8,128)(2,1)S(1)}, u32[]{:S(2)}, u32[]{:S(2)}) collective-permute-start(bf16[4,32,4608]{2,1,0:T(8,128)(2,1)S(1)} %pad_maximum_fusion.1.refs_9_), channel_id=1, source_target_pairs={{0,96},{32,0},{64,32},{96,64},{1,97},{33,1},{65,33},{97,65},{2,98}... | collective-permute-start | bytes 3538952 | tf_op jit(solution)/shard_map/ppermute | solution.py:158
  71.8 17.6 %collective-permute-start.16 = (bf16[4,32,3584]{2,1,0:T(8,128)(2,1)}, bf16[4,32,3584]{2,1,0:T(8,128)(2,1)S(1)}, u32[]{:S(2)}, u32[]{:S(2)}) collective-permute-start(bf16[4,32,3584]{2,1,0:T(8,128)(2,1)} %pad_maximum_fusion.3.refs_1_), channel_id=1, source_target_pairs={{0,3},{1,0},{2,1},{3,2},{4,7},{5,4},{6,5},{7,6},{8,11},{9,8},{10,9... | collective-permute-start | bytes 2752520 | tf_op jit(solution)/shard_map/ppermute | solution.py:158
  72.7 24.4 %collective-permute-start.19 = (bf16[4,32,4608]{2,1,0:T(8,128)(2,1)}, bf16[4,32,4608]{2,1,0:T(8,128)(2,1)S(1)}, u32[]{:S(2)}, u32[]{:S(2)}) collective-permute-start(bf16[4,32,4608]{2,1,0:T(8,128)(2,1)} %collective-permute-done.13.refs_10_), channel_id=1, source_target_pairs={{0,16},{16,0},{1,17},{17,1},{2,18},{18,2},{3,19},{19,3},{4,20},{20... | collective-permute-start | bytes 3538952 | tf_op jit(solution)/shard_map/ppermute | solution.py:153
  73.0 26.1 %collective-permute-start.17 = (bf16[4,32,3584]{2,1,0:T(8,128)(2,1)S(1)}, bf16[4,32,3584]{2,1,0:T(8,128)(2,1)S(1)}, u32[]{:S(2)}, u32[]{:S(2)}) collective-permute-start(bf16[4,32,3584]{2,1,0:T(8,128)(2,1)S(1)} %collective-permute-done.11.refs_2_), channel_id=1, source_target_pairs={{0,1},{1,2},{2,3},{3,0},{4,5},{5,6},{6,7},{7,4},{8,9},{9,10},{10,1... | collective-permute-start | bytes 2752520 | tf_op jit(solution)/shard_map/ppermute | solution.py:158
  74.2 36.6 %collective-permute-start.21 = (bf16[4,32,4608]{2,1,0:T(8,128)(2,1)}, bf16[4,32,4608]{2,1,0:T(8,128)(2,1)}, u32[]{:S(2)}, u32[]{:S(2)}) collective-permute-start(bf16[4,32,4608]{2,1,0:T(8,128)(2,1)} %collective-permute-done.13.refs_10_), channel_id=1, source_target_pairs={{0,32},{32,64},{64,96},{96,0},{1,33},{33,65},{65,97},{97,1},{2,34}... | collective-permute-start | bytes 3538952 | tf_op jit(solution)/shard_map/ppermute | solution.py:158
  89.4 21.4 %collective-permute-start.15 = (bf16[4,32,3584]{2,1,0:T(8,128)(2,1)}, bf16[4,32,3584]{2,1,0:T(8,128)(2,1)}, u32[]{:S(2)}, u32[]{:S(2)}) collective-permute-start(bf16[4,32,3584]{2,1,0:T(8,128)(2,1)} %pad_maximum_fusion.3.refs_1_), channel_id=1, source_target_pairs={{0,1},{1,2},{2,3},{3,0},{4,5},{5,6},{6,7},{7,4},{8,9},{9,10},{10,1... | collective-permute-start | bytes 2752520 | tf_op jit(solution)/shard_map/ppermute | solution.py:158
  94.9 16.6 %collective-permute-start.18 = (bf16[4,32,3584]{2,1,0:T(8,128)(2,1)S(1)}, bf16[4,32,3584]{2,1,0:T(8,128)(2,1)}, u32[]{:S(2)}, u32[]{:S(2)}) collective-permute-start(bf16[4,32,3584]{2,1,0:T(8,128)(2,1)S(1)} %collective-permute-done.16.refs_5_), channel_id=1, source_target_pairs={{0,3},{1,0},{2,1},{3,2},{4,7},{5,4},{6,5},{7,6},{8,11},{9,8},{10,9... | collective-permute-start | bytes 2752520 | tf_op jit(solution)/shard_map/ppermute | solution.py:158
  97.1 13.7 %collective-permute-start.23 = (bf16[2,32,4608]{2,1,0:T(8,128)(2,1)}, bf16[2,32,4608]{2,1,0:T(8,128)(2,1)}, u32[]{:S(2)}, u32[]{:S(2)}) collective-permute-start(bf16[2,32,4608]{2,1,0:T(8,128)(2,1)} %slice.136), channel_id=1, source_target_pairs={{0,96},{32,0},{64,32},{96,64},{1,97},{33,1},{65,33},{97,65},{2,98}... | collective-permute-start | bytes 1769480 | tf_op jit(solution)/shard_map/ppermute | solution.py:158
  99.1 11.7 %collective-permute-start.22 = (bf16[2,32,4608]{2,1,0:T(8,128)(2,1)}, bf16[2,32,4608]{2,1,0:T(8,128)(2,1)}, u32[]{:S(2)}, u32[]{:S(2)}) collective-permute-start(bf16[2,32,4608]{2,1,0:T(8,128)(2,1)} %slice.135), channel_id=1, source_target_pairs={{0,32},{32,64},{64,96},{96,0},{1,33},{33,65},{65,97},{97,1},{2,34}... | collective-permute-start | bytes 1769480 | tf_op jit(solution)/shard_map/ppermute | solution.py:158
  130.9 8.0 %collective-permute-start.25 = (bf16[4,2,1024,128]{3,2,1,0:T(8,128)(2,1)}, bf16[4,2,1024,128]{3,2,1,0:T(8,128)(2,1)S(1)}, u32[]{:S(2)}, u32[]{:S(2)}) collective-permute-start(bf16[4,2,1024,128]{3,2,1,0:T(8,128)(2,1)} %get-tuple-element.46), channel_id=1, source_target_pairs={{0,4},{4,0},{1,5},{5,1},{2,6},{6,2},{3,7},{7,3},{8,12},{12,8},{9,1... | collective-permute-start | bytes 6291464 | tf_op jit(solution)/shard_map/ppermute | solution.py:153
  132.6 29.8 %collective-permute-start.30 = (bf16[4,1024,128]{2,1,0:T(8,128)(2,1)S(1)}, bf16[4,1024,128]{2,1,0:T(8,128)(2,1)S(1)}, u32[]{:S(2)}, u32[]{:S(2)}) collective-permute-start(bf16[4,1024,128]{2,1,0:T(8,128)(2,1)S(1)} %fusion.2), channel_id=1, source_target_pairs={{0,8},{8,0},{1,9},{9,1},{2,10},{10,2},{3,11},{11,3},{4,12},{12,4},... | collective-permute-start | bytes 3145736 | tf_op jit(solution)/shard_map/ppermute | solution.py:153
  139.3 30.7 %collective-permute-start.26 = (bf16[2,1024,128]{2,1,0:T(8,128)(2,1)S(1)}, bf16[2,1024,128]{2,1,0:T(8,128)(2,1)S(1)}, u32[]{:S(2)}, u32[]{:S(2)}) collective-permute-start(bf16[2,1024,128]{2,1,0:T(8,128)(2,1)S(1)} %get-tuple-element.52), channel_id=1, source_target_pairs={{0,1},{1,2},{2,3},{3,0},{4,5},{5,6},{6,7},{7,4},{8,9},{9,10},{10,1... | collective-permute-start | bytes 1572872 | tf_op jit(solution)/shard_map/ppermute | solution.py:158
  139.4 32.0 %collective-permute-start.28 = (bf16[2,1024,128]{2,1,0:T(8,128)(2,1)S(1)}, bf16[2,1024,128]{2,1,0:T(8,128)(2,1)S(1)}, u32[]{:S(2)}, u32[]{:S(2)}) collective-permute-start(bf16[2,1024,128]{2,1,0:T(8,128)(2,1)S(1)} %get-tuple-element.53), channel_id=1, source_target_pairs={{0,3},{1,0},{2,1},{3,2},{4,7},{5,4},{6,5},{7,6},{8,11},{9,8},{10,9... | collective-permute-start | bytes 1572872 | tf_op jit(solution)/shard_map/ppermute | solution.py:158
  147.1 24.7 %collective-permute-start.27 = (bf16[2,1024,128]{2,1,0:T(8,128)(2,1)S(1)}, bf16[2,1024,128]{2,1,0:T(8,128)(2,1)S(1)}, u32[]{:S(2)}, u32[]{:S(2)}) collective-permute-start(bf16[2,1024,128]{2,1,0:T(8,128)(2,1)S(1)} %get-tuple-element.54), channel_id=1, source_target_pairs={{0,2},{1,3},{2,0},{3,1},{4,6},{5,7},{6,4},{7,5},{8,10},{9,11},{10,... | collective-permute-start | bytes 1572872 | tf_op jit(solution)/shard_map/ppermute | solution.py:158
  162.7 15.9 %collective-permute-start.31 = (bf16[1024,128]{1,0:T(8,128)(2,1)S(1)}, bf16[1024,128]{1,0:T(8,128)(2,1)S(1)}, u32[]{:S(2)}, u32[]{:S(2)}) collective-permute-start(bf16[1024,128]{1,0:T(8,128)(2,1)S(1)} %get-tuple-element.49), channel_id=1, source_target_pairs={{0,1},{1,2},{2,3},{3,0},{4,5},{5,6},{6,7},{7,4},{8,9},{9,10},{10,1... | collective-permute-start | bytes 786440 | tf_op jit(solution)/shard_map/ppermute | solution.py:158
  162.7 18.4 %collective-permute-start.33 = (bf16[1024,128]{1,0:T(8,128)(2,1)S(1)}, bf16[1024,128]{1,0:T(8,128)(2,1)S(1)}, u32[]{:S(2)}, u32[]{:S(2)}) collective-permute-start(bf16[1024,128]{1,0:T(8,128)(2,1)S(1)} %get-tuple-element.50), channel_id=1, source_target_pairs={{0,3},{1,0},{2,1},{3,2},{4,7},{5,4},{6,5},{7,6},{8,11},{9,8},{10,9... | collective-permute-start | bytes 786440 | tf_op jit(solution)/shard_map/ppermute | solution.py:158
  170.0 12.9 %collective-permute-start.32 = (bf16[1024,128]{1,0:T(8,128)(2,1)S(1)}, bf16[1024,128]{1,0:T(8,128)(2,1)S(1)}, u32[]{:S(2)}, u32[]{:S(2)}) collective-permute-start(bf16[1024,128]{1,0:T(8,128)(2,1)S(1)} %get-tuple-element.51), channel_id=1, source_target_pairs={{0,2},{1,3},{2,0},{3,1},{4,6},{5,7},{6,4},{7,5},{8,10},{9,11},{10,... | collective-permute-start | bytes 786440 | tf_op jit(solution)/shard_map/ppermute | solution.py:158
  172.2 11.0 %collective-permute-start.29 = (bf16[1024,128]{1,0:T(8,128)(2,1)S(1)}, bf16[1024,128]{1,0:T(8,128)(2,1)S(1)}, u32[]{:S(2)}, u32[]{:S(2)}) collective-permute-start(bf16[1024,128]{1,0:T(8,128)(2,1)S(1)} %fusion.20), channel_id=1, source_target_pairs={{0,8},{8,0},{1,9},{9,1},{2,10},{10,2},{3,11},{11,3},{4,12},{12,4},... | collective-permute-start | bytes 786440 | tf_op jit(solution)/shard_map/ppermute | solution.py:153
  (18 other events, 579.8 us)

commit v13 on v12

--- a/solution.py
+++ b/solution.py
@@ -185,10 +185,12 @@
     a_own, b_own = tie((a_own, b_own))
     a_near = shift(a_own, "fx", 1), shift(a_own, "fx", -1)
     b_near = shift(b_own, "rz", 1), shift(b_own, "rz", -1)
-    a_cross, b_half = tie((swap(a_own[2:], "ry"), b_own[2:]))
-    b_cross = swap(b_half, "ry")
-    a_other = jnp.concatenate([jnp.stack([other[:, :half], shift(other[:, :half], "rz", -1)]), a_cross])
-    b_other = jnp.concatenate([jnp.stack([other[:, half:], shift(other[:, half:], "fx", -1)]), b_cross])
+    a_other = jnp.concatenate(
+        [jnp.stack([other[:, :half], shift(other[:, :half], "rz", -1)]), swap(a_own[2:], "ry")]
+    )
+    b_other = jnp.concatenate(
+        [jnp.stack([other[:, half:], shift(other[:, half:], "fx", -1)]), swap(b_own[2:], "ry")]
+    )
     a_other, b_other, a_near, b_near = tie((a_other, b_other, a_near, b_near))
     a_before, a_after = shift(a_other, "fx", 1), shift(a_other, "fx", -1)
     b_before, b_after = swap(b_near[0], "ry"), shift(b_other, "rz", -1)

time: 184 us -> 178 us (0.967)
  waiting for transfers between devices: 93.1 us -> 78.2 us
  starting transfers between devices: 64.2 us -> 74.9 us
  Pallas kernels: 15 us -> 12.9 us
    ppermute x26, starting transfers between devices: 47.6 us -> 60.3 us  [shift(): return lax.ppermute(value, axis, [(i, (i + by) % n) for i in range(n)])]
    ppermute x26, waiting for transfers between devices: 55.8 us -> 48.2 us  [shift(): return lax.ppermute(value, axis, [(i, (i + by) % n) for i in range(n)])]
    ppermute x8, waiting for transfers between devices: 37.4 us -> 30 us  [swap(): return lax.ppermute(value, axis, [(0, 1), (1, 0)])]
    pallas_call x1, Pallas kernels: 15 us -> 12.9 us  [aggregate(): pl.pallas_call(functools.partial(aggregate_kernel, where, len(arrays)), o...]
    ppermute x8, starting transfers between devices: 16.6 us -> 14.6 us  [swap(): return lax.ppermute(value, axis, [(0, 1), (1, 0)])]
  transfers between devices with their start and end apart: 34 -> 34, of which waited for: 19 -> 16; matrix products, arithmetic and copies ran while one was open for 5% -> 5% of each run, Pallas kernels for 0% -> 0%
where the time goes in v13:
time: 178 us
  waiting for transfers between devices  78.2 us (44%)
  starting transfers between devices  74.9 us (42%)
  Pallas kernels  12.9 us (7%)
  other arithmetic  5.41 us (3%)
  local copies, waits for them, and re-layouts  4.72 us (3%)
    ppermute x26, starting transfers between devices, shift(): return lax.ppermute(value, axis, [(i, (i + by) % n) for i in range(n)])  60.3 us
    ppermute x26, waiting for transfers between devices, shift(): return lax.ppermute(value, axis, [(i, (i + by) % n) for i in range(n)])  48.2 us
    ppermute x8, waiting for transfers between devices, swap(): return lax.ppermute(value, axis, [(0, 1), (1, 0)])  30 us
    ppermute x8, starting transfers between devices, swap(): return lax.ppermute(value, axis, [(0, 1), (1, 0)])  14.6 us
    pallas_call x1, Pallas kernels, aggregate(): pl.pallas_call(functools.partial(aggregate_kernel, where, len(arrays)), o...  12.9 us
  transfers between devices with their start and end apart: 34, of which 16 were waited for; matrix products, arithmetic and copies ran while one was open for 5% of the time, Pallas kernels for 0%

profile of v13, /device:TPU:0, one launch (start us, length us, event | category | flops | bytes accessed | tf_op | source)
XLA Modules:
  0.0 178.4 jit_solution(3874291948301160039)
XLA Ops:
  1.0 2.1 %collective-permute-start.1 = (bf16[32,3584]{1,0:T(8,128)(2,1)S(1)}, bf16[32,3584]{1,0:T(8,128)(2,1)S(1)}, u32[]{:S(2)}, u32[]{:S(2)}) collective-permute-start(bf16[32,3584]{1,0:T(8,128)(2,1)S(1)} %get-tuple-element.27), channel_id=1, source_target_pairs={{0,32},{32,64},{64,96},{96,0},{1,33},{33,65},{65,97},{97,1},{2,34}... | collective-permute-start | bytes 688136 | tf_op jit(solution)/shard_map/ppermute | solution.py:158
  3.1 2.2 %collective-permute-start = (bf16[32,3584]{1,0:T(8,128)(2,1)S(1)}, bf16[32,3584]{1,0:T(8,128)(2,1)S(1)}, u32[]{:S(2)}, u32[]{:S(2)}) collective-permute-start(bf16[32,3584]{1,0:T(8,128)(2,1)S(1)} %get-tuple-element.27), channel_id=1, source_target_pairs={{0,96},{32,0},{64,32},{96,64},{1,97},{33,1},{65,33},{97,65},{2,98}... | collective-permute-start | bytes 688136 | tf_op jit(solution)/shard_map/ppermute | solution.py:158
  6.3 1.6 collective-permute-start.4
  7.8 1.7 collective-permute-start.3
  10.8 2.9 %collective-permute-start.2 = (bf16[32,3584]{1,0:T(8,128)(2,1)S(1)}, bf16[32,3584]{1,0:T(8,128)(2,1)S(1)}, u32[]{:S(2)}, u32[]{:S(2)}) collective-permute-start(bf16[32,3584]{1,0:T(8,128)(2,1)S(1)} %get-tuple-element.27), channel_id=1, source_target_pairs={{0,64},{32,96},{64,0},{96,32},{1,65},{33,97},{65,1},{97,33},{2,66}... | collective-permute-start | bytes 688136 | tf_op jit(solution)/shard_map/ppermute | solution.py:158
  13.7 3.2 %collective-permute-start.6 = (bf16[32,8192]{1,0:T(8,128)(2,1)}, bf16[32,8192]{1,0:T(8,128)(2,1)S(1)}, u32[]{:S(2)}, u32[]{:S(2)}) collective-permute-start(bf16[32,8192]{1,0:T(8,128)(2,1)} %bitcast.79), channel_id=1, source_target_pairs={{0,16},{16,0},{1,17},{17,1},{2,18},{18,2},{3,19},{19,3},{4,20},{20... | collective-permute-start | bytes 1572872 | tf_op jit(solution)/shard_map/ppermute | solution.py:153
  16.9 3.0 %collective-permute-start.5 = (bf16[32,4608]{1,0:T(8,128)(2,1)S(1)}, bf16[32,4608]{1,0:T(8,128)(2,1)S(1)}, u32[]{:S(2)}, u32[]{:S(2)}) collective-permute-start(bf16[32,4608]{1,0:T(8,128)(2,1)S(1)} %get-tuple-element.30), channel_id=1, source_target_pairs={{0,2},{1,3},{2,0},{3,1},{4,6},{5,7},{6,4},{7,5},{8,10},{9,11},{10,... | collective-permute-start | bytes 884744 | tf_op jit(solution)/shard_map/ppermute | solution.py:158
  20.1 7.5 %collective-permute-done.6 = bf16[32,8192]{1,0:T(8,128)(2,1)S(1)} collective-permute-done((bf16[32,8192]{1,0:T(8,128)(2,1)}, bf16[32,8192]{1,0:T(8,128)(2,1)S(1)}, u32[]{:S(2)}, u32[]{:S(2)}) %collective-permute-start.6) | collective-permute-done | bytes 524320 | tf_op jit(solution)/shard_map/ppermute | solution.py:153
  28.9 3.3 %collective-permute-start.8 = (bf16[2,32,3584]{2,1,0:T(8,128)(2,1)S(1)}, bf16[2,32,3584]{2,1,0:T(8,128)(2,1)S(1)}, u32[]{:S(2)}, u32[]{:S(2)}) collective-permute-start(bf16[2,32,3584]{2,1,0:T(8,128)(2,1)S(1)} %slice.102), channel_id=1, source_target_pairs={{0,16},{16,0},{1,17},{17,1},{2,18},{18,2},{3,19},{19,3},{4,20},{20... | collective-permute-start | bytes 1376264 | tf_op jit(solution)/shard_map/ppermute | solution.py:153
  32.3 2.8 %collective-permute-start.9 = (bf16[32,4608]{1,0:T(8,128)(2,1)S(1)}, bf16[32,4608]{1,0:T(8,128)(2,1)S(1)}, u32[]{:S(2)}, u32[]{:S(2)}) collective-permute-start(bf16[32,4608]{1,0:T(8,128)(2,1)S(1)} %get-tuple-element.52), channel_id=1, source_target_pairs={{0,3},{1,0},{2,1},{3,2},{4,7},{5,4},{6,5},{7,6},{8,11},{9,8},{10,9... | collective-permute-start | bytes 884744 | tf_op jit(solution)/shard_map/ppermute | solution.py:158
  37.6 2.5 %collective-permute-done.9 = bf16[32,4608]{1,0:T(8,128)(2,1)S(1)} collective-permute-done((bf16[32,4608]{1,0:T(8,128)(2,1)S(1)}, bf16[32,4608]{1,0:T(8,128)(2,1)S(1)}, u32[]{:S(2)}, u32[]{:S(2)}) %collective-permute-start.9) | collective-permute-done | bytes 294944 | tf_op jit(solution)/shard_map/ppermute | solution.py:158
  40.1 3.0 %collective-permute-start.12 = (bf16[4,32,3584]{2,1,0:T(8,128)(2,1)S(1)}, bf16[4,32,3584]{2,1,0:T(8,128)(2,1)S(1)}, u32[]{:S(2)}, u32[]{:S(2)}) collective-permute-start(bf16[4,32,3584]{2,1,0:T(8,128)(2,1)S(1)} %pad_maximum_fusion.2.refs_0_), channel_id=1, source_target_pairs={{0,3},{1,0},{2,1},{3,2},{4,7},{5,4},{6,5},{7,6},{8,11},{9,8},{10,9... | collective-permute-start | bytes 2752520 | tf_op jit(solution)/shard_map/ppermute | solution.py:158
  46.5 6.2 %collective-permute-done.10 = bf16[2,32,4608]{2,1,0:T(8,128)(2,1)S(1)} collective-permute-done((bf16[2,32,4608]{2,1,0:T(8,128)(2,1)S(1)}, bf16[2,32,4608]{2,1,0:T(8,128)(2,1)S(1)}, u32[]{:S(2)}, u32[]{:S(2)}) %collective-permute-start.10) | collective-permute-done | bytes 589856 | tf_op jit(solution)/shard_map/ppermute | solution.py:153
  52.9 6.1 %collective-permute-done.12.refs_3_ = bf16[4,32,3584]{2,1,0:T(8,128)(2,1)S(1)} collective-permute-done((bf16[4,32,3584]{2,1,0:T(8,128)(2,1)S(1)}, bf16[4,32,3584]{2,1,0:T(8,128)(2,1)S(1)}, u32[]{:S(2)}, u32[]{:S(2)}) %collective-permute-start.12) | collective-permute-done | bytes 917536 | tf_op jit(solution)/shard_map/ppermute | solution.py:158
  59.0 3.2 %collective-permute-done.11.refs_2_ = bf16[4,32,3584]{2,1,0:T(8,128)(2,1)S(1)} collective-permute-done((bf16[4,32,3584]{2,1,0:T(8,128)(2,1)S(1)}, bf16[4,32,3584]{2,1,0:T(8,128)(2,1)S(1)}, u32[]{:S(2)}, u32[]{:S(2)}) %collective-permute-start.11) | collective-permute-done | bytes 917536 | tf_op jit(solution)/shard_map/ppermute | solution.py:158
  62.3 1.5 collective-permute-start.20
  64.1 3.1 %collective-permute-start.19 = (bf16[4,32,4608]{2,1,0:T(8,128)(2,1)}, bf16[4,32,4608]{2,1,0:T(8,128)(2,1)S(1)}, u32[]{:S(2)}, u32[]{:S(2)}) collective-permute-start(bf16[4,32,4608]{2,1,0:T(8,128)(2,1)} %collective-permute-done.13.refs_10_), channel_id=1, source_target_pairs={{0,16},{16,0},{1,17},{17,1},{2,18},{18,2},{3,19},{19,3},{4,20},{20... | collective-permute-start | bytes 3538952 | tf_op jit(solution)/shard_map/ppermute | solution.py:153
  69.5 11.2 %collective-permute-done.16.refs_5_ = bf16[4,32,3584]{2,1,0:T(8,128)(2,1)S(1)} collective-permute-done((bf16[4,32,3584]{2,1,0:T(8,128)(2,1)}, bf16[4,32,3584]{2,1,0:T(8,128)(2,1)S(1)}, u32[]{:S(2)}, u32[]{:S(2)}) %collective-permute-start.16) | collective-permute-done | bytes 917536 | tf_op jit(solution)/shard_map/ppermute | solution.py:158
  82.1 3.9 %collective-permute-done.20.refs_13_ = bf16[4,32,4608]{2,1,0:T(8,128)(2,1)S(1)} collective-permute-done((bf16[4,32,4608]{2,1,0:T(8,128)(2,1)S(1)}, bf16[4,32,4608]{2,1,0:T(8,128)(2,1)S(1)}, u32[]{:S(2)}, u32[]{:S(2)}) %collective-permute-start.20) | collective-permute-done | bytes 1179680 | tf_op jit(solution)/shard_map/ppermute | solution.py:158
  87.9 1.9 %collective-permute-done.19.refs_12_ = bf16[4,32,4608]{2,1,0:T(8,128)(2,1)S(1)} collective-permute-done((bf16[4,32,4608]{2,1,0:T(8,128)(2,1)}, bf16[4,32,4608]{2,1,0:T(8,128)(2,1)S(1)}, u32[]{:S(2)}, u32[]{:S(2)}) %collective-permute-start.19) | collective-permute-done | bytes 1179680 | tf_op jit(solution)/shard_map/ppermute | solution.py:153
  95.4 11.0 %collective-permute-done.15.refs_4_ = bf16[4,32,3584]{2,1,0:T(8,128)(2,1)} collective-permute-done((bf16[4,32,3584]{2,1,0:T(8,128)(2,1)}, bf16[4,32,3584]{2,1,0:T(8,128)(2,1)}, u32[]{:S(2)}, u32[]{:S(2)}) %collective-permute-start.15) | collective-permute-done | bytes 917536 | tf_op jit(solution)/shard_map/ppermute | solution.py:158
  106.5 12.9 %aggregate.1 = (bf16[4,2,1024,128]{3,2,1,0:T(8,128)(2,1)}, bf16[2,4,1024,128]{3,2,1,0:T(8,128)(2,1)}, bf16[4,2,1024,128]{3,2,1,0:T(8,128)(2,1)}, bf16[2,4,1024,128]{3,2,1,0:T(8,128)(2,1)}) custom-call(s32[384]{0:T(512)} %reduce.rows_ref, s32[384]{0:T(512)} %reduce.1.cols_ref, s32[6]{0:T(128)} %stack.65.info_ref, bf16[384,128,128]{2,1,0:T(8,128)(2,1)} %bitcast.76, ...), custom_call_target="tpu_custom_call" | custom-call | tf_op jit(solution)/shard_map/aggregate/pallas_call | solution.py:126
  119.5 4.4 %collective-permute-done.24 = bf16[2,4,1024,128]{3,2,1,0:T(8,128)(2,1)S(1)} collective-permute-done((bf16[2,4,1024,128]{3,2,1,0:T(8,128)(2,1)}, bf16[2,4,1024,128]{3,2,1,0:T(8,128)(2,1)S(1)}, u32[]{:S(2)}, u32[]{:S(2)}) %collective-permute-start.24) | collective-permute-done | bytes 2097184 | tf_op jit(solution)/shard_map/ppermute | solution.py:153
  124.0 1.5 fusion.2
  125.5 3.1 %collective-permute-start.30 = (bf16[4,1024,128]{2,1,0:T(8,128)(2,1)S(1)}, bf16[4,1024,128]{2,1,0:T(8,128)(2,1)S(1)}, u32[]{:S(2)}, u32[]{:S(2)}) collective-permute-start(bf16[4,1024,128]{2,1,0:T(8,128)(2,1)S(1)} %fusion.2), channel_id=1, source_target_pairs={{0,8},{8,0},{1,9},{9,1},{2,10},{10,2},{3,11},{11,3},{4,12},{12,4},... | collective-permute-start | bytes 3145736 | tf_op jit(solution)/shard_map/ppermute | solution.py:153
  128.9 10.6 %collective-permute-start.26 = (bf16[2,1024,128]{2,1,0:T(8,128)(2,1)S(1)}, bf16[2,1024,128]{2,1,0:T(8,128)(2,1)S(1)}, u32[]{:S(2)}, u32[]{:S(2)}) collective-permute-start(bf16[2,1024,128]{2,1,0:T(8,128)(2,1)S(1)} %get-tuple-element.48), channel_id=1, source_target_pairs={{0,1},{1,2},{2,3},{3,0},{4,5},{5,6},{6,7},{7,4},{8,9},{9,10},{10,1... | collective-permute-start | bytes 1572872 | tf_op jit(solution)/shard_map/ppermute | solution.py:158
  140.1 3.1 %collective-permute-start.27 = (bf16[2,1024,128]{2,1,0:T(8,128)(2,1)S(1)}, bf16[2,1024,128]{2,1,0:T(8,128)(2,1)S(1)}, u32[]{:S(2)}, u32[]{:S(2)}) collective-permute-start(bf16[2,1024,128]{2,1,0:T(8,128)(2,1)S(1)} %get-tuple-element.50), channel_id=1, source_target_pairs={{0,2},{1,3},{2,0},{3,1},{4,6},{5,7},{6,4},{7,5},{8,10},{9,11},{10,... | collective-permute-start | bytes 1572872 | tf_op jit(solution)/shard_map/ppermute | solution.py:158
  143.2 9.0 %collective-permute-done.30 = bf16[4,1024,128]{2,1,0:T(8,128)(2,1)S(1)} collective-permute-done((bf16[4,1024,128]{2,1,0:T(8,128)(2,1)S(1)}, bf16[4,1024,128]{2,1,0:T(8,128)(2,1)S(1)}, u32[]{:S(2)}, u32[]{:S(2)}) %collective-permute-start.30) | collective-permute-done | bytes 1048608 | tf_op jit(solution)/shard_map/ppermute | solution.py:153
  152.5 9.9 %collective-permute-start.31 = (bf16[1024,128]{1,0:T(8,128)(2,1)S(1)}, bf16[1024,128]{1,0:T(8,128)(2,1)S(1)}, u32[]{:S(2)}, u32[]{:S(2)}) collective-permute-start(bf16[1024,128]{1,0:T(8,128)(2,1)S(1)} %get-tuple-element.45), channel_id=1, source_target_pairs={{0,1},{1,2},{2,3},{3,0},{4,5},{5,6},{6,7},{7,4},{8,9},{9,10},{10,1... | collective-permute-start | bytes 786440 | tf_op jit(solution)/shard_map/ppermute | solution.py:158
  163.7 2.3 %collective-permute-start.32 = (bf16[1024,128]{1,0:T(8,128)(2,1)S(1)}, bf16[1024,128]{1,0:T(8,128)(2,1)S(1)}, u32[]{:S(2)}, u32[]{:S(2)}) collective-permute-start(bf16[1024,128]{1,0:T(8,128)(2,1)S(1)} %get-tuple-element.47), channel_id=1, source_target_pairs={{0,2},{1,3},{2,0},{3,1},{4,6},{5,7},{6,4},{7,5},{8,10},{9,11},{10,... | collective-permute-start | bytes 786440 | tf_op jit(solution)/shard_map/ppermute | solution.py:158
  167.7 2.9 %collective-permute-done.31 = bf16[1024,128]{1,0:T(8,128)(2,1)S(1)} collective-permute-done((bf16[1024,128]{1,0:T(8,128)(2,1)S(1)}, bf16[1024,128]{1,0:T(8,128)(2,1)S(1)}, u32[]{:S(2)}, u32[]{:S(2)}) %collective-permute-start.31) | collective-permute-done | bytes 262176 | tf_op jit(solution)/shard_map/ppermute | solution.py:158
  171.7 5.0 %collective-permute-done.32 = bf16[1024,128]{1,0:T(8,128)(2,1)S(1)} collective-permute-done((bf16[1024,128]{1,0:T(8,128)(2,1)S(1)}, bf16[1024,128]{1,0:T(8,128)(2,1)S(1)}, u32[]{:S(2)}, u32[]{:S(2)}) %collective-permute-start.32) | collective-permute-done | bytes 262176 | tf_op jit(solution)/shard_map/ppermute | solution.py:158
  (92 shorter events, 28.6 us)
Async XLA Ops:
  1.0 9.8 %collective-permute-start.1 = (bf16[32,3584]{1,0:T(8,128)(2,1)S(1)}, bf16[32,3584]{1,0:T(8,128)(2,1)S(1)}, u32[]{:S(2)}, u32[]{:S(2)}) collective-permute-start(bf16[32,3584]{1,0:T(8,128)(2,1)S(1)} %get-tuple-element.27), channel_id=1, source_target_pairs={{0,32},{32,64},{64,96},{96,0},{1,33},{33,65},{65,97},{97,1},{2,34}... | collective-permute-start | bytes 688136 | tf_op jit(solution)/shard_map/ppermute | solution.py:158
  3.1 7.7 %collective-permute-start = (bf16[32,3584]{1,0:T(8,128)(2,1)S(1)}, bf16[32,3584]{1,0:T(8,128)(2,1)S(1)}, u32[]{:S(2)}, u32[]{:S(2)}) collective-permute-start(bf16[32,3584]{1,0:T(8,128)(2,1)S(1)} %get-tuple-element.27), channel_id=1, source_target_pairs={{0,96},{32,0},{64,32},{96,64},{1,97},{33,1},{65,33},{97,65},{2,98}... | collective-permute-start | bytes 688136 | tf_op jit(solution)/shard_map/ppermute | solution.py:158
  6.3 10.6 %collective-permute-start.4 = (bf16[32,4608]{1,0:T(8,128)(2,1)S(1)}, bf16[32,4608]{1,0:T(8,128)(2,1)S(1)}, u32[]{:S(2)}, u32[]{:S(2)}) collective-permute-start(bf16[32,4608]{1,0:T(8,128)(2,1)S(1)} %get-tuple-element.30), channel_id=1, source_target_pairs={{0,1},{1,2},{2,3},{3,0},{4,5},{5,6},{6,7},{7,4},{8,9},{9,10},{10,1... | collective-permute-start | bytes 884744 | tf_op jit(solution)/shard_map/ppermute | solution.py:158
  7.8 9.1 %collective-permute-start.3 = (bf16[32,4608]{1,0:T(8,128)(2,1)S(1)}, bf16[32,4608]{1,0:T(8,128)(2,1)S(1)}, u32[]{:S(2)}, u32[]{:S(2)}) collective-permute-start(bf16[32,4608]{1,0:T(8,128)(2,1)S(1)} %get-tuple-element.30), channel_id=1, source_target_pairs={{0,3},{1,0},{2,1},{3,2},{4,7},{5,4},{6,5},{7,6},{8,11},{9,8},{10,9... | collective-permute-start | bytes 884744 | tf_op jit(solution)/shard_map/ppermute | solution.py:158
  10.8 9.2 %collective-permute-start.2 = (bf16[32,3584]{1,0:T(8,128)(2,1)S(1)}, bf16[32,3584]{1,0:T(8,128)(2,1)S(1)}, u32[]{:S(2)}, u32[]{:S(2)}) collective-permute-start(bf16[32,3584]{1,0:T(8,128)(2,1)S(1)} %get-tuple-element.27), channel_id=1, source_target_pairs={{0,64},{32,96},{64,0},{96,32},{1,65},{33,97},{65,1},{97,33},{2,66}... | collective-permute-start | bytes 688136 | tf_op jit(solution)/shard_map/ppermute | solution.py:158
  13.7 13.9 %collective-permute-start.6 = (bf16[32,8192]{1,0:T(8,128)(2,1)}, bf16[32,8192]{1,0:T(8,128)(2,1)S(1)}, u32[]{:S(2)}, u32[]{:S(2)}) collective-permute-start(bf16[32,8192]{1,0:T(8,128)(2,1)} %bitcast.79), channel_id=1, source_target_pairs={{0,16},{16,0},{1,17},{17,1},{2,18},{18,2},{3,19},{19,3},{4,20},{20... | collective-permute-start | bytes 1572872 | tf_op jit(solution)/shard_map/ppermute | solution.py:153
  16.9 11.8 %collective-permute-start.5 = (bf16[32,4608]{1,0:T(8,128)(2,1)S(1)}, bf16[32,4608]{1,0:T(8,128)(2,1)S(1)}, u32[]{:S(2)}, u32[]{:S(2)}) collective-permute-start(bf16[32,4608]{1,0:T(8,128)(2,1)S(1)} %get-tuple-element.30), channel_id=1, source_target_pairs={{0,2},{1,3},{2,0},{3,1},{4,6},{5,7},{6,4},{7,5},{8,10},{9,11},{10,... | collective-permute-start | bytes 884744 | tf_op jit(solution)/shard_map/ppermute | solution.py:158
  27.7 8.7 %collective-permute-start.7 = (bf16[32,3584]{1,0:T(8,128)(2,1)S(1)}, bf16[32,3584]{1,0:T(8,128)(2,1)S(1)}, u32[]{:S(2)}, u32[]{:S(2)}) collective-permute-start(bf16[32,3584]{1,0:T(8,128)(2,1)S(1)} %get-tuple-element.54), channel_id=1, source_target_pairs={{0,96},{32,0},{64,32},{96,64},{1,97},{33,1},{65,33},{97,65},{2,98}... | collective-permute-start | bytes 688136 | tf_op jit(solution)/shard_map/ppermute | solution.py:158
  28.9 15.0 %collective-permute-start.8 = (bf16[2,32,3584]{2,1,0:T(8,128)(2,1)S(1)}, bf16[2,32,3584]{2,1,0:T(8,128)(2,1)S(1)}, u32[]{:S(2)}, u32[]{:S(2)}) collective-permute-start(bf16[2,32,3584]{2,1,0:T(8,128)(2,1)S(1)} %slice.102), channel_id=1, source_target_pairs={{0,16},{16,0},{1,17},{17,1},{2,18},{18,2},{3,19},{19,3},{4,20},{20... | collective-permute-start | bytes 1376264 | tf_op jit(solution)/shard_map/ppermute | solution.py:153
  32.3 7.8 %collective-permute-start.9 = (bf16[32,4608]{1,0:T(8,128)(2,1)S(1)}, bf16[32,4608]{1,0:T(8,128)(2,1)S(1)}, u32[]{:S(2)}, u32[]{:S(2)}) collective-permute-start(bf16[32,4608]{1,0:T(8,128)(2,1)S(1)} %get-tuple-element.52), channel_id=1, source_target_pairs={{0,3},{1,0},{2,1},{3,2},{4,7},{5,4},{6,5},{7,6},{8,11},{9,8},{10,9... | collective-permute-start | bytes 884744 | tf_op jit(solution)/shard_map/ppermute | solution.py:158
  35.1 17.6 %collective-permute-start.10 = (bf16[2,32,4608]{2,1,0:T(8,128)(2,1)S(1)}, bf16[2,32,4608]{2,1,0:T(8,128)(2,1)S(1)}, u32[]{:S(2)}, u32[]{:S(2)}) collective-permute-start(bf16[2,32,4608]{2,1,0:T(8,128)(2,1)S(1)} %slice.104), channel_id=1, source_target_pairs={{0,16},{16,0},{1,17},{17,1},{2,18},{18,2},{3,19},{19,3},{4,20},{20... | collective-permute-start | bytes 1769480 | tf_op jit(solution)/shard_map/ppermute | solution.py:153
  35.6 26.7 %collective-permute-start.14 = (bf16[4,32,4608]{2,1,0:T(8,128)(2,1)S(1)}, bf16[4,32,4608]{2,1,0:T(8,128)(2,1)S(1)}, u32[]{:S(2)}, u32[]{:S(2)}) collective-permute-start(bf16[4,32,4608]{2,1,0:T(8,128)(2,1)S(1)} %pad_maximum_fusion.refs_8_), channel_id=1, source_target_pairs={{0,96},{32,0},{64,32},{96,64},{1,97},{33,1},{65,33},{97,65},{2,98}... | collective-permute-start | bytes 3538952 | tf_op jit(solution)/shard_map/ppermute | solution.py:158
  36.4 25.9 %collective-permute-start.13 = (bf16[4,32,4608]{2,1,0:T(8,128)(2,1)S(1)}, bf16[4,32,4608]{2,1,0:T(8,128)(2,1)}, u32[]{:S(2)}, u32[]{:S(2)}) collective-permute-start(bf16[4,32,4608]{2,1,0:T(8,128)(2,1)S(1)} %pad_maximum_fusion.refs_8_), channel_id=1, source_target_pairs={{0,32},{32,64},{64,96},{96,0},{1,33},{33,65},{65,97},{97,1},{2,34}... | collective-permute-start | bytes 3538952 | tf_op jit(solution)/shard_map/ppermute | solution.py:158
  40.1 18.9 %collective-permute-start.12 = (bf16[4,32,3584]{2,1,0:T(8,128)(2,1)S(1)}, bf16[4,32,3584]{2,1,0:T(8,128)(2,1)S(1)}, u32[]{:S(2)}, u32[]{:S(2)}) collective-permute-start(bf16[4,32,3584]{2,1,0:T(8,128)(2,1)S(1)} %pad_maximum_fusion.2.refs_0_), channel_id=1, source_target_pairs={{0,3},{1,0},{2,1},{3,2},{4,7},{5,4},{6,5},{7,6},{8,11},{9,8},{10,9... | collective-permute-start | bytes 2752520 | tf_op jit(solution)/shard_map/ppermute | solution.py:158
  44.0 18.3 %collective-permute-start.11 = (bf16[4,32,3584]{2,1,0:T(8,128)(2,1)S(1)}, bf16[4,32,3584]{2,1,0:T(8,128)(2,1)S(1)}, u32[]{:S(2)}, u32[]{:S(2)}) collective-permute-start(bf16[4,32,3584]{2,1,0:T(8,128)(2,1)S(1)} %pad_maximum_fusion.2.refs_0_), channel_id=1, source_target_pairs={{0,1},{1,2},{2,3},{3,0},{4,5},{5,6},{6,7},{7,4},{8,9},{9,10},{10,1... | collective-permute-start | bytes 2752520 | tf_op jit(solution)/shard_map/ppermute | solution.py:158
  62.3 23.6 %collective-permute-start.20 = (bf16[4,32,4608]{2,1,0:T(8,128)(2,1)S(1)}, bf16[4,32,4608]{2,1,0:T(8,128)(2,1)S(1)}, u32[]{:S(2)}, u32[]{:S(2)}) collective-permute-start(bf16[4,32,4608]{2,1,0:T(8,128)(2,1)S(1)} %pad_maximum_fusion.1.refs_9_), channel_id=1, source_target_pairs={{0,96},{32,0},{64,32},{96,64},{1,97},{33,1},{65,33},{97,65},{2,98}... | collective-permute-start | bytes 3538952 | tf_op jit(solution)/shard_map/ppermute | solution.py:158
  63.8 16.9 %collective-permute-start.16 = (bf16[4,32,3584]{2,1,0:T(8,128)(2,1)}, bf16[4,32,3584]{2,1,0:T(8,128)(2,1)S(1)}, u32[]{:S(2)}, u32[]{:S(2)}) collective-permute-start(bf16[4,32,3584]{2,1,0:T(8,128)(2,1)} %pad_maximum_fusion.3.refs_1_), channel_id=1, source_target_pairs={{0,3},{1,0},{2,1},{3,2},{4,7},{5,4},{6,5},{7,6},{8,11},{9,8},{10,9... | collective-permute-start | bytes 2752520 | tf_op jit(solution)/shard_map/ppermute | solution.py:158
  64.1 25.8 %collective-permute-start.19 = (bf16[4,32,4608]{2,1,0:T(8,128)(2,1)}, bf16[4,32,4608]{2,1,0:T(8,128)(2,1)S(1)}, u32[]{:S(2)}, u32[]{:S(2)}) collective-permute-start(bf16[4,32,4608]{2,1,0:T(8,128)(2,1)} %collective-permute-done.13.refs_10_), channel_id=1, source_target_pairs={{0,16},{16,0},{1,17},{17,1},{2,18},{18,2},{3,19},{19,3},{4,20},{20... | collective-permute-start | bytes 3538952 | tf_op jit(solution)/shard_map/ppermute | solution.py:153
  67.2 24.6 %collective-permute-start.17 = (bf16[4,32,3584]{2,1,0:T(8,128)(2,1)S(1)}, bf16[4,32,3584]{2,1,0:T(8,128)(2,1)S(1)}, u32[]{:S(2)}, u32[]{:S(2)}) collective-permute-start(bf16[4,32,3584]{2,1,0:T(8,128)(2,1)S(1)} %collective-permute-done.11.refs_2_), channel_id=1, source_target_pairs={{0,1},{1,2},{2,3},{3,0},{4,5},{5,6},{6,7},{7,4},{8,9},{9,10},{10,1... | collective-permute-start | bytes 2752520 | tf_op jit(solution)/shard_map/ppermute | solution.py:158
  68.0 38.4 %collective-permute-start.21 = (bf16[4,32,4608]{2,1,0:T(8,128)(2,1)}, bf16[4,32,4608]{2,1,0:T(8,128)(2,1)}, u32[]{:S(2)}, u32[]{:S(2)}) collective-permute-start(bf16[4,32,4608]{2,1,0:T(8,128)(2,1)} %collective-permute-done.13.refs_10_), channel_id=1, source_target_pairs={{0,32},{32,64},{64,96},{96,0},{1,33},{33,65},{65,97},{97,1},{2,34}... | collective-permute-start | bytes 3538952 | tf_op jit(solution)/shard_map/ppermute | solution.py:158
  80.7 25.8 %collective-permute-start.15 = (bf16[4,32,3584]{2,1,0:T(8,128)(2,1)}, bf16[4,32,3584]{2,1,0:T(8,128)(2,1)}, u32[]{:S(2)}, u32[]{:S(2)}) collective-permute-start(bf16[4,32,3584]{2,1,0:T(8,128)(2,1)} %pad_maximum_fusion.3.refs_1_), channel_id=1, source_target_pairs={{0,1},{1,2},{2,3},{3,0},{4,5},{5,6},{6,7},{7,4},{8,9},{9,10},{10,1... | collective-permute-start | bytes 2752520 | tf_op jit(solution)/shard_map/ppermute | solution.py:158
  85.9 20.5 %collective-permute-start.18 = (bf16[4,32,3584]{2,1,0:T(8,128)(2,1)S(1)}, bf16[4,32,3584]{2,1,0:T(8,128)(2,1)}, u32[]{:S(2)}, u32[]{:S(2)}) collective-permute-start(bf16[4,32,3584]{2,1,0:T(8,128)(2,1)S(1)} %collective-permute-done.16.refs_5_), channel_id=1, source_target_pairs={{0,3},{1,0},{2,1},{3,2},{4,7},{5,4},{6,5},{7,6},{8,11},{9,8},{10,9... | collective-permute-start | bytes 2752520 | tf_op jit(solution)/shard_map/ppermute | solution.py:158
  89.9 16.6 %collective-permute-start.23 = (bf16[2,32,4608]{2,1,0:T(8,128)(2,1)}, bf16[2,32,4608]{2,1,0:T(8,128)(2,1)}, u32[]{:S(2)}, u32[]{:S(2)}) collective-permute-start(bf16[2,32,4608]{2,1,0:T(8,128)(2,1)} %slice.136), channel_id=1, source_target_pairs={{0,96},{32,0},{64,32},{96,64},{1,97},{33,1},{65,33},{97,65},{2,98}... | collective-permute-start | bytes 1769480 | tf_op jit(solution)/shard_map/ppermute | solution.py:158
  91.8 14.6 %collective-permute-start.22 = (bf16[2,32,4608]{2,1,0:T(8,128)(2,1)}, bf16[2,32,4608]{2,1,0:T(8,128)(2,1)}, u32[]{:S(2)}, u32[]{:S(2)}) collective-permute-start(bf16[2,32,4608]{2,1,0:T(8,128)(2,1)} %slice.135), channel_id=1, source_target_pairs={{0,32},{32,64},{64,96},{96,0},{1,33},{33,65},{65,97},{97,1},{2,34}... | collective-permute-start | bytes 1769480 | tf_op jit(solution)/shard_map/ppermute | solution.py:158
  125.5 26.7 %collective-permute-start.30 = (bf16[4,1024,128]{2,1,0:T(8,128)(2,1)S(1)}, bf16[4,1024,128]{2,1,0:T(8,128)(2,1)S(1)}, u32[]{:S(2)}, u32[]{:S(2)}) collective-permute-start(bf16[4,1024,128]{2,1,0:T(8,128)(2,1)S(1)} %fusion.2), channel_id=1, source_target_pairs={{0,8},{8,0},{1,9},{9,1},{2,10},{10,2},{3,11},{11,3},{4,12},{12,4},... | collective-permute-start | bytes 3145736 | tf_op jit(solution)/shard_map/ppermute | solution.py:153
  128.9 34.7 %collective-permute-start.26 = (bf16[2,1024,128]{2,1,0:T(8,128)(2,1)S(1)}, bf16[2,1024,128]{2,1,0:T(8,128)(2,1)S(1)}, u32[]{:S(2)}, u32[]{:S(2)}) collective-permute-start(bf16[2,1024,128]{2,1,0:T(8,128)(2,1)S(1)} %get-tuple-element.48), channel_id=1, source_target_pairs={{0,1},{1,2},{2,3},{3,0},{4,5},{5,6},{6,7},{7,4},{8,9},{9,10},{10,1... | collective-permute-start | bytes 1572872 | tf_op jit(solution)/shard_map/ppermute | solution.py:158
  139.6 26.4 %collective-permute-start.28 = (bf16[2,1024,128]{2,1,0:T(8,128)(2,1)S(1)}, bf16[2,1024,128]{2,1,0:T(8,128)(2,1)S(1)}, u32[]{:S(2)}, u32[]{:S(2)}) collective-permute-start(bf16[2,1024,128]{2,1,0:T(8,128)(2,1)S(1)} %get-tuple-element.49), channel_id=1, source_target_pairs={{0,3},{1,0},{2,1},{3,2},{4,7},{5,4},{6,5},{7,6},{8,11},{9,8},{10,9... | collective-permute-start | bytes 1572872 | tf_op jit(solution)/shard_map/ppermute | solution.py:158
  140.1 25.9 %collective-permute-start.27 = (bf16[2,1024,128]{2,1,0:T(8,128)(2,1)S(1)}, bf16[2,1024,128]{2,1,0:T(8,128)(2,1)S(1)}, u32[]{:S(2)}, u32[]{:S(2)}) collective-permute-start(bf16[2,1024,128]{2,1,0:T(8,128)(2,1)S(1)} %get-tuple-element.50), channel_id=1, source_target_pairs={{0,2},{1,3},{2,0},{3,1},{4,6},{5,7},{6,4},{7,5},{8,10},{9,11},{10,... | collective-permute-start | bytes 1572872 | tf_op jit(solution)/shard_map/ppermute | solution.py:158
  152.5 18.1 %collective-permute-start.31 = (bf16[1024,128]{1,0:T(8,128)(2,1)S(1)}, bf16[1024,128]{1,0:T(8,128)(2,1)S(1)}, u32[]{:S(2)}, u32[]{:S(2)}) collective-permute-start(bf16[1024,128]{1,0:T(8,128)(2,1)S(1)} %get-tuple-element.45), channel_id=1, source_target_pairs={{0,1},{1,2},{2,3},{3,0},{4,5},{5,6},{6,7},{7,4},{8,9},{9,10},{10,1... | collective-permute-start | bytes 786440 | tf_op jit(solution)/shard_map/ppermute | solution.py:158
  162.5 9.2 %collective-permute-start.33 = (bf16[1024,128]{1,0:T(8,128)(2,1)S(1)}, bf16[1024,128]{1,0:T(8,128)(2,1)S(1)}, u32[]{:S(2)}, u32[]{:S(2)}) collective-permute-start(bf16[1024,128]{1,0:T(8,128)(2,1)S(1)} %get-tuple-element.46), channel_id=1, source_target_pairs={{0,3},{1,0},{2,1},{3,2},{4,7},{5,4},{6,5},{7,6},{8,11},{9,8},{10,9... | collective-permute-start | bytes 786440 | tf_op jit(solution)/shard_map/ppermute | solution.py:158
  163.7 13.0 %collective-permute-start.32 = (bf16[1024,128]{1,0:T(8,128)(2,1)S(1)}, bf16[1024,128]{1,0:T(8,128)(2,1)S(1)}, u32[]{:S(2)}, u32[]{:S(2)}) collective-permute-start(bf16[1024,128]{1,0:T(8,128)(2,1)S(1)} %get-tuple-element.47), channel_id=1, source_target_pairs={{0,2},{1,3},{2,0},{3,1},{4,6},{5,7},{6,4},{7,5},{8,10},{9,11},{10,... | collective-permute-start | bytes 786440 | tf_op jit(solution)/shard_map/ppermute | solution.py:158
  166.4 10.5 %collective-permute-start.29 = (bf16[1024,128]{1,0:T(8,128)(2,1)S(1)}, bf16[1024,128]{1,0:T(8,128)(2,1)S(1)}, u32[]{:S(2)}, u32[]{:S(2)}) collective-permute-start(bf16[1024,128]{1,0:T(8,128)(2,1)S(1)} %fusion.20), channel_id=1, source_target_pairs={{0,8},{8,0},{1,9},{9,1},{2,10},{10,2},{3,11},{11,3},{4,12},{12,4},... | collective-permute-start | bytes 786440 | tf_op jit(solution)/shard_map/ppermute | solution.py:153
  (18 other events, 548.2 us)

commit v14 on v13

--- a/solution.py
+++ b/solution.py
@@ -172,16 +172,15 @@
 STEPS = (0, 1, -1, 2)
 
 
-def ring(value, axis):
-    after, before = (shift(value, axis, -d) for d in STEPS[1:3])
-    again, after, before = tie((value, after, before))
-    return jnp.stack([value, after, before, shift(again, axis, 2)])
+def rings(*pairs):
+    near = tie([(value, *(shift(value, axis, -d) for d in STEPS[1:3])) for value, axis in pairs])
+    return [jnp.stack([*three, shift(three[0], axis, 2)]) for three, (_, axis) in zip(near, pairs)]
 
 
 def gather_sources(x):
     half = SPLIT * 128
     other = swap(x, "ry")
-    a_own, b_own = ring(x[:, :half], "rz"), ring(x[:, half:], "fx")
+    a_own, b_own = rings((x[:, :half], "rz"), (x[:, half:], "fx"))
     a_own, b_own = tie((a_own, b_own))
     a_near = shift(a_own, "fx", 1), shift(a_own, "fx", -1)
     b_near = shift(b_own, "rz", 1), shift(b_own, "rz", -1)

time: 178 us -> 173 us (0.972)
  starting transfers between devices: 74.9 us -> 64.7 us
  waiting for transfers between devices: 78.2 us -> 82.4 us
    ppermute x26, starting transfers between devices: 60.3 us -> 51.2 us  [shift(): return lax.ppermute(value, axis, [(i, (i + by) % n) for i in range(n)])]
    ppermute x26, waiting for transfers between devices: 48.2 us -> 56.8 us  [shift(): return lax.ppermute(value, axis, [(i, (i + by) % n) for i in range(n)])]
    ppermute x8, waiting for transfers between devices: 30 us -> 25.5 us  [swap(): return lax.ppermute(value, axis, [(0, 1), (1, 0)])]
    another operation x2 -> x0, local copies, waits for them, and re-layouts: 2 us -> none  [ring(): return jnp.stack([value, after, before, shift(again, axis, 2)])]
    slice x0 -> x2, local copies, waits for them, and re-layouts: none -> 1.97 us  [gather_sources(): a_own, b_own = rings((x[:, :half], 'rz'), (x[:, half:], 'fx'))]
  transfers between devices with their start and end apart: 34 -> 34, of which waited for: 16 -> 18; matrix products, arithmetic and copies ran while one was open for 5% -> 6% of each run, Pallas kernels for 0% -> 0%
where the time goes in v14:
time: 173 us; the launch traced here: 172 us
  waiting for transfers between devices  82.4 us (48%)
  starting transfers between devices  64.7 us (37%)
  Pallas kernels  12.8 us (7%)
  other arithmetic  5.35 us (3%)
  local copies, waits for them, and re-layouts  4.66 us (3%)
    ppermute x26, waiting for transfers between devices, shift(): return lax.ppermute(value, axis, [(i, (i + by) % n) for i in range(n)])  56.8 us
    ppermute x26, starting transfers between devices, shift(): return lax.ppermute(value, axis, [(i, (i + by) % n) for i in range(n)])  51.2 us
    ppermute x8, waiting for transfers between devices, swap(): return lax.ppermute(value, axis, [(0, 1), (1, 0)])  25.5 us
    ppermute x8, starting transfers between devices, swap(): return lax.ppermute(value, axis, [(0, 1), (1, 0)])  13.5 us
    pallas_call x1, Pallas kernels, aggregate(): pl.pallas_call(functools.partial(aggregate_kernel, where, len(arrays)), o...  12.8 us
  transfers between devices with their start and end apart: 34, of which 18 were waited for; matrix products, arithmetic and copies ran while one was open for 6% of the time, Pallas kernels for 0%

profile of v14, /device:TPU:0, one launch (start us, length us, event | category | flops | bytes accessed | tf_op | source)
XLA Modules:
  0.0 172.2 jit_solution(16907356830319558154)
XLA Ops:
  0.0 3.3 %collective-permute-start.6 = (bf16[32,8192]{1,0:T(8,128)(2,1)}, bf16[32,8192]{1,0:T(8,128)(2,1)S(1)}, u32[]{:S(2)}, u32[]{:S(2)}) collective-permute-start(bf16[32,8192]{1,0:T(8,128)(2,1)} %bitcast.77), channel_id=1, source_target_pairs={{0,16},{16,0},{1,17},{17,1},{2,18},{18,2},{3,19},{19,3},{4,20},{20... | collective-permute-start | bytes 1572872 | tf_op jit(solution)/shard_map/ppermute | solution.py:153
  5.9 1.7 %collective-permute-start.2 = (bf16[32,4608]{1,0:T(8,128)(2,1)S(1)}, bf16[32,4608]{1,0:T(8,128)(2,1)S(1)}, u32[]{:S(2)}, u32[]{:S(2)}) collective-permute-start(bf16[32,4608]{1,0:T(8,128)(2,1)S(1)} %slice.132), channel_id=1, source_target_pairs={{0,3},{1,0},{2,1},{3,2},{4,7},{5,4},{6,5},{7,6},{8,11},{9,8},{10,9... | collective-permute-start | bytes 884744 | tf_op jit(solution)/shard_map/ppermute | solution.py:158
  8.6 2.0 %collective-permute-start.1 = (bf16[32,3584]{1,0:T(8,128)(2,1)S(1)}, bf16[32,3584]{1,0:T(8,128)(2,1)S(1)}, u32[]{:S(2)}, u32[]{:S(2)}) collective-permute-start(bf16[32,3584]{1,0:T(8,128)(2,1)S(1)} %slice.131), channel_id=1, source_target_pairs={{0,32},{32,64},{64,96},{96,0},{1,33},{33,65},{65,97},{97,1},{2,34}... | collective-permute-start | bytes 688136 | tf_op jit(solution)/shard_map/ppermute | solution.py:158
  10.5 2.2 %collective-permute-start = (bf16[32,3584]{1,0:T(8,128)(2,1)S(1)}, bf16[32,3584]{1,0:T(8,128)(2,1)S(1)}, u32[]{:S(2)}, u32[]{:S(2)}) collective-permute-start(bf16[32,3584]{1,0:T(8,128)(2,1)S(1)} %slice.131), channel_id=1, source_target_pairs={{0,96},{32,0},{64,32},{96,64},{1,97},{33,1},{65,33},{97,65},{2,98}... | collective-permute-start | bytes 688136 | tf_op jit(solution)/shard_map/ppermute | solution.py:158
  12.7 4.7 %collective-permute-done.1 = bf16[32,3584]{1,0:T(8,128)(2,1)S(1)} collective-permute-done((bf16[32,3584]{1,0:T(8,128)(2,1)S(1)}, bf16[32,3584]{1,0:T(8,128)(2,1)S(1)}, u32[]{:S(2)}, u32[]{:S(2)}) %collective-permute-start.1) | collective-permute-done | bytes 229408 | tf_op jit(solution)/shard_map/ppermute | solution.py:158
  17.4 2.9 %collective-permute-start.4 = (bf16[32,3584]{1,0:T(8,128)(2,1)S(1)}, bf16[32,3584]{1,0:T(8,128)(2,1)S(1)}, u32[]{:S(2)}, u32[]{:S(2)}) collective-permute-start(bf16[32,3584]{1,0:T(8,128)(2,1)S(1)} %slice.131), channel_id=1, source_target_pairs={{0,64},{32,96},{64,0},{96,32},{1,65},{33,97},{65,1},{97,33},{2,66}... | collective-permute-start | bytes 688136 | tf_op jit(solution)/shard_map/ppermute | solution.py:158
  20.4 1.8 %collective-permute-start.5 = (bf16[32,4608]{1,0:T(8,128)(2,1)S(1)}, bf16[32,4608]{1,0:T(8,128)(2,1)S(1)}, u32[]{:S(2)}, u32[]{:S(2)}) collective-permute-start(bf16[32,4608]{1,0:T(8,128)(2,1)S(1)} %slice.132), channel_id=1, source_target_pairs={{0,2},{1,3},{2,0},{3,1},{4,6},{5,7},{6,4},{7,5},{8,10},{9,11},{10,... | collective-permute-start | bytes 884744 | tf_op jit(solution)/shard_map/ppermute | solution.py:158
  23.3 1.8 %collective-permute-done.4 = bf16[32,3584]{1,0:T(8,128)(2,1)S(1)} collective-permute-done((bf16[32,3584]{1,0:T(8,128)(2,1)S(1)}, bf16[32,3584]{1,0:T(8,128)(2,1)S(1)}, u32[]{:S(2)}, u32[]{:S(2)}) %collective-permute-start.4) | collective-permute-done | bytes 229408 | tf_op jit(solution)/shard_map/ppermute | solution.py:158
  25.2 3.4 %collective-permute-done.5 = bf16[32,4608]{1,0:T(8,128)(2,1)S(1)} collective-permute-done((bf16[32,4608]{1,0:T(8,128)(2,1)S(1)}, bf16[32,4608]{1,0:T(8,128)(2,1)S(1)}, u32[]{:S(2)}, u32[]{:S(2)}) %collective-permute-start.5) | collective-permute-done | bytes 294944 | tf_op jit(solution)/shard_map/ppermute | solution.py:158
  30.9 3.3 %collective-permute-start.10 = (bf16[2,32,4608]{2,1,0:T(8,128)(2,1)S(1)}, bf16[2,32,4608]{2,1,0:T(8,128)(2,1)S(1)}, u32[]{:S(2)}, u32[]{:S(2)}) collective-permute-start(bf16[2,32,4608]{2,1,0:T(8,128)(2,1)S(1)} %slice.104), channel_id=1, source_target_pairs={{0,16},{16,0},{1,17},{17,1},{2,18},{18,2},{3,19},{19,3},{4,20},{20... | collective-permute-start | bytes 1769480 | tf_op jit(solution)/shard_map/ppermute | solution.py:153
  36.2 1.9 %collective-permute-done.9 = bf16[32,4608]{1,0:T(8,128)(2,1)S(1)} collective-permute-done((bf16[32,4608]{1,0:T(8,128)(2,1)S(1)}, bf16[32,4608]{1,0:T(8,128)(2,1)S(1)}, u32[]{:S(2)}, u32[]{:S(2)}) %collective-permute-start.9) | collective-permute-done | bytes 294944 | tf_op jit(solution)/shard_map/ppermute | solution.py:158
  38.1 1.7 collective-permute-start.12
  39.8 4.1 %collective-permute-done.8 = bf16[2,32,3584]{2,1,0:T(8,128)(2,1)S(1)} collective-permute-done((bf16[2,32,3584]{2,1,0:T(8,128)(2,1)S(1)}, bf16[2,32,3584]{2,1,0:T(8,128)(2,1)S(1)}, u32[]{:S(2)}, u32[]{:S(2)}) %collective-permute-start.8) | collective-permute-done | bytes 458784 | tf_op jit(solution)/shard_map/ppermute | solution.py:153
  45.2 6.8 %collective-permute-done.10 = bf16[2,32,4608]{2,1,0:T(8,128)(2,1)S(1)} collective-permute-done((bf16[2,32,4608]{2,1,0:T(8,128)(2,1)S(1)}, bf16[2,32,4608]{2,1,0:T(8,128)(2,1)S(1)}, u32[]{:S(2)}, u32[]{:S(2)}) %collective-permute-start.10) | collective-permute-done | bytes 589856 | tf_op jit(solution)/shard_map/ppermute | solution.py:153
  52.1 3.6 %collective-permute-done.12.refs_3_ = bf16[4,32,3584]{2,1,0:T(8,128)(2,1)S(1)} collective-permute-done((bf16[4,32,3584]{2,1,0:T(8,128)(2,1)S(1)}, bf16[4,32,3584]{2,1,0:T(8,128)(2,1)S(1)}, u32[]{:S(2)}, u32[]{:S(2)}) %collective-permute-start.12) | collective-permute-done | bytes 917536 | tf_op jit(solution)/shard_map/ppermute | solution.py:158
  55.7 2.8 %collective-permute-done.11.refs_2_ = bf16[4,32,3584]{2,1,0:T(8,128)(2,1)S(1)} collective-permute-done((bf16[4,32,3584]{2,1,0:T(8,128)(2,1)S(1)}, bf16[4,32,3584]{2,1,0:T(8,128)(2,1)S(1)}, u32[]{:S(2)}, u32[]{:S(2)}) %collective-permute-start.11) | collective-permute-done | bytes 917536 | tf_op jit(solution)/shard_map/ppermute | solution.py:158
  59.9 1.7 %collective-permute-start.20 = (bf16[4,32,4608]{2,1,0:T(8,128)(2,1)S(1)}, bf16[4,32,4608]{2,1,0:T(8,128)(2,1)S(1)}, u32[]{:S(2)}, u32[]{:S(2)}) collective-permute-start(bf16[4,32,4608]{2,1,0:T(8,128)(2,1)S(1)} %pad_maximum_fusion.1.refs_9_), channel_id=1, source_target_pairs={{0,96},{32,0},{64,32},{96,64},{1,97},{33,1},{65,33},{97,65},{2,98}... | collective-permute-start | bytes 3538952 | tf_op jit(solution)/shard_map/ppermute | solution.py:158
  62.2 1.7 collective-permute-start.19
  64.6 12.3 %collective-permute-done.16.refs_5_ = bf16[4,32,3584]{2,1,0:T(8,128)(2,1)S(1)} collective-permute-done((bf16[4,32,3584]{2,1,0:T(8,128)(2,1)}, bf16[4,32,3584]{2,1,0:T(8,128)(2,1)S(1)}, u32[]{:S(2)}, u32[]{:S(2)}) %collective-permute-start.16) | collective-permute-done | bytes 917536 | tf_op jit(solution)/shard_map/ppermute | solution.py:158
  77.4 7.0 %collective-permute-done.20.refs_13_ = bf16[4,32,4608]{2,1,0:T(8,128)(2,1)S(1)} collective-permute-done((bf16[4,32,4608]{2,1,0:T(8,128)(2,1)S(1)}, bf16[4,32,4608]{2,1,0:T(8,128)(2,1)S(1)}, u32[]{:S(2)}, u32[]{:S(2)}) %collective-permute-start.20) | collective-permute-done | bytes 1179680 | tf_op jit(solution)/shard_map/ppermute | solution.py:158
  92.0 9.1 %collective-permute-done.15.refs_4_ = bf16[4,32,3584]{2,1,0:T(8,128)(2,1)} collective-permute-done((bf16[4,32,3584]{2,1,0:T(8,128)(2,1)}, bf16[4,32,3584]{2,1,0:T(8,128)(2,1)}, u32[]{:S(2)}, u32[]{:S(2)}) %collective-permute-start.15) | collective-permute-done | bytes 917536 | tf_op jit(solution)/shard_map/ppermute | solution.py:158
  101.1 12.8 %aggregate.1 = (bf16[4,2,1024,128]{3,2,1,0:T(8,128)(2,1)}, bf16[2,4,1024,128]{3,2,1,0:T(8,128)(2,1)}, bf16[4,2,1024,128]{3,2,1,0:T(8,128)(2,1)}, bf16[2,4,1024,128]{3,2,1,0:T(8,128)(2,1)}) custom-call(s32[384]{0:T(512)} %reduce.rows_ref, s32[384]{0:T(512)} %reduce.1.cols_ref, s32[6]{0:T(128)} %stack.65.info_ref, bf16[384,128,128]{2,1,0:T(8,128)(2,1)} %bitcast.74, ...), custom_call_target="tpu_custom_call" | custom-call | tf_op jit(solution)/shard_map/aggregate/pallas_call | solution.py:126
  114.1 4.4 %collective-permute-done.24 = bf16[2,4,1024,128]{3,2,1,0:T(8,128)(2,1)S(1)} collective-permute-done((bf16[2,4,1024,128]{3,2,1,0:T(8,128)(2,1)}, bf16[2,4,1024,128]{3,2,1,0:T(8,128)(2,1)S(1)}, u32[]{:S(2)}, u32[]{:S(2)}) %collective-permute-start.24) | collective-permute-done | bytes 2097184 | tf_op jit(solution)/shard_map/ppermute | solution.py:153
  120.1 4.5 %collective-permute-start.30 = (bf16[4,1024,128]{2,1,0:T(8,128)(2,1)S(1)}, bf16[4,1024,128]{2,1,0:T(8,128)(2,1)S(1)}, u32[]{:S(2)}, u32[]{:S(2)}) collective-permute-start(bf16[4,1024,128]{2,1,0:T(8,128)(2,1)S(1)} %fusion.2), channel_id=1, source_target_pairs={{0,8},{8,0},{1,9},{9,1},{2,10},{10,2},{3,11},{11,3},{4,12},{12,4},... | collective-permute-start | bytes 3145736 | tf_op jit(solution)/shard_map/ppermute | solution.py:153
  125.0 2.1 %collective-permute-start.26 = (bf16[2,1024,128]{2,1,0:T(8,128)(2,1)S(1)}, bf16[2,1024,128]{2,1,0:T(8,128)(2,1)S(1)}, u32[]{:S(2)}, u32[]{:S(2)}) collective-permute-start(bf16[2,1024,128]{2,1,0:T(8,128)(2,1)S(1)} %get-tuple-element.48), channel_id=1, source_target_pairs={{0,1},{1,2},{2,3},{3,0},{4,5},{5,6},{6,7},{7,4},{8,9},{9,10},{10,1... | collective-permute-start | bytes 1572872 | tf_op jit(solution)/shard_map/ppermute | solution.py:158
  127.1 4.2 %collective-permute-start.28 = (bf16[2,1024,128]{2,1,0:T(8,128)(2,1)S(1)}, bf16[2,1024,128]{2,1,0:T(8,128)(2,1)S(1)}, u32[]{:S(2)}, u32[]{:S(2)}) collective-permute-start(bf16[2,1024,128]{2,1,0:T(8,128)(2,1)S(1)} %get-tuple-element.49), channel_id=1, source_target_pairs={{0,3},{1,0},{2,1},{3,2},{4,7},{5,4},{6,5},{7,6},{8,11},{9,8},{10,9... | collective-permute-start | bytes 1572872 | tf_op jit(solution)/shard_map/ppermute | solution.py:158
  131.3 6.5 %collective-permute-start.27 = (bf16[2,1024,128]{2,1,0:T(8,128)(2,1)S(1)}, bf16[2,1024,128]{2,1,0:T(8,128)(2,1)S(1)}, u32[]{:S(2)}, u32[]{:S(2)}) collective-permute-start(bf16[2,1024,128]{2,1,0:T(8,128)(2,1)S(1)} %get-tuple-element.50), channel_id=1, source_target_pairs={{0,2},{1,3},{2,0},{3,1},{4,6},{5,7},{6,4},{7,5},{8,10},{9,11},{10,... | collective-permute-start | bytes 1572872 | tf_op jit(solution)/shard_map/ppermute | solution.py:158
  137.8 10.3 %collective-permute-done.30 = bf16[4,1024,128]{2,1,0:T(8,128)(2,1)S(1)} collective-permute-done((bf16[4,1024,128]{2,1,0:T(8,128)(2,1)S(1)}, bf16[4,1024,128]{2,1,0:T(8,128)(2,1)S(1)}, u32[]{:S(2)}, u32[]{:S(2)}) %collective-permute-start.30) | collective-permute-done | bytes 1048608 | tf_op jit(solution)/shard_map/ppermute | solution.py:153
  149.9 4.2 %collective-permute-start.33 = (bf16[1024,128]{1,0:T(8,128)(2,1)S(1)}, bf16[1024,128]{1,0:T(8,128)(2,1)S(1)}, u32[]{:S(2)}, u32[]{:S(2)}) collective-permute-start(bf16[1024,128]{1,0:T(8,128)(2,1)S(1)} %get-tuple-element.46), channel_id=1, source_target_pairs={{0,3},{1,0},{2,1},{3,2},{4,7},{5,4},{6,5},{7,6},{8,11},{9,8},{10,9... | collective-permute-start | bytes 786440 | tf_op jit(solution)/shard_map/ppermute | solution.py:158
  154.1 6.9 %collective-permute-start.32 = (bf16[1024,128]{1,0:T(8,128)(2,1)S(1)}, bf16[1024,128]{1,0:T(8,128)(2,1)S(1)}, u32[]{:S(2)}, u32[]{:S(2)}) collective-permute-start(bf16[1024,128]{1,0:T(8,128)(2,1)S(1)} %get-tuple-element.47), channel_id=1, source_target_pairs={{0,2},{1,3},{2,0},{3,1},{4,6},{5,7},{6,4},{7,5},{8,10},{9,11},{10,... | collective-permute-start | bytes 786440 | tf_op jit(solution)/shard_map/ppermute | solution.py:158
  161.5 4.2 %collective-permute-done.31 = bf16[1024,128]{1,0:T(8,128)(2,1)S(1)} collective-permute-done((bf16[1024,128]{1,0:T(8,128)(2,1)S(1)}, bf16[1024,128]{1,0:T(8,128)(2,1)S(1)}, u32[]{:S(2)}, u32[]{:S(2)}) %collective-permute-start.31) | collective-permute-done | bytes 262176 | tf_op jit(solution)/shard_map/ppermute | solution.py:158
  165.8 4.7 %collective-permute-done.32 = bf16[1024,128]{1,0:T(8,128)(2,1)S(1)} collective-permute-done((bf16[1024,128]{1,0:T(8,128)(2,1)S(1)}, bf16[1024,128]{1,0:T(8,128)(2,1)S(1)}, u32[]{:S(2)}, u32[]{:S(2)}) %collective-permute-start.32) | collective-permute-done | bytes 262176 | tf_op jit(solution)/shard_map/ppermute | solution.py:158
  (92 shorter events, 26.9 us)
Async XLA Ops:
  0.0 22.2 %collective-permute-start.6 = (bf16[32,8192]{1,0:T(8,128)(2,1)}, bf16[32,8192]{1,0:T(8,128)(2,1)S(1)}, u32[]{:S(2)}, u32[]{:S(2)}) collective-permute-start(bf16[32,8192]{1,0:T(8,128)(2,1)} %bitcast.77), channel_id=1, source_target_pairs={{0,16},{16,0},{1,17},{17,1},{2,18},{18,2},{3,19},{19,3},{4,20},{20... | collective-permute-start | bytes 1572872 | tf_op jit(solution)/shard_map/ppermute | solution.py:153
  4.3 13.1 %collective-permute-start.3 = (bf16[32,4608]{1,0:T(8,128)(2,1)S(1)}, bf16[32,4608]{1,0:T(8,128)(2,1)S(1)}, u32[]{:S(2)}, u32[]{:S(2)}) collective-permute-start(bf16[32,4608]{1,0:T(8,128)(2,1)S(1)} %slice.132), channel_id=1, source_target_pairs={{0,1},{1,2},{2,3},{3,0},{4,5},{5,6},{6,7},{7,4},{8,9},{9,10},{10,1... | collective-permute-start | bytes 884744 | tf_op jit(solution)/shard_map/ppermute | solution.py:158
  5.9 11.6 %collective-permute-start.2 = (bf16[32,4608]{1,0:T(8,128)(2,1)S(1)}, bf16[32,4608]{1,0:T(8,128)(2,1)S(1)}, u32[]{:S(2)}, u32[]{:S(2)}) collective-permute-start(bf16[32,4608]{1,0:T(8,128)(2,1)S(1)} %slice.132), channel_id=1, source_target_pairs={{0,3},{1,0},{2,1},{3,2},{4,7},{5,4},{6,5},{7,6},{8,11},{9,8},{10,9... | collective-permute-start | bytes 884744 | tf_op jit(solution)/shard_map/ppermute | solution.py:158
  8.6 8.9 %collective-permute-start.1 = (bf16[32,3584]{1,0:T(8,128)(2,1)S(1)}, bf16[32,3584]{1,0:T(8,128)(2,1)S(1)}, u32[]{:S(2)}, u32[]{:S(2)}) collective-permute-start(bf16[32,3584]{1,0:T(8,128)(2,1)S(1)} %slice.131), channel_id=1, source_target_pairs={{0,32},{32,64},{64,96},{96,0},{1,33},{33,65},{65,97},{97,1},{2,34}... | collective-permute-start | bytes 688136 | tf_op jit(solution)/shard_map/ppermute | solution.py:158
  10.5 6.9 %collective-permute-start = (bf16[32,3584]{1,0:T(8,128)(2,1)S(1)}, bf16[32,3584]{1,0:T(8,128)(2,1)S(1)}, u32[]{:S(2)}, u32[]{:S(2)}) collective-permute-start(bf16[32,3584]{1,0:T(8,128)(2,1)S(1)} %slice.131), channel_id=1, source_target_pairs={{0,96},{32,0},{64,32},{96,64},{1,97},{33,1},{65,33},{97,65},{2,98}... | collective-permute-start | bytes 688136 | tf_op jit(solution)/shard_map/ppermute | solution.py:158
  17.4 7.6 %collective-permute-start.4 = (bf16[32,3584]{1,0:T(8,128)(2,1)S(1)}, bf16[32,3584]{1,0:T(8,128)(2,1)S(1)}, u32[]{:S(2)}, u32[]{:S(2)}) collective-permute-start(bf16[32,3584]{1,0:T(8,128)(2,1)S(1)} %slice.131), channel_id=1, source_target_pairs={{0,64},{32,96},{64,0},{96,32},{1,65},{33,97},{65,1},{97,33},{2,66}... | collective-permute-start | bytes 688136 | tf_op jit(solution)/shard_map/ppermute | solution.py:158
  20.4 8.2 %collective-permute-start.5 = (bf16[32,4608]{1,0:T(8,128)(2,1)S(1)}, bf16[32,4608]{1,0:T(8,128)(2,1)S(1)}, u32[]{:S(2)}, u32[]{:S(2)}) collective-permute-start(bf16[32,4608]{1,0:T(8,128)(2,1)S(1)} %slice.132), channel_id=1, source_target_pairs={{0,2},{1,3},{2,0},{3,1},{4,6},{5,7},{6,4},{7,5},{8,10},{9,11},{10,... | collective-permute-start | bytes 884744 | tf_op jit(solution)/shard_map/ppermute | solution.py:158
  22.2 13.6 %collective-permute-start.7 = (bf16[32,3584]{1,0:T(8,128)(2,1)S(1)}, bf16[32,3584]{1,0:T(8,128)(2,1)S(1)}, u32[]{:S(2)}, u32[]{:S(2)}) collective-permute-start(bf16[32,3584]{1,0:T(8,128)(2,1)S(1)} %get-tuple-element.54), channel_id=1, source_target_pairs={{0,96},{32,0},{64,32},{96,64},{1,97},{33,1},{65,33},{97,65},{2,98}... | collective-permute-start | bytes 688136 | tf_op jit(solution)/shard_map/ppermute | solution.py:158
  28.8 15.0 %collective-permute-start.8 = (bf16[2,32,3584]{2,1,0:T(8,128)(2,1)S(1)}, bf16[2,32,3584]{2,1,0:T(8,128)(2,1)S(1)}, u32[]{:S(2)}, u32[]{:S(2)}) collective-permute-start(bf16[2,32,3584]{2,1,0:T(8,128)(2,1)S(1)} %slice.102), channel_id=1, source_target_pairs={{0,16},{16,0},{1,17},{17,1},{2,18},{18,2},{3,19},{19,3},{4,20},{20... | collective-permute-start | bytes 1376264 | tf_op jit(solution)/shard_map/ppermute | solution.py:153
  29.2 8.8 %collective-permute-start.9 = (bf16[32,4608]{1,0:T(8,128)(2,1)S(1)}, bf16[32,4608]{1,0:T(8,128)(2,1)S(1)}, u32[]{:S(2)}, u32[]{:S(2)}) collective-permute-start(bf16[32,4608]{1,0:T(8,128)(2,1)S(1)} %get-tuple-element.52), channel_id=1, source_target_pairs={{0,3},{1,0},{2,1},{3,2},{4,7},{5,4},{6,5},{7,6},{8,11},{9,8},{10,9... | collective-permute-start | bytes 884744 | tf_op jit(solution)/shard_map/ppermute | solution.py:158
  30.9 21.1 %collective-permute-start.10 = (bf16[2,32,4608]{2,1,0:T(8,128)(2,1)S(1)}, bf16[2,32,4608]{2,1,0:T(8,128)(2,1)S(1)}, u32[]{:S(2)}, u32[]{:S(2)}) collective-permute-start(bf16[2,32,4608]{2,1,0:T(8,128)(2,1)S(1)} %slice.104), channel_id=1, source_target_pairs={{0,16},{16,0},{1,17},{17,1},{2,18},{18,2},{3,19},{19,3},{4,20},{20... | collective-permute-start | bytes 1769480 | tf_op jit(solution)/shard_map/ppermute | solution.py:153
  34.2 24.8 %collective-permute-start.14 = (bf16[4,32,4608]{2,1,0:T(8,128)(2,1)S(1)}, bf16[4,32,4608]{2,1,0:T(8,128)(2,1)S(1)}, u32[]{:S(2)}, u32[]{:S(2)}) collective-permute-start(bf16[4,32,4608]{2,1,0:T(8,128)(2,1)S(1)} %pad_maximum_fusion.refs_8_), channel_id=1, source_target_pairs={{0,96},{32,0},{64,32},{96,64},{1,97},{33,1},{65,33},{97,65},{2,98}... | collective-permute-start | bytes 3538952 | tf_op jit(solution)/shard_map/ppermute | solution.py:158
  35.8 24.1 %collective-permute-start.13 = (bf16[4,32,4608]{2,1,0:T(8,128)(2,1)S(1)}, bf16[4,32,4608]{2,1,0:T(8,128)(2,1)}, u32[]{:S(2)}, u32[]{:S(2)}) collective-permute-start(bf16[4,32,4608]{2,1,0:T(8,128)(2,1)S(1)} %pad_maximum_fusion.refs_8_), channel_id=1, source_target_pairs={{0,32},{32,64},{64,96},{96,0},{1,33},{33,65},{65,97},{97,1},{2,34}... | collective-permute-start | bytes 3538952 | tf_op jit(solution)/shard_map/ppermute | solution.py:158
  38.1 17.6 %collective-permute-start.12 = (bf16[4,32,3584]{2,1,0:T(8,128)(2,1)S(1)}, bf16[4,32,3584]{2,1,0:T(8,128)(2,1)S(1)}, u32[]{:S(2)}, u32[]{:S(2)}) collective-permute-start(bf16[4,32,3584]{2,1,0:T(8,128)(2,1)S(1)} %pad_maximum_fusion.2.refs_0_), channel_id=1, source_target_pairs={{0,3},{1,0},{2,1},{3,2},{4,7},{5,4},{6,5},{7,6},{8,11},{9,8},{10,9... | collective-permute-start | bytes 2752520 | tf_op jit(solution)/shard_map/ppermute | solution.py:158
  43.8 14.7 %collective-permute-start.11 = (bf16[4,32,3584]{2,1,0:T(8,128)(2,1)S(1)}, bf16[4,32,3584]{2,1,0:T(8,128)(2,1)S(1)}, u32[]{:S(2)}, u32[]{:S(2)}) collective-permute-start(bf16[4,32,3584]{2,1,0:T(8,128)(2,1)S(1)} %pad_maximum_fusion.2.refs_0_), channel_id=1, source_target_pairs={{0,1},{1,2},{2,3},{3,0},{4,5},{5,6},{6,7},{7,4},{8,9},{9,10},{10,1... | collective-permute-start | bytes 2752520 | tf_op jit(solution)/shard_map/ppermute | solution.py:158
  59.9 24.4 %collective-permute-start.20 = (bf16[4,32,4608]{2,1,0:T(8,128)(2,1)S(1)}, bf16[4,32,4608]{2,1,0:T(8,128)(2,1)S(1)}, u32[]{:S(2)}, u32[]{:S(2)}) collective-permute-start(bf16[4,32,4608]{2,1,0:T(8,128)(2,1)S(1)} %pad_maximum_fusion.1.refs_9_), channel_id=1, source_target_pairs={{0,96},{32,0},{64,32},{96,64},{1,97},{33,1},{65,33},{97,65},{2,98}... | collective-permute-start | bytes 3538952 | tf_op jit(solution)/shard_map/ppermute | solution.py:158
  61.7 15.2 %collective-permute-start.16 = (bf16[4,32,3584]{2,1,0:T(8,128)(2,1)}, bf16[4,32,3584]{2,1,0:T(8,128)(2,1)S(1)}, u32[]{:S(2)}, u32[]{:S(2)}) collective-permute-start(bf16[4,32,3584]{2,1,0:T(8,128)(2,1)} %pad_maximum_fusion.3.refs_1_), channel_id=1, source_target_pairs={{0,3},{1,0},{2,1},{3,2},{4,7},{5,4},{6,5},{7,6},{8,11},{9,8},{10,9... | collective-permute-start | bytes 2752520 | tf_op jit(solution)/shard_map/ppermute | solution.py:158
  62.2 24.0 %collective-permute-start.19 = (bf16[4,32,4608]{2,1,0:T(8,128)(2,1)}, bf16[4,32,4608]{2,1,0:T(8,128)(2,1)S(1)}, u32[]{:S(2)}, u32[]{:S(2)}) collective-permute-start(bf16[4,32,4608]{2,1,0:T(8,128)(2,1)} %collective-permute-done.13.refs_10_), channel_id=1, source_target_pairs={{0,16},{16,0},{1,17},{17,1},{2,18},{18,2},{3,19},{19,3},{4,20},{20... | collective-permute-start | bytes 3538952 | tf_op jit(solution)/shard_map/ppermute | solution.py:153
  63.9 24.7 %collective-permute-start.17 = (bf16[4,32,3584]{2,1,0:T(8,128)(2,1)S(1)}, bf16[4,32,3584]{2,1,0:T(8,128)(2,1)S(1)}, u32[]{:S(2)}, u32[]{:S(2)}) collective-permute-start(bf16[4,32,3584]{2,1,0:T(8,128)(2,1)S(1)} %collective-permute-done.11.refs_2_), channel_id=1, source_target_pairs={{0,1},{1,2},{2,3},{3,0},{4,5},{5,6},{6,7},{7,4},{8,9},{9,10},{10,1... | collective-permute-start | bytes 2752520 | tf_op jit(solution)/shard_map/ppermute | solution.py:158
  64.3 36.8 %collective-permute-start.21 = (bf16[4,32,4608]{2,1,0:T(8,128)(2,1)}, bf16[4,32,4608]{2,1,0:T(8,128)(2,1)}, u32[]{:S(2)}, u32[]{:S(2)}) collective-permute-start(bf16[4,32,4608]{2,1,0:T(8,128)(2,1)} %collective-permute-done.13.refs_10_), channel_id=1, source_target_pairs={{0,32},{32,64},{64,96},{96,0},{1,33},{33,65},{65,97},{97,1},{2,34}... | collective-permute-start | bytes 3538952 | tf_op jit(solution)/shard_map/ppermute | solution.py:158
  76.9 24.2 %collective-permute-start.15 = (bf16[4,32,3584]{2,1,0:T(8,128)(2,1)}, bf16[4,32,3584]{2,1,0:T(8,128)(2,1)}, u32[]{:S(2)}, u32[]{:S(2)}) collective-permute-start(bf16[4,32,3584]{2,1,0:T(8,128)(2,1)} %pad_maximum_fusion.3.refs_1_), channel_id=1, source_target_pairs={{0,1},{1,2},{2,3},{3,0},{4,5},{5,6},{6,7},{7,4},{8,9},{9,10},{10,1... | collective-permute-start | bytes 2752520 | tf_op jit(solution)/shard_map/ppermute | solution.py:158
  84.3 16.8 %collective-permute-start.18 = (bf16[4,32,3584]{2,1,0:T(8,128)(2,1)S(1)}, bf16[4,32,3584]{2,1,0:T(8,128)(2,1)}, u32[]{:S(2)}, u32[]{:S(2)}) collective-permute-start(bf16[4,32,3584]{2,1,0:T(8,128)(2,1)S(1)} %collective-permute-done.16.refs_5_), channel_id=1, source_target_pairs={{0,3},{1,0},{2,1},{3,2},{4,7},{5,4},{6,5},{7,6},{8,11},{9,8},{10,9... | collective-permute-start | bytes 2752520 | tf_op jit(solution)/shard_map/ppermute | solution.py:158
  86.2 14.9 %collective-permute-start.23 = (bf16[2,32,4608]{2,1,0:T(8,128)(2,1)}, bf16[2,32,4608]{2,1,0:T(8,128)(2,1)}, u32[]{:S(2)}, u32[]{:S(2)}) collective-permute-start(bf16[2,32,4608]{2,1,0:T(8,128)(2,1)} %slice.136), channel_id=1, source_target_pairs={{0,96},{32,0},{64,32},{96,64},{1,97},{33,1},{65,33},{97,65},{2,98}... | collective-permute-start | bytes 1769480 | tf_op jit(solution)/shard_map/ppermute | solution.py:158
  88.6 12.4 %collective-permute-start.22 = (bf16[2,32,4608]{2,1,0:T(8,128)(2,1)}, bf16[2,32,4608]{2,1,0:T(8,128)(2,1)}, u32[]{:S(2)}, u32[]{:S(2)}) collective-permute-start(bf16[2,32,4608]{2,1,0:T(8,128)(2,1)} %slice.135), channel_id=1, source_target_pairs={{0,32},{32,64},{64,96},{96,0},{1,33},{33,65},{65,97},{97,1},{2,34}... | collective-permute-start | bytes 1769480 | tf_op jit(solution)/shard_map/ppermute | solution.py:158
  120.1 28.0 %collective-permute-start.30 = (bf16[4,1024,128]{2,1,0:T(8,128)(2,1)S(1)}, bf16[4,1024,128]{2,1,0:T(8,128)(2,1)S(1)}, u32[]{:S(2)}, u32[]{:S(2)}) collective-permute-start(bf16[4,1024,128]{2,1,0:T(8,128)(2,1)S(1)} %fusion.2), channel_id=1, source_target_pairs={{0,8},{8,0},{1,9},{9,1},{2,10},{10,2},{3,11},{11,3},{4,12},{12,4},... | collective-permute-start | bytes 3145736 | tf_op jit(solution)/shard_map/ppermute | solution.py:153
  125.0 29.1 %collective-permute-start.26 = (bf16[2,1024,128]{2,1,0:T(8,128)(2,1)S(1)}, bf16[2,1024,128]{2,1,0:T(8,128)(2,1)S(1)}, u32[]{:S(2)}, u32[]{:S(2)}) collective-permute-start(bf16[2,1024,128]{2,1,0:T(8,128)(2,1)S(1)} %get-tuple-element.48), channel_id=1, source_target_pairs={{0,1},{1,2},{2,3},{3,0},{4,5},{5,6},{6,7},{7,4},{8,9},{9,10},{10,1... | collective-permute-start | bytes 1572872 | tf_op jit(solution)/shard_map/ppermute | solution.py:158
  127.1 34.0 %collective-permute-start.28 = (bf16[2,1024,128]{2,1,0:T(8,128)(2,1)S(1)}, bf16[2,1024,128]{2,1,0:T(8,128)(2,1)S(1)}, u32[]{:S(2)}, u32[]{:S(2)}) collective-permute-start(bf16[2,1024,128]{2,1,0:T(8,128)(2,1)S(1)} %get-tuple-element.49), channel_id=1, source_target_pairs={{0,3},{1,0},{2,1},{3,2},{4,7},{5,4},{6,5},{7,6},{8,11},{9,8},{10,9... | collective-permute-start | bytes 1572872 | tf_op jit(solution)/shard_map/ppermute | solution.py:158
  131.3 29.8 %collective-permute-start.27 = (bf16[2,1024,128]{2,1,0:T(8,128)(2,1)S(1)}, bf16[2,1024,128]{2,1,0:T(8,128)(2,1)S(1)}, u32[]{:S(2)}, u32[]{:S(2)}) collective-permute-start(bf16[2,1024,128]{2,1,0:T(8,128)(2,1)S(1)} %get-tuple-element.50), channel_id=1, source_target_pairs={{0,2},{1,3},{2,0},{3,1},{4,6},{5,7},{6,4},{7,5},{8,10},{9,11},{10,... | collective-permute-start | bytes 1572872 | tf_op jit(solution)/shard_map/ppermute | solution.py:158
  148.4 17.3 %collective-permute-start.31 = (bf16[1024,128]{1,0:T(8,128)(2,1)S(1)}, bf16[1024,128]{1,0:T(8,128)(2,1)S(1)}, u32[]{:S(2)}, u32[]{:S(2)}) collective-permute-start(bf16[1024,128]{1,0:T(8,128)(2,1)S(1)} %get-tuple-element.45), channel_id=1, source_target_pairs={{0,1},{1,2},{2,3},{3,0},{4,5},{5,6},{6,7},{7,4},{8,9},{9,10},{10,1... | collective-permute-start | bytes 786440 | tf_op jit(solution)/shard_map/ppermute | solution.py:158
  149.9 15.8 %collective-permute-start.33 = (bf16[1024,128]{1,0:T(8,128)(2,1)S(1)}, bf16[1024,128]{1,0:T(8,128)(2,1)S(1)}, u32[]{:S(2)}, u32[]{:S(2)}) collective-permute-start(bf16[1024,128]{1,0:T(8,128)(2,1)S(1)} %get-tuple-element.46), channel_id=1, source_target_pairs={{0,3},{1,0},{2,1},{3,2},{4,7},{5,4},{6,5},{7,6},{8,11},{9,8},{10,9... | collective-permute-start | bytes 786440 | tf_op jit(solution)/shard_map/ppermute | solution.py:158
  154.1 16.3 %collective-permute-start.32 = (bf16[1024,128]{1,0:T(8,128)(2,1)S(1)}, bf16[1024,128]{1,0:T(8,128)(2,1)S(1)}, u32[]{:S(2)}, u32[]{:S(2)}) collective-permute-start(bf16[1024,128]{1,0:T(8,128)(2,1)S(1)} %get-tuple-element.47), channel_id=1, source_target_pairs={{0,2},{1,3},{2,0},{3,1},{4,6},{5,7},{6,4},{7,5},{8,10},{9,11},{10,... | collective-permute-start | bytes 786440 | tf_op jit(solution)/shard_map/ppermute | solution.py:158
  161.4 9.3 %collective-permute-start.29 = (bf16[1024,128]{1,0:T(8,128)(2,1)S(1)}, bf16[1024,128]{1,0:T(8,128)(2,1)S(1)}, u32[]{:S(2)}, u32[]{:S(2)}) collective-permute-start(bf16[1024,128]{1,0:T(8,128)(2,1)S(1)} %fusion.20), channel_id=1, source_target_pairs={{0,8},{8,0},{1,9},{9,1},{2,10},{10,2},{3,11},{11,3},{4,12},{12,4},... | collective-permute-start | bytes 786440 | tf_op jit(solution)/shard_map/ppermute | solution.py:153
  (18 other events, 522.9 us)

commit v15 on v14

--- a/solution.py
+++ b/solution.py
@@ -9,7 +9,7 @@
 from jax.sharding import PartitionSpec as P
 
 LOAD = 32
-STEPS_AT_ONCE = (16, 4, 1)
+STEPS_AT_ONCE = (32, 8, 1)
 PACK = 256
 SPLIT = 28
 FIRST_X = 1024

time: 173 us -> 172 us (level)
  starting transfers between devices: 64.7 us -> 50.3 us
  waiting for transfers between devices: 82.4 us -> 90.1 us
  Pallas kernels: 12.8 us -> 18.2 us
    ppermute x26, starting transfers between devices: 51.2 us -> 39.1 us  [shift(): return lax.ppermute(value, axis, [(i, (i + by) % n) for i in range(n)])]
    ppermute x8, waiting for transfers between devices: 25.5 us -> 33.6 us  [swap(): return lax.ppermute(value, axis, [(0, 1), (1, 0)])]
    pallas_call x1, Pallas kernels: 12.8 us -> 18.2 us  [aggregate(): pl.pallas_call(functools.partial(aggregate_kernel, where, len(arrays)), o...]
    ppermute x8, starting transfers between devices: 13.5 us -> 11.2 us  [swap(): return lax.ppermute(value, axis, [(0, 1), (1, 0)])]
  transfers between devices with their start and end apart: 34 -> 34, of which waited for: 18 -> 19; matrix products, arithmetic and copies ran while one was open for 6% -> 6% of each run, Pallas kernels for 0% -> 0%
where the time goes in v15:
time: 172 us; the launch traced here: 171 us
  waiting for transfers between devices  90.1 us (52%)
  starting transfers between devices  50.3 us (29%)
  Pallas kernels  18.2 us (11%)
  other arithmetic  5.35 us (3%)
  local copies, waits for them, and re-layouts  4.66 us (3%)
    ppermute x26, waiting for transfers between devices, shift(): return lax.ppermute(value, axis, [(i, (i + by) % n) for i in range(n)])  56.5 us
    ppermute x26, starting transfers between devices, shift(): return lax.ppermute(value, axis, [(i, (i + by) % n) for i in range(n)])  39.1 us
    ppermute x8, waiting for transfers between devices, swap(): return lax.ppermute(value, axis, [(0, 1), (1, 0)])  33.6 us
    pallas_call x1, Pallas kernels, aggregate(): pl.pallas_call(functools.partial(aggregate_kernel, where, len(arrays)), o...  18.2 us
    ppermute x8, starting transfers between devices, swap(): return lax.ppermute(value, axis, [(0, 1), (1, 0)])  11.2 us
  transfers between devices with their start and end apart: 34, of which 19 were waited for; matrix products, arithmetic and copies ran while one was open for 6% of the time, Pallas kernels for 0%

profile of v15, /device:TPU:0, one launch (start us, length us, event | category | flops | bytes accessed | tf_op | source)
XLA Modules:
  0.0 170.9 jit_solution(7333817129124373081)
XLA Ops:
  0.0 3.3 %collective-permute-start.6 = (bf16[32,8192]{1,0:T(8,128)(2,1)}, bf16[32,8192]{1,0:T(8,128)(2,1)S(1)}, u32[]{:S(2)}, u32[]{:S(2)}) collective-permute-start(bf16[32,8192]{1,0:T(8,128)(2,1)} %bitcast.77), channel_id=1, source_target_pairs={{0,16},{16,0},{1,17},{17,1},{2,18},{18,2},{3,19},{19,3},{4,20},{20... | collective-permute-start | bytes 1572872 | tf_op jit(solution)/shard_map/ppermute | solution.py:153
  5.9 1.7 %collective-permute-start.2 = (bf16[32,4608]{1,0:T(8,128)(2,1)S(1)}, bf16[32,4608]{1,0:T(8,128)(2,1)S(1)}, u32[]{:S(2)}, u32[]{:S(2)}) collective-permute-start(bf16[32,4608]{1,0:T(8,128)(2,1)S(1)} %slice.132), channel_id=1, source_target_pairs={{0,3},{1,0},{2,1},{3,2},{4,7},{5,4},{6,5},{7,6},{8,11},{9,8},{10,9... | collective-permute-start | bytes 884744 | tf_op jit(solution)/shard_map/ppermute | solution.py:158
  8.6 2.0 %collective-permute-start.1 = (bf16[32,3584]{1,0:T(8,128)(2,1)S(1)}, bf16[32,3584]{1,0:T(8,128)(2,1)S(1)}, u32[]{:S(2)}, u32[]{:S(2)}) collective-permute-start(bf16[32,3584]{1,0:T(8,128)(2,1)S(1)} %slice.131), channel_id=1, source_target_pairs={{0,32},{32,64},{64,96},{96,0},{1,33},{33,65},{65,97},{97,1},{2,34}... | collective-permute-start | bytes 688136 | tf_op jit(solution)/shard_map/ppermute | solution.py:158
  10.5 2.2 %collective-permute-start = (bf16[32,3584]{1,0:T(8,128)(2,1)S(1)}, bf16[32,3584]{1,0:T(8,128)(2,1)S(1)}, u32[]{:S(2)}, u32[]{:S(2)}) collective-permute-start(bf16[32,3584]{1,0:T(8,128)(2,1)S(1)} %slice.131), channel_id=1, source_target_pairs={{0,96},{32,0},{64,32},{96,64},{1,97},{33,1},{65,33},{97,65},{2,98}... | collective-permute-start | bytes 688136 | tf_op jit(solution)/shard_map/ppermute | solution.py:158
  12.7 4.7 %collective-permute-done.1 = bf16[32,3584]{1,0:T(8,128)(2,1)S(1)} collective-permute-done((bf16[32,3584]{1,0:T(8,128)(2,1)S(1)}, bf16[32,3584]{1,0:T(8,128)(2,1)S(1)}, u32[]{:S(2)}, u32[]{:S(2)}) %collective-permute-start.1) | collective-permute-done | bytes 229408 | tf_op jit(solution)/shard_map/ppermute | solution.py:158
  17.4 2.9 %collective-permute-start.4 = (bf16[32,3584]{1,0:T(8,128)(2,1)S(1)}, bf16[32,3584]{1,0:T(8,128)(2,1)S(1)}, u32[]{:S(2)}, u32[]{:S(2)}) collective-permute-start(bf16[32,3584]{1,0:T(8,128)(2,1)S(1)} %slice.131), channel_id=1, source_target_pairs={{0,64},{32,96},{64,0},{96,32},{1,65},{33,97},{65,1},{97,33},{2,66}... | collective-permute-start | bytes 688136 | tf_op jit(solution)/shard_map/ppermute | solution.py:158
  20.4 1.8 %collective-permute-start.5 = (bf16[32,4608]{1,0:T(8,128)(2,1)S(1)}, bf16[32,4608]{1,0:T(8,128)(2,1)S(1)}, u32[]{:S(2)}, u32[]{:S(2)}) collective-permute-start(bf16[32,4608]{1,0:T(8,128)(2,1)S(1)} %slice.132), channel_id=1, source_target_pairs={{0,2},{1,3},{2,0},{3,1},{4,6},{5,7},{6,4},{7,5},{8,10},{9,11},{10,... | collective-permute-start | bytes 884744 | tf_op jit(solution)/shard_map/ppermute | solution.py:158
  23.3 1.8 %collective-permute-done.4 = bf16[32,3584]{1,0:T(8,128)(2,1)S(1)} collective-permute-done((bf16[32,3584]{1,0:T(8,128)(2,1)S(1)}, bf16[32,3584]{1,0:T(8,128)(2,1)S(1)}, u32[]{:S(2)}, u32[]{:S(2)}) %collective-permute-start.4) | collective-permute-done | bytes 229408 | tf_op jit(solution)/shard_map/ppermute | solution.py:158
  25.2 3.4 %collective-permute-done.5 = bf16[32,4608]{1,0:T(8,128)(2,1)S(1)} collective-permute-done((bf16[32,4608]{1,0:T(8,128)(2,1)S(1)}, bf16[32,4608]{1,0:T(8,128)(2,1)S(1)}, u32[]{:S(2)}, u32[]{:S(2)}) %collective-permute-start.5) | collective-permute-done | bytes 294944 | tf_op jit(solution)/shard_map/ppermute | solution.py:158
  30.9 3.3 %collective-permute-start.10 = (bf16[2,32,4608]{2,1,0:T(8,128)(2,1)S(1)}, bf16[2,32,4608]{2,1,0:T(8,128)(2,1)S(1)}, u32[]{:S(2)}, u32[]{:S(2)}) collective-permute-start(bf16[2,32,4608]{2,1,0:T(8,128)(2,1)S(1)} %slice.104), channel_id=1, source_target_pairs={{0,16},{16,0},{1,17},{17,1},{2,18},{18,2},{3,19},{19,3},{4,20},{20... | collective-permute-start | bytes 1769480 | tf_op jit(solution)/shard_map/ppermute | solution.py:153
  36.2 1.9 %collective-permute-done.9 = bf16[32,4608]{1,0:T(8,128)(2,1)S(1)} collective-permute-done((bf16[32,4608]{1,0:T(8,128)(2,1)S(1)}, bf16[32,4608]{1,0:T(8,128)(2,1)S(1)}, u32[]{:S(2)}, u32[]{:S(2)}) %collective-permute-start.9) | collective-permute-done | bytes 294944 | tf_op jit(solution)/shard_map/ppermute | solution.py:158
  39.8 4.1 %collective-permute-done.8 = bf16[2,32,3584]{2,1,0:T(8,128)(2,1)S(1)} collective-permute-done((bf16[2,32,3584]{2,1,0:T(8,128)(2,1)S(1)}, bf16[2,32,3584]{2,1,0:T(8,128)(2,1)S(1)}, u32[]{:S(2)}, u32[]{:S(2)}) %collective-permute-start.8) | collective-permute-done | bytes 458784 | tf_op jit(solution)/shard_map/ppermute | solution.py:153
  45.2 6.8 %collective-permute-done.10 = bf16[2,32,4608]{2,1,0:T(8,128)(2,1)S(1)} collective-permute-done((bf16[2,32,4608]{2,1,0:T(8,128)(2,1)S(1)}, bf16[2,32,4608]{2,1,0:T(8,128)(2,1)S(1)}, u32[]{:S(2)}, u32[]{:S(2)}) %collective-permute-start.10) | collective-permute-done | bytes 589856 | tf_op jit(solution)/shard_map/ppermute | solution.py:153
  52.1 3.6 %collective-permute-done.12.refs_3_ = bf16[4,32,3584]{2,1,0:T(8,128)(2,1)S(1)} collective-permute-done((bf16[4,32,3584]{2,1,0:T(8,128)(2,1)S(1)}, bf16[4,32,3584]{2,1,0:T(8,128)(2,1)S(1)}, u32[]{:S(2)}, u32[]{:S(2)}) %collective-permute-start.12) | collective-permute-done | bytes 917536 | tf_op jit(solution)/shard_map/ppermute | solution.py:158
  55.7 2.8 %collective-permute-done.11.refs_2_ = bf16[4,32,3584]{2,1,0:T(8,128)(2,1)S(1)} collective-permute-done((bf16[4,32,3584]{2,1,0:T(8,128)(2,1)S(1)}, bf16[4,32,3584]{2,1,0:T(8,128)(2,1)S(1)}, u32[]{:S(2)}, u32[]{:S(2)}) %collective-permute-start.11) | collective-permute-done | bytes 917536 | tf_op jit(solution)/shard_map/ppermute | solution.py:158
  59.9 1.7 %collective-permute-start.20 = (bf16[4,32,4608]{2,1,0:T(8,128)(2,1)S(1)}, bf16[4,32,4608]{2,1,0:T(8,128)(2,1)S(1)}, u32[]{:S(2)}, u32[]{:S(2)}) collective-permute-start(bf16[4,32,4608]{2,1,0:T(8,128)(2,1)S(1)} %pad_maximum_fusion.1.refs_9_), channel_id=1, source_target_pairs={{0,96},{32,0},{64,32},{96,64},{1,97},{33,1},{65,33},{97,65},{2,98}... | collective-permute-start | bytes 3538952 | tf_op jit(solution)/shard_map/ppermute | solution.py:158
  62.2 1.7 collective-permute-start.19
  64.6 12.3 %collective-permute-done.16.refs_5_ = bf16[4,32,3584]{2,1,0:T(8,128)(2,1)S(1)} collective-permute-done((bf16[4,32,3584]{2,1,0:T(8,128)(2,1)}, bf16[4,32,3584]{2,1,0:T(8,128)(2,1)S(1)}, u32[]{:S(2)}, u32[]{:S(2)}) %collective-permute-start.16) | collective-permute-done | bytes 917536 | tf_op jit(solution)/shard_map/ppermute | solution.py:158
  77.4 7.0 %collective-permute-done.20.refs_13_ = bf16[4,32,4608]{2,1,0:T(8,128)(2,1)S(1)} collective-permute-done((bf16[4,32,4608]{2,1,0:T(8,128)(2,1)S(1)}, bf16[4,32,4608]{2,1,0:T(8,128)(2,1)S(1)}, u32[]{:S(2)}, u32[]{:S(2)}) %collective-permute-start.20) | collective-permute-done | bytes 1179680 | tf_op jit(solution)/shard_map/ppermute | solution.py:158
  92.0 9.1 %collective-permute-done.15.refs_4_ = bf16[4,32,3584]{2,1,0:T(8,128)(2,1)} collective-permute-done((bf16[4,32,3584]{2,1,0:T(8,128)(2,1)}, bf16[4,32,3584]{2,1,0:T(8,128)(2,1)}, u32[]{:S(2)}, u32[]{:S(2)}) %collective-permute-start.15) | collective-permute-done | bytes 917536 | tf_op jit(solution)/shard_map/ppermute | solution.py:158
  101.1 18.2 %aggregate.1 = (bf16[4,2,1024,128]{3,2,1,0:T(8,128)(2,1)}, bf16[2,4,1024,128]{3,2,1,0:T(8,128)(2,1)}, bf16[4,2,1024,128]{3,2,1,0:T(8,128)(2,1)}, bf16[2,4,1024,128]{3,2,1,0:T(8,128)(2,1)}) custom-call(s32[384]{0:T(512)} %reduce.rows_ref, s32[384]{0:T(512)} %reduce.1.cols_ref, s32[6]{0:T(128)} %stack.65.info_ref, bf16[384,128,128]{2,1,0:T(8,128)(2,1)} %bitcast.74, ...), custom_call_target="tpu_custom_call" | custom-call | tf_op jit(solution)/shard_map/aggregate/pallas_call | solution.py:126
  119.4 4.4 %collective-permute-done.24 = bf16[2,4,1024,128]{3,2,1,0:T(8,128)(2,1)S(1)} collective-permute-done((bf16[2,4,1024,128]{3,2,1,0:T(8,128)(2,1)}, bf16[2,4,1024,128]{3,2,1,0:T(8,128)(2,1)S(1)}, u32[]{:S(2)}, u32[]{:S(2)}) %collective-permute-start.24) | collective-permute-done | bytes 2097184 | tf_op jit(solution)/shard_map/ppermute | solution.py:153
  125.5 2.6 %collective-permute-done.25 = bf16[4,2,1024,128]{3,2,1,0:T(8,128)(2,1)S(1)} collective-permute-done((bf16[4,2,1024,128]{3,2,1,0:T(8,128)(2,1)}, bf16[4,2,1024,128]{3,2,1,0:T(8,128)(2,1)S(1)}, u32[]{:S(2)}, u32[]{:S(2)}) %collective-permute-start.25) | collective-permute-done | bytes 2097184 | tf_op jit(solution)/shard_map/ppermute | solution.py:153
  128.6 4.5 %collective-permute-start.26 = (bf16[2,1024,128]{2,1,0:T(8,128)(2,1)S(1)}, bf16[2,1024,128]{2,1,0:T(8,128)(2,1)S(1)}, u32[]{:S(2)}, u32[]{:S(2)}) collective-permute-start(bf16[2,1024,128]{2,1,0:T(8,128)(2,1)S(1)} %get-tuple-element.48), channel_id=1, source_target_pairs={{0,1},{1,2},{2,3},{3,0},{4,5},{5,6},{6,7},{7,4},{8,9},{9,10},{10,1... | collective-permute-start | bytes 1572872 | tf_op jit(solution)/shard_map/ppermute | solution.py:158
  133.1 2.1 %collective-permute-start.27 = (bf16[2,1024,128]{2,1,0:T(8,128)(2,1)S(1)}, bf16[2,1024,128]{2,1,0:T(8,128)(2,1)S(1)}, u32[]{:S(2)}, u32[]{:S(2)}) collective-permute-start(bf16[2,1024,128]{2,1,0:T(8,128)(2,1)S(1)} %get-tuple-element.50), channel_id=1, source_target_pairs={{0,2},{1,3},{2,0},{3,1},{4,6},{5,7},{6,4},{7,5},{8,10},{9,11},{10,... | collective-permute-start | bytes 1572872 | tf_op jit(solution)/shard_map/ppermute | solution.py:158
  135.3 15.7 %collective-permute-done.30 = bf16[4,1024,128]{2,1,0:T(8,128)(2,1)S(1)} collective-permute-done((bf16[4,1024,128]{2,1,0:T(8,128)(2,1)S(1)}, bf16[4,1024,128]{2,1,0:T(8,128)(2,1)S(1)}, u32[]{:S(2)}, u32[]{:S(2)}) %collective-permute-start.30) | collective-permute-done | bytes 1048608 | tf_op jit(solution)/shard_map/ppermute | solution.py:153
  151.3 4.5 %collective-permute-start.31 = (bf16[1024,128]{1,0:T(8,128)(2,1)S(1)}, bf16[1024,128]{1,0:T(8,128)(2,1)S(1)}, u32[]{:S(2)}, u32[]{:S(2)}) collective-permute-start(bf16[1024,128]{1,0:T(8,128)(2,1)S(1)} %get-tuple-element.45), channel_id=1, source_target_pairs={{0,1},{1,2},{2,3},{3,0},{4,5},{5,6},{6,7},{7,4},{8,9},{9,10},{10,1... | collective-permute-start | bytes 786440 | tf_op jit(solution)/shard_map/ppermute | solution.py:158
  156.2 1.7 %collective-permute-start.32 = (bf16[1024,128]{1,0:T(8,128)(2,1)S(1)}, bf16[1024,128]{1,0:T(8,128)(2,1)S(1)}, u32[]{:S(2)}, u32[]{:S(2)}) collective-permute-start(bf16[1024,128]{1,0:T(8,128)(2,1)S(1)} %get-tuple-element.47), channel_id=1, source_target_pairs={{0,2},{1,3},{2,0},{3,1},{4,6},{5,7},{6,4},{7,5},{8,10},{9,11},{10,... | collective-permute-start | bytes 786440 | tf_op jit(solution)/shard_map/ppermute | solution.py:158
  158.3 2.2 %collective-permute-start.29 = (bf16[1024,128]{1,0:T(8,128)(2,1)S(1)}, bf16[1024,128]{1,0:T(8,128)(2,1)S(1)}, u32[]{:S(2)}, u32[]{:S(2)}) collective-permute-start(bf16[1024,128]{1,0:T(8,128)(2,1)S(1)} %fusion.20), channel_id=1, source_target_pairs={{0,8},{8,0},{1,9},{9,1},{2,10},{10,2},{3,11},{11,3},{4,12},{12,4},... | collective-permute-start | bytes 786440 | tf_op jit(solution)/shard_map/ppermute | solution.py:153
  160.6 2.5 %collective-permute-done.31 = bf16[1024,128]{1,0:T(8,128)(2,1)S(1)} collective-permute-done((bf16[1024,128]{1,0:T(8,128)(2,1)S(1)}, bf16[1024,128]{1,0:T(8,128)(2,1)S(1)}, u32[]{:S(2)}, u32[]{:S(2)}) %collective-permute-start.31) | collective-permute-done | bytes 262176 | tf_op jit(solution)/shard_map/ppermute | solution.py:158
  163.1 1.9 %collective-permute-done.33 = bf16[1024,128]{1,0:T(8,128)(2,1)S(1)} collective-permute-done((bf16[1024,128]{1,0:T(8,128)(2,1)S(1)}, bf16[1024,128]{1,0:T(8,128)(2,1)S(1)}, u32[]{:S(2)}, u32[]{:S(2)}) %collective-permute-start.33) | collective-permute-done | bytes 262176 | tf_op jit(solution)/shard_map/ppermute | solution.py:158
  165.1 4.1 %collective-permute-done.32 = bf16[1024,128]{1,0:T(8,128)(2,1)S(1)} collective-permute-done((bf16[1024,128]{1,0:T(8,128)(2,1)S(1)}, bf16[1024,128]{1,0:T(8,128)(2,1)S(1)}, u32[]{:S(2)}, u32[]{:S(2)}) %collective-permute-start.32) | collective-permute-done | bytes 262176 | tf_op jit(solution)/shard_map/ppermute | solution.py:158
  (92 shorter events, 27.4 us)
Async XLA Ops:
  0.0 22.2 %collective-permute-start.6 = (bf16[32,8192]{1,0:T(8,128)(2,1)}, bf16[32,8192]{1,0:T(8,128)(2,1)S(1)}, u32[]{:S(2)}, u32[]{:S(2)}) collective-permute-start(bf16[32,8192]{1,0:T(8,128)(2,1)} %bitcast.77), channel_id=1, source_target_pairs={{0,16},{16,0},{1,17},{17,1},{2,18},{18,2},{3,19},{19,3},{4,20},{20... | collective-permute-start | bytes 1572872 | tf_op jit(solution)/shard_map/ppermute | solution.py:153
  4.3 13.1 %collective-permute-start.3 = (bf16[32,4608]{1,0:T(8,128)(2,1)S(1)}, bf16[32,4608]{1,0:T(8,128)(2,1)S(1)}, u32[]{:S(2)}, u32[]{:S(2)}) collective-permute-start(bf16[32,4608]{1,0:T(8,128)(2,1)S(1)} %slice.132), channel_id=1, source_target_pairs={{0,1},{1,2},{2,3},{3,0},{4,5},{5,6},{6,7},{7,4},{8,9},{9,10},{10,1... | collective-permute-start | bytes 884744 | tf_op jit(solution)/shard_map/ppermute | solution.py:158
  5.9 11.6 %collective-permute-start.2 = (bf16[32,4608]{1,0:T(8,128)(2,1)S(1)}, bf16[32,4608]{1,0:T(8,128)(2,1)S(1)}, u32[]{:S(2)}, u32[]{:S(2)}) collective-permute-start(bf16[32,4608]{1,0:T(8,128)(2,1)S(1)} %slice.132), channel_id=1, source_target_pairs={{0,3},{1,0},{2,1},{3,2},{4,7},{5,4},{6,5},{7,6},{8,11},{9,8},{10,9... | collective-permute-start | bytes 884744 | tf_op jit(solution)/shard_map/ppermute | solution.py:158
  8.6 8.9 %collective-permute-start.1 = (bf16[32,3584]{1,0:T(8,128)(2,1)S(1)}, bf16[32,3584]{1,0:T(8,128)(2,1)S(1)}, u32[]{:S(2)}, u32[]{:S(2)}) collective-permute-start(bf16[32,3584]{1,0:T(8,128)(2,1)S(1)} %slice.131), channel_id=1, source_target_pairs={{0,32},{32,64},{64,96},{96,0},{1,33},{33,65},{65,97},{97,1},{2,34}... | collective-permute-start | bytes 688136 | tf_op jit(solution)/shard_map/ppermute | solution.py:158
  10.5 6.9 %collective-permute-start = (bf16[32,3584]{1,0:T(8,128)(2,1)S(1)}, bf16[32,3584]{1,0:T(8,128)(2,1)S(1)}, u32[]{:S(2)}, u32[]{:S(2)}) collective-permute-start(bf16[32,3584]{1,0:T(8,128)(2,1)S(1)} %slice.131), channel_id=1, source_target_pairs={{0,96},{32,0},{64,32},{96,64},{1,97},{33,1},{65,33},{97,65},{2,98}... | collective-permute-start | bytes 688136 | tf_op jit(solution)/shard_map/ppermute | solution.py:158
  17.4 7.6 %collective-permute-start.4 = (bf16[32,3584]{1,0:T(8,128)(2,1)S(1)}, bf16[32,3584]{1,0:T(8,128)(2,1)S(1)}, u32[]{:S(2)}, u32[]{:S(2)}) collective-permute-start(bf16[32,3584]{1,0:T(8,128)(2,1)S(1)} %slice.131), channel_id=1, source_target_pairs={{0,64},{32,96},{64,0},{96,32},{1,65},{33,97},{65,1},{97,33},{2,66}... | collective-permute-start | bytes 688136 | tf_op jit(solution)/shard_map/ppermute | solution.py:158
  20.4 8.2 %collective-permute-start.5 = (bf16[32,4608]{1,0:T(8,128)(2,1)S(1)}, bf16[32,4608]{1,0:T(8,128)(2,1)S(1)}, u32[]{:S(2)}, u32[]{:S(2)}) collective-permute-start(bf16[32,4608]{1,0:T(8,128)(2,1)S(1)} %slice.132), channel_id=1, source_target_pairs={{0,2},{1,3},{2,0},{3,1},{4,6},{5,7},{6,4},{7,5},{8,10},{9,11},{10,... | collective-permute-start | bytes 884744 | tf_op jit(solution)/shard_map/ppermute | solution.py:158
  22.2 13.6 %collective-permute-start.7 = (bf16[32,3584]{1,0:T(8,128)(2,1)S(1)}, bf16[32,3584]{1,0:T(8,128)(2,1)S(1)}, u32[]{:S(2)}, u32[]{:S(2)}) collective-permute-start(bf16[32,3584]{1,0:T(8,128)(2,1)S(1)} %get-tuple-element.54), channel_id=1, source_target_pairs={{0,96},{32,0},{64,32},{96,64},{1,97},{33,1},{65,33},{97,65},{2,98}... | collective-permute-start | bytes 688136 | tf_op jit(solution)/shard_map/ppermute | solution.py:158
  28.8 15.0 %collective-permute-start.8 = (bf16[2,32,3584]{2,1,0:T(8,128)(2,1)S(1)}, bf16[2,32,3584]{2,1,0:T(8,128)(2,1)S(1)}, u32[]{:S(2)}, u32[]{:S(2)}) collective-permute-start(bf16[2,32,3584]{2,1,0:T(8,128)(2,1)S(1)} %slice.102), channel_id=1, source_target_pairs={{0,16},{16,0},{1,17},{17,1},{2,18},{18,2},{3,19},{19,3},{4,20},{20... | collective-permute-start | bytes 1376264 | tf_op jit(solution)/shard_map/ppermute | solution.py:153
  29.2 8.8 %collective-permute-start.9 = (bf16[32,4608]{1,0:T(8,128)(2,1)S(1)}, bf16[32,4608]{1,0:T(8,128)(2,1)S(1)}, u32[]{:S(2)}, u32[]{:S(2)}) collective-permute-start(bf16[32,4608]{1,0:T(8,128)(2,1)S(1)} %get-tuple-element.52), channel_id=1, source_target_pairs={{0,3},{1,0},{2,1},{3,2},{4,7},{5,4},{6,5},{7,6},{8,11},{9,8},{10,9... | collective-permute-start | bytes 884744 | tf_op jit(solution)/shard_map/ppermute | solution.py:158
  30.9 21.1 %collective-permute-start.10 = (bf16[2,32,4608]{2,1,0:T(8,128)(2,1)S(1)}, bf16[2,32,4608]{2,1,0:T(8,128)(2,1)S(1)}, u32[]{:S(2)}, u32[]{:S(2)}) collective-permute-start(bf16[2,32,4608]{2,1,0:T(8,128)(2,1)S(1)} %slice.104), channel_id=1, source_target_pairs={{0,16},{16,0},{1,17},{17,1},{2,18},{18,2},{3,19},{19,3},{4,20},{20... | collective-permute-start | bytes 1769480 | tf_op jit(solution)/shard_map/ppermute | solution.py:153
  34.2 24.8 %collective-permute-start.14 = (bf16[4,32,4608]{2,1,0:T(8,128)(2,1)S(1)}, bf16[4,32,4608]{2,1,0:T(8,128)(2,1)S(1)}, u32[]{:S(2)}, u32[]{:S(2)}) collective-permute-start(bf16[4,32,4608]{2,1,0:T(8,128)(2,1)S(1)} %pad_maximum_fusion.refs_8_), channel_id=1, source_target_pairs={{0,96},{32,0},{64,32},{96,64},{1,97},{33,1},{65,33},{97,65},{2,98}... | collective-permute-start | bytes 3538952 | tf_op jit(solution)/shard_map/ppermute | solution.py:158
  35.8 24.1 %collective-permute-start.13 = (bf16[4,32,4608]{2,1,0:T(8,128)(2,1)S(1)}, bf16[4,32,4608]{2,1,0:T(8,128)(2,1)}, u32[]{:S(2)}, u32[]{:S(2)}) collective-permute-start(bf16[4,32,4608]{2,1,0:T(8,128)(2,1)S(1)} %pad_maximum_fusion.refs_8_), channel_id=1, source_target_pairs={{0,32},{32,64},{64,96},{96,0},{1,33},{33,65},{65,97},{97,1},{2,34}... | collective-permute-start | bytes 3538952 | tf_op jit(solution)/shard_map/ppermute | solution.py:158
  38.1 17.6 %collective-permute-start.12 = (bf16[4,32,3584]{2,1,0:T(8,128)(2,1)S(1)}, bf16[4,32,3584]{2,1,0:T(8,128)(2,1)S(1)}, u32[]{:S(2)}, u32[]{:S(2)}) collective-permute-start(bf16[4,32,3584]{2,1,0:T(8,128)(2,1)S(1)} %pad_maximum_fusion.2.refs_0_), channel_id=1, source_target_pairs={{0,3},{1,0},{2,1},{3,2},{4,7},{5,4},{6,5},{7,6},{8,11},{9,8},{10,9... | collective-permute-start | bytes 2752520 | tf_op jit(solution)/shard_map/ppermute | solution.py:158
  43.8 14.7 %collective-permute-start.11 = (bf16[4,32,3584]{2,1,0:T(8,128)(2,1)S(1)}, bf16[4,32,3584]{2,1,0:T(8,128)(2,1)S(1)}, u32[]{:S(2)}, u32[]{:S(2)}) collective-permute-start(bf16[4,32,3584]{2,1,0:T(8,128)(2,1)S(1)} %pad_maximum_fusion.2.refs_0_), channel_id=1, source_target_pairs={{0,1},{1,2},{2,3},{3,0},{4,5},{5,6},{6,7},{7,4},{8,9},{9,10},{10,1... | collective-permute-start | bytes 2752520 | tf_op jit(solution)/shard_map/ppermute | solution.py:158
  59.9 24.4 %collective-permute-start.20 = (bf16[4,32,4608]{2,1,0:T(8,128)(2,1)S(1)}, bf16[4,32,4608]{2,1,0:T(8,128)(2,1)S(1)}, u32[]{:S(2)}, u32[]{:S(2)}) collective-permute-start(bf16[4,32,4608]{2,1,0:T(8,128)(2,1)S(1)} %pad_maximum_fusion.1.refs_9_), channel_id=1, source_target_pairs={{0,96},{32,0},{64,32},{96,64},{1,97},{33,1},{65,33},{97,65},{2,98}... | collective-permute-start | bytes 3538952 | tf_op jit(solution)/shard_map/ppermute | solution.py:158
  61.7 15.2 %collective-permute-start.16 = (bf16[4,32,3584]{2,1,0:T(8,128)(2,1)}, bf16[4,32,3584]{2,1,0:T(8,128)(2,1)S(1)}, u32[]{:S(2)}, u32[]{:S(2)}) collective-permute-start(bf16[4,32,3584]{2,1,0:T(8,128)(2,1)} %pad_maximum_fusion.3.refs_1_), channel_id=1, source_target_pairs={{0,3},{1,0},{2,1},{3,2},{4,7},{5,4},{6,5},{7,6},{8,11},{9,8},{10,9... | collective-permute-start | bytes 2752520 | tf_op jit(solution)/shard_map/ppermute | solution.py:158
  62.2 24.0 %collective-permute-start.19 = (bf16[4,32,4608]{2,1,0:T(8,128)(2,1)}, bf16[4,32,4608]{2,1,0:T(8,128)(2,1)S(1)}, u32[]{:S(2)}, u32[]{:S(2)}) collective-permute-start(bf16[4,32,4608]{2,1,0:T(8,128)(2,1)} %collective-permute-done.13.refs_10_), channel_id=1, source_target_pairs={{0,16},{16,0},{1,17},{17,1},{2,18},{18,2},{3,19},{19,3},{4,20},{20... | collective-permute-start | bytes 3538952 | tf_op jit(solution)/shard_map/ppermute | solution.py:153
  63.9 24.7 %collective-permute-start.17 = (bf16[4,32,3584]{2,1,0:T(8,128)(2,1)S(1)}, bf16[4,32,3584]{2,1,0:T(8,128)(2,1)S(1)}, u32[]{:S(2)}, u32[]{:S(2)}) collective-permute-start(bf16[4,32,3584]{2,1,0:T(8,128)(2,1)S(1)} %collective-permute-done.11.refs_2_), channel_id=1, source_target_pairs={{0,1},{1,2},{2,3},{3,0},{4,5},{5,6},{6,7},{7,4},{8,9},{9,10},{10,1... | collective-permute-start | bytes 2752520 | tf_op jit(solution)/shard_map/ppermute | solution.py:158
  64.3 36.8 %collective-permute-start.21 = (bf16[4,32,4608]{2,1,0:T(8,128)(2,1)}, bf16[4,32,4608]{2,1,0:T(8,128)(2,1)}, u32[]{:S(2)}, u32[]{:S(2)}) collective-permute-start(bf16[4,32,4608]{2,1,0:T(8,128)(2,1)} %collective-permute-done.13.refs_10_), channel_id=1, source_target_pairs={{0,32},{32,64},{64,96},{96,0},{1,33},{33,65},{65,97},{97,1},{2,34}... | collective-permute-start | bytes 3538952 | tf_op jit(solution)/shard_map/ppermute | solution.py:158
  76.9 24.2 %collective-permute-start.15 = (bf16[4,32,3584]{2,1,0:T(8,128)(2,1)}, bf16[4,32,3584]{2,1,0:T(8,128)(2,1)}, u32[]{:S(2)}, u32[]{:S(2)}) collective-permute-start(bf16[4,32,3584]{2,1,0:T(8,128)(2,1)} %pad_maximum_fusion.3.refs_1_), channel_id=1, source_target_pairs={{0,1},{1,2},{2,3},{3,0},{4,5},{5,6},{6,7},{7,4},{8,9},{9,10},{10,1... | collective-permute-start | bytes 2752520 | tf_op jit(solution)/shard_map/ppermute | solution.py:158
  84.3 16.8 %collective-permute-start.18 = (bf16[4,32,3584]{2,1,0:T(8,128)(2,1)S(1)}, bf16[4,32,3584]{2,1,0:T(8,128)(2,1)}, u32[]{:S(2)}, u32[]{:S(2)}) collective-permute-start(bf16[4,32,3584]{2,1,0:T(8,128)(2,1)S(1)} %collective-permute-done.16.refs_5_), channel_id=1, source_target_pairs={{0,3},{1,0},{2,1},{3,2},{4,7},{5,4},{6,5},{7,6},{8,11},{9,8},{10,9... | collective-permute-start | bytes 2752520 | tf_op jit(solution)/shard_map/ppermute | solution.py:158
  86.2 14.9 %collective-permute-start.23 = (bf16[2,32,4608]{2,1,0:T(8,128)(2,1)}, bf16[2,32,4608]{2,1,0:T(8,128)(2,1)}, u32[]{:S(2)}, u32[]{:S(2)}) collective-permute-start(bf16[2,32,4608]{2,1,0:T(8,128)(2,1)} %slice.136), channel_id=1, source_target_pairs={{0,96},{32,0},{64,32},{96,64},{1,97},{33,1},{65,33},{97,65},{2,98}... | collective-permute-start | bytes 1769480 | tf_op jit(solution)/shard_map/ppermute | solution.py:158
  88.6 12.4 %collective-permute-start.22 = (bf16[2,32,4608]{2,1,0:T(8,128)(2,1)}, bf16[2,32,4608]{2,1,0:T(8,128)(2,1)}, u32[]{:S(2)}, u32[]{:S(2)}) collective-permute-start(bf16[2,32,4608]{2,1,0:T(8,128)(2,1)} %slice.135), channel_id=1, source_target_pairs={{0,32},{32,64},{64,96},{96,0},{1,33},{33,65},{65,97},{97,1},{2,34}... | collective-permute-start | bytes 1769480 | tf_op jit(solution)/shard_map/ppermute | solution.py:158
  125.4 25.5 %collective-permute-start.30 = (bf16[4,1024,128]{2,1,0:T(8,128)(2,1)S(1)}, bf16[4,1024,128]{2,1,0:T(8,128)(2,1)S(1)}, u32[]{:S(2)}, u32[]{:S(2)}) collective-permute-start(bf16[4,1024,128]{2,1,0:T(8,128)(2,1)S(1)} %fusion.2), channel_id=1, source_target_pairs={{0,8},{8,0},{1,9},{9,1},{2,10},{10,2},{3,11},{11,3},{4,12},{12,4},... | collective-permute-start | bytes 3145736 | tf_op jit(solution)/shard_map/ppermute | solution.py:153
  128.6 27.6 %collective-permute-start.26 = (bf16[2,1024,128]{2,1,0:T(8,128)(2,1)S(1)}, bf16[2,1024,128]{2,1,0:T(8,128)(2,1)S(1)}, u32[]{:S(2)}, u32[]{:S(2)}) collective-permute-start(bf16[2,1024,128]{2,1,0:T(8,128)(2,1)S(1)} %get-tuple-element.48), channel_id=1, source_target_pairs={{0,1},{1,2},{2,3},{3,0},{4,5},{5,6},{6,7},{7,4},{8,9},{9,10},{10,1... | collective-permute-start | bytes 1572872 | tf_op jit(solution)/shard_map/ppermute | solution.py:158
  133.1 24.8 %collective-permute-start.28 = (bf16[2,1024,128]{2,1,0:T(8,128)(2,1)S(1)}, bf16[2,1024,128]{2,1,0:T(8,128)(2,1)S(1)}, u32[]{:S(2)}, u32[]{:S(2)}) collective-permute-start(bf16[2,1024,128]{2,1,0:T(8,128)(2,1)S(1)} %get-tuple-element.49), channel_id=1, source_target_pairs={{0,3},{1,0},{2,1},{3,2},{4,7},{5,4},{6,5},{7,6},{8,11},{9,8},{10,9... | collective-permute-start | bytes 1572872 | tf_op jit(solution)/shard_map/ppermute | solution.py:158
  133.1 24.8 %collective-permute-start.27 = (bf16[2,1024,128]{2,1,0:T(8,128)(2,1)S(1)}, bf16[2,1024,128]{2,1,0:T(8,128)(2,1)S(1)}, u32[]{:S(2)}, u32[]{:S(2)}) collective-permute-start(bf16[2,1024,128]{2,1,0:T(8,128)(2,1)S(1)} %get-tuple-element.50), channel_id=1, source_target_pairs={{0,2},{1,3},{2,0},{3,1},{4,6},{5,7},{6,4},{7,5},{8,10},{9,11},{10,... | collective-permute-start | bytes 1572872 | tf_op jit(solution)/shard_map/ppermute | solution.py:158
  151.3 11.8 %collective-permute-start.31 = (bf16[1024,128]{1,0:T(8,128)(2,1)S(1)}, bf16[1024,128]{1,0:T(8,128)(2,1)S(1)}, u32[]{:S(2)}, u32[]{:S(2)}) collective-permute-start(bf16[1024,128]{1,0:T(8,128)(2,1)S(1)} %get-tuple-element.45), channel_id=1, source_target_pairs={{0,1},{1,2},{2,3},{3,0},{4,5},{5,6},{6,7},{7,4},{8,9},{9,10},{10,1... | collective-permute-start | bytes 786440 | tf_op jit(solution)/shard_map/ppermute | solution.py:158
  155.8 9.2 %collective-permute-start.33 = (bf16[1024,128]{1,0:T(8,128)(2,1)S(1)}, bf16[1024,128]{1,0:T(8,128)(2,1)S(1)}, u32[]{:S(2)}, u32[]{:S(2)}) collective-permute-start(bf16[1024,128]{1,0:T(8,128)(2,1)S(1)} %get-tuple-element.46), channel_id=1, source_target_pairs={{0,3},{1,0},{2,1},{3,2},{4,7},{5,4},{6,5},{7,6},{8,11},{9,8},{10,9... | collective-permute-start | bytes 786440 | tf_op jit(solution)/shard_map/ppermute | solution.py:158
  156.2 13.0 %collective-permute-start.32 = (bf16[1024,128]{1,0:T(8,128)(2,1)S(1)}, bf16[1024,128]{1,0:T(8,128)(2,1)S(1)}, u32[]{:S(2)}, u32[]{:S(2)}) collective-permute-start(bf16[1024,128]{1,0:T(8,128)(2,1)S(1)} %get-tuple-element.47), channel_id=1, source_target_pairs={{0,2},{1,3},{2,0},{3,1},{4,6},{5,7},{6,4},{7,5},{8,10},{9,11},{10,... | collective-permute-start | bytes 786440 | tf_op jit(solution)/shard_map/ppermute | solution.py:158
  158.3 11.1 %collective-permute-start.29 = (bf16[1024,128]{1,0:T(8,128)(2,1)S(1)}, bf16[1024,128]{1,0:T(8,128)(2,1)S(1)}, u32[]{:S(2)}, u32[]{:S(2)}) collective-permute-start(bf16[1024,128]{1,0:T(8,128)(2,1)S(1)} %fusion.20), channel_id=1, source_target_pairs={{0,8},{8,0},{1,9},{9,1},{2,10},{10,2},{3,11},{11,3},{4,12},{12,4},... | collective-permute-start | bytes 786440 | tf_op jit(solution)/shard_map/ppermute | solution.py:153
  (18 other events, 519.3 us)
